TPU v7x, 32 devices: a whole 2x2x4 slice. The times are simulated.
32 devices in a mesh: dp: 16 (over z, x, core), seq: 2 (over y).
Axes of the slice: x: 2, y: 2, z: 4, core: 2. Of those that a mesh axis runs over, the one named last changes fastest.
Arguments:
- tokens: bfloat16 [16, 512, 1152], P('dp', 'seq'), may hold values from -6 to 6
- segment_ids: int32 [16, 512], P('dp'), may hold values from 0 to 3, never falling along the last dimension, each value on 1 to 256 neighbouring positions
- cotangent: bfloat16 [16, 512, 1152], P('dp', 'seq'), may hold values from -6 to 6
- query_weight: bfloat16 [1152, 1024], P(('dp', 'seq')), may hold values from -0.1875 to 0.1875
- key_weight: bfloat16 [1152, 256], P(('dp', 'seq')), may hold values from -0.1875 to 0.1875
- value_weight: bfloat16 [1152, 256], P(('dp', 'seq')), may hold values from -0.1875 to 0.1875
- output_weight: bfloat16 [1024, 1152], P(('dp', 'seq')), may hold values from -0.1875 to 0.1875
- gate_weight: bfloat16 [1152, 6912], P(('dp', 'seq')), may hold values from -0.1875 to 0.1875
- up_weight: bfloat16 [1152, 6912], P(('dp', 'seq')), may hold values from -0.1875 to 0.1875
- down_weight: bfloat16 [6912, 1152], P(('dp', 'seq')), may hold values from -0.078125 to 0.078125
- input_gain: bfloat16 [1152], P(('dp', 'seq')), may hold values from 0.25 to 1.75
- query_gain: bfloat16 [256], P(('dp', 'seq')), may hold values from 0.25 to 1.75
- key_gain: bfloat16 [256], P(('dp', 'seq')), may hold values from 0.25 to 1.75
- attnout_gain: bfloat16 [1152], P(('dp', 'seq')), may hold values from 0.25 to 1.75
- ffnin_gain: bfloat16 [1152], P(('dp', 'seq')), may hold values from 0.25 to 1.75
- ffnout_gain: bfloat16 [1152], P(('dp', 'seq')), may hold values from 0.25 to 1.75
Outputs:
- output: bfloat16 [16, 512, 1152], P('dp', 'seq')
- input_grad: float32 [16, 512, 1152], P('dp', 'seq')
- grad_query: float32 [1152, 1024], P(('dp', 'seq'))
- grad_key: float32 [1152, 256], P(('dp', 'seq'))
- grad_value: float32 [1152, 256], P(('dp', 'seq'))
- grad_output: float32 [1024, 1152], P(('dp', 'seq'))
- grad_gate: float32 [1152, 6912], P(('dp', 'seq'))
- grad_up: float32 [1152, 6912], P(('dp', 'seq'))
- grad_down: float32 [6912, 1152], P(('dp', 'seq'))
- grad_input_gain: float32 [1152], P(('dp', 'seq'))
- grad_query_gain: float32 [256], P(('dp', 'seq'))
- grad_key_gain: float32 [256], P(('dp', 'seq'))
- grad_attnout_gain: float32 [1152], P(('dp', 'seq'))
- grad_ffnin_gain: float32 [1152], P(('dp', 'seq'))
- grad_ffnout_gain: float32 [1152], P(('dp', 'seq'))
Inputs may be any that keep to these rules, and one draw needn't show every extreme that they name: `segment_ids`: in each row the ids never fall and every id occurs; each document spans 1 to 256 positions, one exactly 256.
All inputs are finite; a program needn't handle non-finite values.
Results may differ from a plain program's by a relative error of at most 0.019.
Values may be sent and summed in bfloat16 or wider, within the bound.
A program may use at most 448 MiB of HBM per device.

v0:
```python
import jax
import jax.numpy as jnp
from jax import lax
from jax.sharding import PartitionSpec as P

epsilon = 1e-06
rope_base = 1000000.0
masked_score = -1e30


def inverse_rms(values):
    return lax.rsqrt(jnp.mean(values * values, axis=-1, keepdims=True) + epsilon)


def rms_back(grad_normed, normed, inverse):
    return inverse * (grad_normed - normed * jnp.mean(grad_normed * normed, axis=-1, keepdims=True))


def doc_positions(segments):
    length = segments.shape[-1]
    places = jnp.arange(length, dtype=jnp.int32)
    earlier = jnp.concatenate([segments[:, :1] - 1, segments[:, :-1]], axis=1)
    starts = jnp.where(segments != earlier, places[None, :], jnp.zeros_like(segments))
    return (places[None, :] - lax.cummax(starts, axis=1)).astype(jnp.float32)


def rope_tables(positions, head_width):
    half_width = head_width // 2
    frequency = rope_base ** (-(2.0 / head_width) * jnp.arange(half_width, dtype=jnp.float32))
    angles = positions[..., None] * frequency
    return (jnp.cos(angles), jnp.sin(angles))


def rotate(values, cos_table, sin_table):
    half_width = values.shape[-1] // 2
    first_half = values[..., :half_width]
    second_half = values[..., half_width:]
    return jnp.concatenate(
        [
            first_half * cos_table - second_half * sin_table,
            second_half * cos_table + first_half * sin_table,
        ],
        axis=-1,
    )


def matmul(left, right):
    return jnp.dot(left, right, preferred_element_type=jnp.float32)


def contract_rows(left, right):
    return lax.dot_general(
        left, right, (((0,), (0,)), ((), ())), preferred_element_type=jnp.float32
    )


def contract_cols(left, right):
    return lax.dot_general(
        left, right, (((1,), (1,)), ((), ())), preferred_element_type=jnp.float32
    )


def gelu_pair(gate_proj, up_proj):
    return jax.nn.gelu(gate_proj, approximate=True) * up_proj


def add_sources(received, sources):
    return jnp.sum(
        received.reshape((sources, received.shape[0] // sources) + received.shape[1:]), axis=0
    )


def body(
    tokens,
    segment_ids,
    cotangent,
    query_weight,
    key_weight,
    value_weight,
    output_weight,
    gate_weight,
    up_weight,
    down_weight,
    input_gain,
    query_gain,
    key_gain,
    attnout_gain,
    ffnin_gain,
    ffnout_gain,
):
    (
        query_full,
        key_full,
        value_full,
        output_full,
        input_scale,
        query_scale,
        key_scale,
        attnout_scale,
        ffnin_scale,
        ffnout_scale,
    ) = (
        lax.all_gather(query_weight, ("dp", "seq"), axis=0, tiled=True),
        lax.all_gather(key_weight, ("dp", "seq"), axis=0, tiled=True),
        lax.all_gather(value_weight, ("dp", "seq"), axis=0, tiled=True),
        lax.all_gather(output_weight, ("dp", "seq"), axis=0, tiled=True),
        lax.all_gather(input_gain, ("dp", "seq"), axis=0, tiled=True),
        lax.all_gather(query_gain, ("dp", "seq"), axis=0, tiled=True),
        lax.all_gather(key_gain, ("dp", "seq"), axis=0, tiled=True),
        lax.all_gather(attnout_gain, ("dp", "seq"), axis=0, tiled=True),
        lax.all_gather(ffnin_gain, ("dp", "seq"), axis=0, tiled=True),
        lax.all_gather(ffnout_gain, ("dp", "seq"), axis=0, tiled=True),
    )
    input_scale = input_scale.astype(jnp.float32)
    query_scale = query_scale.astype(jnp.float32)
    key_scale = key_scale.astype(jnp.float32)
    attnout_scale = attnout_scale.astype(jnp.float32)
    ffnin_scale = ffnin_scale.astype(jnp.float32)
    ffnout_scale = ffnout_scale.astype(jnp.float32)
    hidden = tokens[0].astype(jnp.float32)
    incoming = cotangent[0].astype(jnp.float32)
    local_rows = hidden.shape[0]
    head_width = key_weight.shape[1]
    head_count = query_weight.shape[1] // head_width
    seq_count = lax.axis_size("seq")
    full_length = local_rows * seq_count
    offset = lax.axis_index("seq") * local_rows
    segment_row = segment_ids[0]
    my_positions = lax.dynamic_slice_in_dim(doc_positions(segment_ids)[0], offset, local_rows)
    my_segments = lax.dynamic_slice_in_dim(segment_row, offset, local_rows)
    cos_table, sin_table = rope_tables(my_positions, head_width)
    scale = head_width ** (-0.5)
    inv_input = inverse_rms(hidden)
    norm_input = hidden * inv_input
    normed = (norm_input * input_scale).astype(jnp.bfloat16)
    query_raw = matmul(normed, query_full).reshape(local_rows, head_count, head_width)
    key_raw = matmul(normed, key_full)
    value_raw = matmul(normed, value_full)
    inv_query = inverse_rms(query_raw)
    norm_query = query_raw * inv_query
    queries = (
        rotate(norm_query * query_scale, cos_table[:, None, :], sin_table[:, None, :]) * scale
    ).astype(jnp.bfloat16)
    inv_key = inverse_rms(key_raw)
    norm_key = key_raw * inv_key
    keys_local = rotate(norm_key * key_scale, cos_table, sin_table).astype(jnp.bfloat16)
    values_local = value_raw.astype(jnp.bfloat16)
    key_rows, value_rows = (
        lax.all_gather(keys_local, "seq", axis=0, tiled=True),
        lax.all_gather(values_local, "seq", axis=0, tiled=True),
    )
    query_places = offset + jnp.arange(local_rows, dtype=jnp.int32)
    key_places = jnp.arange(full_length, dtype=jnp.int32)
    allowed = (my_segments[:, None] == segment_row[None, :]) & (
        query_places[:, None] >= key_places[None, :]
    )

    def masked_scores():
        raw_scores = jnp.einsum(
            "qhd,kd->hqk", queries, key_rows, preferred_element_type=jnp.float32
        )
        return jnp.where(allowed[None], raw_scores, masked_score)

    scores = masked_scores()
    peak = jnp.max(scores, axis=-1, keepdims=True)
    log_total = peak + jnp.log(jnp.sum(jnp.exp(scores - peak), axis=-1, keepdims=True))
    probs_low = jnp.exp(scores - log_total).astype(jnp.bfloat16)
    attn_mix = jnp.einsum("hqk,kd->qhd", probs_low, value_rows, preferred_element_type=jnp.float32)
    attn_flat = attn_mix.astype(jnp.bfloat16).reshape(local_rows, head_count * head_width)
    attn_raw = matmul(attn_flat, output_full)
    inv_attn = inverse_rms(attn_raw)
    norm_attn = attn_raw * inv_attn
    middle = hidden + norm_attn * attnout_scale
    inv_middle = inverse_rms(middle)
    norm_middle = middle * inv_middle
    ffn_in = (norm_middle * ffnin_scale).astype(jnp.bfloat16)
    gate_full, up_full, down_full = (
        lax.all_gather(gate_weight, ("dp", "seq"), axis=0, tiled=True),
        lax.all_gather(up_weight, ("dp", "seq"), axis=0, tiled=True),
        lax.all_gather(down_weight, ("dp", "seq"), axis=0, tiled=True),
    )
    gate_proj = matmul(ffn_in, gate_full)
    up_proj = matmul(ffn_in, up_full)
    activated, gelu_back = jax.vjp(gelu_pair, gate_proj, up_proj)
    activated_low = activated.astype(jnp.bfloat16)
    ffn_raw = matmul(activated_low, down_full)
    inv_ffn = inverse_rms(ffn_raw)
    norm_ffn = ffn_raw * inv_ffn
    result = middle + norm_ffn * ffnout_scale
    ffnout_gain_grad = jnp.sum(incoming * norm_ffn, axis=0)
    ffn_raw_grad = rms_back(incoming * ffnout_scale, norm_ffn, inv_ffn).astype(jnp.bfloat16)
    result, ffnout_gain_grad, ffn_raw_grad = (result, ffnout_gain_grad, ffn_raw_grad)
    act_grad = contract_cols(ffn_raw_grad, down_full)
    gate_grad, up_grad = gelu_back(act_grad)
    gate_low = gate_grad.astype(jnp.bfloat16)
    up_low = up_grad.astype(jnp.bfloat16)
    ffn_in_grad = contract_cols(gate_low, gate_full) + contract_cols(up_low, up_full)
    all_count = lax.axis_size(("dp", "seq"))
    gate_terms, up_terms, down_terms = (
        lax.all_to_all(
            contract_rows(ffn_in, gate_low).astype(jnp.bfloat16),
            ("dp", "seq"),
            split_axis=0,
            concat_axis=0,
            tiled=True,
        ).astype(jnp.float32),
        lax.all_to_all(
            contract_rows(ffn_in, up_low).astype(jnp.bfloat16),
            ("dp", "seq"),
            split_axis=0,
            concat_axis=0,
            tiled=True,
        ).astype(jnp.float32),
        lax.all_to_all(
            contract_rows(activated_low, ffn_raw_grad).astype(jnp.bfloat16),
            ("dp", "seq"),
            split_axis=0,
            concat_axis=0,
            tiled=True,
        ).astype(jnp.float32),
    )
    gate_wgrad = add_sources(gate_terms, all_count)
    up_wgrad = add_sources(up_terms, all_count)
    down_wgrad = add_sources(down_terms, all_count)
    ffnin_gain_grad = jnp.sum(ffn_in_grad * norm_middle, axis=0)
    middle_grad = incoming + rms_back(ffn_in_grad * ffnin_scale, norm_middle, inv_middle)
    attnout_gain_grad = jnp.sum(middle_grad * norm_attn, axis=0)
    attn_raw_grad = rms_back(middle_grad * attnout_scale, norm_attn, inv_attn).astype(jnp.bfloat16)
    output_wgrad = contract_rows(attn_flat, attn_raw_grad)
    mix_grad = (
        contract_cols(attn_raw_grad, output_full)
        .astype(jnp.bfloat16)
        .reshape(local_rows, head_count, head_width)
    )
    probs_again = jnp.exp(masked_scores() - log_total)
    prob_grad = jnp.einsum("qhd,kd->hqk", mix_grad, value_rows, preferred_element_type=jnp.float32)
    row_delta = jnp.sum(prob_grad * probs_again, axis=-1, keepdims=True)
    score_grad = (probs_again * (prob_grad - row_delta)).astype(jnp.bfloat16)
    value_grad_rows = jnp.einsum(
        "hqk,qhd->kd",
        probs_again.astype(jnp.bfloat16),
        mix_grad,
        preferred_element_type=jnp.float32,
    )
    key_grad_rows = jnp.einsum(
        "hqk,qhd->kd", score_grad, queries, preferred_element_type=jnp.float32
    )
    query_grad = jnp.einsum("hqk,kd->qhd", score_grad, key_rows, preferred_element_type=jnp.float32)
    key_grad, value_grad = (
        lax.psum_scatter(
            key_grad_rows.astype(jnp.bfloat16), "seq", scatter_dimension=0, tiled=True
        ).astype(jnp.float32),
        lax.psum_scatter(
            value_grad_rows.astype(jnp.bfloat16), "seq", scatter_dimension=0, tiled=True
        ).astype(jnp.float32),
    )
    query_norm_grad = rotate(query_grad * scale, cos_table[:, None, :], -sin_table[:, None, :])
    query_gain_grad = jnp.sum(query_norm_grad * norm_query, axis=(0, 1))
    query_raw_low = rms_back(query_norm_grad * query_scale, norm_query, inv_query).astype(
        jnp.bfloat16
    )
    query_raw_low = query_raw_low.reshape(local_rows, head_count * head_width)
    key_norm_grad = rotate(key_grad, cos_table, -sin_table)
    key_gain_grad = jnp.sum(key_norm_grad * norm_key, axis=0)
    key_raw_low = rms_back(key_norm_grad * key_scale, norm_key, inv_key).astype(jnp.bfloat16)
    value_raw_low = value_grad.astype(jnp.bfloat16)
    query_wgrad = contract_rows(normed, query_raw_low)
    key_wgrad = contract_rows(normed, key_raw_low)
    value_wgrad = contract_rows(normed, value_raw_low)
    normed_grad = (
        contract_cols(query_raw_low, query_full)
        + contract_cols(key_raw_low, key_full)
        + contract_cols(value_raw_low, value_full)
    )
    input_gain_grad = jnp.sum(normed_grad * norm_input, axis=0)
    input_grad = middle_grad + rms_back(normed_grad * input_scale, norm_input, inv_input)
    (
        query_share,
        key_share,
        value_share,
        output_share,
        input_gain_share,
        query_gain_share,
        key_gain_share,
        attnout_gain_share,
        ffnin_gain_share,
        ffnout_gain_share,
    ) = (
        lax.psum_scatter(query_wgrad, ("dp", "seq"), scatter_dimension=0, tiled=True),
        lax.psum_scatter(key_wgrad, ("dp", "seq"), scatter_dimension=0, tiled=True),
        lax.psum_scatter(value_wgrad, ("dp", "seq"), scatter_dimension=0, tiled=True),
        lax.psum_scatter(output_wgrad, ("dp", "seq"), scatter_dimension=0, tiled=True),
        lax.psum_scatter(input_gain_grad, ("dp", "seq"), scatter_dimension=0, tiled=True),
        lax.psum_scatter(query_gain_grad, ("dp", "seq"), scatter_dimension=0, tiled=True),
        lax.psum_scatter(key_gain_grad, ("dp", "seq"), scatter_dimension=0, tiled=True),
        lax.psum_scatter(attnout_gain_grad, ("dp", "seq"), scatter_dimension=0, tiled=True),
        lax.psum_scatter(ffnin_gain_grad, ("dp", "seq"), scatter_dimension=0, tiled=True),
        lax.psum_scatter(ffnout_gain_grad, ("dp", "seq"), scatter_dimension=0, tiled=True),
    )
    return (
        result.astype(jnp.bfloat16)[None],
        input_grad[None],
        query_share,
        key_share,
        value_share,
        output_share,
        gate_wgrad,
        up_wgrad,
        down_wgrad,
        input_gain_share,
        query_gain_share,
        key_gain_share,
        attnout_gain_share,
        ffnin_gain_share,
        ffnout_gain_share,
    )


def solution(mesh):
    placed = (
        P("dp", "seq", None),
        P("dp", None),
        P("dp", "seq", None),
        P(("dp", "seq"), None),
        P(("dp", "seq"), None),
        P(("dp", "seq"), None),
        P(("dp", "seq"), None),
        P(("dp", "seq"), None),
        P(("dp", "seq"), None),
        P(("dp", "seq"), None),
        P(("dp", "seq")),
        P(("dp", "seq")),
        P(("dp", "seq")),
        P(("dp", "seq")),
        P(("dp", "seq")),
        P(("dp", "seq")),
    )
    return jax.shard_map(
        body,
        mesh=mesh,
        in_specs=placed,
        out_specs=(
            P("dp", "seq", None),
            P("dp", "seq", None),
            P(("dp", "seq"), None),
            P(("dp", "seq"), None),
            P(("dp", "seq"), None),
            P(("dp", "seq"), None),
            P(("dp", "seq"), None),
            P(("dp", "seq"), None),
            P(("dp", "seq"), None),
            P(("dp", "seq")),
            P(("dp", "seq")),
            P(("dp", "seq")),
            P(("dp", "seq")),
            P(("dp", "seq")),
            P(("dp", "seq")),
        ),
        check_vma=False,
    )
```

profile of v0, /device:TPU:8, one launch (start us, length us, event | category | flops | bytes accessed | tf_op | source)
XLA Modules:
  0.0 1990.0 jit_solution(7380283980346564550)
XLA Ops:
  15.8 41.2 %all-reduce.19 = (bf16[1152]{0:T(1024)(128)(2,1)S(1)}, bf16[256]{0:T(256)(128)(2,1)S(1)}, bf16[256]{0:T(256)(128)(2,1)S(1)}, bf16[1152]{0:T(1024)(128)(2,1)S(1)}...) all-reduce(bf16[1152]{0:T(1024)(128)(2,1)S(1)} %dynamic-update-slic, ...), channel_id=1, replica_groups=mesh['dp'=16,'seq'=2] {'dp','seq'}, use_global_device_ids=true, to_apply=%add | all-reduce | flops 5120 | bytes 20480
  57.0 57.8 %all-gather = bf16[32,36,256]{2,1,0:T(8,128)(2,1)S(1)} all-gather(bf16[1,36,256]{2,1,0:T(8,128)(2,1)} %bitcast.191), channel_id=1, replica_groups=mesh['dp'=16,'seq'=2] {'dp','seq'}, dimensions={0}, use_global_device_ids=true | all-gather | bytes 608256 | tf_op jit(solution)/shard_map/all_gather | solution.py:105
  117.0 70.1 %all-gather.1 = bf16[32,36,256]{2,1,0:T(8,128)(2,1)S(1)} all-gather(bf16[1,36,256]{2,1,0:T(8,128)(2,1)S(1)} %bitcast.192), channel_id=1, replica_groups=mesh['dp'=16,'seq'=2] {'dp','seq'}, dimensions={0}, use_global_device_ids=true | all-gather | bytes 608256 | tf_op jit(solution)/shard_map/all_gather | solution.py:104
  196.7 9.4 all_gather.50
  227.8 28.8 %all-gather.17.cloned.1.call-done = bf16[32,36,6912]{2,1,0:T(8,128)(2,1)} async-done(((bf16[1,36,6912]{2,1,0:T(8,128)(2,1)}), bf16[32,36,6912]{2,1,0:T(8,128)(2,1)}) %all-gather.17.cloned.1.call-update) | async-done | bytes 15925264 | tf_op jit(solution)/shard_map/all_gather | solution.py:178
  256.6 18.4 reshape.393
  275.0 102.3 %all-gather.19.cloned.1.call-done = bf16[32,36,6912]{2,1,0:T(8,128)(2,1)} async-done(((bf16[1,36,6912]{2,1,0:T(8,128)(2,1)}), bf16[32,36,6912]{2,1,0:T(8,128)(2,1)}) %all-gather.19.cloned.1.call-update) | async-done | bytes 15925264 | tf_op jit(solution)/shard_map/all_gather | solution.py:179
  377.3 18.5 reshape.395
  395.8 12.5 fusion.94
  408.3 11.0 multiply_convert_fusion.1
  419.3 70.2 %all-gather.13.cloned.1.call-done = bf16[6912,1152]{1,0:T(8,128)(2,1)} async-done(((bf16[216,1152]{1,0:T(8,128)(2,1)}), bf16[6912,1152]{1,0:T(8,128)(2,1)}) %all-gather.13.cloned.1.call-update) | async-done | bytes 15925264 | tf_op jit(solution)/shard_map/all_gather | solution.py:180
  489.4 10.6 multiply_reduce_fusion.4
  501.8 15.8 multiply_convert_fusion
  517.6 9.9 convolution_convert_fusion.1
  527.5 18.1 all_to_all.18
  550.6 10.9 convolution_convert_fusion.2
  561.6 372.9 %all-to-all-done = bf16[32,36,6912]{2,1,0:T(8,128)(2,1)} async-done(((bf16[32,36,6912]{2,1,0:T(8,128)(2,1)}), bf16[32,36,6912]{2,1,0:T(8,128)(2,1)}, u32[]{:S(2)}, u32[]{:S(2)}) %all-to-all-start) | async-done | bytes 15925280 | tf_op jit(solution)/shard_map/all_to_all | solution.py:200
  934.4 16.4 all-to-all-start.2
  950.8 9.8 convolution_convert_fusion
  960.6 18.1 all_to_all.20
  978.8 317.4 %all-to-all-done.2 = bf16[32,216,1152]{2,1,0:T(8,128)(2,1)} async-done(((bf16[32,216,1152]{2,1,0:T(8,128)(2,1)}), bf16[32,216,1152]{2,1,0:T(8,128)(2,1)}, u32[]{:S(2)}, u32[]{:S(2)}) %all-to-all-start.2) | async-done | bytes 15925280 | tf_op jit(solution)/shard_map/all_to_all | solution.py:214
  1296.1 13.3 all-to-all-start.1
  1309.5 12.4 fusion.95
  1321.9 12.7 multiply_reduce_fusion
  1351.4 10.3 reduce-scatter.10.cloned.1.call-done
  1370.9 68.4 %reduce-scatter.12.cloned.1.call-done = bf16[256,256]{1,0:T(8,128)(2,1)} async-done(((bf16[512,256]{1,0:T(8,128)(2,1)}), bf16[256,256]{1,0:T(8,128)(2,1)}) %reduce-scatter.12.cloned.1.call-update) | async-done | bytes 131088 | tf_op jit(solution)/shard_map/reduce_scatter | solution.py:253
  1444.8 402.6 %fusion.91 = (f32[40,1024]{1,0:T(8,128)}, f32[40,256]{1,0:T(8,128)}, f32[40,256]{1,0:T(8,128)S(1)}) fusion(f32[1152,1024]{1,0:T(8,128)} %fusion.45, f32[1152,256]{1,0:T(8,128)} %fusion.86, f32[1152,256]{1,0:T(8,128)} %fusion.84), kind=kCustom, calls=%all-reduce-scatter.3 | all-reduce-scatter fusion | flops 1966081 | bytes 7323648
  1848.1 16.7 collective-permute-start.6
  1864.8 8.7 collective-permute-start.5
  1886.4 42.1 %all-reduce.18 = (f32[1152]{0:T(1024)S(1)}, f32[256]{0:T(256)S(1)}, f32[256]{0:T(256)S(1)}, f32[1152]{0:T(1024)S(1)}, f32[1152]{0:T(1024)S(1)}, /*index=5*/f32[1152]{0:T(1024)S(1)}) all-reduce(f32[1152]{0:T(1024)S(1)} %get-tuple-element.23, f32[256]{0:T(256)S(1)} %get-tuple-element.19, ...), channel_id=8, replica_groups=mesh['dp'=16,'seq'=2] {'dp','seq'}, use_global_device_ids=true, to_apply=%region_27.28.clone | all-reduce | flops 5120 | bytes 40960
  1966.6 8.1 convert_reduce_fusion.1
  1974.7 8.1 convert_reduce_fusion
  (313 shorter events, 130.1 us)
Async XLA Ops:
  7.2 107.8 %copy-start.59 = (s32[1,512]{1,0:T(1,128)S(1)}, s32[1,512]{1,0:T(1,128)}, u32[]{:S(2)}) copy-start(s32[1,512]{1,0:T(1,128)} %param.17) | copy-start | bytes 6148
  7.2 109.8 %copy-start.60 = (bf16[36,256]{1,0:T(8,128)(2,1)S(1)}, bf16[36,256]{1,0:T(8,128)(2,1)}, u32[]{:S(2)}) copy-start(bf16[36,256]{1,0:T(8,128)(2,1)} %param.20) | copy-start | bytes 55300
  7.2 199.1 %all-gather.15.cloned.1.call-start = ((), (), s32[]{:S(2)}) async-start(), calls=%async_computation.11 | async-start | bytes 2703360 | tf_op jit(solution)/shard_map/all_gather | solution.py:103
  7.9 215.8 %all-gather.11.cloned.1.call-start = ((), (), s32[]{:S(2)}) async-start(), calls=%async_computation.6 | async-start | bytes 2433024 | tf_op jit(solution)/shard_map/all_gather | solution.py:106
  8.7 247.9 %all-gather.17.cloned.1.call-start = ((), (), s32[]{:S(2)}) async-start(), calls=%async_computation.12 | async-start | bytes 18247680 | tf_op jit(solution)/shard_map/all_gather | solution.py:178
  9.4 367.9 %all-gather.19.cloned.1.call-start = ((), (), s32[]{:S(2)}) async-start(), calls=%async_computation.13 | async-start | bytes 18247680 | tf_op jit(solution)/shard_map/all_gather | solution.py:179
  10.0 479.4 %all-gather.13.cloned.1.call-start = ((), (), s32[]{:S(2)}) async-start(), calls=%async_computation.7 | async-start | bytes 16422912 | tf_op jit(solution)/shard_map/all_gather | solution.py:180
  10.6 176.8 %copy-start = (bf16[1,256,1152]{2,1,0:T(8,128)(2,1)S(1)}, bf16[1,256,1152]{2,1,0:T(8,128)(2,1)}, u32[]{:S(2)}) copy-start(bf16[1,256,1152]{2,1,0:T(8,128)(2,1)} %param.16) | copy-start | bytes 1769476
  57.0 169.6 %copy-start.49 = (f32[1152]{0:T(1024)}, f32[1152]{0:T(1024)S(1)}, u32[]{:S(2)}) copy-start(f32[1152]{0:T(1024)S(1)} %convert_element_type.151) | copy-start | bytes 13828
  114.9 74.8 %copy-start.20 = (bf16[1152,256]{1,0:T(8,128)(2,1)}, bf16[1152,256]{1,0:T(8,128)(2,1)S(1)}, u32[]{:S(2)}) copy-start(bf16[1152,256]{1,0:T(8,128)(2,1)S(1)} %reshape.387) | copy-start | bytes 1769476
  115.0 96.9 %copy-start.46 = (f32[1152]{0:T(1024)}, f32[1152]{0:T(1024)S(1)}, u32[]{:S(2)}) copy-start(f32[1152]{0:T(1024)S(1)} %convert_element_type.138) | copy-start | bytes 13828
  115.0 99.6 %copy-start.65 = (f32[256]{0:T(256)}, f32[256]{0:T(256)S(1)}, u32[]{:S(2)}) copy-start(f32[256]{0:T(256)S(1)} %convert_element_type.146) | copy-start | bytes 3076
  545.6 388.8 %all-to-all-start = ((bf16[32,36,6912]{2,1,0:T(8,128)(2,1)}), bf16[32,36,6912]{2,1,0:T(8,128)(2,1)}, u32[]{:S(2)}, u32[]{:S(2)}) async-start(bf16[32,36,6912]{2,1,0:T(8,128)(2,1)} %all_to_all.18), calls=%async_computation.3 | async-start | bytes 35389440 | tf_op jit(solution)/shard_map/all_to_all | solution.py:200
  934.4 361.7 %all-to-all-start.2 = ((bf16[32,216,1152]{2,1,0:T(8,128)(2,1)}), bf16[32,216,1152]{2,1,0:T(8,128)(2,1)}, u32[]{:S(2)}, u32[]{:S(2)}) async-start(bf16[32,216,1152]{2,1,0:T(8,128)(2,1)} %bitcast.177), calls=%async_computation.5 | async-start | bytes 31850496 | tf_op jit(solution)/shard_map/all_to_all | solution.py:214
  1296.1 678.6 %all-to-all-start.1 = ((bf16[32,36,6912]{2,1,0:T(8,128)(2,1)}), bf16[32,36,6912]{2,1,0:T(8,128)(2,1)}, u32[]{:S(2)}, u32[]{:S(2)}) async-start(bf16[32,36,6912]{2,1,0:T(8,128)(2,1)} %all_to_all.20), calls=%async_computation.4 | async-start | bytes 35389440 | tf_op jit(solution)/shard_map/all_to_all | solution.py:207
  1309.4 52.3 %reduce-scatter.10.cloned.1.call-start = ((), (), s32[]{:S(2)}) async-start(), calls=%async_computation.8 | async-start | bytes 393216 | tf_op jit(solution)/shard_map/reduce_scatter | solution.py:250
  1343.8 95.5 %reduce-scatter.12.cloned.1.call-start = ((), (), s32[]{:S(2)}) async-start(), calls=%async_computation.9 | async-start | bytes 393216 | tf_op jit(solution)/shard_map/reduce_scatter | solution.py:253
  1346.2 636.5 %reduce-scatter.14.cloned.1.call-start = ((), (), s32[]{:S(2)}) async-start(), calls=%async_computation.10 | async-start | bytes 4866048 | tf_op jit(solution)/shard_map/reduce_scatter | solution.py:292
  1444.8 433.2 %copy-start.5 = (bf16[1152,1024]{1,0:T(8,128)(2,1)S(1)}, bf16[1152,1024]{1,0:T(8,128)(2,1)}, u32[]{:S(2)}) copy-start(bf16[1152,1024]{1,0:T(8,128)(2,1)} %copy-done.4) | copy-start | bytes 7077892
  1848.1 83.9 %collective-permute-start.6 = (f32[40,256]{1,0:T(8,128)}, f32[40,256]{1,0:T(8,128)}, u32[]{:S(2)}, u32[]{:S(2)}) collective-permute-start(f32[40,256]{1,0:T(8,128)} %get-tuple-element.43), channel_id=1, source_target_pairs={{0,3},{1,4},{2,5},{3,6},{4,7},{5,8},{6,9},{7,10},{8,11},{9,12},{10... | collective-permute-start | bytes 122888
  1864.8 69.4 %collective-permute-start.5 = (f32[40,256]{1,0:T(8,128)}, f32[40,256]{1,0:T(8,128)}, u32[]{:S(2)}, u32[]{:S(2)}) collective-permute-start(f32[40,256]{1,0:T(8,128)} %get-tuple-element.43), channel_id=1, source_target_pairs={{0,2},{1,3},{2,4},{3,5},{4,6},{5,7},{6,8},{7,9},{8,10},{9,11},{10,... | collective-permute-start | bytes 122888
  1873.6 64.9 %collective-permute-start.4 = (f32[40,256]{1,0:T(8,128)}, f32[40,256]{1,0:T(8,128)}, u32[]{:S(2)}, u32[]{:S(2)}) collective-permute-start(f32[40,256]{1,0:T(8,128)} %get-tuple-element.43), channel_id=1, source_target_pairs={{0,1},{1,2},{2,3},{3,4},{4,5},{5,6},{6,7},{7,8},{8,9},{9,10},{10,1... | collective-permute-start | bytes 122888
  1875.5 7.5 collective-permute-start.7
  1880.5 66.1 %collective-permute-start.10 = (f32[40,256]{1,0:T(8,128)S(1)}, f32[40,256]{1,0:T(8,128)S(1)}, u32[]{:S(2)}, u32[]{:S(2)}) collective-permute-start(f32[40,256]{1,0:T(8,128)S(1)} %get-tuple-element.44), channel_id=1, source_target_pairs={{0,3},{1,4},{2,5},{3,6},{4,7},{5,8},{6,9},{7,10},{8,11},{9,12},{10... | collective-permute-start | bytes 122888
  1883.0 61.7 %collective-permute-start.11 = (f32[4,256]{1,0:T(4,128)S(1)}, f32[4,256]{1,0:T(4,128)S(1)}, u32[]{:S(2)}, u32[]{:S(2)}) collective-permute-start(f32[4,256]{1,0:T(4,128)S(1)} %slice.58), channel_id=1, source_target_pairs={{0,4},{1,5},{2,6},{3,7},{4,8},{5,9},{6,10},{7,11},{8,12},{9,13},{1... | collective-permute-start | bytes 12296
  1885.0 56.4 %copy-start.48 = (f32[40,256]{1,0:T(8,128)S(1)}, f32[40,256]{1,0:T(8,128)}, u32[]{:S(2)}) copy-start(f32[40,256]{1,0:T(8,128)} %get-tuple-element.43) | copy-start | bytes 122884
  1932.0 25.6 %collective-permute-start.2 = (f32[40,1024]{1,0:T(8,128)S(1)}, f32[40,1024]{1,0:T(8,128)S(1)}, u32[]{:S(2)}, u32[]{:S(2)}) collective-permute-start(f32[40,1024]{1,0:T(8,128)S(1)} %copy-done.43), channel_id=1, source_target_pairs={{0,3},{1,4},{2,5},{3,6},{4,7},{5,8},{6,9},{7,10},{8,11},{9,12},{10... | collective-permute-start | bytes 491528
  1934.2 23.4 %collective-permute-start.1 = (f32[40,1024]{1,0:T(8,128)S(1)}, f32[40,1024]{1,0:T(8,128)S(1)}, u32[]{:S(2)}, u32[]{:S(2)}) collective-permute-start(f32[40,1024]{1,0:T(8,128)S(1)} %copy-done.43), channel_id=1, source_target_pairs={{0,2},{1,3},{2,4},{3,5},{4,6},{5,7},{6,8},{7,9},{8,10},{9,11},{10,... | collective-permute-start | bytes 491528
  1938.4 19.2 collective-permute-start
  1944.7 6.3 collective-permute-start.9
  1946.7 7.1 collective-permute-start.8
  1951.1 6.5 collective-permute-start.3
  (68 other events, 474.6 us)
Sparse Core Ops, SparseCore 0:
  10.9 58.2 all-gather.14
  72.2 56.6 all-gather.10
  131.8 124.7 all-gather.16
  259.4 117.8 all-gather.18
  380.0 109.3 all-gather.12
  1343.9 17.7 reduce-scatter.9
  1364.0 75.2 reduce-scatter.11
  1445.4 188.9 reduce-scatter.13
where the time goes:
time: 2000 us; the launch traced here: 1990 us
  waiting for transfers between devices  976 us (49%)
  blocking collectives  630 us (32%)
  matrix products  131 us (7%)
  local copies, waits for them, and re-layouts  110 us (6%)
  starting transfers between devices  87.1 us (4%)
  other arithmetic  40.2 us (2%)
    unnamed x3, blocking collectives  486 us
    all_to_all x1, waiting for transfers between devices, body(): lax.all_to_all(contract_rows(ffn_in, gate_low).astype(jnp.bfloat16), ('dp...  373 us
    all_to_all x1, waiting for transfers between devices, body(): lax.all_to_all(contract_rows(activated_low, ffn_raw_grad).astype(jnp.bflo...  317 us
    all_gather x1, waiting for transfers between devices, body(): lax.all_gather(up_weight, ('dp', 'seq'), axis=0, tiled=True)  102 us
    all_gather x1, waiting for transfers between devices, body(): lax.all_gather(down_weight, ('dp', 'seq'), axis=0, tiled=True)  70.2 us
    all_gather x1, blocking collectives, body(): lax.all_gather(key_weight, ('dp', 'seq'), axis=0, tiled=True)  70.1 us
    reduce_scatter x1, waiting for transfers between devices, body(): lax.psum_scatter(value_grad_rows.astype(jnp.bfloat16), 'seq', scatter_dim...  68.4 us
    unnamed x187, local copies, waits for them, and re-layouts  65 us
  transfers between devices with their start and end apart: 23, of which 8 were waited for; matrix products, arithmetic and copies ran while one was open for 30% of the time, Pallas kernels for 0%

commit v1 on v0

v1 whole, which is shorter than its diff:
```python
import jax
import jax.numpy as jnp
from jax import lax
from jax.sharding import Mesh
from jax.sharding import PartitionSpec as P

epsilon = 1e-06
rope_base = 1000000.0
masked_score = -1e30


def inverse_rms(values):
    return lax.rsqrt(jnp.mean(values * values, axis=-1, keepdims=True) + epsilon)


def rms_back(grad_normed, normed, inverse):
    return inverse * (grad_normed - normed * jnp.mean(grad_normed * normed, axis=-1, keepdims=True))


def doc_positions(segments):
    length = segments.shape[0]
    smaller = segments[None, :] < segments[:, None]
    starts = jnp.sum(smaller.astype(jnp.int32), axis=1)
    return (jnp.arange(length, dtype=jnp.int32) - starts).astype(jnp.float32)


def rope_tables(positions, head_width):
    half_width = head_width // 2
    frequency = rope_base ** (-(2.0 / head_width) * jnp.arange(half_width, dtype=jnp.float32))
    angles = positions[..., None] * frequency
    return (jnp.cos(angles), jnp.sin(angles))


def rotate(values, cos_table, sin_table):
    half_width = values.shape[-1] // 2
    first_half = values[..., :half_width]
    second_half = values[..., half_width:]
    return jnp.concatenate(
        [
            first_half * cos_table - second_half * sin_table,
            second_half * cos_table + first_half * sin_table,
        ],
        axis=-1,
    )


def matmul(left, right):
    return jnp.dot(left, right, preferred_element_type=jnp.float32)


def contract_rows(left, right):
    return lax.dot_general(
        left, right, (((0,), (0,)), ((), ())), preferred_element_type=jnp.float32
    )


def contract_cols(left, right):
    return lax.dot_general(
        left, right, (((1,), (1,)), ((), ())), preferred_element_type=jnp.float32
    )


def gelu_pair(gate_proj, up_proj):
    return jax.nn.gelu(gate_proj, approximate=True) * up_proj


ALL = ("z", "x", "core", "seq")
PLANE = ("x", "core", "seq")


def exchange(blocks, axes):
    return lax.all_to_all(blocks, axes, split_axis=0, concat_axis=0, tiled=True)


def plane_gather(local):
    return lax.all_gather(local, PLANE, axis=0, tiled=True)


def plane_scatter_sum(partial):
    members = lax.axis_size(PLANE)
    terms = exchange(partial.reshape((members, -1) + partial.shape[1:]), PLANE)
    return jnp.sum(terms.astype(jnp.float32), axis=0)


def body(
    tokens,
    segment_ids,
    cotangent,
    query_weight,
    key_weight,
    value_weight,
    output_weight,
    gate_weight,
    up_weight,
    down_weight,
    input_gain,
    query_gain,
    key_gain,
    attnout_gain,
    ffnin_gain,
    ffnout_gain,
):
    bf16, f32 = jnp.bfloat16, jnp.float32
    devices = lax.axis_size(ALL)
    members = lax.axis_size(PLANE)
    planes = lax.axis_size("z")
    seq_count = lax.axis_size("seq")
    width_rows = query_weight.shape[0]
    hidden_rows = down_weight.shape[0]
    head_width = key_weight.shape[1]
    query_width = query_weight.shape[1]
    head_count = query_width // head_width
    qkv_width = query_width + 2 * head_width
    mix_rows = output_weight.shape[0]
    padded = (width_rows + 1 + 7) // 8 * 8

    gains = (input_gain, query_gain, key_gain, attnout_gain, ffnin_gain, ffnout_gain)
    gain_row = jnp.concatenate(gains)
    gain_widths = [g.shape[0] for g in gains]
    gain_row = jnp.pad(gain_row, (0, qkv_width - gain_row.shape[0]))
    qkv_local = jnp.concatenate([query_weight, key_weight, value_weight], axis=1)
    packed = jnp.concatenate([qkv_local, gain_row[None]], axis=0)
    packed = jnp.pad(packed, ((0, padded - width_rows - 1), (0, 0)))
    packed_all = lax.all_gather(packed, ALL, axis=0, tiled=False)
    qkv_full = packed_all[:, :width_rows].reshape(devices * width_rows, qkv_width)
    scales, at = [], 0
    for width in gain_widths:
        scales.append(packed_all[:, width_rows, at : at + width].reshape(-1).astype(f32))
        at += width
    input_scale, query_scale, key_scale, attnout_scale, ffnin_scale, ffnout_scale = scales
    output_full = lax.all_gather(output_weight, ALL, axis=0, tiled=True)

    def column_blocks(weight):
        pieces = weight.reshape(width_rows, planes, members, hidden_rows)
        return pieces.transpose(2, 0, 1, 3).reshape(members, width_rows, planes * hidden_rows)

    gate_up = jnp.concatenate([column_blocks(gate_weight), column_blocks(up_weight)], axis=1)
    gate_up = jnp.broadcast_to(gate_up[None], (planes,) + gate_up.shape)
    gate_up = exchange(gate_up.reshape((devices,) + gate_up.shape[2:]), ALL)
    gate_full = gate_up[:, :width_rows].reshape(devices * width_rows, planes * hidden_rows)
    up_full = gate_up[:, width_rows:].reshape(devices * width_rows, planes * hidden_rows)
    down_full = exchange(jnp.broadcast_to(down_weight[None], (planes,) + down_weight.shape), "z")
    down_full = down_full.reshape(planes * hidden_rows, down_weight.shape[1])

    hidden = tokens[0].astype(f32)
    incoming = cotangent[0].astype(f32)
    local_rows = hidden.shape[0]
    full_length = local_rows * seq_count
    offset = lax.axis_index("seq") * local_rows
    segment_row = segment_ids[0]

    def mine(rows):
        return lax.dynamic_slice_in_dim(rows, offset, local_rows)

    my_segments = mine(segment_row)
    cos_full, sin_full = rope_tables(doc_positions(segment_row), head_width)
    cos_table, sin_table = mine(cos_full), mine(sin_full)
    scale = head_width ** (-0.5)

    row_hidden = lax.all_gather(tokens[0], "seq", axis=0, tiled=True).astype(f32)
    row_normed = (row_hidden * inverse_rms(row_hidden) * input_scale).astype(bf16)
    key_value_raw = matmul(row_normed, qkv_full[:, query_width:])
    row_key_raw = key_value_raw[:, :head_width]
    value_rows = key_value_raw[:, head_width:].astype(bf16)
    key_rows = rotate(
        row_key_raw * inverse_rms(row_key_raw) * key_scale, cos_full, sin_full
    ).astype(bf16)

    inv_input = inverse_rms(hidden)
    norm_input = hidden * inv_input
    normed = (norm_input * input_scale).astype(bf16)
    query_raw = matmul(normed, qkv_full[:, :query_width]).reshape(
        local_rows, head_count, head_width
    )
    inv_query = inverse_rms(query_raw)
    norm_query = query_raw * inv_query
    queries = (
        rotate(norm_query * query_scale, cos_table[:, None, :], sin_table[:, None, :]) * scale
    ).astype(bf16)
    key_raw = mine(row_key_raw)
    inv_key = inverse_rms(key_raw)
    norm_key = key_raw * inv_key

    query_places = offset + jnp.arange(local_rows, dtype=jnp.int32)
    key_places = jnp.arange(full_length, dtype=jnp.int32)
    allowed = (my_segments[:, None] == segment_row[None, :]) & (
        query_places[:, None] >= key_places[None, :]
    )
    raw_scores = jnp.einsum("qhd,kd->hqk", queries, key_rows, preferred_element_type=f32)
    scores = jnp.where(allowed[None], raw_scores, masked_score)
    peak = jnp.max(scores, axis=-1, keepdims=True)
    log_total = peak + jnp.log(jnp.sum(jnp.exp(scores - peak), axis=-1, keepdims=True))
    probs = jnp.exp(scores - log_total)
    probs_low = probs.astype(bf16)
    attn_mix = jnp.einsum("hqk,kd->qhd", probs_low, value_rows, preferred_element_type=f32)
    attn_flat = attn_mix.astype(bf16).reshape(local_rows, query_width)
    attn_raw = matmul(attn_flat, output_full)
    inv_attn = inverse_rms(attn_raw)
    norm_attn = attn_raw * inv_attn
    middle = hidden + norm_attn * attnout_scale
    inv_middle = inverse_rms(middle)
    norm_middle = middle * inv_middle
    ffn_in = (norm_middle * ffnin_scale).astype(bf16)

    plane_in = plane_gather(ffn_in)
    gate_proj = matmul(plane_in, gate_full)
    up_proj = matmul(plane_in, up_full)
    activated, gelu_back = jax.vjp(gelu_pair, gate_proj, up_proj)
    activated_low = activated.astype(bf16)
    ffn_raw = plane_scatter_sum(matmul(activated_low, down_full).astype(bf16))
    inv_ffn = inverse_rms(ffn_raw)
    norm_ffn = ffn_raw * inv_ffn
    result = middle + norm_ffn * ffnout_scale
    ffnout_gain_grad = jnp.sum(incoming * norm_ffn, axis=0)
    ffn_raw_grad = rms_back(incoming * ffnout_scale, norm_ffn, inv_ffn).astype(bf16)

    plane_grad = plane_gather(ffn_raw_grad)
    act_grad = contract_cols(plane_grad, down_full)
    gate_grad, up_grad = gelu_back(act_grad)
    gate_low = gate_grad.astype(bf16)
    up_low = up_grad.astype(bf16)
    ffn_in_grad = plane_scatter_sum(
        (contract_cols(gate_low, gate_full) + contract_cols(up_low, up_full)).astype(bf16)
    )
    down_terms = exchange(
        contract_rows(activated_low, plane_grad)
        .astype(bf16)
        .reshape(planes, hidden_rows, down_weight.shape[1]),
        "z",
    )
    down_wgrad = jnp.sum(down_terms.astype(f32), axis=0)

    def row_blocks(grad):
        return grad.astype(bf16).reshape(devices, width_rows, planes * hidden_rows)

    gate_up_terms = exchange(
        jnp.concatenate(
            [
                row_blocks(contract_rows(plane_in, gate_low)),
                row_blocks(contract_rows(plane_in, up_low)),
            ],
            axis=1,
        ),
        ALL,
    )
    gate_up_sum = jnp.sum(
        gate_up_terms.astype(f32).reshape(
            planes, members, 2, width_rows, planes, hidden_rows
        ),
        axis=0,
    )
    gate_up_sum = gate_up_sum.transpose(1, 2, 3, 0, 4).reshape(
        2, width_rows, planes * members * hidden_rows
    )
    gate_wgrad, up_wgrad = gate_up_sum[0], gate_up_sum[1]

    ffnin_gain_grad = jnp.sum(ffn_in_grad * norm_middle, axis=0)
    middle_grad = incoming + rms_back(ffn_in_grad * ffnin_scale, norm_middle, inv_middle)
    attnout_gain_grad = jnp.sum(middle_grad * norm_attn, axis=0)
    attn_raw_grad = rms_back(middle_grad * attnout_scale, norm_attn, inv_attn).astype(bf16)
    output_wgrad = contract_rows(attn_flat, attn_raw_grad)
    mix_grad = (
        contract_cols(attn_raw_grad, output_full)
        .astype(bf16)
        .reshape(local_rows, head_count, head_width)
    )
    prob_grad = jnp.einsum("qhd,kd->hqk", mix_grad, value_rows, preferred_element_type=f32)
    row_delta = jnp.sum(prob_grad * probs, axis=-1, keepdims=True)
    score_grad = (probs * (prob_grad - row_delta)).astype(bf16)
    value_grad_rows = jnp.einsum("hqk,qhd->kd", probs_low, mix_grad, preferred_element_type=f32)
    key_grad_rows = jnp.einsum("hqk,qhd->kd", score_grad, queries, preferred_element_type=f32)
    query_grad = jnp.einsum("hqk,kd->qhd", score_grad, key_rows, preferred_element_type=f32)
    key_value_terms = exchange(
        jnp.concatenate([key_grad_rows, value_grad_rows], axis=1)
        .astype(bf16)
        .reshape(seq_count, local_rows, 2 * head_width),
        "seq",
    )
    key_value_grad = jnp.sum(key_value_terms.astype(f32), axis=0)
    key_grad, value_grad = key_value_grad[:, :head_width], key_value_grad[:, head_width:]
    query_norm_grad = rotate(query_grad * scale, cos_table[:, None, :], -sin_table[:, None, :])
    query_gain_grad = jnp.sum(query_norm_grad * norm_query, axis=(0, 1))
    query_raw_low = (
        rms_back(query_norm_grad * query_scale, norm_query, inv_query)
        .astype(bf16)
        .reshape(local_rows, query_width)
    )
    key_norm_grad = rotate(key_grad, cos_table, -sin_table)
    key_gain_grad = jnp.sum(key_norm_grad * norm_key, axis=0)
    key_raw_low = rms_back(key_norm_grad * key_scale, norm_key, inv_key).astype(bf16)
    qkv_raw_low = jnp.concatenate([query_raw_low, key_raw_low, value_grad.astype(bf16)], axis=1)
    qkv_wgrad = contract_rows(normed, qkv_raw_low)
    normed_grad = contract_cols(qkv_raw_low, qkv_full)
    input_gain_grad = jnp.sum(normed_grad * norm_input, axis=0)
    input_grad = middle_grad + rms_back(normed_grad * input_scale, norm_input, inv_input)

    def to_owners(grad):
        rows, columns = grad.shape[0] // devices, grad.shape[1]
        blocks = grad.astype(bf16).reshape(planes, members, rows, columns)
        terms = exchange(blocks.transpose(1, 0, 2, 3), PLANE)
        summed = jnp.sum(terms.astype(f32), axis=0).astype(bf16)
        return jnp.sum(exchange(summed, "z").astype(f32), axis=0)

    output_share = to_owners(output_wgrad)
    gain_grads = (
        input_gain_grad,
        query_gain_grad,
        key_gain_grad,
        attnout_gain_grad,
        ffnin_gain_grad,
        ffnout_gain_grad,
    )
    gain_rows = jnp.concatenate([g.reshape(devices, -1) for g in gain_grads], axis=1)
    gain_rows = jnp.pad(gain_rows, ((0, 0), (0, qkv_width - gain_rows.shape[1])))
    qkv_blocks = jnp.concatenate(
        [qkv_wgrad.reshape(devices, width_rows, qkv_width), gain_rows[:, None]], axis=1
    )
    qkv_blocks = jnp.pad(qkv_blocks, ((0, 0), (0, padded - width_rows - 1), (0, 0)))
    qkv_share = to_owners(qkv_blocks.reshape(devices * padded, qkv_width))
    gain_shares, at = [], 0
    for width in gain_widths:
        gain_shares.append(qkv_share[width_rows, at : at + width])
        at += width
    return (
        result.astype(bf16)[None],
        input_grad[None],
        qkv_share[:width_rows, :query_width],
        qkv_share[:width_rows, query_width : query_width + head_width],
        qkv_share[:width_rows, query_width + head_width :],
        output_share,
        gate_wgrad,
        up_wgrad,
        down_wgrad,
        *gain_shares,
    )


def solution(mesh):
    dp, seq = mesh.shape["dp"], mesh.shape["seq"]
    split = Mesh(mesh.devices.reshape(dp // 4, 2, 2, seq), ALL)
    rows = P(("z", "x", "core"), "seq", None)
    matrix, vector = P(ALL, None), P(ALL)
    return jax.shard_map(
        body,
        mesh=split,
        in_specs=(rows, P(("z", "x", "core"), None), rows) + (matrix,) * 7 + (vector,) * 6,
        out_specs=(rows, rows) + (matrix,) * 7 + (vector,) * 6,
        check_vma=False,
    )
```

time: 2000 us -> 785 us (0.39)
  blocking collectives: 630 us -> 0 us
  waiting for transfers between devices: 976 us -> 412 us
  other arithmetic: 40.2 us -> 67.4 us
  starting transfers between devices: 87.1 us -> 60 us
  matrix products: 131 us -> 109 us
    unnamed x3 -> x0, blocking collectives: 486 us -> none
    all_to_all x3 -> x11, waiting for transfers between devices: 690 us -> 225 us  [exchange(): return lax.all_to_all(blocks, axes, split_axis=0, concat_axis=0, tiled=True)]
    all_gather x4 -> x0, blocking collectives: 144 us -> none  [the longest x1 70.1 us: body(): lax.all_gather(key_weight, ('dp', 'seq'), axis=0, tiled=True)]
    reduce_scatter x3 -> x0, waiting for transfers between devices: 78.6 us -> none  [the longest x1 68.4 us: body(): lax.psum_scatter(value_grad_rows.astype(jnp.bfloat16), 'seq', scatter_dim...]
    unnamed x187 -> x127, local copies, waits for them, and re-layouts: 65 us -> 11.1 us
    unnamed x12 -> x0, starting transfers between devices: 51.9 us -> none
    reshape x0 -> x21, local copies, waits for them, and re-layouts: none -> 48.1 us  [the longest x1 12.2 us: body(): gate_up_terms.astype(f32)]
    all_to_all x2 -> x0, local copies, waits for them, and re-layouts: 36.3 us -> none  [the longest x1 18.1 us: body(): lax.all_to_all(contract_rows(ffn_in, gate_low).astype(jnp.bfloat16), ('dp...]
  transfers between devices with their start and end apart: 23 -> 16, of which waited for: 8 -> 13; matrix products, arithmetic and copies ran while one was open for 30% -> 28% of each run, Pallas kernels for 0% -> 0%
where the time goes in v1:
time: 785 us; the launch traced here: 777 us
  waiting for transfers between devices  412 us (52%)
  local copies, waits for them, and re-layouts  114 us (15%)
  matrix products  109 us (14%)
  other arithmetic  67.4 us (9%)
  starting transfers between devices  60 us (8%)
  between operations  15.2 us (2%)
    all_to_all x11, waiting for transfers between devices, exchange(): return lax.all_to_all(blocks, axes, split_axis=0, concat_axis=0, tiled=True)  225 us
    all_gather x1, waiting for transfers between devices, body(): packed_all = lax.all_gather(packed, ALL, axis=0, tiled=False)  88.6 us
    all_to_all x11, starting transfers between devices, exchange(): return lax.all_to_all(blocks, axes, split_axis=0, concat_axis=0, tiled=True)  59 us
    all_gather x2, waiting for transfers between devices, plane_gather(): return lax.all_gather(local, PLANE, axis=0, tiled=True)  55.7 us
    dot_general x6, matrix products, matmul(): return jnp.dot(left, right, preferred_element_type=jnp.float32)  35.1 us
    dot_general x5, matrix products, contract_cols(): lax.dot_general(left, right, (((1,), (1,)), ((), ())), preferred_element_...  32.8 us
    dot_general x5, matrix products, contract_rows(): lax.dot_general(left, right, (((0,), (0,)), ((), ())), preferred_element_...  32.2 us
    all_gather x1, waiting for transfers between devices, body(): output_full = lax.all_gather(output_weight, ALL, axis=0, tiled=True)  25.3 us
  transfers between devices with their start and end apart: 16, of which 13 were waited for; matrix products, arithmetic and copies ran while one was open for 28% of the time, Pallas kernels for 0%

profile of v1, /device:TPU:8, one launch (start us, length us, event | category | flops | bytes accessed | tf_op | source)
XLA Modules:
  0.0 777.5 jit_solution(3174932612226022172)
XLA Ops:
  22.3 6.1 all-to-all-start
  30.5 16.3 %all-gather.14.cloned.1.call-done = bf16[1,512,1152]{2,1,0:T(8,128)(2,1)} async-done(((bf16[1,256,1152]{2,1,0:T(8,128)(2,1)}), bf16[1,512,1152]{2,1,0:T(8,128)(2,1)}) %all-gather.14.cloned.1.call-update) | async-done | bytes 1179664 | tf_op jit(solution)/shard_map/all_gather | solution.py:160
  48.4 88.6 %all-gather.16.cloned.1.call-done = bf16[1280,1536]{1,0:T(8,128)(2,1)} async-done(((bf16[40,1536]{1,0:T(8,128)(2,1)}), bf16[1280,1536]{1,0:T(8,128)(2,1)}) %all-gather.16.cloned.1.call-update) | async-done | bytes 3932176 | tf_op jit(solution)/shard_map/all_gather | solution.py:124
  138.0 5.7 reshape.363
  171.9 25.3 %all-gather.8.cloned.1.call-done = bf16[1024,1152]{1,0:T(8,128)(2,1)} async-done(((bf16[32,1152]{1,0:T(8,128)(2,1)}), bf16[1024,1152]{1,0:T(8,128)(2,1)}) %all-gather.8.cloned.1.call-update) | async-done | bytes 2359312 | tf_op jit(solution)/shard_map/all_gather | solution.py:131
  207.4 6.2 all-to-all-start.1
  213.6 5.4 fusion.100
  227.4 16.6 %all-gather.10.cloned.1.call-done = bf16[2048,1152]{1,0:T(8,128)(2,1)} async-done(((bf16[256,1152]{1,0:T(8,128)(2,1)}), bf16[2048,1152]{1,0:T(8,128)(2,1)}) %all-gather.10.cloned.1.call-update) | async-done | bytes 4718608 | tf_op jit(solution)/shard_map/all_gather | solution.py:76
  244.0 7.6 fusion.106
  254.6 9.2 %multiply_convert_fusion.1 = (bf16[2048,864]{0,1:T(8,128)(2,1)}, f32[2048,864]{0,1:T(8,128)}) fusion(f32[2048,864]{0,1:T(8,128)S(1)} %fusion.106, bf16[2048,1152]{1,0:T(8,128)(2,1)S(1)} %copy-done.59, bf16[1152,864]{1,0:T(8,128)(2,1)S(1)} %copy-done.22), kind=kOutput, calls=%fused_computation.17 | convolution fusion | flops 4094558208 | bytes 24403968 | tf_op jit(solution)/shard_map/dot_general | solution.py:48
  263.8 9.2 %convolution_convert_fusion = bf16[2048,1152]{1,0:T(8,128)(2,1)} fusion(bf16[2048,864]{0,1:T(8,128)(2,1)} %get-tuple-element.75, bf16[864,1152]{1,0:T(8,128)(2,1)} %bitcast.18), kind=kOutput, calls=%fused_computation.8 | convolution fusion | flops 4079222784 | bytes 10248192 | tf_op jit(solution)/shard_map/dot_general | solution.py:48
  279.3 52.2 %all-to-all-done.2 = bf16[8,256,1152]{2,1,0:T(8,128)(2,1)} async-done(((bf16[8,256,1152]{2,1,0:T(8,128)(2,1)}), bf16[8,256,1152]{2,1,0:T(8,128)(2,1)}, u32[]{:S(2)}, u32[]{:S(2)}) %all-to-all-start.2) | async-done | bytes 4718624 | tf_op jit(solution)/shard_map/all_to_all | solution.py:72
  337.4 39.1 %all-gather.12.cloned.1.call-done = bf16[2048,1152]{1,0:T(8,128)(2,1)} async-done(((bf16[256,1152]{1,0:T(8,128)(2,1)}), bf16[2048,1152]{1,0:T(8,128)(2,1)}) %all-gather.12.cloned.1.call-update) | async-done | bytes 4718608 | tf_op jit(solution)/shard_map/all_gather | solution.py:76
  376.4 14.8 %multiply_convert_fusion = (bf16[2048,864]{0,1:T(8,128)(2,1)S(1)}, bf16[2048,864]{0,1:T(8,128)(2,1)S(1)}) fusion(f32[2048,864]{0,1:T(8,128)} %copy-done.60, f32[2048,864]{0,1:T(8,128)} %get-tuple-element.76, bf16[2048,1152]{1,0:T(8,128)(2,1)} %all-gather.12.cloned.1.call-done, bf16[864,1152]{1,0:T(8,128)(2,1)} %bitcast.18), kind=kOutput, calls=%fused_computation.16 | convolution fusion | flops 4119330816 | bytes 27942912 | tf_op jit(solution)/shard_map/dot_general | solution.py:58
  391.3 5.8 fusion.107
  397.1 7.9 %add_convert_fusion = bf16[2048,1152]{1,0:T(8,128)(2,1)} fusion(f32[2048,1152]{1,0:T(8,128)S(1)} %fusion.107, bf16[2048,864]{0,1:T(8,128)(2,1)S(1)} %get-tuple-element.36, bf16[1152,864]{1,0:T(8,128)(2,1)S(1)} %copy-done.23), kind=kOutput, calls=%fused_computation.3 | convolution fusion | flops 4081582080 | bytes 19685376 | tf_op jit(solution)/shard_map/dot_general | solution.py:58
  412.5 51.0 %all-to-all-done.3 = bf16[8,256,1152]{2,1,0:T(8,128)(2,1)} async-done(((bf16[8,256,1152]{2,1,0:T(8,128)(2,1)}), bf16[8,256,1152]{2,1,0:T(8,128)(2,1)}, u32[]{:S(2)}, u32[]{:S(2)}) %all-to-all-start.3) | async-done | bytes 4718624 | tf_op jit(solution)/shard_map/all_to_all | solution.py:72
  486.4 5.9 all-to-all-done.4
  499.3 9.5 %convolution_convert_fusion.5 = bf16[864,1152]{1,0:T(8,128)(2,1)} fusion(bf16[2048,864]{0,1:T(8,128)(2,1)} %get-tuple-element.75, bf16[2048,1152]{1,0:T(8,128)(2,1)} %all-gather.12.cloned.1.call-done), kind=kOutput, calls=%fused_computation.27 | convolution fusion | flops 4077858816 | bytes 10248192 | tf_op jit(solution)/shard_map/dot_general | solution.py:52
  510.4 15.0 %all-to-all-done.7 = bf16[8,4,32,1152]{3,2,1,0:T(8,128)(2,1)S(1)} async-done(((bf16[8,4,32,1152]{3,2,1,0:T(8,128)(2,1)}), bf16[8,4,32,1152]{3,2,1,0:T(8,128)(2,1)S(1)}, u32[]{:S(2)}, u32[]{:S(2)}) %all-to-all-start.7) | async-done | bytes 2359328 | tf_op jit(solution)/shard_map/all_to_all | solution.py:72
  525.4 5.1 all-to-all-start.10
  567.2 6.2 all-to-all-done.10
  573.4 6.8 all-to-all-start.8
  592.1 8.1 %convolution_convert_fusion.3 = bf16[1152,864]{0,1:T(8,128)(2,1)S(1)} fusion(bf16[2048,864]{0,1:T(8,128)(2,1)} %copy-done.62, bf16[2048,1152]{1,0:T(8,128)(2,1)} %all-gather.10.cloned.1.call-done), kind=kOutput, calls=%fused_computation.25 | convolution fusion | flops 4077858816 | bytes 10248192 | tf_op jit(solution)/shard_map/dot_general | solution.py:52
  605.2 9.4 %convolution_convert_fusion.4 = bf16[1152,864]{0,1:T(8,128)(2,1)} fusion(bf16[2048,864]{0,1:T(8,128)(2,1)} %copy-done.61, bf16[2048,1152]{1,0:T(8,128)(2,1)} %all-gather.10.cloned.1.call-done), kind=kOutput, calls=%fused_computation.26 | convolution fusion | flops 4077858816 | bytes 10248192 | tf_op jit(solution)/shard_map/dot_general | solution.py:52
  622.6 4.8 pad_maximum_fusion
  627.4 10.1 %all-to-all-done.5 = bf16[8,4,40,1536]{3,2,1,0:T(8,128)(2,1)} async-done(((bf16[8,4,40,1536]{3,2,1,0:T(8,128)(2,1)}), bf16[8,4,40,1536]{3,2,1,0:T(8,128)(2,1)}, u32[]{:S(2)}, u32[]{:S(2)}) %all-to-all-start.5) | async-done | bytes 3932192 | tf_op jit(solution)/shard_map/all_to_all | solution.py:72
  637.5 5.2 all-to-all-start.9
  649.3 82.7 %all-to-all-done.9 = bf16[32,72,864]{2,1,0:T(8,128)(2,1)} async-done(((bf16[32,72,864]{2,1,0:T(8,128)(2,1)}), bf16[32,72,864]{2,1,0:T(8,128)(2,1)}, u32[]{:S(2)}, u32[]{:S(2)}) %all-to-all-start.9) | async-done | bytes 3981344 | tf_op jit(solution)/shard_map/all_to_all | solution.py:72
  732.0 8.4 %all-to-all-start.6 = ((bf16[4,40,1536]{2,1,0:T(8,128)(2,1)}), bf16[4,40,1536]{2,1,0:T(8,128)(2,1)}, u32[]{:S(2)}, u32[]{:S(2)}) async-start(bf16[4,40,1536]{2,1,0:T(8,128)(2,1)} %reduce_sum.320), calls=%async_computation.6 | async-start | bytes 983040 | tf_op jit(solution)/shard_map/all_to_all | solution.py:72
  742.5 12.2 %reshape.397 = f32[4,8,2,36,4,216]{5,4,3,2,1,0:T(4,128)} reshape(bf16[32,72,864]{2,1,0:T(8,128)(2,1)} %all-to-all-done.9) | data formatting | bytes 11943936 | tf_op jit(solution)/shard_map/reshape | solution.py:247
  754.7 7.0 reduce_sum.324
  (290 shorter events, 198.9 us)
Async XLA Ops:
  7.2 10.1 %copy-start.28 = (bf16[36,6912]{1,0:T(8,128)(2,1)S(1)}, bf16[36,6912]{1,0:T(8,128)(2,1)}, u32[]{:S(2)}) copy-start(bf16[36,6912]{1,0:T(8,128)(2,1)} %param.23) | copy-start | bytes 1492996
  7.2 39.7 %all-gather.14.cloned.1.call-start = ((), (), s32[]{:S(2)}) async-start(), calls=%async_computation.14 | async-start | bytes 1769472 | tf_op jit(solution)/shard_map/all_gather | solution.py:160
  7.9 129.1 %all-gather.16.cloned.1.call-start = ((), (), s32[]{:S(2)}) async-start(), calls=%async_computation.15 | async-start | bytes 4055040 | tf_op jit(solution)/shard_map/all_gather | solution.py:124
  22.3 182.6 %all-to-all-start = ((bf16[32,72,864]{2,1,0:T(8,128)(2,1)}), bf16[32,72,864]{2,1,0:T(8,128)(2,1)}, u32[]{:S(2)}, u32[]{:S(2)}) async-start(bf16[32,72,864]{2,1,0:T(8,128)(2,1)} %bitcast.214), calls=%async_computation | async-start | bytes 8257536 | tf_op jit(solution)/shard_map/all_to_all | solution.py:72
  28.4 168.8 %all-gather.8.cloned.1.call-start = ((), (), s32[]{:S(2)}) async-start(), calls=%async_computation.11 | async-start | bytes 2433024 | tf_op jit(solution)/shard_map/all_gather | solution.py:131
  29.2 214.8 %all-gather.10.cloned.1.call-start = ((), (), s32[]{:S(2)}) async-start(), calls=%async_computation.12 | async-start | bytes 5308416 | tf_op jit(solution)/shard_map/all_gather | solution.py:76
  30.0 120.6 %copy-start.54 = (f32[256]{0:T(256)}, f32[256]{0:T(256)S(1)}, u32[]{:S(2)}) copy-start(f32[256]{0:T(256)S(1)} %add_rsqrt_fusion.7) | copy-start | bytes 3076
  30.0 113.7 %copy-start.56 = (s32[1,256]{1,0:T(1,128)}, s32[1,256]{1,0:T(1,128)S(1)}, u32[]{:S(2)}) copy-start(s32[1,256]{1,0:T(1,128)S(1)} %constant_dynamic-slice_fusion.2) | copy-start | bytes 3076
  157.4 13.0 %copy-start.18 = (f32[512,512]{0,1:T(8,128)}, f32[512,512]{0,1:T(8,128)S(1)}, u32[]{:S(2)}) copy-start(f32[512,512]{0,1:T(8,128)S(1)} %fusion.46) | copy-start | bytes 3145732
  170.4 30.5 %copy-start.40 = (f32[4,256]{1,0:T(4,128)}, f32[4,256]{1,0:T(4,128)S(1)}, u32[]{:S(2)}) copy-start(f32[4,256]{1,0:T(4,128)S(1)} %log_add_fusion) | copy-start | bytes 12292
  171.9 29.6 %copy-start.39 = (f32[32,36]{1,0:T(8,128)S(1)}, f32[32,36]{1,0:T(8,128)}, u32[]{:S(2)}) copy-start(f32[32,36]{1,0:T(8,128)} %get-tuple-element.16) | copy-start | bytes 13828
  207.4 56.4 %all-to-all-start.1 = ((bf16[4,216,1152]{2,1,0:T(8,128)(2,1)}), bf16[4,216,1152]{2,1,0:T(8,128)(2,1)}, u32[]{:S(2)}, u32[]{:S(2)}) async-start(bf16[4,216,1152]{2,1,0:T(8,128)(2,1)} %broadcast_in_dim.29), calls=%async_computation.1 | async-start | bytes 3981312 | tf_op jit(solution)/shard_map/all_to_all | solution.py:72
  244.0 10.6 %copy-start.22 = (bf16[1152,864]{1,0:T(8,128)(2,1)S(1)}, bf16[1152,864]{1,0:T(8,128)(2,1)}, u32[]{:S(2)}) copy-start(bf16[1152,864]{1,0:T(8,128)(2,1)} %reshape.371) | copy-start | bytes 5971972
  244.0 10.6 %copy-start.59 = (bf16[2048,1152]{1,0:T(8,128)(2,1)S(1)}, bf16[2048,1152]{1,0:T(8,128)(2,1)}, u32[]{:S(2)}) copy-start(bf16[2048,1152]{1,0:T(8,128)(2,1)} %all-gather.10.cloned.1.call-done) | copy-start | bytes 14155780
  273.0 58.5 %all-to-all-start.2 = ((bf16[8,256,1152]{2,1,0:T(8,128)(2,1)}), bf16[8,256,1152]{2,1,0:T(8,128)(2,1)}, u32[]{:S(2)}, u32[]{:S(2)}) async-start(bf16[8,256,1152]{2,1,0:T(8,128)(2,1)} %bitcast.221), calls=%async_computation.2 | async-start | bytes 9437184 | tf_op jit(solution)/shard_map/all_to_all | solution.py:72
  277.6 98.8 %all-gather.12.cloned.1.call-start = ((), (), s32[]{:S(2)}) async-start(), calls=%async_computation.13 | async-start | bytes 5308416 | tf_op jit(solution)/shard_map/all_gather | solution.py:76
  376.4 14.8 %copy-start.21 = (bf16[1152,864]{1,0:T(8,128)(2,1)S(1)}, bf16[1152,864]{1,0:T(8,128)(2,1)}, u32[]{:S(2)}) copy-start(bf16[1152,864]{1,0:T(8,128)(2,1)} %reshape.370) | copy-start | bytes 5971972
  405.0 58.5 %all-to-all-start.3 = ((bf16[8,256,1152]{2,1,0:T(8,128)(2,1)}), bf16[8,256,1152]{2,1,0:T(8,128)(2,1)}, u32[]{:S(2)}, u32[]{:S(2)}) async-start(bf16[8,256,1152]{2,1,0:T(8,128)(2,1)} %bitcast.220), calls=%async_computation.3 | async-start | bytes 9437184 | tf_op jit(solution)/shard_map/all_to_all | solution.py:72
  480.4 11.9 %all-to-all-start.4 = ((bf16[2,256,512]{1,2,0:T(8,128)(2,1)}), bf16[2,256,512]{1,2,0:T(8,128)(2,1)S(1)}, u32[]{:S(2)}, u32[]{:S(2)}) async-start(bf16[2,256,512]{1,2,0:T(8,128)(2,1)} %pad_maximum_fusion.4), calls=%async_computation.4 | async-start | bytes 1048576 | tf_op jit(solution)/shard_map/all_to_all | solution.py:72
  493.1 32.3 %all-to-all-start.7 = ((bf16[8,4,32,1152]{3,2,1,0:T(8,128)(2,1)}), bf16[8,4,32,1152]{3,2,1,0:T(8,128)(2,1)S(1)}, u32[]{:S(2)}, u32[]{:S(2)}) async-start(bf16[8,4,32,1152]{3,2,1,0:T(8,128)(2,1)} %bitcast.217), calls=%async_computation.7 | async-start | bytes 4718592 | tf_op jit(solution)/shard_map/all_to_all | solution.py:72
  499.3 9.6 %copy-start.14 = (bf16[4,256,512]{1,2,0:T(8,128)(2,1)S(1)}, bf16[4,256,512]{1,2,0:T(8,128)(2,1)}, u32[]{:S(2)}) copy-start(bf16[4,256,512]{1,2,0:T(8,128)(2,1)} %copy-done.13) | copy-start | bytes 3145732
  499.3 9.6 %copy-start.30 = (bf16[512,128]{0,1:T(8,128)(2,1)S(1)}, bf16[512,128]{0,1:T(8,128)(2,1)}, u32[]{:S(2)}) copy-start(bf16[512,128]{0,1:T(8,128)(2,1)} %get-tuple-element.67) | copy-start | bytes 393220
  525.4 48.0 %all-to-all-start.10 = ((bf16[4,216,1152]{2,1,0:T(8,128)(2,1)}), bf16[4,216,1152]{2,1,0:T(8,128)(2,1)}, u32[]{:S(2)}, u32[]{:S(2)}) async-start(bf16[4,216,1152]{2,1,0:T(8,128)(2,1)} %bitcast.232), calls=%async_computation.10 | async-start | bytes 3981312 | tf_op jit(solution)/shard_map/all_to_all | solution.py:72
  540.2 10.7 %copy-start.16 = (f32[512,256]{0,1:T(8,128)S(1)}, f32[512,256]{0,1:T(8,128)}, u32[]{:S(2)}) copy-start(f32[512,256]{0,1:T(8,128)} %get-tuple-element.48) | copy-start | bytes 1572868
  540.2 10.7 %copy-start.47 = (f32[256]{0:T(256)S(1)}, f32[256]{0:T(256)}, u32[]{:S(2)}) copy-start(f32[256]{0:T(256)} %copy-done.46) | copy-start | bytes 3076
  540.2 10.7 %copy-start.57 = (f32[256]{0:T(256)S(1)}, f32[256]{0:T(256)}, u32[]{:S(2)}) copy-start(f32[256]{0:T(256)} %add_rsqrt_fusion.3) | copy-start | bytes 3076
  573.4 13.9 %all-to-all-start.8 = ((bf16[4,32,1152]{2,1,0:T(8,128)(2,1)}), bf16[4,32,1152]{2,1,0:T(8,128)(2,1)S(1)}, u32[]{:S(2)}, u32[]{:S(2)}) async-start(bf16[4,32,1152]{2,1,0:T(8,128)(2,1)} %reduce_sum.322), calls=%async_computation.8 | async-start | bytes 589824 | tf_op jit(solution)/shard_map/all_to_all | solution.py:72
  587.3 50.2 %all-to-all-start.5 = ((bf16[8,4,40,1536]{3,2,1,0:T(8,128)(2,1)}), bf16[8,4,40,1536]{3,2,1,0:T(8,128)(2,1)}, u32[]{:S(2)}, u32[]{:S(2)}) async-start(bf16[8,4,40,1536]{3,2,1,0:T(8,128)(2,1)} %bitcast.215), calls=%async_computation.5 | async-start | bytes 7864320 | tf_op jit(solution)/shard_map/all_to_all | solution.py:72
  637.5 94.5 %all-to-all-start.9 = ((bf16[32,72,864]{2,1,0:T(8,128)(2,1)}), bf16[32,72,864]{2,1,0:T(8,128)(2,1)}, u32[]{:S(2)}, u32[]{:S(2)}) async-start(bf16[32,72,864]{2,1,0:T(8,128)(2,1)} %pad_maximum_fusion), calls=%async_computation.9 | async-start | bytes 8257536 | tf_op jit(solution)/shard_map/all_to_all | solution.py:72
  645.6 94.9 %copy-start.4 = (f32[256,1152]{1,0:T(8,128)S(1)}, f32[256,1152]{1,0:T(8,128)}, u32[]{:S(2)}) copy-start(f32[256,1152]{1,0:T(8,128)} %copy-done.3) | copy-start | bytes 3538948
  645.6 94.9 %copy-start.10 = (f32[256,1152]{1,0:T(8,128)S(1)}, f32[256,1152]{1,0:T(8,128)}, u32[]{:S(2)}) copy-start(f32[256,1152]{1,0:T(8,128)} %copy-done.9) | copy-start | bytes 3538948
  732.0 35.1 %all-to-all-start.6 = ((bf16[4,40,1536]{2,1,0:T(8,128)(2,1)}), bf16[4,40,1536]{2,1,0:T(8,128)(2,1)}, u32[]{:S(2)}, u32[]{:S(2)}) async-start(bf16[4,40,1536]{2,1,0:T(8,128)(2,1)} %reduce_sum.320), calls=%async_computation.6 | async-start | bytes 983040 | tf_op jit(solution)/shard_map/all_to_all | solution.py:72
  (47 other events, 158.9 us)
Sparse Core Ops, SparseCore 0:
  9.6 37.2 all-gather.13
  50.3 86.6 all-gather.15
  139.9 57.2 all-gather.7
  205.1 38.8 all-gather.9
  337.5 38.8 all-gather.11

commit v2 on v1

--- a/solution.py
+++ b/solution.py
@@ -1,6 +1,10 @@
+import functools
+
 import jax
 import jax.numpy as jnp
 from jax import lax
+from jax.experimental import pallas as pl
+from jax.experimental.pallas import tpu as pltpu
 from jax.sharding import Mesh
 from jax.sharding import PartitionSpec as P
 
@@ -67,19 +71,311 @@
 ALL = ("z", "x", "core", "seq")
 PLANE = ("x", "core", "seq")
 
+MESH_ID = pl.DeviceIdType.MESH
+VMEM_BYTES = 48 * 2**20
+
 
 def exchange(blocks, axes):
     return lax.all_to_all(blocks, axes, split_axis=0, concat_axis=0, tiled=True)
 
 
-def plane_gather(local):
-    return lax.all_gather(local, PLANE, axis=0, tiled=True)
-
-
-def plane_scatter_sum(partial):
-    members = lax.axis_size(PLANE)
-    terms = exchange(partial.reshape((members, -1) + partial.shape[1:]), PLANE)
-    return jnp.sum(terms.astype(jnp.float32), axis=0)
+def busy(microseconds):
+    return pl.CostEstimate(flops=0, bytes_accessed=microseconds * 3_000_000, transcendentals=0)
+
+
+def plane_places():
+    z, x, core, seq = (lax.axis_index(name) for name in ALL)
+    sibling = (z, x, 1 - core, seq)
+    along_x = (z, 1 - x, core, seq)
+    along_y = (z, x, core, 1 - seq)
+
+    def member(other_x, other_core, other_y):
+        at_x = 1 - x if other_x else x
+        at_core = 1 - core if other_core else core
+        at_y = 1 - seq if other_y else seq
+        return (at_x * 2 + at_core) * 2 + at_y
+
+    return sibling, along_x, along_y, member
+
+
+def greet(places):
+    barrier = pltpu.get_barrier_semaphore()
+    for place in places:
+        pl.semaphore_signal(barrier, inc=1, device_id=place, device_id_type=MESH_ID)
+    pl.semaphore_wait(barrier, len(places))
+
+
+def sender(send_sems, recv_sems):
+    def send(kind, source, target, place):
+        copy = pltpu.make_async_remote_copy(
+            src_ref=source,
+            dst_ref=target,
+            send_sem=send_sems.at[kind],
+            recv_sem=recv_sems.at[kind],
+            device_id=place,
+            device_id_type=MESH_ID,
+        )
+        copy.start()
+        return copy
+
+    return send
+
+
+def plane_spread(own_ref, out_ref, send_sems, recv_sems, local_sem):
+    sibling, along_x, along_y, member = plane_places()
+    half = own_ref.shape[0] // 2
+    top, bottom = pl.ds(0, half), pl.ds(half, half)
+    me = member(0, 0, 0)
+    keep = pltpu.make_async_copy(own_ref, out_ref.at[me], local_sem)
+    keep.start()
+    send = sender(send_sems, recv_sems)
+
+    def forward(kind, block, rows, place):
+        return send(kind, out_ref.at[block, rows], out_ref.at[block, rows], place)
+
+    own_x_top = send(1, own_ref.at[top], out_ref.at[me, top], along_x)
+    own_y_bottom = send(3, own_ref.at[bottom], out_ref.at[me, bottom], along_y)
+    own_sibling = send(0, own_ref, out_ref.at[me], sibling)
+    own_x_bottom = send(2, own_ref.at[bottom], out_ref.at[me, bottom], along_x)
+    own_y_top = send(4, own_ref.at[top], out_ref.at[me, top], along_y)
+    x_block, y_block, diagonal = member(1, 0, 0), member(0, 0, 1), member(1, 0, 1)
+    own_x_top.wait_recv()
+    diagonal_top = forward(5, x_block, top, along_y)
+    x_top = forward(7, x_block, top, sibling)
+    own_y_bottom.wait_recv()
+    diagonal_bottom = forward(6, y_block, bottom, along_x)
+    y_bottom = forward(9, y_block, bottom, sibling)
+    own_x_bottom.wait_recv()
+    x_bottom = forward(8, x_block, bottom, sibling)
+    own_y_top.wait_recv()
+    y_top = forward(10, y_block, top, sibling)
+    diagonal_top.wait_recv()
+    far_top = forward(11, diagonal, top, sibling)
+    diagonal_bottom.wait_recv()
+    far_bottom = forward(12, diagonal, bottom, sibling)
+    for copy in (own_sibling, x_top, y_bottom, x_bottom, y_top, far_top, far_bottom):
+        copy.wait_recv()
+    for copy in (
+        own_x_top,
+        own_y_bottom,
+        own_sibling,
+        own_x_bottom,
+        own_y_top,
+        diagonal_top,
+        diagonal_bottom,
+        x_top,
+        y_bottom,
+        x_bottom,
+        y_top,
+        far_top,
+        far_bottom,
+    ):
+        copy.wait_send()
+    keep.wait()
+
+
+def gather_kernel(own_ref, out_ref, *sems):
+    greet(plane_places()[:3])
+    plane_spread(own_ref, out_ref, *sems)
+
+
+def wide_gather_kernel(planes, own_ref, out_ref, held, z_send, z_recv, own_sem, *sems):
+    z, x, core, seq = (lax.axis_index(name) for name in ALL)
+    others = [(lax.rem(z + k, planes), x, core, seq) for k in range(1, planes)]
+    greet((*plane_places()[:3], *others))
+    slot = held.at[z]
+    keep = pltpu.make_async_copy(own_ref, slot, own_sem)
+    keep.start()
+    send = sender(z_send, z_recv)
+    copies = [send(k, own_ref, slot, place) for k, place in enumerate(others)]
+    for copy in copies:
+        copy.wait_recv()
+    keep.wait()
+    plane_spread(held, out_ref, *sems)
+    for copy in copies:
+        copy.wait_send()
+
+
+GATHER_SEMS = [
+    pltpu.SemaphoreType.DMA((13,)),
+    pltpu.SemaphoreType.DMA((13,)),
+    pltpu.SemaphoreType.DMA,
+]
+
+
+def wide_gather(local, planes, collective_id):
+    rows, columns = local.shape
+    members = 8
+    return pl.pallas_call(
+        functools.partial(wide_gather_kernel, planes),
+        out_shape=jax.ShapeDtypeStruct((members, planes, rows, columns), local.dtype),
+        in_specs=[pl.BlockSpec(memory_space=pltpu.VMEM)],
+        out_specs=pl.BlockSpec(memory_space=pl.ANY),
+        scratch_shapes=[
+            pltpu.VMEM((planes, rows, columns), local.dtype),
+            pltpu.SemaphoreType.DMA((planes - 1,)),
+            pltpu.SemaphoreType.DMA((planes - 1,)),
+            pltpu.SemaphoreType.DMA,
+            *GATHER_SEMS,
+        ],
+        cost_estimate=busy(35),
+        compiler_params=pltpu.CompilerParams(
+            collective_id=collective_id, has_side_effects=True, vmem_limit_bytes=VMEM_BYTES
+        ),
+    )(local)
+
+
+def plane_gather(local, collective_id):
+    rows, columns = local.shape
+    members = 8
+    out = pl.pallas_call(
+        gather_kernel,
+        out_shape=jax.ShapeDtypeStruct((members, rows // 16, 16, columns), local.dtype),
+        in_specs=[pl.BlockSpec(memory_space=pl.ANY)],
+        out_specs=pl.BlockSpec(memory_space=pl.ANY),
+        scratch_shapes=GATHER_SEMS,
+        cost_estimate=busy(25),
+        compiler_params=pltpu.CompilerParams(
+            collective_id=collective_id, has_side_effects=True, vmem_limit_bytes=VMEM_BYTES
+        ),
+    )(local.reshape(rows // 16, 16, columns))
+    return out.reshape(members * rows, columns)
+
+
+def add_rows(target, sources, start, count):
+    def one(i, carry):
+        total = sources[0][i].astype(jnp.float32)
+        for source in sources[1:]:
+            total = total + source[i].astype(jnp.float32)
+        target[i] = total.astype(target.dtype)
+        return carry
+
+    lax.fori_loop(start, start + count, one, 0)
+
+
+def plane_sum(part_ref, own_sum, near, sums, from_x, from_y, far_x, far_y, send_sems, recv_sems):
+    sibling, along_x, along_y, member = plane_places()
+    rows = own_sum.shape[0]
+    half = rows // 2
+    top, bottom = pl.ds(0, half), pl.ds(half, half)
+    send = sender(send_sems, recv_sems)
+    chips = ((1, 1), (1, 0), (0, 1), (0, 0))
+    mine = [part_ref.at[member(at_x, 0, at_y)] for at_x, at_y in chips]
+    to_sibling = [
+        send(k, part_ref.at[member(at_x, 1, at_y)], near.at[k], sibling)
+        for k, (at_x, at_y) in enumerate(chips)
+    ]
+    to_sibling[0].wait_recv()
+    add_rows(sums.at[0], (mine[0], near.at[0]), 0, rows)
+    diagonal_x = send(4, sums.at[0, bottom], far_x.at[bottom], along_x)
+    diagonal_y = send(5, sums.at[0, top], far_y.at[top], along_y)
+    to_sibling[1].wait_recv()
+    add_rows(sums.at[1], (mine[1], near.at[1]), half, half)
+    direct_x = send(6, sums.at[1, bottom], from_x.at[bottom], along_x)
+    to_sibling[2].wait_recv()
+    add_rows(sums.at[2], (mine[2], near.at[2]), 0, half)
+    direct_y = send(7, sums.at[2, top], from_y.at[top], along_y)
+    to_sibling[3].wait_recv()
+    diagonal_y.wait_recv()
+    add_rows(sums.at[1], (mine[1], near.at[1], far_y), 0, half)
+    joint_x = send(8, sums.at[1, top], from_x.at[top], along_x)
+    diagonal_x.wait_recv()
+    add_rows(sums.at[2], (mine[2], near.at[2], far_x), half, half)
+    joint_y = send(9, sums.at[2, bottom], from_y.at[bottom], along_y)
+    direct_x.wait_recv()
+    direct_y.wait_recv()
+    joint_x.wait_recv()
+    joint_y.wait_recv()
+    add_rows(own_sum, (mine[3], near.at[3], from_x, from_y), 0, rows)
+    for copy in (*to_sibling, diagonal_x, diagonal_y, direct_x, direct_y, joint_x, joint_y):
+        copy.wait_send()
+
+
+def plane_sum_kernel(part_ref, out_ref, *scratch):
+    sibling, along_x, along_y, _ = plane_places()
+    greet((sibling, along_x, along_y))
+    plane_sum(part_ref, out_ref, *scratch)
+
+
+def plane_sum_scratch(shape, dtype):
+    block = pltpu.VMEM(shape, dtype)
+    return [
+        pltpu.VMEM((4, *shape), dtype),
+        pltpu.VMEM((3, *shape), dtype),
+        block,
+        block,
+        block,
+        block,
+        pltpu.SemaphoreType.DMA((10,)),
+        pltpu.SemaphoreType.DMA((10,)),
+    ]
+
+
+def plane_scatter_sum(partial, collective_id):
+    members = 8
+    rows, columns = partial.shape[0] // members, partial.shape[1]
+    shape = (rows // 16, 16, columns)
+    out = pl.pallas_call(
+        plane_sum_kernel,
+        out_shape=jax.ShapeDtypeStruct(shape, jnp.float32),
+        in_specs=[pl.BlockSpec(memory_space=pltpu.VMEM)],
+        out_specs=pl.BlockSpec(memory_space=pltpu.VMEM),
+        scratch_shapes=plane_sum_scratch(shape, partial.dtype),
+        cost_estimate=busy(25),
+        compiler_params=pltpu.CompilerParams(
+            collective_id=collective_id, has_side_effects=True, vmem_limit_bytes=VMEM_BYTES
+        ),
+    )(partial.reshape(members, *shape))
+    return out.reshape(rows, columns)
+
+
+def owner_sum_kernel(planes, part_ref, out_ref, own_sum, leaving, arriving, z_send, z_recv, *scratch):
+    sibling, along_x, along_y, _ = plane_places()
+    z, x, core, seq = (lax.axis_index(name) for name in ALL)
+    others = [(lax.rem(z + k, planes), x, core, seq) for k in range(1, planes)]
+    greet((sibling, along_x, along_y, *others))
+    plane_sum(part_ref, own_sum, *scratch)
+    send = sender(z_send, z_recv)
+
+    def narrow(i, carry):
+        leaving[i] = own_sum[i].astype(leaving.dtype)
+        return carry
+
+    lax.fori_loop(0, planes, narrow, 0)
+    copies = [
+        send(k, leaving.at[place[0]], arriving.at[k], place) for k, place in enumerate(others)
+    ]
+    for copy in copies:
+        copy.wait_recv()
+
+    value = own_sum[z]
+    for k in range(planes - 1):
+        value = value + arriving[k].astype(jnp.float32)
+    out_ref[...] = value
+    for copy in copies:
+        copy.wait_send()
+
+
+def owner_sum(blocks, collective_id):
+    members, planes, rows, columns = blocks.shape
+    return pl.pallas_call(
+        functools.partial(owner_sum_kernel, planes),
+        out_shape=jax.ShapeDtypeStruct((rows, columns), jnp.float32),
+        in_specs=[pl.BlockSpec(memory_space=pltpu.VMEM)],
+        out_specs=pl.BlockSpec(memory_space=pltpu.VMEM),
+        scratch_shapes=[
+            pltpu.VMEM((planes, rows, columns), jnp.float32),
+            pltpu.VMEM((planes, rows, columns), blocks.dtype),
+            pltpu.VMEM((planes - 1, rows, columns), blocks.dtype),
+            pltpu.SemaphoreType.DMA((planes - 1,)),
+            pltpu.SemaphoreType.DMA((planes - 1,)),
+            *plane_sum_scratch((planes, rows, columns), blocks.dtype),
+        ],
+        cost_estimate=busy(35),
+        compiler_params=pltpu.CompilerParams(
+            collective_id=collective_id, has_side_effects=True, vmem_limit_bytes=VMEM_BYTES
+        ),
+    )(blocks)
 
 
 def body(
@@ -121,7 +417,8 @@
     qkv_local = jnp.concatenate([query_weight, key_weight, value_weight], axis=1)
     packed = jnp.concatenate([qkv_local, gain_row[None]], axis=0)
     packed = jnp.pad(packed, ((0, padded - width_rows - 1), (0, 0)))
-    packed_all = lax.all_gather(packed, ALL, axis=0, tiled=False)
+    packed_all = wide_gather(packed, planes, 0).transpose(1, 0, 2, 3)
+    packed_all = packed_all.reshape(devices, padded, qkv_width)
     qkv_full = packed_all[:, :width_rows].reshape(devices * width_rows, qkv_width)
     scales, at = [], 0
     for width in gain_widths:
@@ -139,8 +436,7 @@
     gate_up = exchange(gate_up.reshape((devices,) + gate_up.shape[2:]), ALL)
     gate_full = gate_up[:, :width_rows].reshape(devices * width_rows, planes * hidden_rows)
     up_full = gate_up[:, width_rows:].reshape(devices * width_rows, planes * hidden_rows)
-    down_full = exchange(jnp.broadcast_to(down_weight[None], (planes,) + down_weight.shape), "z")
-    down_full = down_full.reshape(planes * hidden_rows, down_weight.shape[1])
+    down_full = lax.all_gather(down_weight, "z", axis=0, tiled=True)
 
     hidden = tokens[0].astype(f32)
     incoming = cotangent[0].astype(f32)
@@ -157,7 +453,15 @@
     cos_table, sin_table = mine(cos_full), mine(sin_full)
     scale = head_width ** (-0.5)
 
-    row_hidden = lax.all_gather(tokens[0], "seq", axis=0, tiled=True).astype(f32)
+    other_half = [(0, 1), (1, 0)]
+    first = lax.axis_index("seq") == 0
+    other_tokens = lax.ppermute(tokens[0], "seq", other_half)
+    row_hidden = jnp.concatenate(
+        [
+            jnp.where(first, tokens[0], other_tokens),
+            jnp.where(first, other_tokens, tokens[0]),
+        ]
+    ).astype(f32)
     row_normed = (row_hidden * inverse_rms(row_hidden) * input_scale).astype(bf16)
     key_value_raw = matmul(row_normed, qkv_full[:, query_width:])
     row_key_raw = key_value_raw[:, :head_width]
@@ -202,25 +506,25 @@
     norm_middle = middle * inv_middle
     ffn_in = (norm_middle * ffnin_scale).astype(bf16)
 
-    plane_in = plane_gather(ffn_in)
+    plane_in = plane_gather(ffn_in, 1)
     gate_proj = matmul(plane_in, gate_full)
     up_proj = matmul(plane_in, up_full)
     activated, gelu_back = jax.vjp(gelu_pair, gate_proj, up_proj)
     activated_low = activated.astype(bf16)
-    ffn_raw = plane_scatter_sum(matmul(activated_low, down_full).astype(bf16))
+    ffn_raw = plane_scatter_sum(matmul(activated_low, down_full).astype(bf16), 2)
     inv_ffn = inverse_rms(ffn_raw)
     norm_ffn = ffn_raw * inv_ffn
     result = middle + norm_ffn * ffnout_scale
     ffnout_gain_grad = jnp.sum(incoming * norm_ffn, axis=0)
     ffn_raw_grad = rms_back(incoming * ffnout_scale, norm_ffn, inv_ffn).astype(bf16)
 
-    plane_grad = plane_gather(ffn_raw_grad)
+    plane_grad = plane_gather(ffn_raw_grad, 3)
     act_grad = contract_cols(plane_grad, down_full)
     gate_grad, up_grad = gelu_back(act_grad)
     gate_low = gate_grad.astype(bf16)
     up_low = up_grad.astype(bf16)
     ffn_in_grad = plane_scatter_sum(
-        (contract_cols(gate_low, gate_full) + contract_cols(up_low, up_full)).astype(bf16)
+        (contract_cols(gate_low, gate_full) + contract_cols(up_low, up_full)).astype(bf16), 4
     )
     down_terms = exchange(
         contract_rows(activated_low, plane_grad)
@@ -245,10 +549,11 @@
     )
     gate_up_sum = jnp.sum(
         gate_up_terms.astype(f32).reshape(
-            planes, members, 2, width_rows, planes, hidden_rows
+            planes, members, 2 * width_rows, planes * hidden_rows
         ),
         axis=0,
     )
+    gate_up_sum = gate_up_sum.reshape(members, 2, width_rows, planes, hidden_rows)
     gate_up_sum = gate_up_sum.transpose(1, 2, 3, 0, 4).reshape(
         2, width_rows, planes * members * hidden_rows
     )
@@ -270,13 +575,11 @@
     value_grad_rows = jnp.einsum("hqk,qhd->kd", probs_low, mix_grad, preferred_element_type=f32)
     key_grad_rows = jnp.einsum("hqk,qhd->kd", score_grad, queries, preferred_element_type=f32)
     query_grad = jnp.einsum("hqk,kd->qhd", score_grad, key_rows, preferred_element_type=f32)
-    key_value_terms = exchange(
-        jnp.concatenate([key_grad_rows, value_grad_rows], axis=1)
-        .astype(bf16)
-        .reshape(seq_count, local_rows, 2 * head_width),
-        "seq",
-    )
-    key_value_grad = jnp.sum(key_value_terms.astype(f32), axis=0)
+    key_value_rows = jnp.concatenate([key_grad_rows, value_grad_rows], axis=1)
+    theirs = lax.dynamic_slice_in_dim(key_value_rows, local_rows - offset, local_rows)
+    key_value_grad = mine(key_value_rows) + lax.ppermute(
+        theirs.astype(bf16), "seq", other_half
+    ).astype(f32)
     key_grad, value_grad = key_value_grad[:, :head_width], key_value_grad[:, head_width:]
     query_norm_grad = rotate(query_grad * scale, cos_table[:, None, :], -sin_table[:, None, :])
     query_gain_grad = jnp.sum(query_norm_grad * norm_query, axis=(0, 1))
@@ -294,14 +597,12 @@
     input_gain_grad = jnp.sum(normed_grad * norm_input, axis=0)
     input_grad = middle_grad + rms_back(normed_grad * input_scale, norm_input, inv_input)
 
-    def to_owners(grad):
+    def to_owners(grad, collective_id):
         rows, columns = grad.shape[0] // devices, grad.shape[1]
         blocks = grad.astype(bf16).reshape(planes, members, rows, columns)
-        terms = exchange(blocks.transpose(1, 0, 2, 3), PLANE)
-        summed = jnp.sum(terms.astype(f32), axis=0).astype(bf16)
-        return jnp.sum(exchange(summed, "z").astype(f32), axis=0)
-
-    output_share = to_owners(output_wgrad)
+        return owner_sum(blocks.transpose(1, 0, 2, 3), collective_id)
+
+    output_share = to_owners(output_wgrad, 5)
     gain_grads = (
         input_gain_grad,
         query_gain_grad,
@@ -316,7 +617,7 @@
         [qkv_wgrad.reshape(devices, width_rows, qkv_width), gain_rows[:, None]], axis=1
     )
     qkv_blocks = jnp.pad(qkv_blocks, ((0, 0), (0, padded - width_rows - 1), (0, 0)))
-    qkv_share = to_owners(qkv_blocks.reshape(devices * padded, qkv_width))
+    qkv_share = to_owners(qkv_blocks.reshape(devices * padded, qkv_width), 6)
     gain_shares, at = [], 0
     for width in gain_widths:
         gain_shares.append(qkv_share[width_rows, at : at + width])

time: 785 us -> 678 us (0.86)
  waiting for transfers between devices: 412 us -> 4.51 us
  Pallas kernels: 0 us -> 389 us
  starting transfers between devices: 60 us -> 18.6 us
  other arithmetic: 67.4 us -> 41.9 us
  local copies, waits for them, and re-layouts: 114 us -> 103 us
  matrix products: 109 us -> 99.1 us
    pallas_call x0 -> x7, Pallas kernels: none -> 389 us  [the longest x1 163 us: wide_gather(): pl.pallas_call(functools.partial(wide_gather_kernel, planes), out_shape=j...]
    all_to_all x11 -> x3, waiting for transfers between devices: 225 us -> 0.01 us  [exchange(): return lax.all_to_all(blocks, axes, split_axis=0, concat_axis=0, tiled=True)]
    all_gather x4 -> x1, waiting for transfers between devices: 161 us -> 0.01 us  [body(): down_full = lax.all_gather(down_weight, 'z', axis=0, tiled=True)]
    all_to_all x11 -> x3, starting transfers between devices: 59 us -> 15.8 us  [exchange(): return lax.all_to_all(blocks, axes, split_axis=0, concat_axis=0, tiled=True)]
    all_gather x1, waiting for transfers between devices: 25.3 us -> 0.02 us  [body(): output_full = lax.all_gather(output_weight, ALL, axis=0, tiled=True)]
    reduce_sum x9 -> x1, other arithmetic: 22.4 us -> 4.35 us  [body(): jnp.sum(gate_up_terms.astype(f32).reshape(planes, members, 2 * width_rows...]
    reshape x1, local copies, waits for them, and re-layouts: 12.2 us -> 3.44 us  [body(): gate_up_sum.reshape(members, 2, width_rows, planes, hidden_rows)]
    dot_general x5, matrix products: 32.2 us -> 24.3 us  [contract_rows(): lax.dot_general(left, right, (((0,), (0,)), ((), ())), preferred_element_...]
  transfers between devices with their start and end apart: 16 -> 7, of which waited for: 13 -> 1; matrix products, arithmetic and copies ran while one was open for 28% -> 25% of each run, Pallas kernels for 0% -> 51%
where the time goes in v2:
time: 678 us; the launch traced here: 672 us
  Pallas kernels  389 us (57%)
  local copies, waits for them, and re-layouts  103 us (15%)
  matrix products  99.1 us (15%)
  other arithmetic  41.9 us (6%)
  starting transfers between devices  18.6 us (3%)
  between operations  15.7 us (2%)
    pallas_call x1, Pallas kernels, wide_gather(): pl.pallas_call(functools.partial(wide_gather_kernel, planes), out_shape=j...  163 us
    pallas_call x2, Pallas kernels, owner_sum(): pl.pallas_call(functools.partial(owner_sum_kernel, planes), out_shape=jax...  129 us
    pallas_call x2, Pallas kernels, plane_scatter_sum(): pl.pallas_call(plane_sum_kernel, out_shape=jax.ShapeDtypeStruct(shape, jn...  48.8 us
    pallas_call x2, Pallas kernels, plane_gather(): pl.pallas_call(gather_kernel, out_shape=jax.ShapeDtypeStruct((members, ro...  48.2 us
    dot_general x5, matrix products, contract_cols(): lax.dot_general(left, right, (((1,), (1,)), ((), ())), preferred_element_...  37 us
    dot_general x6, matrix products, matmul(): return jnp.dot(left, right, preferred_element_type=jnp.float32)  32 us
    dot_general x5, matrix products, contract_rows(): lax.dot_general(left, right, (((0,), (0,)), ((), ())), preferred_element_...  24.3 us
    all_to_all x3, starting transfers between devices, exchange(): return lax.all_to_all(blocks, axes, split_axis=0, concat_axis=0, tiled=True)  15.8 us
  transfers between devices with their start and end apart: 7, of which 1 were waited for; matrix products, arithmetic and copies ran while one was open for 25% of the time, Pallas kernels for 51%

profile of v2, /device:TPU:8, one launch (start us, length us, event | category | flops | bytes accessed | tf_op | source)
XLA Modules:
  0.0 671.7 jit_solution(14186452791433435387)
XLA Ops:
  18.2 5.1 all-to-all-start
  24.4 163.0 %shard_map.274 = bf16[8,4,40,1536]{3,2,1,0:T(8,128)(2,1)S(1)} custom-call(bf16[40,1536]{1,0:T(8,128)(2,1)S(1)} %fusion.62.own_ref), custom_call_target="tpu_custom_call" | custom-call | bytes 105000000 | tf_op jit(solution)/shard_map/pallas_call | solution.py:209
  194.0 3.9 reshape.412
  203.3 4.3 copy.126
  242.8 24.1 %shard_map.275 = bf16[8,16,16,1152]{3,2,1,0:T(8,128)(2,1)S(1)} custom-call(bf16[16,16,1152]{2,1,0:T(8,128)(2,1)S(1)} %bitcast.205), custom_call_target="tpu_custom_call" | custom-call | bytes 75000000 | tf_op jit(solution)/shard_map/pallas_call | solution.py:231
  269.0 5.4 fusion.88
  274.4 4.2 reshape.421
  278.6 4.2 reshape.422
  282.8 8.2 %fusion.93 = f32[2048,864]{0,1:T(8,128)S(1)} fusion(bf16[2048,1152]{1,0:T(8,128)(2,1)} %bitcast.195, bf16[1152,864]{1,0:T(8,128)(2,1)} %reshape.421), kind=kOutput, calls=%fused_computation.213 | convolution fusion | flops 4076863488 | bytes 13787136 | tf_op jit(solution)/shard_map/dot_general | solution.py:52
  293.9 9.3 %multiply_convert_fusion.1 = (bf16[2048,864]{0,1:T(8,128)(2,1)}, f32[2048,864]{0,1:T(8,128)}) fusion(f32[2048,864]{0,1:T(8,128)S(1)} %fusion.93, bf16[2048,1152]{1,0:T(8,128)(2,1)S(1)} %bitcast.198, bf16[1152,864]{1,0:T(8,128)(2,1)S(1)} %copy-done.36), kind=kOutput, calls=%fused_computation.16 | convolution fusion | flops 4094558208 | bytes 24403968 | tf_op jit(solution)/shard_map/dot_general | solution.py:52
  303.2 7.9 %convolution_convert_fusion = bf16[2048,1152]{1,0:T(8,128)(2,1)S(1)} fusion(bf16[2048,864]{0,1:T(8,128)(2,1)} %get-tuple-element.77, bf16[864,1152]{1,0:T(8,128)(2,1)} %all-gather.5.cloned.1.call-done), kind=kOutput, calls=%fused_computation.7 | convolution fusion | flops 4079222784 | bytes 10248192 | tf_op jit(solution)/shard_map/dot_general | solution.py:52
  311.1 24.7 %shard_map.276 = f32[16,16,1152]{2,1,0:T(8,128)S(1)} custom-call(bf16[8,16,16,1152]{3,2,1,0:T(8,128)(2,1)S(1)} %bitcast.194), custom_call_target="tpu_custom_call" | custom-call | bytes 75000000 | tf_op jit(solution)/shard_map/pallas_call | solution.py:318
  344.3 24.1 %shard_map.277 = bf16[8,16,16,1152]{3,2,1,0:T(8,128)(2,1)S(1)} custom-call(bf16[16,16,1152]{2,1,0:T(8,128)(2,1)S(1)} %multiply_convert_fusion.3.own_ref), custom_call_target="tpu_custom_call" | custom-call | bytes 75000000 | tf_op jit(solution)/shard_map/pallas_call | solution.py:231
  368.5 8.2 %convolution_convert_fusion.5 = bf16[864,1152]{1,0:T(8,128)(2,1)} fusion(bf16[2048,864]{0,1:T(8,128)(2,1)} %get-tuple-element.77, bf16[2048,1152]{1,0:T(8,128)(2,1)S(1)} %bitcast.203), kind=kOutput, calls=%fused_computation.26 | convolution fusion | flops 4077858816 | bytes 10248192 | tf_op jit(solution)/shard_map/dot_general | solution.py:56
  376.6 12.5 %multiply_convert_fusion = (bf16[2048,864]{0,1:T(8,128)(2,1)}, bf16[2048,864]{0,1:T(8,128)(2,1)}) fusion(f32[2048,864]{0,1:T(8,128)S(1)} %bitcast.226, f32[2048,864]{0,1:T(8,128)} %get-tuple-element.78, bf16[2048,1152]{1,0:T(8,128)(2,1)S(1)} %bitcast.204, bf16[864,1152]{1,0:T(8,128)(2,1)S(1)} %copy-done.83), kind=kOutput, calls=%fused_computation.15 | convolution fusion | flops 4119330816 | bytes 27942912 | tf_op jit(solution)/shard_map/dot_general | solution.py:62
  389.2 8.2 %convolution_convert_fusion.4 = bf16[1152,864]{0,1:T(8,128)(2,1)} fusion(bf16[2048,864]{0,1:T(8,128)(2,1)} %get-tuple-element.39, bf16[2048,1152]{1,0:T(8,128)(2,1)S(1)} %bitcast.201), kind=kOutput, calls=%fused_computation.25 | convolution fusion | flops 4077858816 | bytes 10248192 | tf_op jit(solution)/shard_map/dot_general | solution.py:56
  397.3 5.9 convolution_convert_fusion.3
  403.3 5.2 all-to-all-start.2
  408.5 10.1 %fusion.94 = f32[2048,1152]{1,0:T(8,128)} fusion(bf16[2048,864]{0,1:T(8,128)(2,1)} %get-tuple-element.39, bf16[1152,864]{1,0:T(8,128)(2,1)} %reshape.421), kind=kOutput, calls=%fused_computation.214 | convolution fusion | flops 4076863488 | bytes 14966784 | tf_op jit(solution)/shard_map/dot_general | solution.py:62
  418.5 4.1 copy.157
  422.6 4.0 reshape.437
  426.7 4.1 copy.158
  430.8 4.0 reshape.438
  434.8 9.3 %add_convert_fusion = bf16[2048,1152]{1,0:T(8,128)(2,1)S(1)} fusion(f32[2048,1152]{1,0:T(8,128)} %fusion.94, bf16[2048,864]{0,1:T(8,128)(2,1)} %get-tuple-element.38, bf16[1152,864]{1,0:T(8,128)(2,1)} %reshape.422), kind=kOutput, calls=%fused_computation.2 | convolution fusion | flops 4081582080 | bytes 19685376 | tf_op jit(solution)/shard_map/dot_general | solution.py:62
  444.1 24.2 %shard_map.278 = f32[16,16,1152]{2,1,0:T(8,128)S(1)} custom-call(bf16[8,16,16,1152]{3,2,1,0:T(8,128)(2,1)S(1)} %bitcast.193), custom_call_target="tpu_custom_call" | custom-call | bytes 75000000 | tf_op jit(solution)/shard_map/pallas_call | solution.py:318
  473.9 5.5 all-to-all-start.1
  481.5 96.0 %shard_map.280 = f32[32,1152]{1,0:T(8,128)S(1)} custom-call(bf16[8,4,32,1152]{3,2,1,0:T(8,128)(2,1)S(1)} %bitcast.192), custom_call_target="tpu_custom_call" | custom-call | bytes 105000000 | tf_op jit(solution)/shard_map/pallas_call | solution.py:361
  597.3 3.4 collective-permute-done.1
  602.5 3.4 fusion.29
  611.1 33.3 %shard_map.279 = f32[40,1536]{1,0:T(8,128)S(1)} custom-call(bf16[8,4,40,1536]{3,2,1,0:T(8,128)(2,1)S(1)} %bitcast.191), custom_call_target="tpu_custom_call" | custom-call | bytes 105000000 | tf_op jit(solution)/shard_map/pallas_call | solution.py:361
  649.8 4.4 convert_reduce_fusion
  654.1 3.4 reshape.441
  (329 shorter events, 118.5 us)
Async XLA Ops:
  7.2 232.1 %all-gather.3.cloned.1.call-start = ((), (), s32[]{:S(2)}) async-start(), calls=%async_computation.3 | async-start | bytes 2433024 | tf_op jit(solution)/shard_map/all_gather | solution.py:428
  7.9 217.4 %collective-permute-start = (bf16[256,1152]{1,0:T(8,128)(2,1)}, bf16[256,1152]{1,0:T(8,128)(2,1)}, u32[]{:S(2)}, u32[]{:S(2)}) collective-permute-start(bf16[256,1152]{1,0:T(8,128)(2,1)} %bitcast.208), channel_id=1, source_target_pairs={{0,1},{1,0},{2,3},{3,2},{4,5},{5,4},{6,7},{7,6},{8,9},{9,8},{10,11... | collective-permute-start | bytes 1769480 | tf_op jit(solution)/shard_map/ppermute | solution.py:458
  18.2 6.0 copy-start.81
  18.2 6.1 copy-start.48
  18.2 6.1 copy-start.59
  18.2 6.1 copy-start.60
  18.2 250.7 %all-to-all-start = ((bf16[32,72,864]{2,1,0:T(8,128)(2,1)}), bf16[32,72,864]{2,1,0:T(8,128)(2,1)}, u32[]{:S(2)}, u32[]{:S(2)}) async-start(bf16[32,72,864]{2,1,0:T(8,128)(2,1)} %bitcast.206), calls=%async_computation | async-start | bytes 8257536 | tf_op jit(solution)/shard_map/all_to_all | solution.py:79
  23.4 279.8 %all-gather.5.cloned.1.call-start = ((), (), s32[]{:S(2)}) async-start(), calls=%async_computation.4 | async-start | bytes 2488320 | tf_op jit(solution)/shard_map/all_gather | solution.py:439
  197.9 29.1 %copy-start.5 = (bf16[1152,1536]{1,0:T(8,128)(2,1)}, bf16[1152,1536]{1,0:T(8,128)(2,1)S(1)}, u32[]{:S(2)}) copy-start(bf16[1152,1536]{1,0:T(8,128)(2,1)S(1)} %reshape.412) | copy-start | bytes 10616836
  228.2 7.8 %copy-start.21 = (f32[512,256]{0,1:T(8,128)}, f32[512,256]{0,1:T(8,128)S(1)}, u32[]{:S(2)}) copy-start(f32[512,256]{0,1:T(8,128)S(1)} %get-tuple-element.49) | copy-start | bytes 1572868
  242.6 24.3 %copy-start.71 = (f32[256]{0:T(256)}, f32[256]{0:T(256)S(1)}, u32[]{:S(2)}) copy-start(f32[256]{0:T(256)S(1)} %add_rsqrt_fusion.5) | copy-start | bytes 3076
  278.6 15.4 %slice-start = ((s8[4718592]{0:T(1024)(128)(4,1)}), s8[524288]{0:T(1024)(128)(4,1)S(1)}, s32[]{:S(2)}) async-start(s8[4718592]{0:T(1024)(128)(4,1)} %bitcast.196), calls=%async_computation.5 | async-start | bytes 1048576
  282.8 11.1 %slice-start.1 = ((s8[4718592]{0:T(1024)(128)(4,1)}), s8[4194304]{0:T(1024)(128)(4,1)S(1)}, s32[]{:S(2)}) async-start(s8[4718592]{0:T(1024)(128)(4,1)} %bitcast.196), calls=%async_computation.6 | async-start | bytes 8388608
  282.8 11.1 %copy-start.36 = (bf16[1152,864]{1,0:T(8,128)(2,1)S(1)}, bf16[1152,864]{1,0:T(8,128)(2,1)}, u32[]{:S(2)}) copy-start(bf16[1152,864]{1,0:T(8,128)(2,1)} %reshape.422) | copy-start | bytes 5971972
  344.3 32.3 %slice-start.4 = ((s8[7077888]{0:T(1024)(128)(4,1)}), s8[2883584]{0:T(1024)(128)(4,1)S(1)}, s32[]{:S(2)}) async-start(s8[7077888]{0:T(1024)(128)(4,1)} %bitcast.225), calls=%async_computation.9 | async-start | bytes 5767168
  368.4 8.2 %copy-start.83 = (bf16[864,1152]{1,0:T(8,128)(2,1)S(1)}, bf16[864,1152]{1,0:T(8,128)(2,1)}, u32[]{:S(2)}) copy-start(bf16[864,1152]{1,0:T(8,128)(2,1)} %all-gather.5.cloned.1.call-done) | copy-start | bytes 5971972
  368.4 8.2 %slice-start.5 = ((s8[7077888]{0:T(1024)(128)(4,1)}), s8[4194304]{0:T(1024)(128)(4,1)S(1)}, s32[]{:S(2)}) async-start(s8[7077888]{0:T(1024)(128)(4,1)} %bitcast.225), calls=%async_computation.10 | async-start | bytes 8388608
  368.4 20.7 %slice-start.2 = ((s8[4718592]{0:T(1024)(128)(4,1)}), s8[4194304]{0:T(1024)(128)(4,1)S(1)}, s32[]{:S(2)}) async-start(s8[4718592]{0:T(1024)(128)(4,1)} %bitcast.199), calls=%async_computation.7 | async-start | bytes 8388608
  376.6 12.5 %slice-start.3 = ((s8[4718592]{0:T(1024)(128)(4,1)}), s8[524288]{0:T(1024)(128)(4,1)S(1)}, s32[]{:S(2)}) async-start(s8[4718592]{0:T(1024)(128)(4,1)} %bitcast.199), calls=%async_computation.8 | async-start | bytes 1048576
  389.1 8.2 %copy-start.85 = (bf16[2048,864]{0,1:T(8,128)(2,1)S(1)}, bf16[2048,864]{0,1:T(8,128)(2,1)}, u32[]{:S(2)}) copy-start(bf16[2048,864]{0,1:T(8,128)(2,1)} %get-tuple-element.38) | copy-start | bytes 10616836
  403.3 70.6 %all-to-all-start.2 = ((bf16[4,216,1152]{2,1,0:T(8,128)(2,1)}), bf16[4,216,1152]{2,1,0:T(8,128)(2,1)}, u32[]{:S(2)}, u32[]{:S(2)}) async-start(bf16[4,216,1152]{2,1,0:T(8,128)(2,1)} %bitcast.220), calls=%async_computation.2 | async-start | bytes 3981312 | tf_op jit(solution)/shard_map/all_to_all | solution.py:79
  444.1 24.2 %copy-start.11 = (bf16[32,36,864]{2,1,0:T(8,128)(2,1)S(1)}, bf16[32,36,864]{2,1,0:T(8,128)(2,1)}, u32[]{:S(2)}) copy-start(bf16[32,36,864]{2,1,0:T(8,128)(2,1)} %reshape.437) | copy-start | bytes 5971972
  444.1 24.2 %copy-start.12 = (bf16[32,36,864]{2,1,0:T(8,128)(2,1)S(1)}, bf16[32,36,864]{2,1,0:T(8,128)(2,1)}, u32[]{:S(2)}) copy-start(bf16[32,36,864]{2,1,0:T(8,128)(2,1)} %reshape.438) | copy-start | bytes 5971972
  473.9 175.9 %all-to-all-start.1 = ((bf16[32,72,864]{2,1,0:T(8,128)(2,1)}), bf16[32,72,864]{2,1,0:T(8,128)(2,1)}, u32[]{:S(2)}, u32[]{:S(2)}) async-start(bf16[32,72,864]{2,1,0:T(8,128)(2,1)} %pad_maximum_fusion), calls=%async_computation.1 | async-start | bytes 8257536 | tf_op jit(solution)/shard_map/all_to_all | solution.py:79
  481.5 96.0 %copy-start.23 = (bf16[1024,1152]{1,0:T(8,128)(2,1)S(1)}, bf16[1024,1152]{1,0:T(8,128)(2,1)}, u32[]{:S(2)}) copy-start(bf16[1024,1152]{1,0:T(8,128)(2,1)} %all-gather.3.cloned.1.call-done) | copy-start | bytes 7077892
  592.7 8.0 %collective-permute-start.1 = (bf16[256,512]{0,1:T(8,128)(2,1)S(1)}, bf16[256,512]{0,1:T(8,128)(2,1)}, u32[]{:S(2)}, u32[]{:S(2)}) collective-permute-start(bf16[256,512]{0,1:T(8,128)(2,1)S(1)} %fusion.49), channel_id=1, source_target_pairs={{0,1},{1,0},{2,3},{3,2},{4,5},{5,4},{6,7},{7,6},{8,9},{9,8},{10,11... | collective-permute-start | bytes 786440 | tf_op jit(solution)/shard_map/ppermute | solution.py:580
  594.0 6.8 %copy-start.16 = (f32[512,256]{0,1:T(8,128)S(1)}, f32[512,256]{0,1:T(8,128)}, u32[]{:S(2)}) copy-start(f32[512,256]{0,1:T(8,128)} %copy-done.15) | copy-start | bytes 1572868
  594.2 7.6 %copy-start.32 = (f32[256,128]{0,1:T(8,128)S(1)}, f32[256,128]{0,1:T(8,128)}, u32[]{:S(2)}) copy-start(f32[256,128]{0,1:T(8,128)} %copy-done.31) | copy-start | bytes 393220
  594.2 7.6 %copy-start.40 = (f32[256,128]{0,1:T(8,128)S(1)}, f32[256,128]{0,1:T(8,128)}, u32[]{:S(2)}) copy-start(f32[256,128]{0,1:T(8,128)} %copy-done.39) | copy-start | bytes 393220
  594.3 7.6 %copy-start.22 = (f32[512,256]{0,1:T(8,128)S(1)}, f32[512,256]{0,1:T(8,128)}, u32[]{:S(2)}) copy-start(f32[512,256]{0,1:T(8,128)} %copy-done.21) | copy-start | bytes 1572868
  594.3 7.6 %copy-start.62 = (f32[256]{0:T(256)S(1)}, f32[256]{0:T(256)}, u32[]{:S(2)}) copy-start(f32[256]{0:T(256)} %reshape.444) | copy-start | bytes 3076
  594.3 7.6 %copy-start.73 = (f32[256]{0:T(256)S(1)}, f32[256]{0:T(256)}, u32[]{:S(2)}) copy-start(f32[256]{0:T(256)} %add_rsqrt_fusion.4) | copy-start | bytes 3076
  (67 other events, 174.8 us)
Sparse Core Ops, SparseCore 0:
  10.9 77.5 all-gather.2
  90.1 65.7 all-gather.4

commit v3 on v2

--- a/solution.py
+++ b/solution.py
@@ -410,6 +410,14 @@
     mix_rows = output_weight.shape[0]
     padded = (width_rows + 1 + 7) // 8 * 8
 
+    def column_blocks(weight):
+        pieces = weight.reshape(width_rows, planes, members, hidden_rows)
+        return pieces.transpose(2, 0, 1, 3).reshape(members, width_rows, planes * hidden_rows)
+
+    gate_up = jnp.concatenate([column_blocks(gate_weight), column_blocks(up_weight)], axis=1)
+    gate_up = jnp.broadcast_to(gate_up[None], (planes,) + gate_up.shape)
+    gate_up = gate_up.reshape((devices,) + gate_up.shape[2:])
+
     gains = (input_gain, query_gain, key_gain, attnout_gain, ffnin_gain, ffnout_gain)
     gain_row = jnp.concatenate(gains)
     gain_widths = [g.shape[0] for g in gains]
@@ -417,26 +425,26 @@
     qkv_local = jnp.concatenate([query_weight, key_weight, value_weight], axis=1)
     packed = jnp.concatenate([qkv_local, gain_row[None]], axis=0)
     packed = jnp.pad(packed, ((0, padded - width_rows - 1), (0, 0)))
-    packed_all = wide_gather(packed, planes, 0).transpose(1, 0, 2, 3)
-    packed_all = packed_all.reshape(devices, padded, qkv_width)
+    output_wide = jnp.pad(output_weight, ((0, 0), (0, qkv_width - output_weight.shape[1])))
+    packed = jnp.concatenate([packed, output_wide], axis=0)
+    packed_all = wide_gather(packed, planes, 0)
+    gate_up, down_local, packed_all = lax.optimization_barrier(
+        (gate_up, down_weight, packed_all)
+    )
+    gate_up = exchange(gate_up, ALL)
+    gate_full = gate_up[:, :width_rows].reshape(devices * width_rows, planes * hidden_rows)
+    up_full = gate_up[:, width_rows:].reshape(devices * width_rows, planes * hidden_rows)
+    down_full = lax.all_gather(down_local, "z", axis=0, tiled=True)
+    packed_all = packed_all.transpose(1, 0, 2, 3)
+    packed_all = packed_all.reshape(devices, padded + mix_rows, qkv_width)
     qkv_full = packed_all[:, :width_rows].reshape(devices * width_rows, qkv_width)
+    output_full = packed_all[:, padded:, : output_weight.shape[1]]
+    output_full = output_full.reshape(devices * mix_rows, output_weight.shape[1])
     scales, at = [], 0
     for width in gain_widths:
         scales.append(packed_all[:, width_rows, at : at + width].reshape(-1).astype(f32))
         at += width
     input_scale, query_scale, key_scale, attnout_scale, ffnin_scale, ffnout_scale = scales
-    output_full = lax.all_gather(output_weight, ALL, axis=0, tiled=True)
-
-    def column_blocks(weight):
-        pieces = weight.reshape(width_rows, planes, members, hidden_rows)
-        return pieces.transpose(2, 0, 1, 3).reshape(members, width_rows, planes * hidden_rows)
-
-    gate_up = jnp.concatenate([column_blocks(gate_weight), column_blocks(up_weight)], axis=1)
-    gate_up = jnp.broadcast_to(gate_up[None], (planes,) + gate_up.shape)
-    gate_up = exchange(gate_up.reshape((devices,) + gate_up.shape[2:]), ALL)
-    gate_full = gate_up[:, :width_rows].reshape(devices * width_rows, planes * hidden_rows)
-    up_full = gate_up[:, width_rows:].reshape(devices * width_rows, planes * hidden_rows)
-    down_full = lax.all_gather(down_weight, "z", axis=0, tiled=True)
 
     hidden = tokens[0].astype(f32)
     incoming = cotangent[0].astype(f32)
@@ -523,42 +531,31 @@
     gate_grad, up_grad = gelu_back(act_grad)
     gate_low = gate_grad.astype(bf16)
     up_low = up_grad.astype(bf16)
-    ffn_in_grad = plane_scatter_sum(
-        (contract_cols(gate_low, gate_full) + contract_cols(up_low, up_full)).astype(bf16), 4
-    )
-    down_terms = exchange(
-        contract_rows(activated_low, plane_grad)
-        .astype(bf16)
-        .reshape(planes, hidden_rows, down_weight.shape[1]),
-        "z",
-    )
-    down_wgrad = jnp.sum(down_terms.astype(f32), axis=0)
+    down_blocks = contract_rows(activated_low, plane_grad).reshape(
+        planes, hidden_rows, down_weight.shape[1]
+    )
+    plane = lax.axis_index("z")
+    down_wgrad = lax.dynamic_index_in_dim(down_blocks, plane, 0, keepdims=False)
+    down_low = down_blocks.astype(bf16)
+    for k in range(1, planes):
+        leaving = lax.dynamic_index_in_dim(down_low, lax.rem(plane + k, planes), 0, keepdims=False)
+        shift = [(i, (i + k) % planes) for i in range(planes)]
+        down_wgrad = down_wgrad + lax.ppermute(leaving, "z", shift).astype(f32)
 
     def row_blocks(grad):
         return grad.astype(bf16).reshape(devices, width_rows, planes * hidden_rows)
 
-    gate_up_terms = exchange(
-        jnp.concatenate(
-            [
-                row_blocks(contract_rows(plane_in, gate_low)),
-                row_blocks(contract_rows(plane_in, up_low)),
-            ],
-            axis=1,
-        ),
-        ALL,
-    )
-    gate_up_sum = jnp.sum(
-        gate_up_terms.astype(f32).reshape(
-            planes, members, 2 * width_rows, planes * hidden_rows
-        ),
-        axis=0,
-    )
-    gate_up_sum = gate_up_sum.reshape(members, 2, width_rows, planes, hidden_rows)
-    gate_up_sum = gate_up_sum.transpose(1, 2, 3, 0, 4).reshape(
-        2, width_rows, planes * members * hidden_rows
-    )
-    gate_wgrad, up_wgrad = gate_up_sum[0], gate_up_sum[1]
-
+    gate_up_blocks = jnp.concatenate(
+        [
+            row_blocks(contract_rows(plane_in, gate_low)),
+            row_blocks(contract_rows(plane_in, up_low)),
+        ],
+        axis=1,
+    )
+    ffn_in_part = (contract_cols(gate_low, gate_full) + contract_cols(up_low, up_full)).astype(bf16)
+    gate_up_blocks, ffn_in_part = lax.optimization_barrier((gate_up_blocks, ffn_in_part))
+    gate_up_terms = exchange(gate_up_blocks, ALL)
+    ffn_in_grad = plane_scatter_sum(ffn_in_part, 4)
     ffnin_gain_grad = jnp.sum(ffn_in_grad * norm_middle, axis=0)
     middle_grad = incoming + rms_back(ffn_in_grad * ffnin_scale, norm_middle, inv_middle)
     attnout_gain_grad = jnp.sum(middle_grad * norm_attn, axis=0)
@@ -597,12 +594,6 @@
     input_gain_grad = jnp.sum(normed_grad * norm_input, axis=0)
     input_grad = middle_grad + rms_back(normed_grad * input_scale, norm_input, inv_input)
 
-    def to_owners(grad, collective_id):
-        rows, columns = grad.shape[0] // devices, grad.shape[1]
-        blocks = grad.astype(bf16).reshape(planes, members, rows, columns)
-        return owner_sum(blocks.transpose(1, 0, 2, 3), collective_id)
-
-    output_share = to_owners(output_wgrad, 5)
     gain_grads = (
         input_gain_grad,
         query_gain_grad,
@@ -613,11 +604,31 @@
     )
     gain_rows = jnp.concatenate([g.reshape(devices, -1) for g in gain_grads], axis=1)
     gain_rows = jnp.pad(gain_rows, ((0, 0), (0, qkv_width - gain_rows.shape[1])))
-    qkv_blocks = jnp.concatenate(
+    blocks = jnp.concatenate(
         [qkv_wgrad.reshape(devices, width_rows, qkv_width), gain_rows[:, None]], axis=1
     )
-    qkv_blocks = jnp.pad(qkv_blocks, ((0, 0), (0, padded - width_rows - 1), (0, 0)))
-    qkv_share = to_owners(qkv_blocks.reshape(devices * padded, qkv_width), 6)
+    blocks = jnp.pad(blocks.astype(bf16), ((0, 0), (0, padded - width_rows - 1), (0, 0)))
+    output_blocks = output_wgrad.astype(bf16).reshape(devices, mix_rows, -1)
+    output_blocks = jnp.pad(
+        output_blocks, ((0, 0), (0, 0), (0, qkv_width - output_blocks.shape[2]))
+    )
+    blocks = jnp.concatenate([blocks, output_blocks], axis=1)
+    blocks = blocks.reshape(planes, members, padded + mix_rows, qkv_width)
+    blocks, gate_up_terms = lax.optimization_barrier((blocks, gate_up_terms))
+    share = owner_sum(blocks.transpose(1, 0, 2, 3), 5)
+    gate_up_sum = jnp.sum(
+        gate_up_terms.astype(f32).reshape(
+            planes, members, 2 * width_rows, planes * hidden_rows
+        ),
+        axis=0,
+    )
+    gate_up_sum = gate_up_sum.reshape(members, 2, width_rows, planes, hidden_rows)
+    gate_up_sum = gate_up_sum.transpose(1, 2, 3, 0, 4).reshape(
+        2, width_rows, planes * members * hidden_rows
+    )
+    gate_wgrad, up_wgrad = gate_up_sum[0], gate_up_sum[1]
+
+    qkv_share, output_share = share[:padded], share[padded:, : output_weight.shape[1]]
     gain_shares, at = [], 0
     for width in gain_widths:
         gain_shares.append(qkv_share[width_rows, at : at + width])

time: 678 us -> 597 us (0.88)
  Pallas kernels: 389 us -> 225 us
  waiting for transfers between devices: 4.51 us -> 61.8 us
  local copies, waits for them, and re-layouts: 103 us -> 123 us
  other arithmetic: 41.9 us -> 49.8 us
    pallas_call x1, Pallas kernels: 163 us -> 54.9 us  [wide_gather(): pl.pallas_call(functools.partial(wide_gather_kernel, planes), out_shape=j...]
    pallas_call x2 -> x1, Pallas kernels: 129 us -> 61.3 us  [owner_sum(): pl.pallas_call(functools.partial(owner_sum_kernel, planes), out_shape=jax...]
    all_to_all x3 -> x2, waiting for transfers between devices: 0.01 us -> 54.5 us  [exchange(): return lax.all_to_all(blocks, axes, split_axis=0, concat_axis=0, tiled=True)]
    pallas_call x2, Pallas kernels: 48.2 us -> 58.7 us  [plane_gather(): pl.pallas_call(gather_kernel, out_shape=jax.ShapeDtypeStruct((members, ro...]
    all_to_all x3 -> x2, starting transfers between devices: 15.8 us -> 10.2 us  [exchange(): return lax.all_to_all(blocks, axes, split_axis=0, concat_axis=0, tiled=True)]
    unnamed x186 -> x213, local copies, waits for them, and re-layouts: 13.1 us -> 16.4 us
  transfers between devices with their start and end apart: 7 -> 8, of which waited for: 1 -> 3; matrix products, arithmetic and copies ran while one was open for 25% -> 30% of each run, Pallas kernels for 51% -> 19%
where the time goes in v3:
time: 597 us; the launch traced here: 590 us
  Pallas kernels  225 us (38%)
  local copies, waits for them, and re-layouts  123 us (21%)
  matrix products  96.4 us (16%)
  waiting for transfers between devices  61.8 us (10%)
  other arithmetic  49.8 us (8%)
  starting transfers between devices  19 us (3%)
  between operations  15.6 us (3%)
    pallas_call x1, Pallas kernels, owner_sum(): pl.pallas_call(functools.partial(owner_sum_kernel, planes), out_shape=jax...  61.3 us
    pallas_call x2, Pallas kernels, plane_gather(): pl.pallas_call(gather_kernel, out_shape=jax.ShapeDtypeStruct((members, ro...  58.7 us
    pallas_call x1, Pallas kernels, wide_gather(): pl.pallas_call(functools.partial(wide_gather_kernel, planes), out_shape=j...  54.9 us
    all_to_all x2, waiting for transfers between devices, exchange(): return lax.all_to_all(blocks, axes, split_axis=0, concat_axis=0, tiled=True)  54.5 us
    pallas_call x2, Pallas kernels, plane_scatter_sum(): pl.pallas_call(plane_sum_kernel, out_shape=jax.ShapeDtypeStruct(shape, jn...  49.7 us
    dot_general x5, matrix products, contract_cols(): lax.dot_general(left, right, (((1,), (1,)), ((), ())), preferred_element_...  35.2 us
    dot_general x6, matrix products, matmul(): return jnp.dot(left, right, preferred_element_type=jnp.float32)  32.3 us
    dot_general x5, matrix products, contract_rows(): lax.dot_general(left, right, (((0,), (0,)), ((), ())), preferred_element_...  21.6 us
  transfers between devices with their start and end apart: 8, of which 3 were waited for; matrix products, arithmetic and copies ran while one was open for 30% of the time, Pallas kernels for 19%

profile of v3, /device:TPU:8, one launch (start us, length us, event | category | flops | bytes accessed | tf_op | source)
XLA Modules:
  0.0 590.3 jit_solution(6250734928961816521)
XLA Ops:
  15.9 54.9 %shard_map.274 = bf16[8,4,72,1536]{3,2,1,0:T(8,128)(2,1)} custom-call(bf16[72,1536]{1,0:T(8,128)(2,1)S(1)} %fusion.73.own_ref), custom_call_target="tpu_custom_call" | custom-call | bytes 105000000 | tf_op jit(solution)/shard_map/pallas_call | solution.py:209
  73.2 4.8 all-to-all-start
  87.9 4.0 reshape.418
  97.1 4.3 copy.127
  136.1 35.0 %shard_map.275 = bf16[8,16,16,1152]{3,2,1,0:T(8,128)(2,1)S(1)} custom-call(bf16[16,16,1152]{2,1,0:T(8,128)(2,1)S(1)} %bitcast.218), custom_call_target="tpu_custom_call" | custom-call | bytes 75000000 | tf_op jit(solution)/shard_map/pallas_call | solution.py:231
  174.6 24.3 %all-to-all-done = bf16[32,72,864]{2,1,0:T(8,128)(2,1)} async-done(((bf16[32,72,864]{2,1,0:T(8,128)(2,1)}), bf16[32,72,864]{2,1,0:T(8,128)(2,1)}, u32[]{:S(2)}, u32[]{:S(2)}) %all-to-all-start) | async-done | bytes 3981344 | tf_op jit(solution)/shard_map/all_to_all | solution.py:79
  198.9 5.4 fusion.107
  204.3 4.2 reshape.423
  208.5 4.2 reshape.424
  212.7 8.2 %fusion.113 = f32[2048,864]{0,1:T(8,128)S(1)} fusion(bf16[2048,1152]{1,0:T(8,128)(2,1)} %bitcast.208, bf16[1152,864]{1,0:T(8,128)(2,1)} %reshape.423), kind=kOutput, calls=%fused_computation.237 | convolution fusion | flops 4076863488 | bytes 13787136 | tf_op jit(solution)/shard_map/dot_general | solution.py:52
  223.9 9.2 %fusion.18 = (bf16[864,2048]{1,0:T(8,128)(2,1)}, f32[2048,864]{0,1:T(8,128)}) fusion(f32[2048,864]{0,1:T(8,128)S(1)} %fusion.113, bf16[2048,1152]{1,0:T(8,128)(2,1)S(1)} %bitcast.211, bf16[1152,864]{1,0:T(8,128)(2,1)S(1)} %copy-done.42), kind=kOutput, calls=%fused_computation.26 | convolution fusion | flops 4094558208 | bytes 24403968 | tf_op jit(solution)/shard_map/dot_general | solution.py:52
  233.1 10.0 %convolution_convert_fusion = bf16[2048,1152]{1,0:T(8,128)(2,1)S(1)} fusion(bf16[864,1152]{1,0:T(8,128)(2,1)} %all-gather.2.cloned.1.call-done, f32[2048,864]{0,1:T(8,128)} %get-tuple-element.98, f32[2048,864]{0,1:T(8,128)} %copy-done.96), kind=kOutput, calls=%fused_computation.10 | convolution fusion | flops 4096917504 | bytes 20865024 | tf_op jit(solution)/shard_map/dot_general | solution.py:52
  243.1 26.1 %shard_map.276 = f32[16,16,1152]{2,1,0:T(8,128)S(1)} custom-call(bf16[8,16,16,1152]{3,2,1,0:T(8,128)(2,1)S(1)} %bitcast.207), custom_call_target="tpu_custom_call" | custom-call | bytes 75000000 | tf_op jit(solution)/shard_map/pallas_call | solution.py:318
  277.8 23.7 %shard_map.277 = bf16[8,16,16,1152]{3,2,1,0:T(8,128)(2,1)S(1)} custom-call(bf16[16,16,1152]{2,1,0:T(8,128)(2,1)S(1)} %multiply_convert_fusion.4.own_ref), custom_call_target="tpu_custom_call" | custom-call | bytes 75000000 | tf_op jit(solution)/shard_map/pallas_call | solution.py:231
  301.5 15.1 %fusion.9 = (bf16[2048,864]{0,1:T(8,128)(2,1)}, bf16[2048,864]{0,1:T(8,128)(2,1)}) fusion(f32[2048,864]{0,1:T(8,128)} %copy-done.96, f32[2048,864]{0,1:T(8,128)} %get-tuple-element.98, bf16[2048,1152]{1,0:T(8,128)(2,1)S(1)} %bitcast.216, bf16[864,1152]{1,0:T(8,128)(2,1)} %all-gather.2.cloned.1.call-done), kind=kOutput, calls=%fused_computation.17 | convolution fusion | flops 4119330816 | bytes 27942912 | tf_op jit(solution)/shard_map/dot_general | solution.py:62
  316.7 7.7 %fusion.114 = f32[2048,1152]{1,0:T(8,128)S(1)} fusion(bf16[2048,864]{0,1:T(8,128)(2,1)} %get-tuple-element.52, bf16[1152,864]{1,0:T(8,128)(2,1)S(1)} %copy-done.44), kind=kOutput, calls=%fused_computation.238 | convolution fusion | flops 4076863488 | bytes 14966784 | tf_op jit(solution)/shard_map/dot_general | solution.py:62
  324.4 5.9 convolution_convert_fusion.4
  330.3 6.4 %fusion.112 = (bf16[4,216,1152]{2,1,0:T(8,128)(2,1)S(1)}, f32[4,216,1152]{2,1,0:T(8,128)}) fusion(bf16[4,216,2048]{2,1,0:T(8,128)(2,1)S(1)} %bitcast.245, bf16[2048,1152,1]{1,0,2:T(8,128)(2,1)S(1)} %bitcast.217), kind=kOutput, calls=%fused_computation.236 | convolution fusion | flops 4077858816 | bytes 14229504 | tf_op jit(solution)/shard_map/dot_general | solution.py:56
  338.4 4.2 collective-permute-start.3
  343.4 5.9 convolution_convert_fusion.3
  349.3 7.3 %add_convert_fusion = bf16[2048,1152]{1,0:T(8,128)(2,1)} fusion(f32[2048,1152]{1,0:T(8,128)S(1)} %fusion.114, bf16[2048,864]{0,1:T(8,128)(2,1)S(1)} %copy-done.99, bf16[1152,864]{1,0:T(8,128)(2,1)S(1)} %copy-done.43), kind=kOutput, calls=%fused_computation.5 | convolution fusion | flops 4081582080 | bytes 19685376 | tf_op jit(solution)/shard_map/dot_general | solution.py:62
  356.5 4.1 copy.138
  364.6 4.1 copy.139
  368.6 4.0 reshape.429
  372.7 5.7 pad_maximum_fusion
  378.4 23.6 %shard_map.278 = f32[16,16,1152]{2,1,0:T(8,128)S(1)} custom-call(bf16[8,16,16,1152]{3,2,1,0:T(8,128)(2,1)S(1)} %bitcast.206), custom_call_target="tpu_custom_call" | custom-call | bytes 75000000 | tf_op jit(solution)/shard_map/pallas_call | solution.py:318
  404.4 5.4 all-to-all-start.1
  440.2 6.9 %collective-permute-done.1 = bf16[256,512]{0,1:T(8,128)(2,1)} collective-permute-done((bf16[256,512]{0,1:T(8,128)(2,1)}, bf16[256,512]{0,1:T(8,128)(2,1)}, u32[]{:S(2)}, u32[]{:S(2)}) %collective-permute-start.1) | collective-permute-done | bytes 262176 | tf_op jit(solution)/shard_map/ppermute | solution.py:577
  468.8 30.2 %all-to-all-done.1 = bf16[32,72,864]{2,1,0:T(8,128)(2,1)} async-done(((bf16[32,72,864]{2,1,0:T(8,128)(2,1)}), bf16[32,72,864]{2,1,0:T(8,128)(2,1)}, u32[]{:S(2)}, u32[]{:S(2)}) %all-to-all-start.1) | async-done | bytes 3981344 | tf_op jit(solution)/shard_map/all_to_all | solution.py:79
  498.9 6.7 %copy.174 = bf16[4,8,72,1536]{3,2,0,1:T(8,128)(2,1)} copy(bf16[4,8,72,1536]{3,2,1,0:T(8,128)(2,1)} %bitcast.219) | data formatting | bytes 14155776 | tf_op jit(solution)/shard_map/optimization_barrier | solution.py:617
  505.6 61.3 %shard_map.279 = f32[72,1536]{1,0:T(8,128)S(1)} custom-call(bf16[8,4,72,1536]{3,2,1,0:T(8,128)(2,1)} %bitcast.220), custom_call_target="tpu_custom_call" | custom-call | bytes 105000000 | tf_op jit(solution)/shard_map/pallas_call | solution.py:361
  570.1 4.3 convert_reduce_fusion
  (361 shorter events, 147.5 us)
Async XLA Ops:
  7.2 115.1 %collective-permute-start = (bf16[256,1152]{1,0:T(8,128)(2,1)}, bf16[256,1152]{1,0:T(8,128)(2,1)}, u32[]{:S(2)}, u32[]{:S(2)}) collective-permute-start(bf16[256,1152]{1,0:T(8,128)(2,1)} %bitcast.228), channel_id=1, source_target_pairs={{0,1},{1,0},{2,3},{3,2},{4,5},{5,4},{6,7},{7,6},{8,9},{9,8},{10,11... | collective-permute-start | bytes 1769480 | tf_op jit(solution)/shard_map/ppermute | solution.py:466
  73.2 125.8 %all-to-all-start = ((bf16[32,72,864]{2,1,0:T(8,128)(2,1)}), bf16[32,72,864]{2,1,0:T(8,128)(2,1)}, u32[]{:S(2)}, u32[]{:S(2)}) async-start(bf16[32,72,864]{2,1,0:T(8,128)(2,1)} %bitcast.226), calls=%async_computation | async-start | bytes 8257536 | tf_op jit(solution)/shard_map/all_to_all | solution.py:79
  78.0 155.1 %all-gather.2.cloned.1.call-start = ((), (), s32[]{:S(2)}) async-start(), calls=%async_computation.2 | async-start | bytes 2488320 | tf_op jit(solution)/shard_map/all_gather | solution.py:437
  91.9 32.1 %copy-start.6 = (bf16[1152,1536]{1,0:T(8,128)(2,1)}, bf16[1152,1536]{1,0:T(8,128)(2,1)S(1)}, u32[]{:S(2)}) copy-start(bf16[1152,1536]{1,0:T(8,128)(2,1)S(1)} %reshape.418) | copy-start | bytes 10616836
  136.1 37.1 %copy-start.55 = (f32[256,128]{0,1:T(8,128)S(1)}, f32[256,128]{0,1:T(8,128)}, u32[]{:S(2)}) copy-start(f32[256,128]{0,1:T(8,128)} %get-tuple-element.47) | copy-start | bytes 393220
  136.1 37.9 %copy-start.24 = (f32[512,256]{0,1:T(8,128)S(1)}, f32[512,256]{0,1:T(8,128)}, u32[]{:S(2)}) copy-start(f32[512,256]{0,1:T(8,128)} %get-tuple-element.66) | copy-start | bytes 1572868
  208.5 15.4 %slice-start.2 = ((s8[4718592]{0:T(1024)(128)(4,1)}), s8[524288]{0:T(1024)(128)(4,1)S(1)}, s32[]{:S(2)}) async-start(s8[4718592]{0:T(1024)(128)(4,1)} %bitcast.209), calls=%async_computation.5 | async-start | bytes 1048576
  212.7 11.2 %slice-start.3 = ((s8[4718592]{0:T(1024)(128)(4,1)}), s8[4194304]{0:T(1024)(128)(4,1)S(1)}, s32[]{:S(2)}) async-start(s8[4718592]{0:T(1024)(128)(4,1)} %bitcast.209), calls=%async_computation.6 | async-start | bytes 8388608
  212.7 11.2 %copy-start.42 = (bf16[1152,864]{1,0:T(8,128)(2,1)S(1)}, bf16[1152,864]{1,0:T(8,128)(2,1)}, u32[]{:S(2)}) copy-start(bf16[1152,864]{1,0:T(8,128)(2,1)} %reshape.424) | copy-start | bytes 5971972
  277.8 46.6 %slice-start.4 = ((s8[4718592]{0:T(1024)(128)(4,1)}), s8[524288]{0:T(1024)(128)(4,1)S(1)}, s32[]{:S(2)}) async-start(s8[4718592]{0:T(1024)(128)(4,1)} %bitcast.212), calls=%async_computation.7 | async-start | bytes 1048576
  301.5 15.1 %copy-start.44 = (bf16[1152,864]{1,0:T(8,128)(2,1)S(1)}, bf16[1152,864]{1,0:T(8,128)(2,1)}, u32[]{:S(2)}) copy-start(bf16[1152,864]{1,0:T(8,128)(2,1)} %reshape.423) | copy-start | bytes 5971972
  301.5 22.9 %slice-start.5 = ((s8[4718592]{0:T(1024)(128)(4,1)}), s8[4194304]{0:T(1024)(128)(4,1)S(1)}, s32[]{:S(2)}) async-start(s8[4718592]{0:T(1024)(128)(4,1)} %bitcast.212), calls=%async_computation.8 | async-start | bytes 8388608
  316.6 7.8 %copy-start.97 = (bf16[2048,864]{0,1:T(8,128)(2,1)S(1)}, bf16[2048,864]{0,1:T(8,128)(2,1)}, u32[]{:S(2)}) copy-start(bf16[2048,864]{0,1:T(8,128)(2,1)} %get-tuple-element.52) | copy-start | bytes 10616836
  330.3 13.0 %copy-start.98 = (bf16[2048,864]{0,1:T(8,128)(2,1)S(1)}, bf16[2048,864]{0,1:T(8,128)(2,1)}, u32[]{:S(2)}) copy-start(bf16[2048,864]{0,1:T(8,128)(2,1)} %get-tuple-element.53) | copy-start | bytes 10616836
  337.9 128.0 %collective-permute-start.2 = (bf16[216,1152]{1,0:T(8,128)(2,1)}, bf16[216,1152]{1,0:T(8,128)(2,1)}, u32[]{:S(2)}, u32[]{:S(2)}) collective-permute-start(bf16[216,1152]{1,0:T(8,128)(2,1)} %get-tuple-element.58), channel_id=1, source_target_pairs={{0,8},{8,16},{16,24},{24,0},{1,9},{9,17},{17,25},{25,1},{2,10},{10... | collective-permute-start | bytes 1493000 | tf_op jit(solution)/shard_map/ppermute | solution.py:543
  338.4 127.6 %collective-permute-start.3 = (bf16[216,1152]{1,0:T(8,128)(2,1)}, bf16[216,1152]{1,0:T(8,128)(2,1)}, u32[]{:S(2)}, u32[]{:S(2)}) collective-permute-start(bf16[216,1152]{1,0:T(8,128)(2,1)} %get-tuple-element.60), channel_id=1, source_target_pairs={{0,16},{8,24},{16,0},{24,8},{1,17},{9,25},{17,1},{25,9},{2,18},{10... | collective-permute-start | bytes 1493000 | tf_op jit(solution)/shard_map/ppermute | solution.py:543
  342.6 123.3 %collective-permute-start.4 = (bf16[216,1152]{1,0:T(8,128)(2,1)}, bf16[216,1152]{1,0:T(8,128)(2,1)}, u32[]{:S(2)}, u32[]{:S(2)}) collective-permute-start(bf16[216,1152]{1,0:T(8,128)(2,1)} %get-tuple-element.59), channel_id=1, source_target_pairs={{0,24},{8,0},{16,8},{24,16},{1,25},{9,1},{17,9},{25,17},{2,26},{10... | collective-permute-start | bytes 1493000 | tf_op jit(solution)/shard_map/ppermute | solution.py:543
  368.6 9.8 %slice-start = ((s8[4718592]{0:T(1024)(128)(4,1)}), s8[524288]{0:T(1024)(128)(4,1)S(1)}, s32[]{:S(2)}) async-start(s8[4718592]{0:T(1024)(128)(4,1)} %bitcast.204), calls=%async_computation.3 | async-start | bytes 1048576
  378.4 23.6 %copy-start.82 = (f32[256]{0:T(256)S(1)}, f32[256]{0:T(256)}, u32[]{:S(2)}) copy-start(f32[256]{0:T(256)} %copy-done.81) | copy-start | bytes 3076
  404.4 94.6 %all-to-all-start.1 = ((bf16[32,72,864]{2,1,0:T(8,128)(2,1)}), bf16[32,72,864]{2,1,0:T(8,128)(2,1)}, u32[]{:S(2)}, u32[]{:S(2)}) async-start(bf16[32,72,864]{2,1,0:T(8,128)(2,1)} %pad_maximum_fusion), calls=%async_computation.1 | async-start | bytes 8257536 | tf_op jit(solution)/shard_map/all_to_all | solution.py:79
  431.3 6.5 %copy-start.27 = (bf16[256,1152]{1,0:T(8,128)(2,1)S(1)}, bf16[256,1152]{1,0:T(8,128)(2,1)}, u32[]{:S(2)}) copy-start(bf16[256,1152]{1,0:T(8,128)(2,1)} %copy-done.26) | copy-start | bytes 1769476
  431.3 6.5 %copy-start.34 = (bf16[256,4,256]{2,0,1:T(8,128)(2,1)S(1)}, bf16[256,4,256]{2,0,1:T(8,128)(2,1)}, u32[]{:S(2)}) copy-start(bf16[256,4,256]{2,0,1:T(8,128)(2,1)} %copy-done.33) | copy-start | bytes 1572868
  434.1 13.0 %collective-permute-start.1 = (bf16[256,512]{0,1:T(8,128)(2,1)}, bf16[256,512]{0,1:T(8,128)(2,1)}, u32[]{:S(2)}, u32[]{:S(2)}) collective-permute-start(bf16[256,512]{0,1:T(8,128)(2,1)} %fusion.62), channel_id=1, source_target_pairs={{0,1},{1,0},{2,3},{3,2},{4,5},{5,4},{6,7},{7,6},{8,9},{9,8},{10,11... | collective-permute-start | bytes 786440 | tf_op jit(solution)/shard_map/ppermute | solution.py:577
  437.8 9.3 %copy-start.20 = (f32[512,256]{0,1:T(8,128)S(1)}, f32[512,256]{0,1:T(8,128)}, u32[]{:S(2)}) copy-start(f32[512,256]{0,1:T(8,128)} %copy-done.19) | copy-start | bytes 1572868
  437.8 9.3 %copy-start.36 = (f32[512,256]{0,1:T(8,128)S(1)}, f32[512,256]{0,1:T(8,128)}, u32[]{:S(2)}) copy-start(f32[512,256]{0,1:T(8,128)} %copy-done.35) | copy-start | bytes 1572868
  437.8 11.0 %copy-start.38 = (f32[256,128]{0,1:T(8,128)S(1)}, f32[256,128]{0,1:T(8,128)}, u32[]{:S(2)}) copy-start(f32[256,128]{0,1:T(8,128)} %copy-done.37) | copy-start | bytes 393220
  437.9 11.0 %copy-start.48 = (f32[256,128]{0,1:T(8,128)S(1)}, f32[256,128]{0,1:T(8,128)}, u32[]{:S(2)}) copy-start(f32[256,128]{0,1:T(8,128)} %copy-done.47) | copy-start | bytes 393220
  437.9 11.0 %copy-start.25 = (f32[512,256]{0,1:T(8,128)S(1)}, f32[512,256]{0,1:T(8,128)}, u32[]{:S(2)}) copy-start(f32[512,256]{0,1:T(8,128)} %get-tuple-element.66) | copy-start | bytes 1572868
  437.9 11.0 %copy-start.74 = (f32[256]{0:T(256)S(1)}, f32[256]{0:T(256)}, u32[]{:S(2)}) copy-start(f32[256]{0:T(256)} %reshape.446) | copy-start | bytes 3076
  437.9 11.0 %copy-start.83 = (f32[256]{0:T(256)S(1)}, f32[256]{0:T(256)}, u32[]{:S(2)}) copy-start(f32[256]{0:T(256)} %add_rsqrt_fusion.4) | copy-start | bytes 3076
  440.2 13.5 %copy-start.7 = (bf16[1152,1536]{1,0:T(8,128)(2,1)S(1)}, bf16[1152,1536]{1,0:T(8,128)(2,1)}, u32[]{:S(2)}) copy-start(bf16[1152,1536]{1,0:T(8,128)(2,1)} %copy-done.6) | copy-start | bytes 10616836
  440.2 13.5 %copy-start.65 = (f32[1152]{0:T(1024)S(1)}, f32[1152]{0:T(1024)}, u32[]{:S(2)}) copy-start(f32[1152]{0:T(1024)} %reshape.445) | copy-start | bytes 13828
  (82 other events, 194.7 us)
Sparse Core Ops, SparseCore 0:
  80.4 86.6 all-gather.1

commit v4 on v3

--- a/solution.py
+++ b/solution.py
@@ -179,21 +179,19 @@
     plane_spread(own_ref, out_ref, *sems)
 
 
-def wide_gather_kernel(planes, own_ref, out_ref, held, z_send, z_recv, own_sem, *sems):
+def z_gather_kernel(planes, own_ref, out_ref, send_sems, recv_sems, own_sem):
     z, x, core, seq = (lax.axis_index(name) for name in ALL)
     others = [(lax.rem(z + k, planes), x, core, seq) for k in range(1, planes)]
-    greet((*plane_places()[:3], *others))
-    slot = held.at[z]
-    keep = pltpu.make_async_copy(own_ref, slot, own_sem)
+    greet(others)
+    keep = pltpu.make_async_copy(own_ref, out_ref.at[z], own_sem)
     keep.start()
-    send = sender(z_send, z_recv)
-    copies = [send(k, own_ref, slot, place) for k, place in enumerate(others)]
+    send = sender(send_sems, recv_sems)
+    copies = [send(k, own_ref, out_ref.at[z], place) for k, place in enumerate(others)]
     for copy in copies:
         copy.wait_recv()
-    keep.wait()
-    plane_spread(held, out_ref, *sems)
     for copy in copies:
         copy.wait_send()
+    keep.wait()
 
 
 GATHER_SEMS = [
@@ -203,22 +201,18 @@
 ]
 
 
-def wide_gather(local, planes, collective_id):
-    rows, columns = local.shape
-    members = 8
+def z_gather(local, planes, collective_id):
     return pl.pallas_call(
-        functools.partial(wide_gather_kernel, planes),
-        out_shape=jax.ShapeDtypeStruct((members, planes, rows, columns), local.dtype),
+        functools.partial(z_gather_kernel, planes),
+        out_shape=jax.ShapeDtypeStruct((planes, *local.shape), local.dtype),
         in_specs=[pl.BlockSpec(memory_space=pltpu.VMEM)],
         out_specs=pl.BlockSpec(memory_space=pl.ANY),
         scratch_shapes=[
-            pltpu.VMEM((planes, rows, columns), local.dtype),
             pltpu.SemaphoreType.DMA((planes - 1,)),
             pltpu.SemaphoreType.DMA((planes - 1,)),
             pltpu.SemaphoreType.DMA,
-            *GATHER_SEMS,
         ],
-        cost_estimate=busy(35),
+        cost_estimate=busy(20),
         compiler_params=pltpu.CompilerParams(
             collective_id=collective_id, has_side_effects=True, vmem_limit_bytes=VMEM_BYTES
         ),
@@ -226,11 +220,10 @@
 
 
 def plane_gather(local, collective_id):
-    rows, columns = local.shape
     members = 8
-    out = pl.pallas_call(
+    return pl.pallas_call(
         gather_kernel,
-        out_shape=jax.ShapeDtypeStruct((members, rows // 16, 16, columns), local.dtype),
+        out_shape=jax.ShapeDtypeStruct((members, *local.shape), local.dtype),
         in_specs=[pl.BlockSpec(memory_space=pl.ANY)],
         out_specs=pl.BlockSpec(memory_space=pl.ANY),
         scratch_shapes=GATHER_SEMS,
@@ -238,8 +231,13 @@
         compiler_params=pltpu.CompilerParams(
             collective_id=collective_id, has_side_effects=True, vmem_limit_bytes=VMEM_BYTES
         ),
-    )(local.reshape(rows // 16, 16, columns))
-    return out.reshape(members * rows, columns)
+    )(local)
+
+
+def gather_rows(local, collective_id):
+    rows, columns = local.shape
+    out = plane_gather(local.reshape(rows // 16, 16, columns), collective_id)
+    return out.reshape(-1, columns)
 
 
 def add_rows(target, sources, start, count):
@@ -427,10 +425,11 @@
     packed = jnp.pad(packed, ((0, padded - width_rows - 1), (0, 0)))
     output_wide = jnp.pad(output_weight, ((0, 0), (0, qkv_width - output_weight.shape[1])))
     packed = jnp.concatenate([packed, output_wide], axis=0)
-    packed_all = wide_gather(packed, planes, 0)
+    packed_all = z_gather(packed, planes, 0)
     gate_up, down_local, packed_all = lax.optimization_barrier(
         (gate_up, down_weight, packed_all)
     )
+    packed_all = plane_gather(packed_all, 6)
     gate_up = exchange(gate_up, ALL)
     gate_full = gate_up[:, :width_rows].reshape(devices * width_rows, planes * hidden_rows)
     up_full = gate_up[:, width_rows:].reshape(devices * width_rows, planes * hidden_rows)
@@ -514,7 +513,7 @@
     norm_middle = middle * inv_middle
     ffn_in = (norm_middle * ffnin_scale).astype(bf16)
 
-    plane_in = plane_gather(ffn_in, 1)
+    plane_in = gather_rows(ffn_in, 1)
     gate_proj = matmul(plane_in, gate_full)
     up_proj = matmul(plane_in, up_full)
     activated, gelu_back = jax.vjp(gelu_pair, gate_proj, up_proj)
@@ -526,7 +525,7 @@
     ffnout_gain_grad = jnp.sum(incoming * norm_ffn, axis=0)
     ffn_raw_grad = rms_back(incoming * ffnout_scale, norm_ffn, inv_ffn).astype(bf16)
 
-    plane_grad = plane_gather(ffn_raw_grad, 3)
+    plane_grad = gather_rows(ffn_raw_grad, 3)
     act_grad = contract_cols(plane_grad, down_full)
     gate_grad, up_grad = gelu_back(act_grad)
     gate_low = gate_grad.astype(bf16)
@@ -614,7 +613,6 @@
     )
     blocks = jnp.concatenate([blocks, output_blocks], axis=1)
     blocks = blocks.reshape(planes, members, padded + mix_rows, qkv_width)
-    blocks, gate_up_terms = lax.optimization_barrier((blocks, gate_up_terms))
     share = owner_sum(blocks.transpose(1, 0, 2, 3), 5)
     gate_up_sum = jnp.sum(
         gate_up_terms.astype(f32).reshape(

time: 597 us -> 576 us (0.965)
  waiting for transfers between devices: 61.8 us -> 8.23 us
  Pallas kernels: 225 us -> 254 us
    all_to_all x2, waiting for transfers between devices: 54.5 us -> 0.01 us  [exchange(): return lax.all_to_all(blocks, axes, split_axis=0, concat_axis=0, tiled=True)]
    pallas_call x3 -> x4, Pallas kernels: 114 us -> 132 us  [the longest x3 110 us: plane_gather(): pl.pallas_call(gather_kernel, out_shape=jax.ShapeDtypeStruct((members, *l...]
    pallas_call x1, Pallas kernels: 61.3 us -> 72.5 us  [owner_sum(): pl.pallas_call(functools.partial(owner_sum_kernel, planes), out_shape=jax...]
    optimization_barrier x1 -> x0, local copies, waits for them, and re-layouts: 6.66 us -> none  [body(): blocks, gate_up_terms = lax.optimization_barrier((blocks, gate_up_terms))]
    unnamed x213 -> x211, local copies, waits for them, and re-layouts: 16.4 us -> 15.8 us
  transfers between devices with their start and end apart: 8 -> 8, of which waited for: 3 -> 1; matrix products, arithmetic and copies ran while one was open for 30% -> 33% of each run, Pallas kernels for 19% -> 36%
where the time goes in v4:
time: 576 us; the launch traced here: 569 us
  Pallas kernels  254 us (44%)
  local copies, waits for them, and re-layouts  119 us (21%)
  matrix products  97.8 us (17%)
  other arithmetic  52 us (9%)
  starting transfers between devices  21.9 us (4%)
  between operations  15.6 us (3%)
  waiting for transfers between devices  8.23 us (1%)
    pallas_call x3, Pallas kernels, plane_gather(): pl.pallas_call(gather_kernel, out_shape=jax.ShapeDtypeStruct((members, *l...  110 us
    pallas_call x1, Pallas kernels, owner_sum(): pl.pallas_call(functools.partial(owner_sum_kernel, planes), out_shape=jax...  72.5 us
    pallas_call x2, Pallas kernels, plane_scatter_sum(): pl.pallas_call(plane_sum_kernel, out_shape=jax.ShapeDtypeStruct(shape, jn...  48.9 us
    dot_general x5, matrix products, contract_cols(): lax.dot_general(left, right, (((1,), (1,)), ((), ())), preferred_element_...  35.2 us
    dot_general x6, matrix products, matmul(): return jnp.dot(left, right, preferred_element_type=jnp.float32)  32.3 us
    pallas_call x1, Pallas kernels, z_gather(): pl.pallas_call(functools.partial(z_gather_kernel, planes), out_shape=jax....  22.5 us
    dot_general x5, matrix products, contract_rows(): lax.dot_general(left, right, (((0,), (0,)), ((), ())), preferred_element_...  21.7 us
    unnamed x211, local copies, waits for them, and re-layouts  15.8 us
  transfers between devices with their start and end apart: 8, of which 1 were waited for; matrix products, arithmetic and copies ran while one was open for 33% of the time, Pallas kernels for 36%

profile of v4, /device:TPU:8, one launch (start us, length us, event | category | flops | bytes accessed | tf_op | source)
XLA Modules:
  0.0 568.6 jit_solution(15712068213202064739)
XLA Ops:
  15.9 22.5 %shard_map.274.own_ref = bf16[4,72,1536]{2,1,0:T(8,128)(2,1)S(1)} custom-call(bf16[72,1536]{1,0:T(8,128)(2,1)S(1)} %fusion.73.own_ref), custom_call_target="tpu_custom_call" | custom-call | bytes 60000000 | tf_op jit(solution)/shard_map/pallas_call | solution.py:205
  40.8 5.0 all-to-all-start
  46.5 55.9 %shard_map.275 = bf16[8,4,72,1536]{3,2,1,0:T(8,128)(2,1)} custom-call(bf16[4,72,1536]{2,1,0:T(8,128)(2,1)S(1)} %shard_map.274.own_ref), custom_call_target="tpu_custom_call" | custom-call | bytes 75000000 | tf_op jit(solution)/shard_map/pallas_call | solution.py:224
  102.5 3.7 copy.126
  111.7 3.9 reshape.418
  120.8 4.3 copy.127
  159.8 30.1 %shard_map.276 = bf16[8,16,16,1152]{3,2,1,0:T(8,128)(2,1)S(1)} custom-call(bf16[16,16,1152]{2,1,0:T(8,128)(2,1)S(1)} %bitcast.218), custom_call_target="tpu_custom_call" | custom-call | bytes 75000000 | tf_op jit(solution)/shard_map/pallas_call | solution.py:224
  193.4 5.4 fusion.107
  198.8 4.2 reshape.423
  203.0 4.2 reshape.424
  207.2 8.2 %fusion.113 = f32[2048,864]{0,1:T(8,128)S(1)} fusion(bf16[2048,1152]{1,0:T(8,128)(2,1)} %bitcast.208, bf16[1152,864]{1,0:T(8,128)(2,1)} %reshape.423), kind=kOutput, calls=%fused_computation.237 | convolution fusion | flops 4076863488 | bytes 13787136 | tf_op jit(solution)/shard_map/dot_general | solution.py:52
  218.4 9.2 %fusion.18 = (bf16[864,2048]{1,0:T(8,128)(2,1)}, f32[2048,864]{0,1:T(8,128)}) fusion(f32[2048,864]{0,1:T(8,128)S(1)} %fusion.113, bf16[2048,1152]{1,0:T(8,128)(2,1)S(1)} %bitcast.211, bf16[1152,864]{1,0:T(8,128)(2,1)S(1)} %copy-done.42), kind=kOutput, calls=%fused_computation.26 | convolution fusion | flops 4094558208 | bytes 24403968 | tf_op jit(solution)/shard_map/dot_general | solution.py:52
  227.6 10.1 %convolution_convert_fusion = bf16[2048,1152]{1,0:T(8,128)(2,1)S(1)} fusion(bf16[864,1152]{1,0:T(8,128)(2,1)} %all-gather.2.cloned.1.call-done, f32[2048,864]{0,1:T(8,128)} %get-tuple-element.94, f32[2048,864]{0,1:T(8,128)} %copy-done.95), kind=kOutput, calls=%fused_computation.10 | convolution fusion | flops 4096917504 | bytes 20865024 | tf_op jit(solution)/shard_map/dot_general | solution.py:52
  237.7 24.7 %shard_map.277 = f32[16,16,1152]{2,1,0:T(8,128)S(1)} custom-call(bf16[8,16,16,1152]{3,2,1,0:T(8,128)(2,1)S(1)} %bitcast.207), custom_call_target="tpu_custom_call" | custom-call | bytes 75000000 | tf_op jit(solution)/shard_map/pallas_call | solution.py:316
  270.9 23.7 %shard_map.278 = bf16[8,16,16,1152]{3,2,1,0:T(8,128)(2,1)S(1)} custom-call(bf16[16,16,1152]{2,1,0:T(8,128)(2,1)S(1)} %multiply_convert_fusion.4.own_ref), custom_call_target="tpu_custom_call" | custom-call | bytes 75000000 | tf_op jit(solution)/shard_map/pallas_call | solution.py:224
  294.6 15.1 %fusion.9 = (bf16[2048,864]{0,1:T(8,128)(2,1)}, bf16[2048,864]{0,1:T(8,128)(2,1)}) fusion(f32[2048,864]{0,1:T(8,128)} %copy-done.95, f32[2048,864]{0,1:T(8,128)} %get-tuple-element.94, bf16[2048,1152]{1,0:T(8,128)(2,1)S(1)} %bitcast.216, bf16[864,1152]{1,0:T(8,128)(2,1)} %all-gather.2.cloned.1.call-done), kind=kOutput, calls=%fused_computation.17 | convolution fusion | flops 4119330816 | bytes 27942912 | tf_op jit(solution)/shard_map/dot_general | solution.py:62
  309.7 7.7 %fusion.114 = f32[2048,1152]{1,0:T(8,128)S(1)} fusion(bf16[2048,864]{0,1:T(8,128)(2,1)} %get-tuple-element.48, bf16[1152,864]{1,0:T(8,128)(2,1)S(1)} %copy-done.44), kind=kOutput, calls=%fused_computation.238 | convolution fusion | flops 4076863488 | bytes 14966784 | tf_op jit(solution)/shard_map/dot_general | solution.py:62
  317.5 5.9 %convolution_convert_fusion.4 = bf16[1152,864]{0,1:T(8,128)(2,1)} fusion(bf16[2048,864]{0,1:T(8,128)(2,1)S(1)} %copy-done.96, bf16[2048,1152]{1,0:T(8,128)(2,1)S(1)} %bitcast.214), kind=kOutput, calls=%fused_computation.37 | convolution fusion | flops 4077858816 | bytes 10248192 | tf_op jit(solution)/shard_map/dot_general | solution.py:56
  323.4 6.4 %fusion.112 = (bf16[4,216,1152]{2,1,0:T(8,128)(2,1)S(1)}, f32[4,216,1152]{2,1,0:T(8,128)}) fusion(bf16[4,216,2048]{2,1,0:T(8,128)(2,1)S(1)} %bitcast.245, bf16[2048,1152,1]{1,0,2:T(8,128)(2,1)S(1)} %bitcast.217), kind=kOutput, calls=%fused_computation.236 | convolution fusion | flops 4077858816 | bytes 14229504 | tf_op jit(solution)/shard_map/dot_general | solution.py:56
  333.6 5.9 %collective-permute-start.3 = (bf16[216,1152]{1,0:T(8,128)(2,1)}, bf16[216,1152]{1,0:T(8,128)(2,1)}, u32[]{:S(2)}, u32[]{:S(2)}) collective-permute-start(bf16[216,1152]{1,0:T(8,128)(2,1)} %get-tuple-element.56), channel_id=1, source_target_pairs={{0,16},{8,24},{16,0},{24,8},{1,17},{9,25},{17,1},{25,9},{2,18},{10... | collective-permute-start | bytes 1493000 | tf_op jit(solution)/shard_map/ppermute | solution.py:542
  339.5 5.9 %convolution_convert_fusion.3 = bf16[1152,864]{0,1:T(8,128)(2,1)} fusion(bf16[2048,864]{0,1:T(8,128)(2,1)S(1)} %copy-done.97, bf16[2048,1152]{1,0:T(8,128)(2,1)S(1)} %bitcast.215), kind=kOutput, calls=%fused_computation.36 | convolution fusion | flops 4077858816 | bytes 10248192 | tf_op jit(solution)/shard_map/dot_general | solution.py:56
  345.5 7.3 %add_convert_fusion = bf16[2048,1152]{1,0:T(8,128)(2,1)} fusion(f32[2048,1152]{1,0:T(8,128)S(1)} %fusion.114, bf16[2048,864]{0,1:T(8,128)(2,1)S(1)} %copy-done.98, bf16[1152,864]{1,0:T(8,128)(2,1)S(1)} %copy-done.43), kind=kOutput, calls=%fused_computation.5 | convolution fusion | flops 4081582080 | bytes 19685376 | tf_op jit(solution)/shard_map/dot_general | solution.py:62
  352.8 4.1 copy.138
  356.8 4.0 reshape.428
  360.8 4.1 copy.139
  364.9 4.1 reshape.429
  369.0 5.7 %pad_maximum_fusion = bf16[32,72,864]{2,1,0:T(8,128)(2,1)} fusion(bf16[32,36,864]{2,1,0:T(8,128)(2,1)} %reshape.429, bf16[32,36,864]{2,1,0:T(8,128)(2,1)} %reshape.428), kind=kLoop, calls=%fused_computation.33 | loop fusion | flops 7962624 | bytes 7962624 | tf_op jit(solution)/shard_map/concatenate | solution.py:547
  374.7 24.2 %shard_map.279 = f32[16,16,1152]{2,1,0:T(8,128)S(1)} custom-call(bf16[8,16,16,1152]{3,2,1,0:T(8,128)(2,1)S(1)} %bitcast.206), custom_call_target="tpu_custom_call" | custom-call | bytes 75000000 | tf_op jit(solution)/shard_map/pallas_call | solution.py:316
  410.3 5.0 all-to-all-start.1
  439.5 7.8 %collective-permute-done.1 = bf16[256,512]{0,1:T(8,128)(2,1)} collective-permute-done((bf16[256,512]{0,1:T(8,128)(2,1)}, bf16[256,512]{0,1:T(8,128)(2,1)}, u32[]{:S(2)}, u32[]{:S(2)}) %collective-permute-start.1) | collective-permute-done | bytes 262176 | tf_op jit(solution)/shard_map/ppermute | solution.py:576
  469.8 72.5 %shard_map.280 = f32[72,1536]{1,0:T(8,128)S(1)} custom-call(bf16[8,4,72,1536]{3,2,1,0:T(8,128)(2,1)} %bitcast.220), custom_call_target="tpu_custom_call" | custom-call | bytes 105000000 | tf_op jit(solution)/shard_map/pallas_call | solution.py:359
  548.2 4.3 convert_reduce_fusion
  (360 shorter events, 147.9 us)
Async XLA Ops:
  7.2 138.8 %collective-permute-start = (bf16[256,1152]{1,0:T(8,128)(2,1)}, bf16[256,1152]{1,0:T(8,128)(2,1)}, u32[]{:S(2)}, u32[]{:S(2)}) collective-permute-start(bf16[256,1152]{1,0:T(8,128)(2,1)} %bitcast.228), channel_id=1, source_target_pairs={{0,1},{1,0},{2,3},{3,2},{4,5},{5,4},{6,7},{7,6},{8,9},{9,8},{10,11... | collective-permute-start | bytes 1769480 | tf_op jit(solution)/shard_map/ppermute | solution.py:465
  40.8 152.6 %all-to-all-start = ((bf16[32,72,864]{2,1,0:T(8,128)(2,1)}), bf16[32,72,864]{2,1,0:T(8,128)(2,1)}, u32[]{:S(2)}, u32[]{:S(2)}) async-start(bf16[32,72,864]{2,1,0:T(8,128)(2,1)} %bitcast.226), calls=%async_computation | async-start | bytes 8257536 | tf_op jit(solution)/shard_map/all_to_all | solution.py:79
  45.8 181.8 %all-gather.2.cloned.1.call-start = ((), (), s32[]{:S(2)}) async-start(), calls=%async_computation.2 | async-start | bytes 2488320 | tf_op jit(solution)/shard_map/all_gather | solution.py:436
  115.6 32.1 %copy-start.6 = (bf16[1152,1536]{1,0:T(8,128)(2,1)}, bf16[1152,1536]{1,0:T(8,128)(2,1)S(1)}, u32[]{:S(2)}) copy-start(bf16[1152,1536]{1,0:T(8,128)(2,1)S(1)} %reshape.418) | copy-start | bytes 10616836
  159.7 32.3 %copy-start.55 = (f32[256,128]{0,1:T(8,128)S(1)}, f32[256,128]{0,1:T(8,128)}, u32[]{:S(2)}) copy-start(f32[256,128]{0,1:T(8,128)} %get-tuple-element.43) | copy-start | bytes 393220
  159.7 33.0 %copy-start.24 = (f32[512,256]{0,1:T(8,128)S(1)}, f32[512,256]{0,1:T(8,128)}, u32[]{:S(2)}) copy-start(f32[512,256]{0,1:T(8,128)} %get-tuple-element.62) | copy-start | bytes 1572868
  203.0 15.4 %slice-start.2 = ((s8[4718592]{0:T(1024)(128)(4,1)}), s8[524288]{0:T(1024)(128)(4,1)S(1)}, s32[]{:S(2)}) async-start(s8[4718592]{0:T(1024)(128)(4,1)} %bitcast.209), calls=%async_computation.5 | async-start | bytes 1048576
  207.2 11.2 %slice-start.3 = ((s8[4718592]{0:T(1024)(128)(4,1)}), s8[4194304]{0:T(1024)(128)(4,1)S(1)}, s32[]{:S(2)}) async-start(s8[4718592]{0:T(1024)(128)(4,1)} %bitcast.209), calls=%async_computation.6 | async-start | bytes 8388608
  207.2 11.2 %copy-start.42 = (bf16[1152,864]{1,0:T(8,128)(2,1)S(1)}, bf16[1152,864]{1,0:T(8,128)(2,1)}, u32[]{:S(2)}) copy-start(bf16[1152,864]{1,0:T(8,128)(2,1)} %reshape.424) | copy-start | bytes 5971972
  270.9 46.6 %slice-start.4 = ((s8[4718592]{0:T(1024)(128)(4,1)}), s8[524288]{0:T(1024)(128)(4,1)S(1)}, s32[]{:S(2)}) async-start(s8[4718592]{0:T(1024)(128)(4,1)} %bitcast.212), calls=%async_computation.7 | async-start | bytes 1048576
  294.6 15.2 %copy-start.44 = (bf16[1152,864]{1,0:T(8,128)(2,1)S(1)}, bf16[1152,864]{1,0:T(8,128)(2,1)}, u32[]{:S(2)}) copy-start(bf16[1152,864]{1,0:T(8,128)(2,1)} %reshape.423) | copy-start | bytes 5971972
  294.6 22.9 %slice-start.5 = ((s8[4718592]{0:T(1024)(128)(4,1)}), s8[4194304]{0:T(1024)(128)(4,1)S(1)}, s32[]{:S(2)}) async-start(s8[4718592]{0:T(1024)(128)(4,1)} %bitcast.212), calls=%async_computation.8 | async-start | bytes 8388608
  309.7 7.8 %copy-start.96 = (bf16[2048,864]{0,1:T(8,128)(2,1)S(1)}, bf16[2048,864]{0,1:T(8,128)(2,1)}, u32[]{:S(2)}) copy-start(bf16[2048,864]{0,1:T(8,128)(2,1)} %get-tuple-element.48) | copy-start | bytes 10616836
  323.4 16.1 %copy-start.97 = (bf16[2048,864]{0,1:T(8,128)(2,1)S(1)}, bf16[2048,864]{0,1:T(8,128)(2,1)}, u32[]{:S(2)}) copy-start(bf16[2048,864]{0,1:T(8,128)(2,1)} %get-tuple-element.49) | copy-start | bytes 10616836
  331.0 214.4 %collective-permute-start.2 = (bf16[216,1152]{1,0:T(8,128)(2,1)}, bf16[216,1152]{1,0:T(8,128)(2,1)}, u32[]{:S(2)}, u32[]{:S(2)}) collective-permute-start(bf16[216,1152]{1,0:T(8,128)(2,1)} %get-tuple-element.54), channel_id=1, source_target_pairs={{0,8},{8,16},{16,24},{24,0},{1,9},{9,17},{17,25},{25,1},{2,10},{10... | collective-permute-start | bytes 1493000 | tf_op jit(solution)/shard_map/ppermute | solution.py:542
  333.6 211.8 %collective-permute-start.3 = (bf16[216,1152]{1,0:T(8,128)(2,1)}, bf16[216,1152]{1,0:T(8,128)(2,1)}, u32[]{:S(2)}, u32[]{:S(2)}) collective-permute-start(bf16[216,1152]{1,0:T(8,128)(2,1)} %get-tuple-element.56), channel_id=1, source_target_pairs={{0,16},{8,24},{16,0},{24,8},{1,17},{9,25},{17,1},{25,9},{2,18},{10... | collective-permute-start | bytes 1493000 | tf_op jit(solution)/shard_map/ppermute | solution.py:542
  339.5 205.9 %collective-permute-start.4 = (bf16[216,1152]{1,0:T(8,128)(2,1)}, bf16[216,1152]{1,0:T(8,128)(2,1)}, u32[]{:S(2)}, u32[]{:S(2)}) collective-permute-start(bf16[216,1152]{1,0:T(8,128)(2,1)} %get-tuple-element.55), channel_id=1, source_target_pairs={{0,24},{8,0},{16,8},{24,16},{1,25},{9,1},{17,9},{25,17},{2,26},{10... | collective-permute-start | bytes 1493000 | tf_op jit(solution)/shard_map/ppermute | solution.py:542
  364.9 9.8 %slice-start = ((s8[4718592]{0:T(1024)(128)(4,1)}), s8[524288]{0:T(1024)(128)(4,1)S(1)}, s32[]{:S(2)}) async-start(s8[4718592]{0:T(1024)(128)(4,1)} %bitcast.204), calls=%async_computation.3 | async-start | bytes 1048576
  374.7 24.2 %copy-start.81 = (f32[256]{0:T(256)S(1)}, f32[256]{0:T(256)}, u32[]{:S(2)}) copy-start(f32[256]{0:T(256)} %copy-done.80) | copy-start | bytes 3076
  410.3 138.0 %all-to-all-start.1 = ((bf16[32,72,864]{2,1,0:T(8,128)(2,1)}), bf16[32,72,864]{2,1,0:T(8,128)(2,1)}, u32[]{:S(2)}, u32[]{:S(2)}) async-start(bf16[32,72,864]{2,1,0:T(8,128)(2,1)} %pad_maximum_fusion), calls=%async_computation.1 | async-start | bytes 8257536 | tf_op jit(solution)/shard_map/all_to_all | solution.py:79
  430.6 6.5 %copy-start.27 = (bf16[256,1152]{1,0:T(8,128)(2,1)S(1)}, bf16[256,1152]{1,0:T(8,128)(2,1)}, u32[]{:S(2)}) copy-start(bf16[256,1152]{1,0:T(8,128)(2,1)} %copy-done.26) | copy-start | bytes 1769476
  430.6 6.5 %copy-start.34 = (bf16[256,4,256]{2,0,1:T(8,128)(2,1)S(1)}, bf16[256,4,256]{2,0,1:T(8,128)(2,1)}, u32[]{:S(2)}) copy-start(bf16[256,4,256]{2,0,1:T(8,128)(2,1)} %copy-done.33) | copy-start | bytes 1572868
  433.4 13.9 %collective-permute-start.1 = (bf16[256,512]{0,1:T(8,128)(2,1)}, bf16[256,512]{0,1:T(8,128)(2,1)}, u32[]{:S(2)}, u32[]{:S(2)}) collective-permute-start(bf16[256,512]{0,1:T(8,128)(2,1)} %fusion.62), channel_id=1, source_target_pairs={{0,1},{1,0},{2,3},{3,2},{4,5},{5,4},{6,7},{7,6},{8,9},{9,8},{10,11... | collective-permute-start | bytes 786440 | tf_op jit(solution)/shard_map/ppermute | solution.py:576
  437.2 10.2 %copy-start.20 = (f32[512,256]{0,1:T(8,128)S(1)}, f32[512,256]{0,1:T(8,128)}, u32[]{:S(2)}) copy-start(f32[512,256]{0,1:T(8,128)} %copy-done.19) | copy-start | bytes 1572868
  437.2 10.2 %copy-start.36 = (f32[512,256]{0,1:T(8,128)S(1)}, f32[512,256]{0,1:T(8,128)}, u32[]{:S(2)}) copy-start(f32[512,256]{0,1:T(8,128)} %copy-done.35) | copy-start | bytes 1572868
  437.2 11.9 %copy-start.38 = (f32[256,128]{0,1:T(8,128)S(1)}, f32[256,128]{0,1:T(8,128)}, u32[]{:S(2)}) copy-start(f32[256,128]{0,1:T(8,128)} %copy-done.37) | copy-start | bytes 393220
  437.2 11.9 %copy-start.48 = (f32[256,128]{0,1:T(8,128)S(1)}, f32[256,128]{0,1:T(8,128)}, u32[]{:S(2)}) copy-start(f32[256,128]{0,1:T(8,128)} %copy-done.47) | copy-start | bytes 393220
  437.2 11.9 %copy-start.25 = (f32[512,256]{0,1:T(8,128)S(1)}, f32[512,256]{0,1:T(8,128)}, u32[]{:S(2)}) copy-start(f32[512,256]{0,1:T(8,128)} %get-tuple-element.62) | copy-start | bytes 1572868
  437.2 11.9 %copy-start.74 = (f32[256]{0:T(256)S(1)}, f32[256]{0:T(256)}, u32[]{:S(2)}) copy-start(f32[256]{0:T(256)} %reshape.446) | copy-start | bytes 3076
  437.2 11.9 %copy-start.82 = (f32[256]{0:T(256)S(1)}, f32[256]{0:T(256)}, u32[]{:S(2)}) copy-start(f32[256]{0:T(256)} %add_rsqrt_fusion.4) | copy-start | bytes 3076
  439.5 14.4 %copy-start.7 = (bf16[1152,1536]{1,0:T(8,128)(2,1)S(1)}, bf16[1152,1536]{1,0:T(8,128)(2,1)}, u32[]{:S(2)}) copy-start(bf16[1152,1536]{1,0:T(8,128)(2,1)} %copy-done.6) | copy-start | bytes 10616836
  439.5 14.4 %copy-start.65 = (f32[1152]{0:T(1024)S(1)}, f32[1152]{0:T(1024)}, u32[]{:S(2)}) copy-start(f32[1152]{0:T(1024)} %reshape.445) | copy-start | bytes 13828
  (81 other events, 188.6 us)
Sparse Core Ops, SparseCore 0:
  48.2 86.7 all-gather.1

commit v5 on v4

--- a/solution.py
+++ b/solution.py
@@ -69,6 +69,29 @@
 
 
 ALL = ("z", "x", "core", "seq")
+
+
+def up_to(size, multiple):
+    return (size + multiple - 1) // multiple * multiple
+
+
+def place_columns(blocks, members, planes, rows, padded, by_member):
+    source = lax.broadcasted_iota(jnp.int32, (blocks * rows, blocks * padded), 0)
+    target = lax.broadcasted_iota(jnp.int32, (blocks * rows, blocks * padded), 1)
+    block = source // rows
+    if by_member:
+        block = block % members * planes + block // members
+    return (target == block * padded + source % rows).astype(jnp.bfloat16)
+
+
+def take_back(padded_values, placing):
+    high = lax.reduce_precision(padded_values, 8, 7)
+    terms = jnp.concatenate([high, padded_values - high], axis=0).astype(jnp.bfloat16)
+    both = contract_cols(terms, placing)
+    rows = padded_values.shape[0]
+    return both[:rows] + both[rows:]
+
+
 PLANE = ("x", "core", "seq")
 
 MESH_ID = pl.DeviceIdType.MESH
@@ -406,13 +429,21 @@
     head_count = query_width // head_width
     qkv_width = query_width + 2 * head_width
     mix_rows = output_weight.shape[0]
-    padded = (width_rows + 1 + 7) // 8 * 8
+    padded = up_to(width_rows + 1, 8)
+    width = devices * width_rows
+    unit_count = planes * hidden_rows
+    unit_pad = up_to(unit_count, 128)
+    by_device = place_columns(devices, members, planes, width_rows, padded, False)
+    by_member = place_columns(devices, members, planes, width_rows, padded, True)
 
     def column_blocks(weight):
         pieces = weight.reshape(width_rows, planes, members, hidden_rows)
-        return pieces.transpose(2, 0, 1, 3).reshape(members, width_rows, planes * hidden_rows)
-
-    gate_up = jnp.concatenate([column_blocks(gate_weight), column_blocks(up_weight)], axis=1)
+        pieces = pieces.transpose(2, 0, 1, 3).reshape(members, width_rows, unit_count)
+        return jnp.pad(
+            pieces, ((0, 0), (0, padded - width_rows), (0, unit_pad - unit_count))
+        )
+
+    gate_up = jnp.concatenate([column_blocks(gate_weight), column_blocks(up_weight)], axis=2)
     gate_up = jnp.broadcast_to(gate_up[None], (planes,) + gate_up.shape)
     gate_up = gate_up.reshape((devices,) + gate_up.shape[2:])
 
@@ -430,20 +461,20 @@
         (gate_up, down_weight, packed_all)
     )
     packed_all = plane_gather(packed_all, 6)
-    gate_up = exchange(gate_up, ALL)
-    gate_full = gate_up[:, :width_rows].reshape(devices * width_rows, planes * hidden_rows)
-    up_full = gate_up[:, width_rows:].reshape(devices * width_rows, planes * hidden_rows)
+    gate_up_full = exchange(gate_up, ALL).reshape(devices * padded, 2 * unit_pad)
     down_full = lax.all_gather(down_local, "z", axis=0, tiled=True)
-    packed_all = packed_all.transpose(1, 0, 2, 3)
-    packed_all = packed_all.reshape(devices, padded + mix_rows, qkv_width)
-    qkv_full = packed_all[:, :width_rows].reshape(devices * width_rows, qkv_width)
-    output_full = packed_all[:, padded:, : output_weight.shape[1]]
+    qkv_full = packed_all[:, :, :padded].reshape(devices * padded, qkv_width)
+    output_full = packed_all[:, :, padded:, : output_weight.shape[1]].transpose(1, 0, 2, 3)
     output_full = output_full.reshape(devices * mix_rows, output_weight.shape[1])
+    gain_rows = packed_all[:, :, width_rows, :].astype(f32)
     scales, at = [], 0
-    for width in gain_widths:
-        scales.append(packed_all[:, width_rows, at : at + width].reshape(-1).astype(f32))
-        at += width
-    input_scale, query_scale, key_scale, attnout_scale, ffnin_scale, ffnout_scale = scales
+    for count in gain_widths:
+        scales.append(gain_rows[:, :, at : at + count].transpose(1, 0, 2).reshape(-1))
+        at += count
+    padded_input_scale = jnp.pad(
+        gain_rows[:, :, :width_rows], ((0, 0), (0, 0), (0, padded - width_rows))
+    ).reshape(-1)
+    _, query_scale, key_scale, attnout_scale, ffnin_scale, ffnout_scale = scales
 
     hidden = tokens[0].astype(f32)
     incoming = cotangent[0].astype(f32)
@@ -463,13 +494,16 @@
     other_half = [(0, 1), (1, 0)]
     first = lax.axis_index("seq") == 0
     other_tokens = lax.ppermute(tokens[0], "seq", other_half)
-    row_hidden = jnp.concatenate(
+    row_tokens = jnp.concatenate(
         [
             jnp.where(first, tokens[0], other_tokens),
             jnp.where(first, other_tokens, tokens[0]),
         ]
-    ).astype(f32)
-    row_normed = (row_hidden * inverse_rms(row_hidden) * input_scale).astype(bf16)
+    )
+    row_hidden = matmul(row_tokens, by_member)
+    row_inverse = lax.rsqrt(jnp.sum(row_hidden * row_hidden, axis=-1, keepdims=True) / width + epsilon)
+    row_norm = row_hidden * row_inverse
+    row_normed = (row_norm * padded_input_scale).astype(bf16)
     key_value_raw = matmul(row_normed, qkv_full[:, query_width:])
     row_key_raw = key_value_raw[:, :head_width]
     value_rows = key_value_raw[:, head_width:].astype(bf16)
@@ -477,9 +511,9 @@
         row_key_raw * inverse_rms(row_key_raw) * key_scale, cos_full, sin_full
     ).astype(bf16)
 
-    inv_input = inverse_rms(hidden)
-    norm_input = hidden * inv_input
-    normed = (norm_input * input_scale).astype(bf16)
+    inv_input = mine(row_inverse)
+    norm_input = mine(row_norm)
+    normed = mine(row_normed)
     query_raw = matmul(normed, qkv_full[:, :query_width]).reshape(
         local_rows, head_count, head_width
     )
@@ -513,12 +547,13 @@
     norm_middle = middle * inv_middle
     ffn_in = (norm_middle * ffnin_scale).astype(bf16)
 
-    plane_in = gather_rows(ffn_in, 1)
-    gate_proj = matmul(plane_in, gate_full)
-    up_proj = matmul(plane_in, up_full)
-    activated, gelu_back = jax.vjp(gelu_pair, gate_proj, up_proj)
+    plane_in = gather_rows(matmul(ffn_in, by_device).astype(bf16), 1)
+    gate_up_proj = matmul(plane_in, gate_up_full)
+    activated, gelu_back = jax.vjp(
+        lambda proj: gelu_pair(proj[:, :unit_pad], proj[:, unit_pad:]), gate_up_proj
+    )
     activated_low = activated.astype(bf16)
-    ffn_raw = plane_scatter_sum(matmul(activated_low, down_full).astype(bf16), 2)
+    ffn_raw = plane_scatter_sum(matmul(activated_low[:, :unit_count], down_full).astype(bf16), 2)
     inv_ffn = inverse_rms(ffn_raw)
     norm_ffn = ffn_raw * inv_ffn
     result = middle + norm_ffn * ffnout_scale
@@ -527,10 +562,9 @@
 
     plane_grad = gather_rows(ffn_raw_grad, 3)
     act_grad = contract_cols(plane_grad, down_full)
-    gate_grad, up_grad = gelu_back(act_grad)
-    gate_low = gate_grad.astype(bf16)
-    up_low = up_grad.astype(bf16)
-    down_blocks = contract_rows(activated_low, plane_grad).reshape(
+    act_grad = jnp.pad(act_grad, ((0, 0), (0, unit_pad - unit_count)))
+    gate_up_low = gelu_back(act_grad)[0].astype(bf16)
+    down_blocks = contract_rows(activated_low[:, :unit_count], plane_grad).reshape(
         planes, hidden_rows, down_weight.shape[1]
     )
     plane = lax.axis_index("z")
@@ -541,20 +575,12 @@
         shift = [(i, (i + k) % planes) for i in range(planes)]
         down_wgrad = down_wgrad + lax.ppermute(leaving, "z", shift).astype(f32)
 
-    def row_blocks(grad):
-        return grad.astype(bf16).reshape(devices, width_rows, planes * hidden_rows)
-
-    gate_up_blocks = jnp.concatenate(
-        [
-            row_blocks(contract_rows(plane_in, gate_low)),
-            row_blocks(contract_rows(plane_in, up_low)),
-        ],
-        axis=1,
-    )
-    ffn_in_part = (contract_cols(gate_low, gate_full) + contract_cols(up_low, up_full)).astype(bf16)
+    gate_up_blocks = contract_rows(plane_in, gate_up_low).astype(bf16)
+    gate_up_blocks = gate_up_blocks.reshape(devices, padded, 2 * unit_pad)
+    ffn_in_part = contract_cols(gate_up_low, gate_up_full).astype(bf16)
     gate_up_blocks, ffn_in_part = lax.optimization_barrier((gate_up_blocks, ffn_in_part))
     gate_up_terms = exchange(gate_up_blocks, ALL)
-    ffn_in_grad = plane_scatter_sum(ffn_in_part, 4)
+    ffn_in_grad = take_back(plane_scatter_sum(ffn_in_part, 4), by_device)
     ffnin_gain_grad = jnp.sum(ffn_in_grad * norm_middle, axis=0)
     middle_grad = incoming + rms_back(ffn_in_grad * ffnin_scale, norm_middle, inv_middle)
     attnout_gain_grad = jnp.sum(middle_grad * norm_attn, axis=0)
@@ -591,46 +617,49 @@
     qkv_wgrad = contract_rows(normed, qkv_raw_low)
     normed_grad = contract_cols(qkv_raw_low, qkv_full)
     input_gain_grad = jnp.sum(normed_grad * norm_input, axis=0)
-    input_grad = middle_grad + rms_back(normed_grad * input_scale, norm_input, inv_input)
+    scaled_grad = normed_grad * padded_input_scale
+    inner = jnp.sum(scaled_grad * norm_input, axis=-1, keepdims=True) / width
+    input_grad = middle_grad + take_back(inv_input * (scaled_grad - norm_input * inner), by_member)
 
     gain_grads = (
-        input_gain_grad,
         query_gain_grad,
         key_gain_grad,
         attnout_gain_grad,
         ffnin_gain_grad,
         ffnout_gain_grad,
     )
-    gain_rows = jnp.concatenate([g.reshape(devices, -1) for g in gain_grads], axis=1)
-    gain_rows = jnp.pad(gain_rows, ((0, 0), (0, qkv_width - gain_rows.shape[1])))
-    blocks = jnp.concatenate(
-        [qkv_wgrad.reshape(devices, width_rows, qkv_width), gain_rows[:, None]], axis=1
-    )
-    blocks = jnp.pad(blocks.astype(bf16), ((0, 0), (0, padded - width_rows - 1), (0, 0)))
-    output_blocks = output_wgrad.astype(bf16).reshape(devices, mix_rows, -1)
+    gain_rows = jnp.concatenate(
+        [input_gain_grad.reshape(members, planes, padded)[:, :, :width_rows]]
+        + [g.reshape(planes, members, -1).transpose(1, 0, 2) for g in gain_grads],
+        axis=2,
+    )
+    gain_rows = jnp.pad(gain_rows, ((0, 0), (0, 0), (0, qkv_width - gain_rows.shape[2])))
+    blocks = qkv_wgrad.reshape(members, planes, padded, qkv_width)
+    row = lax.broadcasted_iota(jnp.int32, blocks.shape, 2)
+    blocks = jnp.where(row == width_rows, gain_rows[:, :, None], blocks).astype(bf16)
+    output_blocks = output_wgrad.astype(bf16).reshape(planes, members, mix_rows, -1)
     output_blocks = jnp.pad(
-        output_blocks, ((0, 0), (0, 0), (0, qkv_width - output_blocks.shape[2]))
-    )
-    blocks = jnp.concatenate([blocks, output_blocks], axis=1)
-    blocks = blocks.reshape(planes, members, padded + mix_rows, qkv_width)
-    share = owner_sum(blocks.transpose(1, 0, 2, 3), 5)
+        output_blocks.transpose(1, 0, 2, 3),
+        ((0, 0), (0, 0), (0, 0), (0, qkv_width - output_blocks.shape[3])),
+    )
+    share = owner_sum(jnp.concatenate([blocks, output_blocks], axis=2), 5)
     gate_up_sum = jnp.sum(
-        gate_up_terms.astype(f32).reshape(
-            planes, members, 2 * width_rows, planes * hidden_rows
-        ),
-        axis=0,
-    )
-    gate_up_sum = gate_up_sum.reshape(members, 2, width_rows, planes, hidden_rows)
-    gate_up_sum = gate_up_sum.transpose(1, 2, 3, 0, 4).reshape(
-        2, width_rows, planes * members * hidden_rows
-    )
-    gate_wgrad, up_wgrad = gate_up_sum[0], gate_up_sum[1]
-
+        gate_up_terms.reshape(planes, members, padded, 2 * unit_pad).astype(f32), axis=0
+    )
+
+    def unit_columns(total):
+        total = total[:, :width_rows, :unit_count].reshape(
+            members, width_rows, planes, hidden_rows
+        )
+        return total.transpose(1, 2, 0, 3).reshape(width_rows, planes * members * hidden_rows)
+
+    gate_wgrad = unit_columns(gate_up_sum[:, :, :unit_pad])
+    up_wgrad = unit_columns(gate_up_sum[:, :, unit_pad:])
     qkv_share, output_share = share[:padded], share[padded:, : output_weight.shape[1]]
     gain_shares, at = [], 0
-    for width in gain_widths:
-        gain_shares.append(qkv_share[width_rows, at : at + width])
-        at += width
+    for count in gain_widths:
+        gain_shares.append(qkv_share[width_rows, at : at + count])
+        at += count
     return (
         result.astype(bf16)[None],
         input_grad[None],

time: 576 us -> 565 us (0.981)
  local copies, waits for them, and re-layouts: 119 us -> 64.9 us
  Pallas kernels: 254 us -> 277 us
  other arithmetic: 52 us -> 61.5 us
  matrix products: 97.8 us -> 105 us
  waiting for transfers between devices: 8.23 us -> 15.4 us
    reshape x16 -> x20, local copies, waits for them, and re-layouts: 32.7 us -> 11.7 us  [the longest x2 3.61 us: unit_columns(): total.transpose(1, 2, 0, 3)]
    mul x1 -> x2, other arithmetic: 0.04 us -> 17.3 us  [gelu_pair(): return jax.nn.gelu(gate_proj, approximate=True) * up_proj]
    convert_element_type x8 -> x0, local copies, waits for them, and re-layouts: 14.6 us -> none  [the longest x2 8.16 us: row_blocks(): return grad.astype(bf16).reshape(devices, width_rows, planes * hidden_rows)]
    slice x8 -> x2, local copies, waits for them, and re-layouts: 14.7 us -> 4.52 us  [the longest x1 4.37 us: body(): qkv_full = packed_all[:, :, :padded].reshape(devices * padded, qkv_width)]
    pallas_call x3, Pallas kernels: 110 us -> 120 us  [plane_gather(): pl.pallas_call(gather_kernel, out_shape=jax.ShapeDtypeStruct((members, *l...]
    pallas_call x1, Pallas kernels: 72.5 us -> 81 us  [owner_sum(): pl.pallas_call(functools.partial(owner_sum_kernel, planes), out_shape=jax...]
    convert_element_type x4, other arithmetic: 3.08 us -> 11.5 us  [the longest x1 8.08 us: body(): activated_low = activated.astype(bf16)]
    ppermute x1, waiting for transfers between devices: 7.83 us -> 15.2 us  [body(): lax.ppermute(theirs.astype(bf16), 'seq', other_half).astype(f32)]
  transfers between devices with their start and end apart: 8 -> 8, of which waited for: 1 -> 1; matrix products, arithmetic and copies ran while one was open for 33% -> 24% of each run, Pallas kernels for 36% -> 41%
where the time goes in v5:
time: 565 us; the launch traced here: 560 us
  Pallas kernels  277 us (49%)
  matrix products  105 us (19%)
  local copies, waits for them, and re-layouts  64.9 us (11%)
  other arithmetic  61.5 us (11%)
  starting transfers between devices  20.6 us (4%)
  between operations  16.1 us (3%)
  waiting for transfers between devices  15.4 us (3%)
    pallas_call x3, Pallas kernels, plane_gather(): pl.pallas_call(gather_kernel, out_shape=jax.ShapeDtypeStruct((members, *l...  120 us
    pallas_call x1, Pallas kernels, owner_sum(): pl.pallas_call(functools.partial(owner_sum_kernel, planes), out_shape=jax...  81 us
    pallas_call x2, Pallas kernels, plane_scatter_sum(): pl.pallas_call(plane_sum_kernel, out_shape=jax.ShapeDtypeStruct(shape, jn...  53.5 us
    dot_general x6, matrix products, contract_cols(): lax.dot_general(left, right, (((1,), (1,)), ((), ())), preferred_element_...  36.1 us
    dot_general x7, matrix products, matmul(): return jnp.dot(left, right, preferred_element_type=jnp.float32)  31.7 us
    dot_general x4, matrix products, contract_rows(): lax.dot_general(left, right, (((0,), (0,)), ((), ())), preferred_element_...  28.3 us
    pallas_call x1, Pallas kernels, z_gather(): pl.pallas_call(functools.partial(z_gather_kernel, planes), out_shape=jax....  22.5 us
    mul x2, other arithmetic, gelu_pair(): return jax.nn.gelu(gate_proj, approximate=True) * up_proj  17.3 us
  transfers between devices with their start and end apart: 8, of which 1 were waited for; matrix products, arithmetic and copies ran while one was open for 24% of the time, Pallas kernels for 41%

profile of v5, /device:TPU:8, one launch (start us, length us, event | category | flops | bytes accessed | tf_op | source)
XLA Modules:
  0.0 560.0 jit_solution(15838093493803635689)
XLA Ops:
  8.8 2.9 reshape.363
  15.9 22.5 %shard_map.274.own_ref = bf16[4,72,1536]{2,1,0:T(8,128)(2,1)S(1)} custom-call(bf16[72,1536]{1,0:T(8,128)(2,1)S(1)} %fusion.69.own_ref), custom_call_target="tpu_custom_call" | custom-call | bytes 60000000 | tf_op jit(solution)/shard_map/pallas_call | solution.py:228
  40.9 5.0 all-to-all-start
  46.7 57.4 %shard_map.275 = bf16[8,4,72,1536]{3,2,1,0:T(8,128)(2,1)} custom-call(bf16[4,72,1536]{2,1,0:T(8,128)(2,1)S(1)} %shard_map.274.own_ref), custom_call_target="tpu_custom_call" | custom-call | bytes 75000000 | tf_op jit(solution)/shard_map/pallas_call | solution.py:247
  105.4 3.3 slice_bitcast_fusion
  111.0 4.4 slice.149
  121.4 2.9 multiply_reduce_fusion
  135.9 2.6 fusion.30
  153.0 38.3 %shard_map.276 = bf16[8,16,16,1280]{3,2,1,0:T(8,128)(2,1)S(1)} custom-call(bf16[16,16,1280]{2,1,0:T(8,128)(2,1)S(1)} %bitcast.212), custom_call_target="tpu_custom_call" | custom-call | bytes 75000000 | tf_op jit(solution)/shard_map/pallas_call | solution.py:247
  195.6 13.6 %fusion.109 = f32[2048,1792]{0,1:T(8,128)S(1)} fusion(bf16[2048,1280]{1,0:T(8,128)(2,1)} %bitcast.207, bf16[1280,1792]{1,0:T(8,128)(2,1)} %bitcast.20), kind=kOutput, calls=%fused_computation.259 | convolution fusion | flops 9395240960 | bytes 24510464 | tf_op jit(solution)/shard_map/dot_general | solution.py:52
  209.2 6.8 %multiply_multiply_fusion.2 = (f32[2048,896]{0,1:T(8,128)}, f32[2048,896]{0,1:T(8,128)}) fusion(f32[2048,1792]{0,1:T(8,128)S(1)} %fusion.109), kind=kLoop, calls=%fused_computation.31 | loop fusion | flops 14680064 | bytes 29360128 | tf_op jit(solution)/shard_map/jvp()/mul | solution.py:68
  216.1 2.7 copy-done.1
  218.8 8.1 %fusion.8 = bf16[2048,864]{0,1:T(8,128)(2,1)} fusion(f32[2048,896]{0,1:T(8,128)} %get-tuple-element.45, f32[2048,896]{0,1:T(8,128)} %get-tuple-element.44), kind=kLoop, calls=%fused_computation.29 | loop fusion | flops 3538944 | bytes 17694720 | tf_op jit(solution)/shard_map/convert_element_type | solution.py:555
  226.9 7.9 %convolution_convert_fusion.1 = bf16[2048,1152]{1,0:T(8,128)(2,1)S(1)} fusion(bf16[2048,864]{0,1:T(8,128)(2,1)} %fusion.8, bf16[864,1152]{1,0:T(8,128)(2,1)} %all-gather.2.cloned.1.call-done), kind=kOutput, calls=%fused_computation.19 | convolution fusion | flops 4079222784 | bytes 10248192 | tf_op jit(solution)/shard_map/dot_general | solution.py:52
  234.8 24.7 %shard_map.277 = f32[16,16,1152]{2,1,0:T(8,128)S(1)} custom-call(bf16[8,16,16,1152]{3,2,1,0:T(8,128)(2,1)S(1)} %bitcast.209), custom_call_target="tpu_custom_call" | custom-call | bytes 75000000 | tf_op jit(solution)/shard_map/pallas_call | solution.py:339
  262.0 23.9 %shard_map.278 = bf16[8,16,16,1152]{3,2,1,0:T(8,128)(2,1)S(1)} custom-call(bf16[16,16,1152]{2,1,0:T(8,128)(2,1)S(1)} %multiply_convert_fusion.2.own_ref), custom_call_target="tpu_custom_call" | custom-call | bytes 75000000 | tf_op jit(solution)/shard_map/pallas_call | solution.py:247
  286.0 8.5 %fusion.110 = f32[2048,864]{0,1:T(8,128)} fusion(bf16[2048,1152]{1,0:T(8,128)(2,1)S(1)} %bitcast.210, bf16[864,1152]{1,0:T(8,128)(2,1)} %all-gather.2.cloned.1.call-done), kind=kOutput, calls=%fused_computation.260 | convolution fusion | flops 4076863488 | bytes 13787136 | tf_op jit(solution)/shard_map/dot_general | solution.py:62
  294.6 10.5 %pad_multiply_fusion = (f32[2048,896]{0,1:T(8,128)}, f32[2048,896]{0,1:T(8,128)}) fusion(f32[2048,864]{0,1:T(8,128)} %fusion.110, f32[2048,1792]{0,1:T(8,128)S(1)} %bitcast.214), kind=kLoop, calls=%fused_computation.30 | loop fusion | flops 40370176 | bytes 36438016 | tf_op jit(solution)/shard_map/transpose(jvp())/mul | solution.py:68
  305.1 16.3 %convolution_convert_fusion = bf16[2048,1280]{1,0:T(8,128)(2,1)} fusion(bf16[1280,1792]{1,0:T(8,128)(2,1)} %bitcast.20, f32[2048,896]{0,1:T(8,128)} %get-tuple-element.43, f32[2048,896]{0,1:T(8,128)} %get-tuple-element.42), kind=kOutput, calls=%fused_computation.18 | convolution fusion | flops 9405202432 | bytes 24510464 | tf_op jit(solution)/shard_map/dot_general | solution.py:62
  321.3 17.5 %convolution_convert_fusion.2 = bf16[1280,1792]{1,0:T(8,128)(2,1)} fusion(bf16[2048,1280]{1,0:T(8,128)(2,1)} %bitcast.208, f32[2048,896]{0,1:T(8,128)} %get-tuple-element.43, f32[2048,896]{0,1:T(8,128)} %get-tuple-element.42), kind=kOutput, calls=%fused_computation.20 | convolution fusion | flops 9404874752 | bytes 24510464 | tf_op jit(solution)/shard_map/dot_general | solution.py:56
  338.9 8.7 %fusion.108 = (bf16[4,216,1152]{2,1,0:T(8,128)(2,1)S(1)}, f32[4,216,1152]{2,1,0:T(8,128)}) fusion(bf16[4,216,2048]{2,1,0:T(8,128)(2,1)} %bitcast.233, bf16[2048,1152,1]{1,0,2:T(8,128)(2,1)S(1)} %bitcast.211), kind=kOutput, calls=%fused_computation.258 | convolution fusion | flops 4077858816 | bytes 14229504 | tf_op jit(solution)/shard_map/dot_general | solution.py:56
  349.9 5.6 %collective-permute-start.3 = (bf16[216,1152]{1,0:T(8,128)(2,1)}, bf16[216,1152]{1,0:T(8,128)(2,1)}, u32[]{:S(2)}, u32[]{:S(2)}) collective-permute-start(bf16[216,1152]{1,0:T(8,128)(2,1)} %get-tuple-element.54), channel_id=1, source_target_pairs={{0,16},{8,24},{16,0},{24,8},{1,17},{9,25},{17,1},{25,9},{2,18},{10... | collective-permute-start | bytes 1493000 | tf_op jit(solution)/shard_map/ppermute | solution.py:576
  355.6 28.9 %shard_map.279 = f32[16,16,1280]{2,1,0:T(8,128)S(1)} custom-call(bf16[8,16,16,1280]{3,2,1,0:T(8,128)(2,1)} %bitcast.222), custom_call_target="tpu_custom_call" | custom-call | bytes 75000000 | tf_op jit(solution)/shard_map/pallas_call | solution.py:339
  400.1 5.2 all-to-all-start.1
  411.2 2.6 copy.262
  422.7 15.2 %collective-permute-done.1 = bf16[256,512]{0,1:T(8,128)(2,1)} collective-permute-done((bf16[256,512]{0,1:T(8,128)(2,1)}, bf16[256,512]{0,1:T(8,128)(2,1)}, u32[]{:S(2)}, u32[]{:S(2)}) %collective-permute-start.1) | collective-permute-done | bytes 262176 | tf_op jit(solution)/shard_map/ppermute | solution.py:602
  439.6 4.9 multiply_reduce_fusion.1
  447.9 3.4 fusion.7.part_ref
  451.3 81.0 %shard_map.280 = f32[72,1536]{1,0:T(8,128)S(1)} custom-call(bf16[8,4,72,1536]{3,2,1,0:T(8,128)(2,1)} %fusion.7.part_ref), custom_call_target="tpu_custom_call" | custom-call | bytes 105000000 | tf_op jit(solution)/shard_map/pallas_call | solution.py:382
  536.0 2.5 fusion.36
  539.7 2.8 fusion.51
  542.5 3.2 convert_reduce_fusion
  (372 shorter events, 100.0 us)
Async XLA Ops:
  7.2 113.0 %collective-permute-start = (bf16[256,1152]{1,0:T(8,128)(2,1)}, bf16[256,1152]{1,0:T(8,128)(2,1)}, u32[]{:S(2)}, u32[]{:S(2)}) collective-permute-start(bf16[256,1152]{1,0:T(8,128)(2,1)} %bitcast.234), channel_id=1, source_target_pairs={{0,1},{1,0},{2,3},{3,2},{4,5},{5,4},{6,7},{7,6},{8,9},{9,8},{10,11... | collective-permute-start | bytes 1769480 | tf_op jit(solution)/shard_map/ppermute | solution.py:496
  40.9 154.8 %all-to-all-start = ((bf16[32,40,1792]{2,1,0:T(8,128)(2,1)}), bf16[32,40,1792]{2,1,0:T(8,128)(2,1)}, u32[]{:S(2)}, u32[]{:S(2)}) async-start(bf16[32,40,1792]{2,1,0:T(8,128)(2,1)} %bitcast.216), calls=%async_computation | async-start | bytes 9175040 | tf_op jit(solution)/shard_map/all_to_all | solution.py:102
  45.8 181.0 %all-gather.2.cloned.1.call-start = ((), (), s32[]{:S(2)}) async-start(), calls=%async_computation.2 | async-start | bytes 2488320 | tf_op jit(solution)/shard_map/all_gather | solution.py:465
  46.6 74.8 %copy-start.73 = (s32[1152]{0:T(1024)}, s32[1152]{0:T(1024)S(1)}, u32[]{:S(2)}) copy-start(s32[1152]{0:T(1024)S(1)} %broadcast_add_fusion) | copy-start | bytes 13828
  46.6 74.8 %copy-start.76 = (s32[1152]{0:T(1024)}, s32[1152]{0:T(1024)S(1)}, u32[]{:S(2)}) copy-start(s32[1152]{0:T(1024)S(1)} %fusion.79) | copy-start | bytes 13828
  46.6 74.8 %copy-start.79 = (s32[1152]{0:T(1024)}, s32[1152]{0:T(1024)S(1)}, u32[]{:S(2)}) copy-start(s32[1152]{0:T(1024)S(1)} %iota_divide_fusion) | copy-start | bytes 13828
  46.7 74.7 %copy-start.82 = (s32[1152]{0:T(1024)}, s32[1152]{0:T(1024)S(1)}, u32[]{:S(2)}) copy-start(s32[1152]{0:T(1024)S(1)} %iota_remainder_fusion) | copy-start | bytes 13828
  46.7 74.7 %copy-start.86 = (pred[1152]{0:T(1024)(128)(4,1)}, pred[1152]{0:T(1024)(128)(4,1)S(1)}, u32[]{:S(2)}) copy-start(pred[1152]{0:T(1024)(128)(4,1)S(1)} %fusion.82) | copy-start | bytes 3460
  46.7 74.7 %copy-start.89 = (pred[1152]{0:T(1024)(128)(4,1)}, pred[1152]{0:T(1024)(128)(4,1)S(1)}, u32[]{:S(2)}) copy-start(pred[1152]{0:T(1024)(128)(4,1)S(1)} %fusion.83) | copy-start | bytes 3460
  115.5 9.4 %copy-start.49 = (f32[1280]{0:T(1024)}, f32[1280]{0:T(1024)S(1)}, u32[]{:S(2)}) copy-start(f32[1280]{0:T(1024)S(1)} %mul.528) | copy-start | bytes 15364
  118.2 30.8 %copy-start.9 = (bf16[4,8,32,1152]{3,2,1,0:T(8,128)(2,1)}, bf16[4,8,32,1152]{3,2,1,0:T(8,128)(2,1)S(1)}, u32[]{:S(2)}) copy-start(bf16[4,8,32,1152]{3,2,1,0:T(8,128)(2,1)S(1)} %copy.226) | copy-start | bytes 7077892
  150.6 109.1 %copy-start.6 = (f32[256,1152]{1,0:T(8,128)}, f32[256,1152]{1,0:T(8,128)S(1)}, u32[]{:S(2)}) copy-start(f32[256,1152]{1,0:T(8,128)S(1)} %get-tuple-element.39) | copy-start | bytes 3538948
  153.0 40.6 %copy-start.54 = (f32[256,4]{0,1:T(4,128)S(1)}, f32[256,4]{0,1:T(4,128)}, u32[]{:S(2)}) copy-start(f32[256,4]{0,1:T(4,128)} %copy-done.53) | copy-start | bytes 12292
  209.2 9.6 %copy-start.1 = (f32[2048,1792]{0,1:T(8,128)}, f32[2048,1792]{0,1:T(8,128)S(1)}, u32[]{:S(2)}) copy-start(f32[2048,1792]{0,1:T(8,128)S(1)} %fusion.109) | copy-start | bytes 44040196
  234.7 25.0 %copy-start.16 = (bf16[1,256,1152]{2,1,0:T(8,128)(2,1)S(1)}, bf16[1,256,1152]{2,1,0:T(8,128)(2,1)}, u32[]{:S(2)}) copy-start(bf16[1,256,1152]{2,1,0:T(8,128)(2,1)} %param.18) | copy-start | bytes 1769476
  234.8 25.0 %copy-start.51 = (f32[1152]{0:T(1024)S(1)}, f32[1152]{0:T(1024)}, u32[]{:S(2)}) copy-start(f32[1152]{0:T(1024)} %mul.581) | copy-start | bytes 13828
  262.0 32.6 %slice-start = ((s8[14680064]{0:T(1024)(128)(4,1)}), s8[2097152]{0:T(1024)(128)(4,1)S(1)}, s32[]{:S(2)}) async-start(s8[14680064]{0:T(1024)(128)(4,1)} %bitcast.213), calls=%async_computation.3 | async-start | bytes 4194304
  348.8 190.9 %collective-permute-start.2 = (bf16[216,1152]{1,0:T(8,128)(2,1)}, bf16[216,1152]{1,0:T(8,128)(2,1)}, u32[]{:S(2)}, u32[]{:S(2)}) collective-permute-start(bf16[216,1152]{1,0:T(8,128)(2,1)} %get-tuple-element.52), channel_id=1, source_target_pairs={{0,8},{8,16},{16,24},{24,0},{1,9},{9,17},{17,25},{25,1},{2,10},{10... | collective-permute-start | bytes 1493000 | tf_op jit(solution)/shard_map/ppermute | solution.py:576
  349.9 189.8 %collective-permute-start.3 = (bf16[216,1152]{1,0:T(8,128)(2,1)}, bf16[216,1152]{1,0:T(8,128)(2,1)}, u32[]{:S(2)}, u32[]{:S(2)}) collective-permute-start(bf16[216,1152]{1,0:T(8,128)(2,1)} %get-tuple-element.54), channel_id=1, source_target_pairs={{0,16},{8,24},{16,0},{24,8},{1,17},{9,25},{17,1},{25,9},{2,18},{10... | collective-permute-start | bytes 1493000 | tf_op jit(solution)/shard_map/ppermute | solution.py:576
  355.6 184.1 %collective-permute-start.4 = (bf16[216,1152]{1,0:T(8,128)(2,1)}, bf16[216,1152]{1,0:T(8,128)(2,1)}, u32[]{:S(2)}, u32[]{:S(2)}) collective-permute-start(bf16[216,1152]{1,0:T(8,128)(2,1)} %get-tuple-element.53), channel_id=1, source_target_pairs={{0,24},{8,0},{16,8},{24,16},{1,25},{9,1},{17,9},{25,17},{2,26},{10... | collective-permute-start | bytes 1493000 | tf_op jit(solution)/shard_map/ppermute | solution.py:576
  400.1 142.4 %all-to-all-start.1 = ((bf16[32,40,1792]{2,1,0:T(8,128)(2,1)}), bf16[32,40,1792]{2,1,0:T(8,128)(2,1)}, u32[]{:S(2)}, u32[]{:S(2)}) async-start(bf16[32,40,1792]{2,1,0:T(8,128)(2,1)} %bitcast.225), calls=%async_computation.1 | async-start | bytes 9175040 | tf_op jit(solution)/shard_map/all_to_all | solution.py:102
  417.4 20.5 %collective-permute-start.1 = (bf16[256,512]{0,1:T(8,128)(2,1)}, bf16[256,512]{0,1:T(8,128)(2,1)}, u32[]{:S(2)}, u32[]{:S(2)}) collective-permute-start(bf16[256,512]{0,1:T(8,128)(2,1)} %fusion.58), channel_id=1, source_target_pairs={{0,1},{1,0},{2,3},{3,2},{4,5},{5,4},{6,7},{7,6},{8,9},{9,8},{10,11... | collective-permute-start | bytes 786440 | tf_op jit(solution)/shard_map/ppermute | solution.py:602
  421.0 16.9 %copy-start.19 = (f32[512,256]{0,1:T(8,128)S(1)}, f32[512,256]{0,1:T(8,128)}, u32[]{:S(2)}) copy-start(f32[512,256]{0,1:T(8,128)} %copy-done.18) | copy-start | bytes 1572868
  421.1 16.9 %copy-start.38 = (f32[512,256]{0,1:T(8,128)S(1)}, f32[512,256]{0,1:T(8,128)}, u32[]{:S(2)}) copy-start(f32[512,256]{0,1:T(8,128)} %copy-done.37) | copy-start | bytes 1572868
  421.1 17.9 %copy-start.46 = (f32[256,128]{0,1:T(8,128)S(1)}, f32[256,128]{0,1:T(8,128)}, u32[]{:S(2)}) copy-start(f32[256,128]{0,1:T(8,128)} %copy-done.45) | copy-start | bytes 393220
  422.7 16.3 %copy-start.26 = (f32[512,256]{0,1:T(8,128)S(1)}, f32[512,256]{0,1:T(8,128)}, u32[]{:S(2)}) copy-start(f32[512,256]{0,1:T(8,128)} %get-tuple-element.66) | copy-start | bytes 1572868
  422.7 16.3 %copy-start.62 = (f32[256]{0:T(256)S(1)}, f32[256]{0:T(256)}, u32[]{:S(2)}) copy-start(f32[256]{0:T(256)} %mul.535) | copy-start | bytes 3076
  422.7 16.3 %copy-start.71 = (f32[256]{0:T(256)S(1)}, f32[256]{0:T(256)}, u32[]{:S(2)}) copy-start(f32[256]{0:T(256)} %add_rsqrt_fusion.4) | copy-start | bytes 3076
  422.7 16.9 %copy-start.50 = (f32[1280]{0:T(1024)S(1)}, f32[1280]{0:T(1024)}, u32[]{:S(2)}) copy-start(f32[1280]{0:T(1024)} %copy-done.49) | copy-start | bytes 15364
  451.3 84.3 %copy-start.15 = (f32[512,1280]{1,0:T(8,128)S(1)}, f32[512,1280]{1,0:T(8,128)}, u32[]{:S(2)}) copy-start(f32[512,1280]{1,0:T(8,128)} %get-tuple-element.41) | copy-start | bytes 7864324
  451.3 84.3 %copy-start.42 = (f32[256,1280]{1,0:T(8,128)S(1)}, f32[256,1280]{1,0:T(8,128)}, u32[]{:S(2)}) copy-start(f32[256,1280]{1,0:T(8,128)} %get-tuple-element.95) | copy-start | bytes 3932164
  451.3 84.3 %copy-start.85 = (f32[256]{0:T(256)S(1)}, f32[256]{0:T(256)}, u32[]{:S(2)}) copy-start(f32[256]{0:T(256)} %dynamic-slice.4) | copy-start | bytes 3076
  (81 other events, 192.9 us)
Sparse Core Ops, SparseCore 0:
  48.3 90.7 all-gather.1

commit v6 on v5

--- a/solution.py
+++ b/solution.py
@@ -62,10 +62,6 @@
     return lax.dot_general(
         left, right, (((1,), (1,)), ((), ())), preferred_element_type=jnp.float32
     )
-
-
-def gelu_pair(gate_proj, up_proj):
-    return jax.nn.gelu(gate_proj, approximate=True) * up_proj
 
 
 ALL = ("z", "x", "core", "seq")
@@ -144,7 +140,7 @@
     return send
 
 
-def plane_spread(own_ref, out_ref, send_sems, recv_sems, local_sem):
+def plane_spread(own_ref, out_ref, send_sems, recv_sems, local_sem, compute=lambda i: None):
     sibling, along_x, along_y, member = plane_places()
     half = own_ref.shape[0] // 2
     top, bottom = pl.ds(0, half), pl.ds(half, half)
@@ -162,22 +158,30 @@
     own_x_bottom = send(2, own_ref.at[bottom], out_ref.at[me, bottom], along_x)
     own_y_top = send(4, own_ref.at[top], out_ref.at[me, top], along_y)
     x_block, y_block, diagonal = member(1, 0, 0), member(0, 0, 1), member(1, 0, 1)
+    compute(0)
     own_x_top.wait_recv()
     diagonal_top = forward(5, x_block, top, along_y)
     x_top = forward(7, x_block, top, sibling)
     own_y_bottom.wait_recv()
     diagonal_bottom = forward(6, y_block, bottom, along_x)
     y_bottom = forward(9, y_block, bottom, sibling)
+    own_sibling.wait_recv()
+    compute(1)
     own_x_bottom.wait_recv()
     x_bottom = forward(8, x_block, bottom, sibling)
     own_y_top.wait_recv()
     y_top = forward(10, y_block, top, sibling)
+    compute(2)
     diagonal_top.wait_recv()
     far_top = forward(11, diagonal, top, sibling)
     diagonal_bottom.wait_recv()
     far_bottom = forward(12, diagonal, bottom, sibling)
-    for copy in (own_sibling, x_top, y_bottom, x_bottom, y_top, far_top, far_bottom):
-        copy.wait_recv()
+    compute(3)
+    compute(4)
+    for i, copies in ((5, (x_top, x_bottom)), (6, (y_bottom, y_top)), (7, (far_top, far_bottom))):
+        for copy in copies:
+            copy.wait_recv()
+        compute(i)
     for copy in (
         own_x_top,
         own_y_bottom,
@@ -274,7 +278,10 @@
     lax.fori_loop(start, start + count, one, 0)
 
 
-def plane_sum(part_ref, own_sum, near, sums, from_x, from_y, far_x, far_y, send_sems, recv_sems):
+def plane_sum(
+    part_ref, own_sum, near, sums, from_x, from_y, far_x, far_y, send_sems, recv_sems,
+    work=lambda point: None,
+):
     sibling, along_x, along_y, member = plane_places()
     rows = own_sum.shape[0]
     half = rows // 2
@@ -286,6 +293,7 @@
         send(k, part_ref.at[member(at_x, 1, at_y)], near.at[k], sibling)
         for k, (at_x, at_y) in enumerate(chips)
     ]
+    work(0)
     to_sibling[0].wait_recv()
     add_rows(sums.at[0], (mine[0], near.at[0]), 0, rows)
     diagonal_x = send(4, sums.at[0, bottom], far_x.at[bottom], along_x)
@@ -297,12 +305,14 @@
     add_rows(sums.at[2], (mine[2], near.at[2]), 0, half)
     direct_y = send(7, sums.at[2, top], from_y.at[top], along_y)
     to_sibling[3].wait_recv()
+    work(1)
     diagonal_y.wait_recv()
     add_rows(sums.at[1], (mine[1], near.at[1], far_y), 0, half)
     joint_x = send(8, sums.at[1, top], from_x.at[top], along_x)
     diagonal_x.wait_recv()
     add_rows(sums.at[2], (mine[2], near.at[2], far_x), half, half)
     joint_y = send(9, sums.at[2, bottom], from_y.at[bottom], along_y)
+    work(2)
     direct_x.wait_recv()
     direct_y.wait_recv()
     joint_x.wait_recv()
@@ -348,6 +358,228 @@
         ),
     )(partial.reshape(members, *shape))
     return out.reshape(rows, columns)
+
+
+gelu_inner = 0.7978845608028654
+gelu_cubic = 0.044715
+
+
+def pad_rows(target, source):
+    rows = source.shape[0]
+    target[pl.ds(0, rows)] = source[...]
+    if target.shape[0] > rows:
+        extra = target.shape[0] - rows
+        target[pl.ds(rows, extra)] = jnp.zeros((extra, target.shape[1]), target.dtype)
+
+
+def ffn_forward_kernel(in_ref, gate_up_ref, down_ref, part_ref, act_ref, to_gate, to_up, down, proj):
+    units = act_ref.shape[1]
+
+    @pl.when(pl.program_id(0) == 0)
+    def _():
+        pad_rows(down, down_ref)
+
+    proj[...] = matmul(in_ref[...], gate_up_ref[...])
+    step = 32
+
+    def one(i, carry):
+        rows = pl.ds(pl.multiple_of(i * step, step), step)
+        gate, up = proj[rows, :units], proj[rows, units:]
+        square = gate * gate
+        bend = jnp.tanh(gelu_inner * gate * (1.0 + gelu_cubic * square))
+        half = 0.5 * (1.0 + bend)
+        value = gate * half
+        slope = half + 0.5 * gate * (1.0 - bend * bend) * (
+            gelu_inner * (1.0 + 3.0 * gelu_cubic * square)
+        )
+        to_gate[rows, :] = slope * up
+        to_up[rows, :] = value
+        act_ref[rows, :] = (value * up).astype(act_ref.dtype)
+        return carry
+
+    lax.fori_loop(0, in_ref.shape[0] // step, one, 0)
+    part_ref[...] = matmul(act_ref[...], down[...]).astype(part_ref.dtype)
+
+
+ROW_BLOCK = 256
+
+
+def whole(array):
+    return pl.BlockSpec(array.shape, lambda i: (0, 0), pipeline_mode=pl.Buffered(1))
+
+
+def row_block(columns):
+    return pl.BlockSpec((ROW_BLOCK, columns), lambda i: (i, 0))
+
+
+def ffn_forward(rows_in, gate_up, down):
+    rows, depth = rows_in.shape
+    units, columns = gate_up.shape[1] // 2, down.shape[1]
+    low = rows_in.dtype
+    return pl.pallas_call(
+        ffn_forward_kernel,
+        grid=(rows // ROW_BLOCK,),
+        in_specs=[row_block(depth), whole(gate_up), whole(down)],
+        out_specs=[row_block(columns), row_block(units), row_block(units), row_block(units)],
+        out_shape=[
+            jax.ShapeDtypeStruct((rows, columns), low),
+            jax.ShapeDtypeStruct((rows, units), low),
+            jax.ShapeDtypeStruct((rows, units), jnp.float32),
+            jax.ShapeDtypeStruct((rows, units), jnp.float32),
+        ],
+        scratch_shapes=[
+            pltpu.VMEM((units, columns), low),
+            pltpu.VMEM((ROW_BLOCK, 2 * units), jnp.float32),
+        ],
+        cost_estimate=busy(20),
+        compiler_params=pltpu.CompilerParams(vmem_limit_bytes=VMEM_BYTES),
+    )(rows_in, gate_up, down)
+
+
+def gather_backward_kernel(
+    own_ref, down_ref, gate_up_ref, to_gate_hbm, to_up_hbm, grad_ref, both_ref, part_ref,
+    down, to_gate, to_up, load_sems, send_sems, recv_sems, local_sem,
+):
+    _, _, _, member = plane_places()
+    units = down.shape[0]
+    pieces, piece, columns = own_ref.shape
+    rows = pieces * piece
+    order = [
+        member(*far)
+        for far in (
+            (0, 0, 0), (0, 1, 0), (1, 0, 0), (0, 0, 1), (1, 0, 1), (1, 1, 0), (0, 1, 1), (1, 1, 1),
+        )
+    ]
+
+    def loads(i):
+        at = pl.ds(pl.multiple_of(order[i] * rows, rows), rows)
+        slot = i % 2
+        return (
+            pltpu.make_async_copy(to_gate_hbm.at[at], to_gate.at[slot], load_sems.at[0, slot]),
+            pltpu.make_async_copy(to_up_hbm.at[at], to_up.at[slot], load_sems.at[1, slot]),
+        )
+
+    def compute(i):
+        if i + 1 < len(order):
+            for load in loads(i + 1):
+                load.start()
+        for load in loads(i):
+            load.wait()
+        block, slot = order[i], i % 2
+        at = pl.ds(pl.multiple_of(block * rows, rows), rows)
+        source = own_ref if i == 0 else grad_ref.at[block]
+        act_grad = contract_cols(source[...].reshape(rows, columns), down[...])
+        both_ref[at, :units] = (act_grad * to_gate[slot]).astype(both_ref.dtype)
+        both_ref[at, units:] = (act_grad * to_up[slot]).astype(both_ref.dtype)
+        part = contract_cols(both_ref[at, :], gate_up_ref[...]).astype(part_ref.dtype)
+        part_ref[block] = part.reshape(pieces, piece, part.shape[1])
+
+    for load in loads(0):
+        load.start()
+    pad_rows(down, down_ref)
+    greet(plane_places()[:3])
+    plane_spread(own_ref, grad_ref, send_sems, recv_sems, local_sem, compute)
+
+
+def gather_backward(own, down, gate_up, to_gate, to_up, collective_id):
+    rows, columns = own.shape
+    members, piece = 8, 16
+    depth, units = gate_up.shape[0], to_gate.shape[1]
+    low = own.dtype
+    vmem, anywhere = pl.BlockSpec(memory_space=pltpu.VMEM), pl.BlockSpec(memory_space=pl.ANY)
+    grad, both, part = pl.pallas_call(
+        gather_backward_kernel,
+        out_shape=[
+            jax.ShapeDtypeStruct((members, rows // piece, piece, columns), low),
+            jax.ShapeDtypeStruct((members * rows, 2 * units), low),
+            jax.ShapeDtypeStruct((members, rows // piece, piece, depth), low),
+        ],
+        in_specs=[vmem, vmem, vmem, anywhere, anywhere],
+        out_specs=[vmem, vmem, vmem],
+        scratch_shapes=[
+            pltpu.VMEM((units, columns), low),
+            pltpu.VMEM((2, rows, units), jnp.float32),
+            pltpu.VMEM((2, rows, units), jnp.float32),
+            pltpu.SemaphoreType.DMA((2, 2)),
+            *GATHER_SEMS,
+        ],
+        cost_estimate=busy(35),
+        compiler_params=pltpu.CompilerParams(
+            collective_id=collective_id, has_side_effects=True, vmem_limit_bytes=VMEM_BYTES
+        ),
+    )(own.reshape(rows // piece, piece, columns), down, gate_up, to_gate, to_up)
+    return grad.reshape(members * rows, columns), both, part
+
+
+def sum_gradients_kernel(
+    part_ref, in_hbm, both_hbm, act_hbm, grad_hbm, sum_ref, gate_up_ref, down_ref,
+    rows_in, both, act, grad, load_sems, *scratch,
+):
+    loads = [
+        pltpu.make_async_copy(source, target, load_sems.at[k])
+        for k, (source, target) in enumerate(
+            ((act_hbm, act), (grad_hbm, grad), (in_hbm, rows_in), (both_hbm, both))
+        )
+    ]
+    for load in loads:
+        load.start()
+    down_step, step = down_ref.shape[1] // 3, 256
+
+    def down_columns(i, carry):
+        at = pl.ds(pl.multiple_of(i * down_step, 128), down_step)
+        down_ref[:, at] = contract_rows(act[...], grad[:, at]).astype(down_ref.dtype)
+        return carry
+
+    def gate_up_columns(i, carry):
+        at = pl.ds(pl.multiple_of(i * step, step), step)
+        gate_up_ref[:, at] = contract_rows(rows_in[...], both[:, at]).astype(gate_up_ref.dtype)
+        return carry
+
+    blocks = gate_up_ref.shape[1] // step
+
+    def work(point):
+        if point == 0:
+            loads[0].wait()
+            loads[1].wait()
+            lax.fori_loop(0, 3, down_columns, 0)
+        if point == 1:
+            loads[2].wait()
+            loads[3].wait()
+            lax.fori_loop(0, 2, gate_up_columns, 0)
+        if point == 2:
+            lax.fori_loop(2, blocks, gate_up_columns, 0)
+
+    greet(plane_places()[:3])
+    plane_sum(part_ref, sum_ref, *scratch, work=work)
+
+
+def sum_gradients(part, rows_in, both, act, grad, collective_id):
+    members, pieces, piece, depth = part.shape
+    low = part.dtype
+    vmem, anywhere = pl.BlockSpec(memory_space=pltpu.VMEM), pl.BlockSpec(memory_space=pl.ANY)
+    total, gate_up, down = pl.pallas_call(
+        sum_gradients_kernel,
+        out_shape=[
+            jax.ShapeDtypeStruct((pieces, piece, depth), jnp.float32),
+            jax.ShapeDtypeStruct((depth, both.shape[1]), low),
+            jax.ShapeDtypeStruct((act.shape[1], grad.shape[1]), low),
+        ],
+        in_specs=[vmem] + [anywhere] * 4,
+        out_specs=[vmem, vmem, vmem],
+        scratch_shapes=[
+            pltpu.VMEM(rows_in.shape, low),
+            pltpu.VMEM(both.shape, low),
+            pltpu.VMEM(act.shape, low),
+            pltpu.VMEM(grad.shape, low),
+            pltpu.SemaphoreType.DMA((4,)),
+            *plane_sum_scratch((pieces, piece, depth), low),
+        ],
+        cost_estimate=busy(35),
+        compiler_params=pltpu.CompilerParams(
+            collective_id=collective_id, has_side_effects=True, vmem_limit_bytes=60 * 2**20
+        ),
+    )(part, rows_in, both, act, grad)
+    return total.reshape(pieces * piece, depth), gate_up, down
 
 
 def owner_sum_kernel(planes, part_ref, out_ref, own_sum, leaving, arriving, z_send, z_recv, *scratch):
@@ -548,39 +780,30 @@
     ffn_in = (norm_middle * ffnin_scale).astype(bf16)
 
     plane_in = gather_rows(matmul(ffn_in, by_device).astype(bf16), 1)
-    gate_up_proj = matmul(plane_in, gate_up_full)
-    activated, gelu_back = jax.vjp(
-        lambda proj: gelu_pair(proj[:, :unit_pad], proj[:, unit_pad:]), gate_up_proj
-    )
-    activated_low = activated.astype(bf16)
-    ffn_raw = plane_scatter_sum(matmul(activated_low[:, :unit_count], down_full).astype(bf16), 2)
+    ffn_part, activated_low, to_gate, to_up = ffn_forward(plane_in, gate_up_full, down_full)
+    ffn_raw = plane_scatter_sum(ffn_part, 2)
     inv_ffn = inverse_rms(ffn_raw)
     norm_ffn = ffn_raw * inv_ffn
     result = middle + norm_ffn * ffnout_scale
     ffnout_gain_grad = jnp.sum(incoming * norm_ffn, axis=0)
     ffn_raw_grad = rms_back(incoming * ffnout_scale, norm_ffn, inv_ffn).astype(bf16)
 
-    plane_grad = gather_rows(ffn_raw_grad, 3)
-    act_grad = contract_cols(plane_grad, down_full)
-    act_grad = jnp.pad(act_grad, ((0, 0), (0, unit_pad - unit_count)))
-    gate_up_low = gelu_back(act_grad)[0].astype(bf16)
-    down_blocks = contract_rows(activated_low[:, :unit_count], plane_grad).reshape(
-        planes, hidden_rows, down_weight.shape[1]
-    )
+    plane_grad, gate_up_low, ffn_in_part = gather_backward(
+        ffn_raw_grad, down_full, gate_up_full, to_gate, to_up, 3
+    )
+    ffn_in_grad, gate_up_blocks, down_blocks = sum_gradients(
+        ffn_in_part, plane_in, gate_up_low, activated_low, plane_grad, 4
+    )
+    ffn_in_grad = take_back(ffn_in_grad, by_device)
+    down_low = down_blocks[:unit_count].reshape(planes, hidden_rows, down_weight.shape[1])
     plane = lax.axis_index("z")
-    down_wgrad = lax.dynamic_index_in_dim(down_blocks, plane, 0, keepdims=False)
-    down_low = down_blocks.astype(bf16)
+    down_wgrad = lax.dynamic_index_in_dim(down_low, plane, 0, keepdims=False).astype(f32)
     for k in range(1, planes):
         leaving = lax.dynamic_index_in_dim(down_low, lax.rem(plane + k, planes), 0, keepdims=False)
         shift = [(i, (i + k) % planes) for i in range(planes)]
         down_wgrad = down_wgrad + lax.ppermute(leaving, "z", shift).astype(f32)
 
-    gate_up_blocks = contract_rows(plane_in, gate_up_low).astype(bf16)
-    gate_up_blocks = gate_up_blocks.reshape(devices, padded, 2 * unit_pad)
-    ffn_in_part = contract_cols(gate_up_low, gate_up_full).astype(bf16)
-    gate_up_blocks, ffn_in_part = lax.optimization_barrier((gate_up_blocks, ffn_in_part))
-    gate_up_terms = exchange(gate_up_blocks, ALL)
-    ffn_in_grad = take_back(plane_scatter_sum(ffn_in_part, 4), by_device)
+    gate_up_terms = exchange(gate_up_blocks.reshape(devices, padded, 2 * unit_pad), ALL)
     ffnin_gain_grad = jnp.sum(ffn_in_grad * norm_middle, axis=0)
     middle_grad = incoming + rms_back(ffn_in_grad * ffnin_scale, norm_middle, inv_middle)
     attnout_gain_grad = jnp.sum(middle_grad * norm_attn, axis=0)

time: 565 us -> 545 us (0.965)
  Pallas kernels: 277 us -> 353 us
  matrix products: 105 us -> 32.2 us
  other arithmetic: 61.5 us -> 38.8 us
  waiting for transfers between devices: 15.4 us -> 8.05 us
    pallas_call x0 -> x3, Pallas kernels: none -> 110 us  [the longest x1 42.9 us: gather_backward(): pl.pallas_call(gather_backward_kernel, out_shape=[jax.ShapeDtypeStruct((m...]
    pallas_call x2 -> x1, Pallas kernels: 53.5 us -> 24.6 us  [plane_scatter_sum(): pl.pallas_call(plane_sum_kernel, out_shape=jax.ShapeDtypeStruct(shape, jn...]
    dot_general x4 -> x2, matrix products: 28.3 us -> 2.07 us  [contract_rows(): lax.dot_general(left, right, (((0,), (0,)), ((), ())), preferred_element_...]
    dot_general x6 -> x4, matrix products: 36.1 us -> 11.3 us  [contract_cols(): lax.dot_general(left, right, (((1,), (1,)), ((), ())), preferred_element_...]
    pallas_call x3 -> x2, Pallas kernels: 120 us -> 95.7 us  [plane_gather(): pl.pallas_call(gather_kernel, out_shape=jax.ShapeDtypeStruct((members, *l...]
    dot_general x7 -> x5, matrix products: 31.7 us -> 10.3 us  [matmul(): return jnp.dot(left, right, preferred_element_type=jnp.float32)]
    pallas_call x1, Pallas kernels: 81 us -> 100 us  [owner_sum(): pl.pallas_call(functools.partial(owner_sum_kernel, planes), out_shape=jax...]
    mul x2 -> x0, other arithmetic: 17.3 us -> none  [gelu_pair(): return jax.nn.gelu(gate_proj, approximate=True) * up_proj]
  transfers between devices with their start and end apart: 8 -> 8, of which waited for: 1 -> 1; matrix products, arithmetic and copies ran while one was open for 24% -> 20% of each run, Pallas kernels for 41% -> 40%
where the time goes in v6:
time: 545 us; the launch traced here: 540 us
  Pallas kernels  353 us (65%)
  local copies, waits for them, and re-layouts  70 us (13%)
  other arithmetic  38.8 us (7%)
  matrix products  32.2 us (6%)
  starting transfers between devices  21 us (4%)
  between operations  16 us (3%)
  waiting for transfers between devices  8.05 us (1%)
    pallas_call x1, Pallas kernels, owner_sum(): pl.pallas_call(functools.partial(owner_sum_kernel, planes), out_shape=jax...  100 us
    pallas_call x2, Pallas kernels, plane_gather(): pl.pallas_call(gather_kernel, out_shape=jax.ShapeDtypeStruct((members, *l...  95.7 us
    pallas_call x1, Pallas kernels, gather_backward(): pl.pallas_call(gather_backward_kernel, out_shape=[jax.ShapeDtypeStruct((m...  42.9 us
    pallas_call x1, Pallas kernels, sum_gradients(): pl.pallas_call(sum_gradients_kernel, out_shape=[jax.ShapeDtypeStruct((pie...  38.2 us
    pallas_call x1, Pallas kernels, ffn_forward(): pl.pallas_call(ffn_forward_kernel, grid=(rows // ROW_BLOCK,), in_specs=[r...  29.4 us
    pallas_call x1, Pallas kernels, plane_scatter_sum(): pl.pallas_call(plane_sum_kernel, out_shape=jax.ShapeDtypeStruct(shape, jn...  24.6 us
    pallas_call x1, Pallas kernels, z_gather(): pl.pallas_call(functools.partial(z_gather_kernel, planes), out_shape=jax....  22.5 us
    unnamed x212, local copies, waits for them, and re-layouts  18.2 us
  transfers between devices with their start and end apart: 8, of which 1 were waited for; matrix products, arithmetic and copies ran while one was open for 20% of the time, Pallas kernels for 40%

profile of v6, /device:TPU:8, one launch (start us, length us, event | category | flops | bytes accessed | tf_op | source)
XLA Modules:
  0.0 539.6 jit_solution(14014995984117614481)
XLA Ops:
  8.8 2.9 reshape.363
  15.9 22.5 %shard_map.274.own_ref = bf16[4,72,1536]{2,1,0:T(8,128)(2,1)S(1)} custom-call(bf16[72,1536]{1,0:T(8,128)(2,1)S(1)} %fusion.62.own_ref), custom_call_target="tpu_custom_call" | custom-call | bytes 60000000 | tf_op jit(solution)/shard_map/pallas_call | solution.py:232
  38.5 2.4 broadcast_in_dim.25
  40.9 5.0 all-to-all-start
  46.7 57.4 %shard_map.275 = bf16[8,4,72,1536]{3,2,1,0:T(8,128)(2,1)} custom-call(bf16[4,72,1536]{2,1,0:T(8,128)(2,1)S(1)} %shard_map.274.own_ref), custom_call_target="tpu_custom_call" | custom-call | bytes 75000000 | tf_op jit(solution)/shard_map/pallas_call | solution.py:251
  105.5 3.3 slice_bitcast_fusion
  111.0 4.3 slice.142
  121.9 2.9 multiply_reduce_fusion
  136.4 2.6 fusion.23
  140.1 2.0 subtract_convert_fusion
  151.5 2.0 convolution_convert_fusion.1
  153.6 38.3 %shard_map.276 = bf16[8,16,16,1280]{3,2,1,0:T(8,128)(2,1)S(1)} custom-call(bf16[16,16,1280]{2,1,0:T(8,128)(2,1)S(1)} %bitcast.192), custom_call_target="tpu_custom_call" | custom-call | bytes 75000000 | tf_op jit(solution)/shard_map/pallas_call | solution.py:251
  191.9 2.4 copy-done
  197.8 29.4 %shard_map.277 = (bf16[2048,1152]{1,0:T(8,128)(2,1)}, bf16[2048,896]{1,0:T(8,128)(2,1)S(1)}, f32[2048,896]{1,0:T(8,128)}, f32[2048,896]{1,0:T(8,128)}) custom-call(bf16[2048,1280]{1,0:T(8,128)(2,1)} %bitcast.189, bf16[1280,1792]{1,0:T(8,128)(2,1)} %bitcast.20.gate_up_ref, bf16[864,1152]{1,0:T(8,128)(2,1)S(1)} %copy-done.1), custom_call_target="tpu_custom_call" | custom-call | bytes 60000000 | tf_op jit(solution)/shard_map/pallas_call | solution.py:419
  229.0 2.3 copy-done.3
  231.4 24.6 %shard_map.278 = f32[16,16,1152]{2,1,0:T(8,128)S(1)} custom-call(bf16[8,16,16,1152]{3,2,1,0:T(8,128)(2,1)S(1)} %bitcast.191), custom_call_target="tpu_custom_call" | custom-call | bytes 75000000 | tf_op jit(solution)/shard_map/pallas_call | solution.py:349
  256.3 3.6 fusion.41
  261.3 42.9 %shard_map.279 = (bf16[8,16,16,1152]{3,2,1,0:T(8,128)(2,1)}, bf16[2048,1792]{1,0:T(8,128)(2,1)}, bf16[8,16,16,1280]{3,2,1,0:T(8,128)(2,1)}) custom-call(bf16[16,16,1152]{2,1,0:T(8,128)(2,1)S(1)} %multiply_convert_fusion.2.own_ref, bf16[864,1152]{1,0:T(8,128)(2,1)S(1)} %copy-done.2, bf16[1280,1792]{1,0:T(8,128)(2,1)} %bitcast.20.gate_up_ref, ...), custom_call_target="tpu_custom_call" | custom-call | bytes 105000000 | tf_op jit(solution)/shard_map/pallas_call | solution.py:490
  304.2 38.2 %shard_map.280 = (f32[16,16,1280]{2,1,0:T(8,128)}, bf16[1280,1792]{1,0:T(8,128)(2,1)}, bf16[896,1152]{1,0:T(8,128)(2,1)}) custom-call(bf16[8,16,16,1280]{3,2,1,0:T(8,128)(2,1)} %get-tuple-element.34.part_ref, bf16[2048,1280]{1,0:T(8,128)(2,1)} %bitcast.190, bf16[2048,1792]{1,0:T(8,128)(2,1)} %get-tuple-element.35.both_hbm, bf16[2048,896]{1,0:T(8,128)(2,1)} %copy-done.4, ...), custom_call_target="tpu_custom_call" | custom-call | bytes 105000000 | tf_op jit(solution)/shard_map/pallas_call | solution.py:560
  346.1 6.8 %collective-permute-start.3 = (bf16[216,1152]{1,0:T(8,128)(2,1)}, bf16[216,1152]{1,0:T(8,128)(2,1)}, u32[]{:S(2)}, u32[]{:S(2)}) collective-permute-start(bf16[216,1152]{1,0:T(8,128)(2,1)} %get-tuple-element.66), channel_id=1, source_target_pairs={{0,16},{8,24},{16,0},{24,8},{1,17},{9,25},{17,1},{25,9},{2,18},{10... | collective-permute-start | bytes 1493000 | tf_op jit(solution)/shard_map/ppermute | solution.py:804
  353.0 2.3 fusion.25
  361.7 2.0 copy.268
  368.5 5.2 all-to-all-start.1
  379.7 2.5 copy.262
  382.2 2.1 convolution_bitcast_fusion.1
  391.1 7.5 %collective-permute-done.1 = bf16[256,512]{0,1:T(8,128)(2,1)} collective-permute-done((bf16[256,512]{0,1:T(8,128)(2,1)}, bf16[256,512]{0,1:T(8,128)(2,1)}, u32[]{:S(2)}, u32[]{:S(2)}) %collective-permute-start.1) | collective-permute-done | bytes 262176 | tf_op jit(solution)/shard_map/ppermute | solution.py:825
  400.3 4.9 multiply_reduce_fusion.1
  408.6 3.4 fusion.1.part_ref
  412.0 100.2 %shard_map.281 = f32[72,1536]{1,0:T(8,128)S(1)} custom-call(bf16[8,4,72,1536]{3,2,1,0:T(8,128)(2,1)} %fusion.1.part_ref), custom_call_target="tpu_custom_call" | custom-call | bytes 105000000 | tf_op jit(solution)/shard_map/pallas_call | solution.py:614
  515.8 2.5 fusion.29
  519.5 2.7 fusion.44
  522.2 3.2 convert_reduce_fusion
  (362 shorter events, 89.4 us)
Async XLA Ops:
  7.2 5.2 copy-start.51
  7.2 113.4 %collective-permute-start = (bf16[256,1152]{1,0:T(8,128)(2,1)}, bf16[256,1152]{1,0:T(8,128)(2,1)}, u32[]{:S(2)}, u32[]{:S(2)}) collective-permute-start(bf16[256,1152]{1,0:T(8,128)(2,1)} %bitcast.213), channel_id=1, source_target_pairs={{0,1},{1,0},{2,3},{3,2},{4,5},{5,4},{6,7},{7,6},{8,9},{9,8},{10,11... | collective-permute-start | bytes 1769480 | tf_op jit(solution)/shard_map/ppermute | solution.py:728
  40.9 155.4 %all-to-all-start = ((bf16[32,40,1792]{2,1,0:T(8,128)(2,1)}), bf16[32,40,1792]{2,1,0:T(8,128)(2,1)}, u32[]{:S(2)}, u32[]{:S(2)}) async-start(bf16[32,40,1792]{2,1,0:T(8,128)(2,1)} %bitcast.194), calls=%async_computation | async-start | bytes 9175040 | tf_op jit(solution)/shard_map/all_to_all | solution.py:98
  45.9 150.4 %all-gather.2.cloned.1.call-start = ((), (), s32[]{:S(2)}) async-start(), calls=%async_computation.2 | async-start | bytes 2488320 | tf_op jit(solution)/shard_map/all_gather | solution.py:697
  46.6 75.2 %copy-start.76 = (s32[1152]{0:T(1024)}, s32[1152]{0:T(1024)S(1)}, u32[]{:S(2)}) copy-start(s32[1152]{0:T(1024)S(1)} %broadcast_add_fusion) | copy-start | bytes 13828
  46.6 75.2 %copy-start.79 = (s32[1152]{0:T(1024)}, s32[1152]{0:T(1024)S(1)}, u32[]{:S(2)}) copy-start(s32[1152]{0:T(1024)S(1)} %fusion.72) | copy-start | bytes 13828
  46.7 75.2 %copy-start.82 = (s32[1152]{0:T(1024)}, s32[1152]{0:T(1024)S(1)}, u32[]{:S(2)}) copy-start(s32[1152]{0:T(1024)S(1)} %iota_divide_fusion) | copy-start | bytes 13828
  46.7 75.2 %copy-start.85 = (s32[1152]{0:T(1024)}, s32[1152]{0:T(1024)S(1)}, u32[]{:S(2)}) copy-start(s32[1152]{0:T(1024)S(1)} %iota_remainder_fusion) | copy-start | bytes 13828
  46.7 75.1 %copy-start.89 = (pred[1152]{0:T(1024)(128)(4,1)}, pred[1152]{0:T(1024)(128)(4,1)S(1)}, u32[]{:S(2)}) copy-start(pred[1152]{0:T(1024)(128)(4,1)S(1)} %fusion.75) | copy-start | bytes 3460
  46.7 75.1 %copy-start.92 = (pred[1152]{0:T(1024)(128)(4,1)}, pred[1152]{0:T(1024)(128)(4,1)S(1)}, u32[]{:S(2)}) copy-start(pred[1152]{0:T(1024)(128)(4,1)S(1)} %fusion.76) | copy-start | bytes 3460
  109.9 5.5 %copy-start.67 = (f32[256]{0:T(256)}, f32[256]{0:T(256)S(1)}, u32[]{:S(2)}) copy-start(f32[256]{0:T(256)S(1)} %mul.497) | copy-start | bytes 3076
  118.1 31.4 %copy-start.12 = (bf16[4,8,32,1152]{3,2,1,0:T(8,128)(2,1)}, bf16[4,8,32,1152]{3,2,1,0:T(8,128)(2,1)S(1)}, u32[]{:S(2)}) copy-start(bf16[4,8,32,1152]{3,2,1,0:T(8,128)(2,1)S(1)} %copy.226) | copy-start | bytes 7077892
  153.6 40.7 %copy-start.57 = (f32[256,4]{0,1:T(4,128)S(1)}, f32[256,4]{0,1:T(4,128)}, u32[]{:S(2)}) copy-start(f32[256,4]{0,1:T(4,128)} %copy-done.56) | copy-start | bytes 12292
  231.4 24.9 %copy-start.54 = (f32[1152]{0:T(1024)S(1)}, f32[1152]{0:T(1024)}, u32[]{:S(2)}) copy-start(f32[1152]{0:T(1024)} %mul.523) | copy-start | bytes 13828
  344.1 8.9 %copy-start.18 = (bf16[864,1152]{1,0:T(8,128)(2,1)}, bf16[864,1152]{1,0:T(8,128)(2,1)S(1)}, u32[]{:S(2)}) copy-start(bf16[864,1152]{1,0:T(8,128)(2,1)S(1)} %slice.173) | copy-start | bytes 5971972
  344.1 8.8 %copy-start.45 = (f32[16,16,1280]{2,1,0:T(8,128)S(1)}, f32[16,16,1280]{2,1,0:T(8,128)}, u32[]{:S(2)}) copy-start(f32[16,16,1280]{2,1,0:T(8,128)} %get-tuple-element.38) | copy-start | bytes 3932164
  345.3 174.2 %collective-permute-start.2 = (bf16[216,1152]{1,0:T(8,128)(2,1)}, bf16[216,1152]{1,0:T(8,128)(2,1)}, u32[]{:S(2)}, u32[]{:S(2)}) collective-permute-start(bf16[216,1152]{1,0:T(8,128)(2,1)} %get-tuple-element.64), channel_id=1, source_target_pairs={{0,8},{8,16},{16,24},{24,0},{1,9},{9,17},{17,25},{25,1},{2,10},{10... | collective-permute-start | bytes 1493000 | tf_op jit(solution)/shard_map/ppermute | solution.py:804
  346.1 173.4 %collective-permute-start.3 = (bf16[216,1152]{1,0:T(8,128)(2,1)}, bf16[216,1152]{1,0:T(8,128)(2,1)}, u32[]{:S(2)}, u32[]{:S(2)}) collective-permute-start(bf16[216,1152]{1,0:T(8,128)(2,1)} %get-tuple-element.66), channel_id=1, source_target_pairs={{0,16},{8,24},{16,0},{24,8},{1,17},{9,25},{17,1},{25,9},{2,18},{10... | collective-permute-start | bytes 1493000 | tf_op jit(solution)/shard_map/ppermute | solution.py:804
  352.9 166.7 %collective-permute-start.4 = (bf16[216,1152]{1,0:T(8,128)(2,1)}, bf16[216,1152]{1,0:T(8,128)(2,1)}, u32[]{:S(2)}, u32[]{:S(2)}) collective-permute-start(bf16[216,1152]{1,0:T(8,128)(2,1)} %get-tuple-element.65), channel_id=1, source_target_pairs={{0,24},{8,0},{16,8},{24,16},{1,25},{9,1},{17,9},{25,17},{2,26},{10... | collective-permute-start | bytes 1493000 | tf_op jit(solution)/shard_map/ppermute | solution.py:804
  368.5 5.2 copy-start.43
  368.5 153.6 %all-to-all-start.1 = ((bf16[32,40,1792]{2,1,0:T(8,128)(2,1)}), bf16[32,40,1792]{2,1,0:T(8,128)(2,1)}, u32[]{:S(2)}, u32[]{:S(2)}) async-start(bf16[32,40,1792]{2,1,0:T(8,128)(2,1)} %bitcast.205), calls=%async_computation.1 | async-start | bytes 9175040 | tf_op jit(solution)/shard_map/all_to_all | solution.py:98
  385.8 12.8 %collective-permute-start.1 = (bf16[256,512]{0,1:T(8,128)(2,1)}, bf16[256,512]{0,1:T(8,128)(2,1)}, u32[]{:S(2)}, u32[]{:S(2)}) collective-permute-start(bf16[256,512]{0,1:T(8,128)(2,1)} %fusion.51), channel_id=1, source_target_pairs={{0,1},{1,0},{2,3},{3,2},{4,5},{5,4},{6,7},{7,6},{8,9},{9,8},{10,11... | collective-permute-start | bytes 786440 | tf_op jit(solution)/shard_map/ppermute | solution.py:825
  389.5 9.2 %copy-start.22 = (f32[512,256]{0,1:T(8,128)S(1)}, f32[512,256]{0,1:T(8,128)}, u32[]{:S(2)}) copy-start(f32[512,256]{0,1:T(8,128)} %copy-done.21) | copy-start | bytes 1572868
  389.5 9.2 %copy-start.41 = (f32[512,256]{0,1:T(8,128)S(1)}, f32[512,256]{0,1:T(8,128)}, u32[]{:S(2)}) copy-start(f32[512,256]{0,1:T(8,128)} %copy-done.40) | copy-start | bytes 1572868
  391.1 8.6 %copy-start.50 = (f32[256,128]{0,1:T(8,128)S(1)}, f32[256,128]{0,1:T(8,128)}, u32[]{:S(2)}) copy-start(f32[256,128]{0,1:T(8,128)} %copy-done.49) | copy-start | bytes 393220
  391.1 8.7 %copy-start.29 = (f32[512,256]{0,1:T(8,128)S(1)}, f32[512,256]{0,1:T(8,128)}, u32[]{:S(2)}) copy-start(f32[512,256]{0,1:T(8,128)} %get-tuple-element.78) | copy-start | bytes 1572868
  391.1 8.7 %copy-start.65 = (f32[256]{0:T(256)S(1)}, f32[256]{0:T(256)}, u32[]{:S(2)}) copy-start(f32[256]{0:T(256)} %mul.482) | copy-start | bytes 3076
  391.1 8.7 %copy-start.74 = (f32[256]{0:T(256)S(1)}, f32[256]{0:T(256)}, u32[]{:S(2)}) copy-start(f32[256]{0:T(256)} %add_rsqrt_fusion.4) | copy-start | bytes 3076
  400.3 5.3 copy-start.31
  412.0 103.4 %copy-start.19 = (f32[512,1280]{1,0:T(8,128)S(1)}, f32[512,1280]{1,0:T(8,128)}, u32[]{:S(2)}) copy-start(f32[512,1280]{1,0:T(8,128)} %get-tuple-element.57) | copy-start | bytes 7864324
  412.0 103.4 %copy-start.46 = (f32[256,1280]{1,0:T(8,128)S(1)}, f32[256,1280]{1,0:T(8,128)}, u32[]{:S(2)}) copy-start(f32[256,1280]{1,0:T(8,128)} %get-tuple-element.107) | copy-start | bytes 3932164
  412.0 103.4 %copy-start.88 = (f32[256]{0:T(256)S(1)}, f32[256]{0:T(256)}, u32[]{:S(2)}) copy-start(f32[256]{0:T(256)} %dynamic-slice.4) | copy-start | bytes 3076
  (80 other events, 147.6 us)
Sparse Core Ops, SparseCore 0:
  48.3 90.7 all-gather.1

commit v7 on v6

--- a/solution.py
+++ b/solution.py
@@ -33,19 +33,6 @@
     frequency = rope_base ** (-(2.0 / head_width) * jnp.arange(half_width, dtype=jnp.float32))
     angles = positions[..., None] * frequency
     return (jnp.cos(angles), jnp.sin(angles))
-
-
-def rotate(values, cos_table, sin_table):
-    half_width = values.shape[-1] // 2
-    first_half = values[..., :half_width]
-    second_half = values[..., half_width:]
-    return jnp.concatenate(
-        [
-            first_half * cos_table - second_half * sin_table,
-            second_half * cos_table + first_half * sin_table,
-        ],
-        axis=-1,
-    )
 
 
 def matmul(left, right):
@@ -437,8 +424,8 @@
 
 
 def gather_backward_kernel(
-    own_ref, down_ref, gate_up_ref, to_gate_hbm, to_up_hbm, grad_ref, both_ref, part_ref,
-    down, to_gate, to_up, load_sems, send_sems, recv_sems, local_sem,
+    own_ref, down_ref, gate_up_ref, to_gate_hbm, to_up_hbm, act_hbm, grad_ref, both_ref, part_ref,
+    down_grad_ref, down, to_gate, to_up, act, act_sem, load_sems, send_sems, recv_sems, local_sem,
 ):
     _, _, _, member = plane_places()
     units = down.shape[0]
@@ -474,32 +461,41 @@
         part = contract_cols(both_ref[at, :], gate_up_ref[...]).astype(part_ref.dtype)
         part_ref[block] = part.reshape(pieces, piece, part.shape[1])
 
+    act_load = pltpu.make_async_copy(act_hbm, act, act_sem)
+    act_load.start()
     for load in loads(0):
         load.start()
     pad_rows(down, down_ref)
     greet(plane_places()[:3])
     plane_spread(own_ref, grad_ref, send_sems, recv_sems, local_sem, compute)
-
-
-def gather_backward(own, down, gate_up, to_gate, to_up, collective_id):
+    act_load.wait()
+    grad = grad_ref[...].reshape(len(order) * rows, columns)
+    down_grad = contract_rows(act[...], grad)
+    down_grad_ref[...] = down_grad[: down_ref.shape[0]].astype(down_grad_ref.dtype)
+
+
+def gather_backward(own, down, gate_up, to_gate, to_up, act, collective_id):
     rows, columns = own.shape
     members, piece = 8, 16
     depth, units = gate_up.shape[0], to_gate.shape[1]
     low = own.dtype
     vmem, anywhere = pl.BlockSpec(memory_space=pltpu.VMEM), pl.BlockSpec(memory_space=pl.ANY)
-    grad, both, part = pl.pallas_call(
+    grad, both, part, down_grad = pl.pallas_call(
         gather_backward_kernel,
         out_shape=[
             jax.ShapeDtypeStruct((members, rows // piece, piece, columns), low),
             jax.ShapeDtypeStruct((members * rows, 2 * units), low),
             jax.ShapeDtypeStruct((members, rows // piece, piece, depth), low),
+            jax.ShapeDtypeStruct(down.shape, low),
         ],
-        in_specs=[vmem, vmem, vmem, anywhere, anywhere],
-        out_specs=[vmem, vmem, vmem],
+        in_specs=[vmem, vmem, vmem, anywhere, anywhere, anywhere],
+        out_specs=[vmem, vmem, vmem, vmem],
         scratch_shapes=[
             pltpu.VMEM((units, columns), low),
             pltpu.VMEM((2, rows, units), jnp.float32),
             pltpu.VMEM((2, rows, units), jnp.float32),
+            pltpu.VMEM(act.shape, low),
+            pltpu.SemaphoreType.DMA,
             pltpu.SemaphoreType.DMA((2, 2)),
             *GATHER_SEMS,
         ],
@@ -507,28 +503,26 @@
         compiler_params=pltpu.CompilerParams(
             collective_id=collective_id, has_side_effects=True, vmem_limit_bytes=VMEM_BYTES
         ),
-    )(own.reshape(rows // piece, piece, columns), down, gate_up, to_gate, to_up)
-    return grad.reshape(members * rows, columns), both, part
+    )(own.reshape(rows // piece, piece, columns), down, gate_up, to_gate, to_up, act)
+    return both, part, down_grad
 
 
 def sum_gradients_kernel(
-    part_ref, in_hbm, both_hbm, act_hbm, grad_hbm, sum_ref, gate_up_ref, down_ref,
-    rows_in, both, act, grad, load_sems, *scratch,
+    part_ref, down_ref, in_hbm, both_hbm, sum_ref, gate_up_ref, down_sum_ref,
+    rows_in, both, arriving, load_sems, z_send, z_recv, *scratch,
 ):
+    planes = down_ref.shape[0]
+    z, x, core, seq = (lax.axis_index(name) for name in ALL)
+    others = [(lax.rem(z + k, planes), x, core, seq) for k in range(1, planes)]
     loads = [
         pltpu.make_async_copy(source, target, load_sems.at[k])
         for k, (source, target) in enumerate(
-            ((act_hbm, act), (grad_hbm, grad), (in_hbm, rows_in), (both_hbm, both))
+            ((in_hbm, rows_in), (both_hbm, both))
         )
     ]
     for load in loads:
         load.start()
-    down_step, step = down_ref.shape[1] // 3, 256
-
-    def down_columns(i, carry):
-        at = pl.ds(pl.multiple_of(i * down_step, 128), down_step)
-        down_ref[:, at] = contract_rows(act[...], grad[:, at]).astype(down_ref.dtype)
-        return carry
+    step = 256
 
     def gate_up_columns(i, carry):
         at = pl.ds(pl.multiple_of(i * step, step), step)
@@ -539,47 +533,57 @@
 
     def work(point):
         if point == 0:
-            loads[0].wait()
-            loads[1].wait()
-            lax.fori_loop(0, 3, down_columns, 0)
+            for load in loads:
+                load.wait()
+            lax.fori_loop(0, 2, gate_up_columns, 0)
         if point == 1:
-            loads[2].wait()
-            loads[3].wait()
-            lax.fori_loop(0, 2, gate_up_columns, 0)
+            lax.fori_loop(2, 3, gate_up_columns, 0)
         if point == 2:
-            lax.fori_loop(2, blocks, gate_up_columns, 0)
-
-    greet(plane_places()[:3])
+            lax.fori_loop(3, blocks, gate_up_columns, 0)
+
+    greet((*plane_places()[:3], *others))
+    send = sender(z_send, z_recv)
+    copies = [
+        send(k, down_ref.at[place[0]], arriving.at[k], place) for k, place in enumerate(others)
+    ]
     plane_sum(part_ref, sum_ref, *scratch, work=work)
-
-
-def sum_gradients(part, rows_in, both, act, grad, collective_id):
+    down_sum = down_ref[z].astype(jnp.float32)
+    for k, copy in enumerate(copies):
+        copy.wait_recv()
+        down_sum = down_sum + arriving[k].astype(jnp.float32)
+    down_sum_ref[...] = down_sum
+    for copy in copies:
+        copy.wait_send()
+
+
+def sum_gradients(part, down, rows_in, both, collective_id):
     members, pieces, piece, depth = part.shape
     low = part.dtype
     vmem, anywhere = pl.BlockSpec(memory_space=pltpu.VMEM), pl.BlockSpec(memory_space=pl.ANY)
-    total, gate_up, down = pl.pallas_call(
+    total, gate_up, down_sum = pl.pallas_call(
         sum_gradients_kernel,
         out_shape=[
             jax.ShapeDtypeStruct((pieces, piece, depth), jnp.float32),
             jax.ShapeDtypeStruct((depth, both.shape[1]), low),
-            jax.ShapeDtypeStruct((act.shape[1], grad.shape[1]), low),
+            jax.ShapeDtypeStruct(down.shape[1:], jnp.float32),
         ],
-        in_specs=[vmem] + [anywhere] * 4,
+        in_specs=[vmem, vmem, anywhere, anywhere],
         out_specs=[vmem, vmem, vmem],
         scratch_shapes=[
             pltpu.VMEM(rows_in.shape, low),
             pltpu.VMEM(both.shape, low),
-            pltpu.VMEM(act.shape, low),
-            pltpu.VMEM(grad.shape, low),
-            pltpu.SemaphoreType.DMA((4,)),
+            pltpu.VMEM((down.shape[0] - 1, *down.shape[1:]), low),
+            pltpu.SemaphoreType.DMA((2,)),
+            pltpu.SemaphoreType.DMA((down.shape[0] - 1,)),
+            pltpu.SemaphoreType.DMA((down.shape[0] - 1,)),
             *plane_sum_scratch((pieces, piece, depth), low),
         ],
         cost_estimate=busy(35),
         compiler_params=pltpu.CompilerParams(
             collective_id=collective_id, has_side_effects=True, vmem_limit_bytes=60 * 2**20
         ),
-    )(part, rows_in, both, act, grad)
-    return total.reshape(pieces * piece, depth), gate_up, down
+    )(part, down, rows_in, both)
+    return total.reshape(pieces * piece, depth), gate_up, down_sum
 
 
 def owner_sum_kernel(planes, part_ref, out_ref, own_sum, leaving, arriving, z_send, z_recv, *scratch):
@@ -629,6 +633,303 @@
             collective_id=collective_id, has_side_effects=True, vmem_limit_bytes=VMEM_BYTES
         ),
     )(blocks)
+
+
+def gain_places(blocks, planes, offset, count, per, by_member):
+    lane = lax.broadcasted_iota(jnp.int32, (256, blocks * per), 0)
+    column = lax.broadcasted_iota(jnp.int32, (256, blocks * per), 1)
+    inner = column % per
+    places = ((lane == offset + inner) & (inner < count)).astype(jnp.float32).astype(jnp.bfloat16)
+    listed = lax.broadcasted_iota(jnp.int32, (blocks, blocks * per), 0)
+    block = lax.broadcasted_iota(jnp.int32, (blocks, blocks * per), 1) // per
+    members = blocks // planes
+    if not by_member:
+        block = block % members * planes + block // members
+    return places, listed == block
+
+
+def spread_gain(rows, planes, *where):
+    places, chosen = gain_places(rows.shape[0], planes, *where)
+    return jnp.sum(jnp.where(chosen, matmul(rows, places), 0.0), axis=0, keepdims=True)
+
+
+def collect_gain(vector, blocks, planes, *where):
+    places, chosen = gain_places(blocks, planes, *where)
+    return contract_cols(jnp.where(chosen, vector, 0.0).astype(jnp.bfloat16), places)
+
+
+def inverse_of(values, count):
+    return lax.rsqrt(jnp.sum(values * values, axis=-1, keepdims=True) / count + epsilon)
+
+
+def back_of(grad_normed, normed, inverse, count):
+    inner = jnp.sum(grad_normed * normed, axis=-1, keepdims=True) / count
+    return inverse * (grad_normed - normed * inner)
+
+
+def turn(values, cos_table, sin_table):
+    half = values.shape[1] // 2
+    first, second = values[:, :half], values[:, half:]
+    return first * cos_table - second * sin_table, second * cos_table + first * sin_table
+
+
+def attention_forward_kernel(
+    gain_at, width_rows, row_ref, hidden_ref, packed_ref, cos_ref, sin_ref, segment_column, segment_row, placing_ref,
+    placed_ref, middle_ref, raw_ref, mix_ref, probs_ref, query_ref, key_ref, value_ref, query_raw_ref,
+    key_raw_ref, qkv_ref, output_ref, input_scale, query_scale, key_scale, attnout_scale, ffnin_scale, ffnout_scale,
+    gain_rows,
+):
+    bf16, f32 = jnp.bfloat16, jnp.float32
+    members, planes, piece, _ = packed_ref.shape
+    blocks = members * planes
+    padded = qkv_ref.shape[0] // blocks
+    mix_rows = piece - padded
+    width = hidden_ref.shape[1]
+    local_rows, full_rows = hidden_ref.shape[0], row_ref.shape[0]
+    head = key_ref.shape[1]
+    heads = query_ref.shape[1] // head
+    offset = pl.multiple_of(lax.axis_index("seq") * local_rows, local_rows)
+    mine = pl.ds(offset, local_rows)
+    for i in range(blocks):
+        member, plane = i // planes, i % planes
+        block = packed_ref[member, plane]
+        qkv_ref[padded * i : padded * (i + 1), :] = block[:padded]
+        natural = mix_rows * (plane * members + member)
+        output_ref[natural : natural + mix_rows, :] = block[padded:, :width]
+        gain_rows[i : i + 1, :] = block[width_rows : width_rows + 1, :256].astype(f32)
+    rows = gain_rows[...].astype(bf16)
+    (at, count), *others = gain_at
+    input_scale[...] = spread_gain(rows, planes, at, count, padded, True)
+    targets = (query_scale, key_scale, attnout_scale, ffnin_scale, ffnout_scale)
+    for target, (at, count) in zip(targets, others):
+        target[...] = spread_gain(rows, planes, at, count, count, False)
+
+    row = row_ref[...].astype(f32)
+    normed = (row * inverse_of(row, width) * input_scale[...]).astype(bf16)
+    key_value = matmul(normed, qkv_ref[:, heads * head :])
+    key_raw = key_value[:, :head]
+    value_ref[...] = key_value[:, head:].astype(bf16)
+    half = head // 2
+    turned = turn(key_raw * inverse_of(key_raw, head) * key_scale[...], cos_ref[...], sin_ref[...])
+    key_ref[:, :half], key_ref[:, half:] = turned[0].astype(bf16), turned[1].astype(bf16)
+
+    row = row_ref[mine, :].astype(f32)
+    normed = (row * inverse_of(row, width) * input_scale[...]).astype(bf16)
+    own = matmul(normed, qkv_ref[:, : (heads + 1) * head])
+    query_raw_ref[...] = own[:, : heads * head]
+    key_raw_ref[...] = own[:, heads * head :]
+    cos_table, sin_table = cos_ref[mine, :], sin_ref[mine, :]
+    places = offset + lax.broadcasted_iota(jnp.int32, (local_rows, full_rows), 0)
+    earlier = places >= lax.broadcasted_iota(jnp.int32, (local_rows, full_rows), 1)
+    allowed = (segment_column[...] == segment_row[...]) & earlier
+    for h in range(heads):
+        at = h * head
+        query_raw = query_raw_ref[:, at : at + head]
+        turned = turn(
+            query_raw * inverse_of(query_raw, head) * query_scale[...], cos_table, sin_table
+        )
+        scale = head ** (-0.5)
+        query_ref[:, at : at + half] = (turned[0] * scale).astype(bf16)
+        query_ref[:, at + half : at + head] = (turned[1] * scale).astype(bf16)
+        scores = contract_cols(query_ref[:, at : at + head], key_ref[...])
+        scores = jnp.where(allowed, scores, masked_score)
+        weights = jnp.exp(scores - jnp.max(scores, axis=-1, keepdims=True))
+        probs = weights / jnp.sum(weights, axis=-1, keepdims=True)
+        probs_ref[h] = probs
+        mix_ref[:, at : at + head] = matmul(probs.astype(bf16), value_ref[...]).astype(bf16)
+    attn_raw = matmul(mix_ref[...], output_ref[...])
+    raw_ref[...] = attn_raw
+    middle = hidden_ref[...].astype(f32) + attn_raw * inverse_of(attn_raw, width) * attnout_scale[...]
+    middle_ref[...] = middle
+    ffn_in = (middle * inverse_of(middle, width) * ffnin_scale[...]).astype(bf16)
+    placed_ref[...] = matmul(ffn_in, placing_ref[...]).astype(bf16)
+
+
+def attention_forward(
+    row_padded, hidden, packed, cos_full, sin_full, segment_column, segment_row, placing, gain_at, width_rows, padded,
+    head_width,
+):
+    bf16, f32 = jnp.bfloat16, jnp.float32
+    members, planes, piece, qkv_width = packed.shape
+    blocks = members * planes
+    local_rows, width = hidden.shape
+    query_width = qkv_width - 2 * head_width
+    heads = query_width // head_width
+    full_rows = row_padded.shape[0]
+    depth = blocks * padded
+    shape = jax.ShapeDtypeStruct
+    vmem = pl.BlockSpec(memory_space=pltpu.VMEM)
+    out_shape = [
+        shape((local_rows, depth), bf16),
+        shape((local_rows, width), f32),
+        shape((local_rows, width), f32),
+        shape((local_rows, query_width), bf16),
+        shape((heads, local_rows, full_rows), f32),
+        shape((local_rows, query_width), bf16),
+        shape((full_rows, head_width), bf16),
+        shape((full_rows, head_width), bf16),
+        shape((local_rows, query_width), f32),
+        shape((local_rows, head_width), f32),
+        shape((depth, qkv_width), bf16),
+        shape((query_width, width), bf16),
+        shape((1, depth), f32),
+        shape((1, head_width), f32),
+        shape((1, head_width), f32),
+        shape((1, width), f32),
+        shape((1, width), f32),
+        shape((1, width), f32),
+    ]
+    return pl.pallas_call(
+        functools.partial(attention_forward_kernel, gain_at, width_rows),
+        out_shape=out_shape,
+        in_specs=[vmem] * 8,
+        out_specs=[vmem] * len(out_shape),
+        scratch_shapes=[pltpu.VMEM((blocks, 256), f32)],
+        cost_estimate=busy(20),
+        compiler_params=pltpu.CompilerParams(vmem_limit_bytes=60 * 2**20),
+    )(row_padded, hidden, packed, cos_full, sin_full, segment_column, segment_row, placing)
+
+
+def attention_backward_kernel(
+    gain_at, width_rows, planes, grad_ref, incoming_ref, middle_ref, raw_ref, mix_ref, probs_ref, query_ref, key_ref,
+    value_ref, query_raw_ref, key_raw_ref, row_ref, qkv_ref, output_ref, cos_ref, sin_ref, input_scale,
+    query_scale, key_scale, attnout_scale, ffnin_scale, ffnout_grad, by_device, by_member,
+    input_grad_ref, blocks_ref, key_value, query_grad, low_ref, leaving, arriving, send_sem, recv_sem,
+):
+    bf16, f32 = jnp.bfloat16, jnp.float32
+    members = blocks_ref.shape[0]
+    blocks = members * planes
+    padded = qkv_ref.shape[0] // blocks
+    mix_rows = blocks_ref.shape[2] - padded
+    local_rows, width = incoming_ref.shape
+    head = key_ref.shape[1]
+    heads = query_ref.shape[1] // head
+    half = head // 2
+    seq = lax.axis_index("seq")
+    mine = pl.ds(pl.multiple_of(seq * local_rows, local_rows), local_rows)
+    theirs = pl.ds(pl.multiple_of((1 - seq) * local_rows, local_rows), local_rows)
+    partner = plane_places()[2]
+    greet((partner,))
+
+    ffn_in_grad = take_back(grad_ref[...], by_device[...])
+    middle = middle_ref[...]
+    inverse = inverse_of(middle, width)
+    normed = middle * inverse
+    ffnin_grad = jnp.sum(ffn_in_grad * normed, axis=0, keepdims=True)
+    middle_grad = incoming_ref[...].astype(f32) + back_of(
+        ffn_in_grad * ffnin_scale[...], normed, inverse, width
+    )
+    input_grad_ref[...] = middle_grad
+    raw = raw_ref[...]
+    inverse = inverse_of(raw, width)
+    normed = raw * inverse
+    attnout_grad = jnp.sum(middle_grad * normed, axis=0, keepdims=True)
+    raw_grad = back_of(middle_grad * attnout_scale[...], normed, inverse, width).astype(bf16)
+    mix_grad = contract_cols(raw_grad, output_ref[...]).astype(bf16)
+    for h in range(heads):
+        at = h * head
+        grad = mix_grad[:, at : at + head]
+        probs = probs_ref[h]
+        prob_grad = contract_cols(grad, value_ref[...])
+        delta = jnp.sum(prob_grad * probs, axis=-1, keepdims=True)
+        score_grad = (probs * (prob_grad - delta)).astype(bf16)
+        to_keys = contract_rows(score_grad, query_ref[:, at : at + head])
+        to_values = contract_rows(probs.astype(bf16), grad)
+        if h == 0:
+            key_value[:, :head], key_value[:, head:] = to_keys, to_values
+        else:
+            key_value[:, :head] += to_keys
+            key_value[:, head:] += to_values
+        query_grad[:, at : at + head] = matmul(score_grad, key_ref[...])
+    leaving[...] = key_value[theirs, :].astype(bf16)
+    copy = sender(send_sem, recv_sem)(0, leaving, arriving, partner)
+
+    output_grad = contract_rows(mix_ref[...], raw_grad).astype(bf16)
+    cos_table, sin_table = cos_ref[mine, :], sin_ref[mine, :]
+
+    def head_back(grad, raw, scale_ref):
+        turned = jnp.concatenate(turn(grad, cos_table, -sin_table), axis=1)
+        inverse = inverse_of(raw, head)
+        normed = raw * inverse
+        gain = jnp.sum(turned * normed, axis=0, keepdims=True)
+        return back_of(turned * scale_ref[...], normed, inverse, head).astype(bf16), gain
+
+    query_gain = jnp.zeros((1, head), f32)
+    for h in range(heads):
+        at = h * head
+        low, gain = head_back(
+            query_grad[:, at : at + head] * head ** (-0.5),
+            query_raw_ref[:, at : at + head],
+            query_scale,
+        )
+        low_ref[:, at : at + head] = low
+        query_gain = query_gain + gain
+    copy.wait_recv()
+    total = key_value[mine, :] + arriving[...].astype(f32)
+    low, key_gain = head_back(total[:, :head], key_raw_ref[...], key_scale)
+    low_ref[:, heads * head : (heads + 1) * head] = low
+    low_ref[:, (heads + 1) * head :] = total[:, head:].astype(bf16)
+
+    row = row_ref[mine, :].astype(f32)
+    inverse = inverse_of(row, width)
+    normed = row * inverse
+    normed_grad = contract_cols(low_ref[...], qkv_ref[...])
+    input_gain = jnp.sum(normed_grad * normed, axis=0, keepdims=True)
+    input_grad_ref[...] += take_back(
+        back_of(normed_grad * input_scale[...], normed, inverse, width), by_member[...]
+    )
+    (at, count), *others = gain_at
+    gains = collect_gain(input_gain, blocks, planes, at, count, padded, True)
+    vectors = (query_gain, key_gain, attnout_grad, ffnin_grad, ffnout_grad[...])
+    for vector, (at, count) in zip(vectors, others):
+        gains = gains + collect_gain(vector, blocks, planes, at, count, count, False)
+    normed = (normed * input_scale[...]).astype(bf16)
+    weights = contract_rows(normed, low_ref[...])
+    row_of = lax.broadcasted_iota(jnp.int32, (padded, 256), 0)
+    columns = blocks_ref.shape[3]
+    for i in range(blocks):
+        member, plane = i // planes, i % planes
+        piece = weights[padded * i : padded * (i + 1)]
+        first = jnp.where(row_of == width_rows, gains[i : i + 1], piece[:, :256])
+        blocks_ref[member, plane, :padded, :256] = first.astype(bf16)
+        blocks_ref[member, plane, :padded, 256:] = piece[:, 256:].astype(bf16)
+        natural = mix_rows * (plane * members + member)
+        blocks_ref[member, plane, padded:, :width] = output_grad[natural : natural + mix_rows]
+        blocks_ref[member, plane, padded:, width:] = jnp.zeros((mix_rows, columns - width), bf16)
+    copy.wait_send()
+
+
+def attention_backward(arrays, gain_at, width_rows, planes, mix_rows, collective_id):
+    bf16, f32 = jnp.bfloat16, jnp.float32
+    grad, incoming, query, key, qkv = arrays[0], arrays[1], arrays[6], arrays[7], arrays[12]
+    local_rows, width = incoming.shape
+    members = 8
+    padded = qkv.shape[0] // (members * planes)
+    pair = pltpu.VMEM((local_rows, 2 * key.shape[1]), bf16)
+    shape = jax.ShapeDtypeStruct
+    vmem = pl.BlockSpec(memory_space=pltpu.VMEM)
+    return pl.pallas_call(
+        functools.partial(attention_backward_kernel, gain_at, width_rows, planes),
+        out_shape=[
+            shape((local_rows, width), f32),
+            shape((members, planes, padded + mix_rows, qkv.shape[1]), bf16),
+        ],
+        in_specs=[vmem] * len(arrays),
+        out_specs=[vmem] * 2,
+        scratch_shapes=[
+            pltpu.VMEM((key.shape[0], 2 * key.shape[1]), f32),
+            pltpu.VMEM(query.shape, f32),
+            pltpu.VMEM((local_rows, qkv.shape[1]), bf16),
+            pair,
+            pair,
+            pltpu.SemaphoreType.DMA((1,)),
+            pltpu.SemaphoreType.DMA((1,)),
+        ],
+        cost_estimate=busy(30),
+        compiler_params=pltpu.CompilerParams(
+            collective_id=collective_id, has_side_effects=True, vmem_limit_bytes=60 * 2**20
+        ),
+    )(*arrays)
 
 
 def body(
@@ -653,7 +954,6 @@
     devices = lax.axis_size(ALL)
     members = lax.axis_size(PLANE)
     planes = lax.axis_size("z")
-    seq_count = lax.axis_size("seq")
     width_rows = query_weight.shape[0]
     hidden_rows = down_weight.shape[0]
     head_width = key_weight.shape[1]
@@ -695,33 +995,15 @@
     packed_all = plane_gather(packed_all, 6)
     gate_up_full = exchange(gate_up, ALL).reshape(devices * padded, 2 * unit_pad)
     down_full = lax.all_gather(down_local, "z", axis=0, tiled=True)
-    qkv_full = packed_all[:, :, :padded].reshape(devices * padded, qkv_width)
-    output_full = packed_all[:, :, padded:, : output_weight.shape[1]].transpose(1, 0, 2, 3)
-    output_full = output_full.reshape(devices * mix_rows, output_weight.shape[1])
-    gain_rows = packed_all[:, :, width_rows, :].astype(f32)
-    scales, at = [], 0
-    for count in gain_widths:
-        scales.append(gain_rows[:, :, at : at + count].transpose(1, 0, 2).reshape(-1))
-        at += count
-    padded_input_scale = jnp.pad(
-        gain_rows[:, :, :width_rows], ((0, 0), (0, 0), (0, padded - width_rows))
-    ).reshape(-1)
-    _, query_scale, key_scale, attnout_scale, ffnin_scale, ffnout_scale = scales
-
-    hidden = tokens[0].astype(f32)
     incoming = cotangent[0].astype(f32)
-    local_rows = hidden.shape[0]
-    full_length = local_rows * seq_count
+    local_rows = tokens.shape[1]
     offset = lax.axis_index("seq") * local_rows
     segment_row = segment_ids[0]
 
     def mine(rows):
         return lax.dynamic_slice_in_dim(rows, offset, local_rows)
 
-    my_segments = mine(segment_row)
     cos_full, sin_full = rope_tables(doc_positions(segment_row), head_width)
-    cos_table, sin_table = mine(cos_full), mine(sin_full)
-    scale = head_width ** (-0.5)
 
     other_half = [(0, 1), (1, 0)]
     first = lax.axis_index("seq") == 0
@@ -732,54 +1014,42 @@
             jnp.where(first, other_tokens, tokens[0]),
         ]
     )
-    row_hidden = matmul(row_tokens, by_member)
-    row_inverse = lax.rsqrt(jnp.sum(row_hidden * row_hidden, axis=-1, keepdims=True) / width + epsilon)
-    row_norm = row_hidden * row_inverse
-    row_normed = (row_norm * padded_input_scale).astype(bf16)
-    key_value_raw = matmul(row_normed, qkv_full[:, query_width:])
-    row_key_raw = key_value_raw[:, :head_width]
-    value_rows = key_value_raw[:, head_width:].astype(bf16)
-    key_rows = rotate(
-        row_key_raw * inverse_rms(row_key_raw) * key_scale, cos_full, sin_full
-    ).astype(bf16)
-
-    inv_input = mine(row_inverse)
-    norm_input = mine(row_norm)
-    normed = mine(row_normed)
-    query_raw = matmul(normed, qkv_full[:, :query_width]).reshape(
-        local_rows, head_count, head_width
-    )
-    inv_query = inverse_rms(query_raw)
-    norm_query = query_raw * inv_query
-    queries = (
-        rotate(norm_query * query_scale, cos_table[:, None, :], sin_table[:, None, :]) * scale
-    ).astype(bf16)
-    key_raw = mine(row_key_raw)
-    inv_key = inverse_rms(key_raw)
-    norm_key = key_raw * inv_key
-
-    query_places = offset + jnp.arange(local_rows, dtype=jnp.int32)
-    key_places = jnp.arange(full_length, dtype=jnp.int32)
-    allowed = (my_segments[:, None] == segment_row[None, :]) & (
-        query_places[:, None] >= key_places[None, :]
-    )
-    raw_scores = jnp.einsum("qhd,kd->hqk", queries, key_rows, preferred_element_type=f32)
-    scores = jnp.where(allowed[None], raw_scores, masked_score)
-    peak = jnp.max(scores, axis=-1, keepdims=True)
-    log_total = peak + jnp.log(jnp.sum(jnp.exp(scores - peak), axis=-1, keepdims=True))
-    probs = jnp.exp(scores - log_total)
-    probs_low = probs.astype(bf16)
-    attn_mix = jnp.einsum("hqk,kd->qhd", probs_low, value_rows, preferred_element_type=f32)
-    attn_flat = attn_mix.astype(bf16).reshape(local_rows, query_width)
-    attn_raw = matmul(attn_flat, output_full)
-    inv_attn = inverse_rms(attn_raw)
-    norm_attn = attn_raw * inv_attn
-    middle = hidden + norm_attn * attnout_scale
-    inv_middle = inverse_rms(middle)
-    norm_middle = middle * inv_middle
-    ffn_in = (norm_middle * ffnin_scale).astype(bf16)
-
-    plane_in = gather_rows(matmul(ffn_in, by_device).astype(bf16), 1)
+    row_padded = matmul(row_tokens, by_member).astype(bf16)
+    gain_at, at = [], 0
+    for count in gain_widths:
+        gain_at.append((at, count))
+        at += count
+    (
+        ffn_in_placed,
+        middle,
+        attn_raw,
+        attn_flat,
+        probs,
+        queries,
+        key_rows,
+        value_rows,
+        query_raw,
+        key_raw,
+        qkv_full,
+        output_full,
+        *scales,
+    ) = attention_forward(
+        row_padded,
+        tokens[0],
+        packed_all,
+        cos_full,
+        sin_full,
+        mine(segment_row)[:, None],
+        segment_row[None],
+        by_device,
+        gain_at,
+        width_rows,
+        padded,
+        head_width,
+    )
+    ffnout_scale = scales.pop()
+
+    plane_in = gather_rows(ffn_in_placed, 1)
     ffn_part, activated_low, to_gate, to_up = ffn_forward(plane_in, gate_up_full, down_full)
     ffn_raw = plane_scatter_sum(ffn_part, 2)
     inv_ffn = inverse_rms(ffn_raw)
@@ -788,84 +1058,44 @@
     ffnout_gain_grad = jnp.sum(incoming * norm_ffn, axis=0)
     ffn_raw_grad = rms_back(incoming * ffnout_scale, norm_ffn, inv_ffn).astype(bf16)
 
-    plane_grad, gate_up_low, ffn_in_part = gather_backward(
-        ffn_raw_grad, down_full, gate_up_full, to_gate, to_up, 3
-    )
-    ffn_in_grad, gate_up_blocks, down_blocks = sum_gradients(
-        ffn_in_part, plane_in, gate_up_low, activated_low, plane_grad, 4
-    )
-    ffn_in_grad = take_back(ffn_in_grad, by_device)
-    down_low = down_blocks[:unit_count].reshape(planes, hidden_rows, down_weight.shape[1])
-    plane = lax.axis_index("z")
-    down_wgrad = lax.dynamic_index_in_dim(down_low, plane, 0, keepdims=False).astype(f32)
-    for k in range(1, planes):
-        leaving = lax.dynamic_index_in_dim(down_low, lax.rem(plane + k, planes), 0, keepdims=False)
-        shift = [(i, (i + k) % planes) for i in range(planes)]
-        down_wgrad = down_wgrad + lax.ppermute(leaving, "z", shift).astype(f32)
-
+    gate_up_low, ffn_in_part, down_blocks = gather_backward(
+        ffn_raw_grad, down_full, gate_up_full, to_gate, to_up, activated_low, 3
+    )
+    down_blocks = down_blocks.reshape(planes, hidden_rows, down_weight.shape[1])
+    ffn_in_grad, gate_up_blocks, down_wgrad = sum_gradients(
+        ffn_in_part, down_blocks, plane_in, gate_up_low, 4
+    )
     gate_up_terms = exchange(gate_up_blocks.reshape(devices, padded, 2 * unit_pad), ALL)
-    ffnin_gain_grad = jnp.sum(ffn_in_grad * norm_middle, axis=0)
-    middle_grad = incoming + rms_back(ffn_in_grad * ffnin_scale, norm_middle, inv_middle)
-    attnout_gain_grad = jnp.sum(middle_grad * norm_attn, axis=0)
-    attn_raw_grad = rms_back(middle_grad * attnout_scale, norm_attn, inv_attn).astype(bf16)
-    output_wgrad = contract_rows(attn_flat, attn_raw_grad)
-    mix_grad = (
-        contract_cols(attn_raw_grad, output_full)
-        .astype(bf16)
-        .reshape(local_rows, head_count, head_width)
-    )
-    prob_grad = jnp.einsum("qhd,kd->hqk", mix_grad, value_rows, preferred_element_type=f32)
-    row_delta = jnp.sum(prob_grad * probs, axis=-1, keepdims=True)
-    score_grad = (probs * (prob_grad - row_delta)).astype(bf16)
-    value_grad_rows = jnp.einsum("hqk,qhd->kd", probs_low, mix_grad, preferred_element_type=f32)
-    key_grad_rows = jnp.einsum("hqk,qhd->kd", score_grad, queries, preferred_element_type=f32)
-    query_grad = jnp.einsum("hqk,kd->qhd", score_grad, key_rows, preferred_element_type=f32)
-    key_value_rows = jnp.concatenate([key_grad_rows, value_grad_rows], axis=1)
-    theirs = lax.dynamic_slice_in_dim(key_value_rows, local_rows - offset, local_rows)
-    key_value_grad = mine(key_value_rows) + lax.ppermute(
-        theirs.astype(bf16), "seq", other_half
-    ).astype(f32)
-    key_grad, value_grad = key_value_grad[:, :head_width], key_value_grad[:, head_width:]
-    query_norm_grad = rotate(query_grad * scale, cos_table[:, None, :], -sin_table[:, None, :])
-    query_gain_grad = jnp.sum(query_norm_grad * norm_query, axis=(0, 1))
-    query_raw_low = (
-        rms_back(query_norm_grad * query_scale, norm_query, inv_query)
-        .astype(bf16)
-        .reshape(local_rows, query_width)
-    )
-    key_norm_grad = rotate(key_grad, cos_table, -sin_table)
-    key_gain_grad = jnp.sum(key_norm_grad * norm_key, axis=0)
-    key_raw_low = rms_back(key_norm_grad * key_scale, norm_key, inv_key).astype(bf16)
-    qkv_raw_low = jnp.concatenate([query_raw_low, key_raw_low, value_grad.astype(bf16)], axis=1)
-    qkv_wgrad = contract_rows(normed, qkv_raw_low)
-    normed_grad = contract_cols(qkv_raw_low, qkv_full)
-    input_gain_grad = jnp.sum(normed_grad * norm_input, axis=0)
-    scaled_grad = normed_grad * padded_input_scale
-    inner = jnp.sum(scaled_grad * norm_input, axis=-1, keepdims=True) / width
-    input_grad = middle_grad + take_back(inv_input * (scaled_grad - norm_input * inner), by_member)
-
-    gain_grads = (
-        query_gain_grad,
-        key_gain_grad,
-        attnout_gain_grad,
-        ffnin_gain_grad,
-        ffnout_gain_grad,
-    )
-    gain_rows = jnp.concatenate(
-        [input_gain_grad.reshape(members, planes, padded)[:, :, :width_rows]]
-        + [g.reshape(planes, members, -1).transpose(1, 0, 2) for g in gain_grads],
-        axis=2,
-    )
-    gain_rows = jnp.pad(gain_rows, ((0, 0), (0, 0), (0, qkv_width - gain_rows.shape[2])))
-    blocks = qkv_wgrad.reshape(members, planes, padded, qkv_width)
-    row = lax.broadcasted_iota(jnp.int32, blocks.shape, 2)
-    blocks = jnp.where(row == width_rows, gain_rows[:, :, None], blocks).astype(bf16)
-    output_blocks = output_wgrad.astype(bf16).reshape(planes, members, mix_rows, -1)
-    output_blocks = jnp.pad(
-        output_blocks.transpose(1, 0, 2, 3),
-        ((0, 0), (0, 0), (0, 0), (0, qkv_width - output_blocks.shape[3])),
-    )
-    share = owner_sum(jnp.concatenate([blocks, output_blocks], axis=2), 5)
+    input_grad, blocks = attention_backward(
+        [
+            ffn_in_grad,
+            cotangent[0],
+            middle,
+            attn_raw,
+            attn_flat,
+            probs,
+            queries,
+            key_rows,
+            value_rows,
+            query_raw,
+            key_raw,
+            row_padded,
+            qkv_full,
+            output_full,
+            cos_full,
+            sin_full,
+            *scales,
+            ffnout_gain_grad[None],
+            by_device,
+            by_member,
+        ],
+        gain_at,
+        width_rows,
+        planes,
+        mix_rows,
+        7,
+    )
+    share = owner_sum(blocks, 5)
     gate_up_sum = jnp.sum(
         gate_up_terms.reshape(planes, members, padded, 2 * unit_pad).astype(f32), axis=0
     )

time: 545 us -> 511 us (0.938)
  Pallas kernels: 353 us -> 421 us
  local copies, waits for them, and re-layouts: 70 us -> 38.9 us
  matrix products: 32.2 us -> 3.8 us
  other arithmetic: 38.8 us -> 15.6 us
  starting transfers between devices: 21 us -> 12.2 us
  waiting for transfers between devices: 8.05 us -> 0.04 us
    pallas_call x0 -> x2, Pallas kernels: none -> 55.4 us  [the longest x1 40.6 us: attention_backward(): pl.pallas_call(functools.partial(attention_backward_kernel, gain_at, widt...]
    dot_general x12 -> x0, matrix products: 22 us -> none  [the longest x4 11.3 us: contract_cols(): lax.dot_general(left, right, (((1,), (1,)), ((), ())), preferred_element_...]
    pallas_call x1, Pallas kernels: 38.2 us -> 56.6 us  [sum_gradients(): pl.pallas_call(sum_gradients_kernel, out_shape=[jax.ShapeDtypeStruct((pie...]
    pallas_call x1, Pallas kernels: 100 us -> 82.8 us  [owner_sum(): pl.pallas_call(functools.partial(owner_sum_kernel, planes), out_shape=jax...]
    pallas_call x2, Pallas kernels: 95.7 us -> 106 us  [plane_gather(): pl.pallas_call(gather_kernel, out_shape=jax.ShapeDtypeStruct((members, *l...]
    ppermute x4 -> x0, starting transfers between devices: 9.07 us -> none  [the longest x3 7.57 us: body(): down_wgrad = down_wgrad + lax.ppermute(leaving, 'z', shift).astype(f32)]
    ppermute x4 -> x0, waiting for transfers between devices: 7.53 us -> none  [the longest x1 7.53 us: body(): lax.ppermute(theirs.astype(bf16), 'seq', other_half).astype(f32)]
    reshape x15 -> x0, local copies, waits for them, and re-layouts: 7.38 us -> none  [the longest x2 3.06 us: body(): matmul(normed, qkv_full[:, :query_width])]
  transfers between devices with their start and end apart: 8 -> 4, of which waited for: 1 -> 0; matrix products, arithmetic and copies ran while one was open for 20% -> 3% of each run, Pallas kernels for 40% -> 48%
where the time goes in v7:
time: 511 us; the launch traced here: 506 us
  Pallas kernels  421 us (82%)
  local copies, waits for them, and re-layouts  38.9 us (8%)
  other arithmetic  15.6 us (3%)
  between operations  14.7 us (3%)
  starting transfers between devices  12.2 us (2%)
    pallas_call x2, Pallas kernels, plane_gather(): pl.pallas_call(gather_kernel, out_shape=jax.ShapeDtypeStruct((members, *l...  106 us
    pallas_call x1, Pallas kernels, owner_sum(): pl.pallas_call(functools.partial(owner_sum_kernel, planes), out_shape=jax...  82.8 us
    pallas_call x1, Pallas kernels, sum_gradients(): pl.pallas_call(sum_gradients_kernel, out_shape=[jax.ShapeDtypeStruct((pie...  56.6 us
    pallas_call x1, Pallas kernels, gather_backward(): pl.pallas_call(gather_backward_kernel, out_shape=[jax.ShapeDtypeStruct((m...  42.8 us
    pallas_call x1, Pallas kernels, attention_backward(): pl.pallas_call(functools.partial(attention_backward_kernel, gain_at, widt...  40.6 us
    pallas_call x1, Pallas kernels, ffn_forward(): pl.pallas_call(ffn_forward_kernel, grid=(rows // ROW_BLOCK,), in_specs=[r...  29.3 us
    pallas_call x1, Pallas kernels, plane_scatter_sum(): pl.pallas_call(plane_sum_kernel, out_shape=jax.ShapeDtypeStruct(shape, jn...  24.6 us
    pallas_call x1, Pallas kernels, z_gather(): pl.pallas_call(functools.partial(z_gather_kernel, planes), out_shape=jax....  22.8 us
  transfers between devices with their start and end apart: 4, of which 0 were waited for; matrix products, arithmetic and copies ran while one was open for 3% of the time, Pallas kernels for 48%

profile of v7, /device:TPU:8, one launch (start us, length us, event | category | flops | bytes accessed | tf_op | source)
XLA Modules:
  0.0 506.1 jit_solution(1433424213295403706)
XLA Ops:
  7.2 4.2 concatenate.21
  11.4 2.9 reshape.148
  15.0 1.7 reshape.150
  18.4 22.8 %shard_map.271.own_ref = bf16[4,72,1536]{2,1,0:T(8,128)(2,1)S(1)} custom-call(bf16[72,1536]{1,0:T(8,128)(2,1)S(1)} %fusion.27.own_ref), custom_call_target="tpu_custom_call" | custom-call | bytes 60000000 | tf_op jit(solution)/shard_map/pallas_call | solution.py:219
  41.2 2.5 broadcast_in_dim.12
  43.7 5.9 %all-to-all-start = ((bf16[32,40,1792]{2,1,0:T(8,128)(2,1)}), bf16[32,40,1792]{2,1,0:T(8,128)(2,1)}, u32[]{:S(2)}, u32[]{:S(2)}) async-start(bf16[32,40,1792]{2,1,0:T(8,128)(2,1)} %bitcast.66), calls=%async_computation | async-start | bytes 9175040 | tf_op jit(solution)/shard_map/all_to_all | solution.py:85
  49.9 1.5 collective-permute-start
  51.5 5.4 %fusion.38 = (bf16[1152,1280]{1,0:T(8,128)(2,1)}, bf16[1152,1280]{1,0:T(8,128)(2,1)}) fusion(s32[1152]{0:T(1024)S(1)} %get-tuple-element.101, s32[1152]{0:T(1024)S(1)} %get-tuple-element.102, pred[1152]{0:T(1024)(128)(4,1)S(1)} %get-tuple-element.104, s32[1152]{0:T(1024)S(1)} %get-tuple-element.100, s32[1152]{0:T(1024)S(1)} %get-tuple-element.103, ...), kind=kLoop, calls=%fused_computation.83 | loop fusion | flops 45711360 | bytes 5918976 | tf_op jit(solution)/shard_map/convert_element_type | solution.py:67
  57.7 65.6 %shard_map.272.packed_ref = bf16[8,4,72,1536]{3,2,1,0:T(8,128)(2,1)} custom-call(bf16[4,72,1536]{2,1,0:T(8,128)(2,1)S(1)} %shard_map.271.own_ref), custom_call_target="tpu_custom_call" | custom-call | bytes 75000000 | tf_op jit(solution)/shard_map/pallas_call | solution.py:238
  123.6 1.8 multiply_sine_fusion
  125.5 3.8 convolution_convert_fusion.row_ref
  129.3 14.8 %shard_map.273 = (bf16[256,1280]{1,0:T(8,128)(2,1)}, f32[256,1152]{1,0:T(8,128)}, f32[256,1152]{1,0:T(8,128)}, bf16[256,1024]{1,0:T(8,128)(2,1)}, f32[4,256,512]...) custom-call(bf16[512,1280]{1,0:T(8,128)(2,1)} %convolution_convert_f, ...), custom_call_target="tpu_custom_call" | custom-call | bytes 60000000 | tf_op jit(solution)/shard_map/pallas_call | solution.py:782
  144.1 1.1 copy-done.6
  145.2 40.9 %shard_map.274 = bf16[8,16,16,1280]{3,2,1,0:T(8,128)(2,1)S(1)} custom-call(bf16[16,16,1280]{2,1,0:T(8,128)(2,1)S(1)} %bitcast.65), custom_call_target="tpu_custom_call" | custom-call | bytes 75000000 | tf_op jit(solution)/shard_map/pallas_call | solution.py:238
  186.1 2.4 copy-done
  188.6 1.5 copy-done.1
  190.1 29.3 %shard_map.275 = (bf16[2048,1152]{1,0:T(8,128)(2,1)}, bf16[2048,896]{1,0:T(8,128)(2,1)S(1)}, f32[2048,896]{1,0:T(8,128)}, f32[2048,896]{1,0:T(8,128)}) custom-call(bf16[2048,1280]{1,0:T(8,128)(2,1)} %bitcast.61, bf16[1280,1792]{1,0:T(8,128)(2,1)} %bitcast.8.gate_up_ref, bf16[864,1152]{1,0:T(8,128)(2,1)S(1)} %copy-done.1), custom_call_target="tpu_custom_call" | custom-call | bytes 60000000 | tf_op jit(solution)/shard_map/pallas_call | solution.py:406
  219.4 1.8 copy-done.4
  221.2 2.3 copy-done.3
  223.5 24.6 %shard_map.276 = f32[16,16,1152]{2,1,0:T(8,128)S(1)} custom-call(bf16[8,16,16,1152]{3,2,1,0:T(8,128)(2,1)S(1)} %bitcast.63), custom_call_target="tpu_custom_call" | custom-call | bytes 75000000 | tf_op jit(solution)/shard_map/pallas_call | solution.py:336
  248.4 3.0 fusion.14
  251.5 1.4 fusion.20.own_ref
  252.9 42.8 %shard_map.277 = (bf16[8,16,16,1152]{3,2,1,0:T(8,128)(2,1)}, bf16[2048,1792]{1,0:T(8,128)(2,1)}, bf16[8,16,16,1280]{3,2,1,0:T(8,128)(2,1)}, bf16[864,1152]{1,0:T(8,128)(2,1)S(1)}) custom-call(bf16[16,16,1152]{2,1,0:T(8,128)(2,1)S(1)} %fusion.20.own_ref, bf16[864,1152]{1,0:T(8,128)(2,1)S(1)} %copy-done.2, bf16[1280,1792]{1,0:T(8,128)(2,1)} %bitcast.8.gate_up_ref, ...), custom_call_target="tpu_custom_call" | custom-call | bytes 105000000 | tf_op jit(solution)/shard_map/pallas_call | solution.py:483
  295.7 1.3 copy-done.5
  297.0 56.6 %shard_map.278 = (f32[16,16,1280]{2,1,0:T(8,128)}, bf16[1280,1792]{1,0:T(8,128)(2,1)}, f32[216,1152]{1,0:T(8,128)}) custom-call(bf16[8,16,16,1280]{3,2,1,0:T(8,128)(2,1)} %get-tuple-element.58.part_ref, bf16[4,216,1152]{2,1,0:T(8,128)(2,1)} %bitcast.64, bf16[2048,1280]{1,0:T(8,128)(2,1)} %bitcast.62, bf16[2048,1792]{1,0:T(8,128)(2,1)} %get-tuple-element.60.both_hbm), custom_call_target="tpu_custom_call" | custom-call | bytes 105000000 | tf_op jit(solution)/shard_map/pallas_call | solution.py:563
  353.5 4.5 all-to-all-start.1
  358.6 40.6 %shard_map.279 = (f32[256,1152]{1,0:T(8,128)}, bf16[8,4,72,1536]{3,2,1,0:T(8,128)(2,1)}) custom-call(f32[256,1280]{1,0:T(8,128)} %bitcast.76, bf16[256,1152]{1,0:T(8,128)(2,1)} %bitcast.68, f32[256,1152]{1,0:T(8,128)} %get-tuple-element.49.middle_ref, f32[256,1152]{1,0:T(8,128)} %get-tuple-element.62.raw_ref, bf16[256,1024]{1,0:T(8,128)(2,1)} %get-tuple-element.63.mix_ref, ...), custom_call_target="tpu_custom_call" | custom-call | bytes 90000000 | tf_op jit(solution)/shard_map/pallas_call | solution.py:911
  399.3 82.8 %shard_map.280 = f32[72,1536]{1,0:T(8,128)S(1)} custom-call(bf16[8,4,72,1536]{3,2,1,0:T(8,128)(2,1)} %get-tuple-element.78.part_ref), custom_call_target="tpu_custom_call" | custom-call | bytes 105000000 | tf_op jit(solution)/shard_map/pallas_call | solution.py:618
  485.3 3.2 convert_reduce_fusion
  490.3 1.8 reshape.164
  493.8 1.8 reshape.162
  495.6 2.4 copy.67
  (69 shorter events, 12.4 us)
Async XLA Ops:
  7.2 7.8 %copy-start.9 = (bf16[36,6912]{1,0:T(8,128)(2,1)S(1)}, bf16[36,6912]{1,0:T(8,128)(2,1)}, u32[]{:S(2)}) copy-start(bf16[36,6912]{1,0:T(8,128)(2,1)} %param.24) | copy-start | bytes 1492996
  17.0 0.9 copy-start.10
  17.0 0.9 copy-start.13
  17.0 0.9 copy-start.14
  17.5 0.9 copy-start.11
  43.7 6.2 %copy-start.7 = (bf16[1,256,1152]{2,1,0:T(8,128)(2,1)S(1)}, bf16[1,256,1152]{2,1,0:T(8,128)(2,1)}, u32[]{:S(2)}) copy-start(bf16[1,256,1152]{2,1,0:T(8,128)(2,1)} %param.16) | copy-start | bytes 1769476
  43.7 144.9 %all-to-all-start = ((bf16[32,40,1792]{2,1,0:T(8,128)(2,1)}), bf16[32,40,1792]{2,1,0:T(8,128)(2,1)}, u32[]{:S(2)}, u32[]{:S(2)}) async-start(bf16[32,40,1792]{2,1,0:T(8,128)(2,1)} %bitcast.66), calls=%async_computation | async-start | bytes 9175040 | tf_op jit(solution)/shard_map/all_to_all | solution.py:85
  49.6 138.9 %all-gather.2.cloned.1.call-start = ((), (), s32[]{:S(2)}) async-start(), calls=%async_computation.2 | async-start | bytes 2488320 | tf_op jit(solution)/shard_map/all_gather | solution.py:997
  49.9 75.6 %collective-permute-start = (bf16[256,1152]{1,0:T(8,128)(2,1)S(1)}, bf16[256,1152]{1,0:T(8,128)(2,1)S(1)}, u32[]{:S(2)}, u32[]{:S(2)}) collective-permute-start(bf16[256,1152]{1,0:T(8,128)(2,1)S(1)} %bitcast.75), channel_id=1, source_target_pairs={{0,1},{1,0},{2,3},{3,2},{4,5},{5,4},{6,7},{7,6},{8,9},{9,8},{10,11... | collective-permute-start | bytes 1769480 | tf_op jit(solution)/shard_map/ppermute | solution.py:1010
  51.5 5.4 %copy-start.12 = (s32[1,512]{1,0:T(1,128)S(1)}, s32[1,512]{1,0:T(1,128)}, u32[]{:S(2)}) copy-start(s32[1,512]{1,0:T(1,128)} %segment_row.1) | copy-start | bytes 6148
  144.1 1.1 copy-start.6
  145.2 43.3 %copy-start.15 = (f32[1,1152]{1,0:T(1,128)S(1)}, f32[1,1152]{1,0:T(1,128)}, u32[]{:S(2)}) copy-start(f32[1,1152]{1,0:T(1,128)} %get-tuple-element.54) | copy-start | bytes 13828
  186.1 2.4 copy-start
  188.6 1.6 copy-start.1
  219.4 1.8 copy-start.4
  221.2 2.3 copy-start.3
  248.4 4.5 copy-start.2
  295.7 1.3 copy-start.5
  353.5 131.7 %all-to-all-start.1 = ((bf16[32,40,1792]{2,1,0:T(8,128)(2,1)}), bf16[32,40,1792]{2,1,0:T(8,128)(2,1)}, u32[]{:S(2)}, u32[]{:S(2)}) async-start(bf16[32,40,1792]{2,1,0:T(8,128)(2,1)} %bitcast.71), calls=%async_computation.1 | async-start | bytes 9175040 | tf_op jit(solution)/shard_map/all_to_all | solution.py:85
  493.8 4.2 copy-start.8
Sparse Core Ops, SparseCore 0:
  52.0 90.7 all-gather.1

commit v8 on v7

--- a/solution.py
+++ b/solution.py
@@ -51,7 +51,9 @@
     )
 
 
-ALL = ("z", "x", "core", "seq")
+ALL = ("far", "z", "x", "core", "seq")
+PLANES = ("far", "z")
+CUBE = ("z", "x", "core", "seq")
 
 
 def up_to(size, multiple):
@@ -89,19 +91,39 @@
     return pl.CostEstimate(flops=0, bytes_accessed=microseconds * 3_000_000, transcendentals=0)
 
 
+def shifted(flip_z, flip_x, flip_core, flip_y):
+    far, *inner = (lax.axis_index(name) for name in ALL)
+    flips = (flip_z, flip_x, flip_core, flip_y)
+    return (far, *(1 - at if flip else at for at, flip in zip(inner, flips)))
+
+
 def plane_places():
-    z, x, core, seq = (lax.axis_index(name) for name in ALL)
-    sibling = (z, x, 1 - core, seq)
-    along_x = (z, 1 - x, core, seq)
-    along_y = (z, x, core, 1 - seq)
-
-    def member(other_x, other_core, other_y):
-        at_x = 1 - x if other_x else x
-        at_core = 1 - core if other_core else core
-        at_y = 1 - seq if other_y else seq
-        return (at_x * 2 + at_core) * 2 + at_y
-
-    return sibling, along_x, along_y, member
+    def member(flip_x, flip_core, flip_y):
+        _, _, x, core, seq = shifted(0, flip_x, flip_core, flip_y)
+        return (x * 2 + core) * 2 + seq
+
+    return shifted(0, 0, 1, 0), shifted(0, 1, 0, 0), shifted(0, 0, 0, 1), member
+
+
+def cube_member(flip_z, flip_x, flip_y, flip_core):
+    _, z, x, core, seq = shifted(flip_z, flip_x, flip_core, flip_y)
+    return ((z * 2 + x) * 2 + core) * 2 + seq
+
+
+def cube_places():
+    return *plane_places()[:3], shifted(1, 0, 0, 0)
+
+
+def other_planes(planes):
+    far, z, x, core, seq = (lax.axis_index(name) for name in ALL)
+    plane = far * 2 + z
+    ring = [lax.rem(plane + k, planes) for k in range(1, planes)]
+    return plane, [(at // 2, lax.rem(at, 2), x, core, seq) for at in ring], ring
+
+
+def other_cubes(cubes):
+    far, z, x, core, seq = (lax.axis_index(name) for name in ALL)
+    return far, [(lax.rem(far + k, cubes), z, x, core, seq) for k in range(1, cubes)]
 
 
 def greet(places):
@@ -127,7 +149,7 @@
     return send
 
 
-def plane_spread(own_ref, out_ref, send_sems, recv_sems, local_sem, compute=lambda i: None):
+def plane_spread(own_ref, out_ref, send_sems, recv_sems, local_sem):
     sibling, along_x, along_y, member = plane_places()
     half = own_ref.shape[0] // 2
     top, bottom = pl.ds(0, half), pl.ds(half, half)
@@ -145,30 +167,22 @@
     own_x_bottom = send(2, own_ref.at[bottom], out_ref.at[me, bottom], along_x)
     own_y_top = send(4, own_ref.at[top], out_ref.at[me, top], along_y)
     x_block, y_block, diagonal = member(1, 0, 0), member(0, 0, 1), member(1, 0, 1)
-    compute(0)
     own_x_top.wait_recv()
     diagonal_top = forward(5, x_block, top, along_y)
     x_top = forward(7, x_block, top, sibling)
     own_y_bottom.wait_recv()
     diagonal_bottom = forward(6, y_block, bottom, along_x)
     y_bottom = forward(9, y_block, bottom, sibling)
-    own_sibling.wait_recv()
-    compute(1)
     own_x_bottom.wait_recv()
     x_bottom = forward(8, x_block, bottom, sibling)
     own_y_top.wait_recv()
     y_top = forward(10, y_block, top, sibling)
-    compute(2)
     diagonal_top.wait_recv()
     far_top = forward(11, diagonal, top, sibling)
     diagonal_bottom.wait_recv()
     far_bottom = forward(12, diagonal, bottom, sibling)
-    compute(3)
-    compute(4)
-    for i, copies in ((5, (x_top, x_bottom)), (6, (y_bottom, y_top)), (7, (far_top, far_bottom))):
-        for copy in copies:
-            copy.wait_recv()
-        compute(i)
+    for copy in (own_sibling, x_top, y_bottom, x_bottom, y_top, far_top, far_bottom):
+        copy.wait_recv()
     for copy in (
         own_x_top,
         own_y_bottom,
@@ -188,19 +202,103 @@
     keep.wait()
 
 
-def gather_kernel(own_ref, out_ref, *sems):
-    greet(plane_places()[:3])
-    plane_spread(own_ref, out_ref, *sems)
-
-
-def z_gather_kernel(planes, own_ref, out_ref, send_sems, recv_sems, own_sem):
-    z, x, core, seq = (lax.axis_index(name) for name in ALL)
-    others = [(lax.rem(z + k, planes), x, core, seq) for k in range(1, planes)]
-    greet(others)
-    keep = pltpu.make_async_copy(own_ref, out_ref.at[z], own_sem)
+def cube_spread(own_ref, out_ref, send_sems, recv_sems, local_sem, compute=lambda i: None):
+    sibling, along_x, along_y, along_z = cube_places()
+    half = own_ref.shape[0] // 2
+    top, bottom = pl.ds(0, half), pl.ds(half, half)
+    me = cube_member(0, 0, 0, 0)
+    keep = pltpu.make_async_copy(own_ref, out_ref.at[me], local_sem)
     keep.start()
     send = sender(send_sems, recv_sems)
-    copies = [send(k, own_ref, out_ref.at[z], place) for k, place in enumerate(others)]
+    x_block, y_block, diagonal = (cube_member(0, *at, 0) for at in ((1, 0), (0, 1), (1, 1)))
+    z_block, zx_block, zy_block, zd_block = (
+        cube_member(1, *at, 0) for at in ((0, 0), (1, 0), (0, 1), (1, 1))
+    )
+
+    def half_on(kind, block, rows, place):
+        return send(kind, out_ref.at[block, rows], out_ref.at[block, rows], place)
+
+    def on(kind, block, place):
+        return send(kind, out_ref.at[block], out_ref.at[block], place)
+
+    own_x_top = send(1, own_ref.at[top], out_ref.at[me, top], along_x)
+    own_y_bottom = send(3, own_ref.at[bottom], out_ref.at[me, bottom], along_y)
+    own_z = send(13, own_ref, out_ref.at[me], along_z)
+    own_sibling = send(0, own_ref, out_ref.at[me], sibling)
+    own_x_bottom = send(2, own_ref.at[bottom], out_ref.at[me, bottom], along_x)
+    own_y_top = send(4, own_ref.at[top], out_ref.at[me, top], along_y)
+    compute(0)
+    own_x_top.wait_recv()
+    diagonal_top = half_on(5, x_block, top, along_y)
+    x_top = half_on(7, x_block, top, sibling)
+    own_y_bottom.wait_recv()
+    diagonal_bottom = half_on(6, y_block, bottom, along_x)
+    y_bottom = half_on(9, y_block, bottom, sibling)
+    own_sibling.wait_recv()
+    compute(1)
+    own_z.wait_recv()
+    z_to_x = on(14, z_block, along_x)
+    z_to_y = on(15, z_block, along_y)
+    z_near = on(16, z_block, sibling)
+    own_x_bottom.wait_recv()
+    x_bottom = half_on(8, x_block, bottom, sibling)
+    own_y_top.wait_recv()
+    y_top = half_on(10, y_block, top, sibling)
+    compute(2)
+    diagonal_top.wait_recv()
+    far_top = half_on(11, diagonal, top, sibling)
+    diagonal_bottom.wait_recv()
+    far_bottom = half_on(12, diagonal, bottom, sibling)
+    diagonal_z = on(17, diagonal, along_z)
+    compute(3)
+    compute(4)
+    z_to_x.wait_recv()
+    zx_near = on(18, zx_block, sibling)
+    z_to_y.wait_recv()
+    zy_near = on(19, zy_block, sibling)
+    compute(5)
+    compute(6)
+    diagonal_z.wait_recv()
+    zd_near = on(20, zd_block, sibling)
+    compute(7)
+    compute(8)
+    last = (
+        (x_top, x_bottom), (y_bottom, y_top), (far_top, far_bottom), (z_near,), (zx_near,), (zy_near,), (zd_near,),
+    )
+    for i, copies in enumerate(last):
+        for copy in copies:
+            copy.wait_recv()
+        compute(9 + i)
+    for copy in (
+        own_x_top, own_y_bottom, own_z, own_sibling, own_x_bottom, own_y_top, diagonal_top, diagonal_bottom,
+        z_to_x, z_to_y, diagonal_z,
+    ):
+        copy.wait_send()
+    for copies in last:
+        for copy in copies:
+            copy.wait_send()
+    keep.wait()
+
+
+CUBE_ORDER = (
+    (0, 0, 0, 0), (0, 0, 0, 1), (0, 1, 0, 0), (0, 0, 1, 0), (1, 0, 0, 0), (0, 1, 1, 0), (1, 1, 0, 0), (1, 0, 1, 0),
+    (1, 1, 1, 0), (0, 1, 0, 1), (0, 0, 1, 1), (0, 1, 1, 1), (1, 0, 0, 1), (1, 1, 0, 1), (1, 0, 1, 1), (1, 1, 1, 1),
+)
+
+
+def cube_gather_kernel(own_ref, out_ref, *sems):
+    greet(cube_places())
+    cube_spread(own_ref, out_ref, *sems)
+
+
+def weights_gather_kernel(cubes, own_ref, down_ref, out_ref, down_out, far_send, far_recv, own_sem, *sems):
+    far, others = other_cubes(cubes)
+    greet((*plane_places()[:3], *others))
+    keep = pltpu.make_async_copy(down_ref, down_out.at[far], own_sem)
+    keep.start()
+    send = sender(far_send, far_recv)
+    copies = [send(k, down_ref, down_out.at[far], place) for k, place in enumerate(others)]
+    plane_spread(own_ref, out_ref, *sems)
     for copy in copies:
         copy.wait_recv()
     for copy in copies:
@@ -208,11 +306,26 @@
     keep.wait()
 
 
-GATHER_SEMS = [
-    pltpu.SemaphoreType.DMA((13,)),
-    pltpu.SemaphoreType.DMA((13,)),
-    pltpu.SemaphoreType.DMA,
-]
+def z_gather_kernel(planes, own_ref, out_ref, send_sems, recv_sems, own_sem):
+    plane, others, _ = other_planes(planes)
+    greet(others)
+    keep = pltpu.make_async_copy(own_ref, out_ref.at[plane], own_sem)
+    keep.start()
+    send = sender(send_sems, recv_sems)
+    copies = [send(k, own_ref, out_ref.at[plane], place) for k, place in enumerate(others)]
+    for copy in copies:
+        copy.wait_recv()
+    for copy in copies:
+        copy.wait_send()
+    keep.wait()
+
+
+def gather_sems(count):
+    return [
+        pltpu.SemaphoreType.DMA((count,)),
+        pltpu.SemaphoreType.DMA((count,)),
+        pltpu.SemaphoreType.DMA,
+    ]
 
 
 def z_gather(local, planes, collective_id):
@@ -233,24 +346,44 @@
     )(local)
 
 
-def plane_gather(local, collective_id):
+def weights_gather(local, down, cubes, collective_id):
     members = 8
+    anywhere = pl.BlockSpec(memory_space=pl.ANY)
     return pl.pallas_call(
-        gather_kernel,
-        out_shape=jax.ShapeDtypeStruct((members, *local.shape), local.dtype),
-        in_specs=[pl.BlockSpec(memory_space=pl.ANY)],
-        out_specs=pl.BlockSpec(memory_space=pl.ANY),
-        scratch_shapes=GATHER_SEMS,
-        cost_estimate=busy(25),
+        functools.partial(weights_gather_kernel, cubes),
+        out_shape=[
+            jax.ShapeDtypeStruct((members, *local.shape), local.dtype),
+            jax.ShapeDtypeStruct((cubes, *down.shape), down.dtype),
+        ],
+        in_specs=[anywhere, anywhere],
+        out_specs=[anywhere, anywhere],
+        scratch_shapes=[
+            pltpu.SemaphoreType.DMA((cubes - 1,)),
+            pltpu.SemaphoreType.DMA((cubes - 1,)),
+            pltpu.SemaphoreType.DMA,
+            *gather_sems(13),
+        ],
+        cost_estimate=busy(30),
         compiler_params=pltpu.CompilerParams(
             collective_id=collective_id, has_side_effects=True, vmem_limit_bytes=VMEM_BYTES
         ),
-    )(local)
+    )(local, down)
 
 
 def gather_rows(local, collective_id):
     rows, columns = local.shape
-    out = plane_gather(local.reshape(rows // 16, 16, columns), collective_id)
+    members = 16
+    out = pl.pallas_call(
+        cube_gather_kernel,
+        out_shape=jax.ShapeDtypeStruct((members, rows // 16, 16, columns), local.dtype),
+        in_specs=[pl.BlockSpec(memory_space=pl.ANY)],
+        out_specs=pl.BlockSpec(memory_space=pl.ANY),
+        scratch_shapes=gather_sems(21),
+        cost_estimate=busy(35),
+        compiler_params=pltpu.CompilerParams(
+            collective_id=collective_id, has_side_effects=True, vmem_limit_bytes=VMEM_BYTES
+        ),
+    )(local.reshape(rows // 16, 16, columns))
     return out.reshape(-1, columns)
 
 
@@ -265,10 +398,7 @@
     lax.fori_loop(start, start + count, one, 0)
 
 
-def plane_sum(
-    part_ref, own_sum, near, sums, from_x, from_y, far_x, far_y, send_sems, recv_sems,
-    work=lambda point: None,
-):
+def plane_sum(part_ref, own_sum, near, sums, from_x, from_y, far_x, far_y, send_sems, recv_sems):
     sibling, along_x, along_y, member = plane_places()
     rows = own_sum.shape[0]
     half = rows // 2
@@ -280,7 +410,6 @@
         send(k, part_ref.at[member(at_x, 1, at_y)], near.at[k], sibling)
         for k, (at_x, at_y) in enumerate(chips)
     ]
-    work(0)
     to_sibling[0].wait_recv()
     add_rows(sums.at[0], (mine[0], near.at[0]), 0, rows)
     diagonal_x = send(4, sums.at[0, bottom], far_x.at[bottom], along_x)
@@ -292,14 +421,12 @@
     add_rows(sums.at[2], (mine[2], near.at[2]), 0, half)
     direct_y = send(7, sums.at[2, top], from_y.at[top], along_y)
     to_sibling[3].wait_recv()
-    work(1)
     diagonal_y.wait_recv()
     add_rows(sums.at[1], (mine[1], near.at[1], far_y), 0, half)
     joint_x = send(8, sums.at[1, top], from_x.at[top], along_x)
     diagonal_x.wait_recv()
     add_rows(sums.at[2], (mine[2], near.at[2], far_x), half, half)
     joint_y = send(9, sums.at[2, bottom], from_y.at[bottom], along_y)
-    work(2)
     direct_x.wait_recv()
     direct_y.wait_recv()
     joint_x.wait_recv()
@@ -309,10 +436,83 @@
         copy.wait_send()
 
 
-def plane_sum_kernel(part_ref, out_ref, *scratch):
-    sibling, along_x, along_y, _ = plane_places()
-    greet((sibling, along_x, along_y))
-    plane_sum(part_ref, out_ref, *scratch)
+def cube_sum(
+    part_ref, own_sum, near, via_z, zx_in, zy_in, far_x, far_y, from_x, from_y, from_z, send_sems, recv_sems,
+    work=lambda point: None,
+):
+    sibling, along_x, along_y, along_z = cube_places()
+    pieces = own_sum.shape[0]
+    half = pieces // 2
+    top, bottom = pl.ds(0, half), pl.ds(half, half)
+    send = sender(send_sems, recv_sems)
+    chips = ((1, 1, 1), (1, 1, 0), (1, 0, 1), (0, 1, 0), (0, 0, 1), (0, 1, 1), (1, 0, 0), (0, 0, 0))
+    z_diagonal, z_x, z_y, at_x, at_y, diagonal, at_z, here = range(8)
+    mine = [part_ref.at[cube_member(*chip, 0)] for chip in chips]
+    to_sibling = [
+        send(k, part_ref.at[cube_member(*chip, 1)], near.at[k], sibling)
+        for k, chip in enumerate(chips)
+    ]
+
+    def add(k, others=(), start=0, count=pieces):
+        add_rows(near.at[k], (mine[k], near.at[k], *others), start, count)
+
+    work(0)
+    to_sibling[z_diagonal].wait_recv()
+    add(z_diagonal)
+    diagonal_z = send(8, near.at[z_diagonal], via_z, along_z)
+    to_sibling[z_x].wait_recv()
+    add(z_x)
+    zx_out = send(9, near.at[z_x], zx_in, along_x)
+    to_sibling[z_y].wait_recv()
+    add(z_y)
+    zy_out = send(10, near.at[z_y], zy_in, along_y)
+    to_sibling[at_x].wait_recv()
+    add(at_x, (), half, half)
+    direct_x = send(13, near.at[at_x, bottom], from_x.at[bottom], along_x)
+    to_sibling[at_y].wait_recv()
+    add(at_y, (), 0, half)
+    direct_y = send(14, near.at[at_y, top], from_y.at[top], along_y)
+    to_sibling[diagonal].wait_recv()
+    to_sibling[at_z].wait_recv()
+    work(1)
+    diagonal_z.wait_recv()
+    add(diagonal, (via_z,))
+    diagonal_x = send(11, near.at[diagonal, bottom], far_x.at[bottom], along_x)
+    diagonal_y = send(12, near.at[diagonal, top], far_y.at[top], along_y)
+    zx_out.wait_recv()
+    zy_out.wait_recv()
+    add(at_z, (zx_in, zy_in))
+    joint_z = send(15, near.at[at_z], from_z, along_z)
+    work(2)
+    diagonal_y.wait_recv()
+    add(at_x, (far_y,), 0, half)
+    joint_x = send(16, near.at[at_x, top], from_x.at[top], along_x)
+    diagonal_x.wait_recv()
+    add(at_y, (far_x,), half, half)
+    joint_y = send(17, near.at[at_y, bottom], from_y.at[bottom], along_y)
+    to_sibling[here].wait_recv()
+    work(3)
+    for copy in (direct_x, direct_y, joint_z, joint_x, joint_y):
+        copy.wait_recv()
+    add_rows(own_sum, (mine[here], near.at[here], from_x, from_y, from_z), 0, pieces)
+    for copy in (
+        *to_sibling, diagonal_z, zx_out, zy_out, direct_x, direct_y, diagonal_x, diagonal_y, joint_z, joint_x, joint_y,
+    ):
+        copy.wait_send()
+
+
+def cube_sum_kernel(part_ref, out_ref, *scratch):
+    greet(cube_places())
+    cube_sum(part_ref, out_ref, *scratch)
+
+
+def cube_sum_scratch(shape, dtype):
+    return [
+        pltpu.VMEM((8, *shape), dtype),
+        *[pltpu.VMEM(shape, dtype)] * 8,
+        pltpu.SemaphoreType.DMA((18,)),
+        pltpu.SemaphoreType.DMA((18,)),
+    ]
 
 
 def plane_sum_scratch(shape, dtype):
@@ -329,17 +529,17 @@
     ]
 
 
-def plane_scatter_sum(partial, collective_id):
-    members = 8
+def cube_scatter_sum(partial, collective_id):
+    members = 16
     rows, columns = partial.shape[0] // members, partial.shape[1]
     shape = (rows // 16, 16, columns)
     out = pl.pallas_call(
-        plane_sum_kernel,
+        cube_sum_kernel,
         out_shape=jax.ShapeDtypeStruct(shape, jnp.float32),
         in_specs=[pl.BlockSpec(memory_space=pltpu.VMEM)],
         out_specs=pl.BlockSpec(memory_space=pltpu.VMEM),
-        scratch_shapes=plane_sum_scratch(shape, partial.dtype),
-        cost_estimate=busy(25),
+        scratch_shapes=cube_sum_scratch(shape, partial.dtype),
+        cost_estimate=busy(35),
         compiler_params=pltpu.CompilerParams(
             collective_id=collective_id, has_side_effects=True, vmem_limit_bytes=VMEM_BYTES
         ),
@@ -427,16 +627,10 @@
     own_ref, down_ref, gate_up_ref, to_gate_hbm, to_up_hbm, act_hbm, grad_ref, both_ref, part_ref,
     down_grad_ref, down, to_gate, to_up, act, act_sem, load_sems, send_sems, recv_sems, local_sem,
 ):
-    _, _, _, member = plane_places()
     units = down.shape[0]
     pieces, piece, columns = own_ref.shape
     rows = pieces * piece
-    order = [
-        member(*far)
-        for far in (
-            (0, 0, 0), (0, 1, 0), (1, 0, 0), (0, 0, 1), (1, 0, 1), (1, 1, 0), (0, 1, 1), (1, 1, 1),
-        )
-    ]
+    order = [cube_member(*flips) for flips in CUBE_ORDER]
 
     def loads(i):
         at = pl.ds(pl.multiple_of(order[i] * rows, rows), rows)
@@ -466,8 +660,8 @@
     for load in loads(0):
         load.start()
     pad_rows(down, down_ref)
-    greet(plane_places()[:3])
-    plane_spread(own_ref, grad_ref, send_sems, recv_sems, local_sem, compute)
+    greet(cube_places())
+    cube_spread(own_ref, grad_ref, send_sems, recv_sems, local_sem, compute)
     act_load.wait()
     grad = grad_ref[...].reshape(len(order) * rows, columns)
     down_grad = contract_rows(act[...], grad)
@@ -476,7 +670,7 @@
 
 def gather_backward(own, down, gate_up, to_gate, to_up, act, collective_id):
     rows, columns = own.shape
-    members, piece = 8, 16
+    members, piece = 16, 16
     depth, units = gate_up.shape[0], to_gate.shape[1]
     low = own.dtype
     vmem, anywhere = pl.BlockSpec(memory_space=pltpu.VMEM), pl.BlockSpec(memory_space=pl.ANY)
@@ -497,11 +691,11 @@
             pltpu.VMEM(act.shape, low),
             pltpu.SemaphoreType.DMA,
             pltpu.SemaphoreType.DMA((2, 2)),
-            *GATHER_SEMS,
+            *gather_sems(21),
         ],
         cost_estimate=busy(35),
         compiler_params=pltpu.CompilerParams(
-            collective_id=collective_id, has_side_effects=True, vmem_limit_bytes=VMEM_BYTES
+            collective_id=collective_id, has_side_effects=True, vmem_limit_bytes=60 * 2**20
         ),
     )(own.reshape(rows // piece, piece, columns), down, gate_up, to_gate, to_up, act)
     return both, part, down_grad
@@ -509,45 +703,42 @@
 
 def sum_gradients_kernel(
     part_ref, down_ref, in_hbm, both_hbm, sum_ref, gate_up_ref, down_sum_ref,
-    rows_in, both, arriving, load_sems, z_send, z_recv, *scratch,
+    columns_in, both, arriving, both_sem, in_sems, far_send, far_recv, *scratch,
 ):
-    planes = down_ref.shape[0]
-    z, x, core, seq = (lax.axis_index(name) for name in ALL)
-    others = [(lax.rem(z + k, planes), x, core, seq) for k in range(1, planes)]
-    loads = [
-        pltpu.make_async_copy(source, target, load_sems.at[k])
-        for k, (source, target) in enumerate(
-            ((in_hbm, rows_in), (both_hbm, both))
-        )
-    ]
-    for load in loads:
-        load.start()
-    step = 256
-
-    def gate_up_columns(i, carry):
-        at = pl.ds(pl.multiple_of(i * step, step), step)
-        gate_up_ref[:, at] = contract_rows(rows_in[...], both[:, at]).astype(gate_up_ref.dtype)
-        return carry
-
-    blocks = gate_up_ref.shape[1] // step
+    cubes = down_ref.shape[0]
+    far, others = other_cubes(cubes)
+    step = columns_in.shape[2]
+    blocks = gate_up_ref.shape[0] // step
+
+    def load(i):
+        at = pl.ds(i * step, step)
+        return pltpu.make_async_copy(in_hbm.at[:, at], columns_in.at[i % 2], in_sems.at[i % 2])
+
+    both_load = pltpu.make_async_copy(both_hbm, both, both_sem)
+    both_load.start()
+    load(0).start()
+
+    def rows_of(i):
+        if i == 0:
+            both_load.wait()
+        if i + 1 < blocks:
+            load(i + 1).start()
+        load(i).wait()
+        rows = contract_rows(columns_in[i % 2], both[...])
+        gate_up_ref[pl.ds(i * step, step), :] = rows.astype(gate_up_ref.dtype)
 
     def work(point):
-        if point == 0:
-            for load in loads:
-                load.wait()
-            lax.fori_loop(0, 2, gate_up_columns, 0)
-        if point == 1:
-            lax.fori_loop(2, 3, gate_up_columns, 0)
-        if point == 2:
-            lax.fori_loop(3, blocks, gate_up_columns, 0)
-
-    greet((*plane_places()[:3], *others))
-    send = sender(z_send, z_recv)
+        spread = ((0,), (1,), (2, 3), tuple(range(4, blocks)))
+        for i in spread[point]:
+            rows_of(i)
+
+    greet((*cube_places(), *others))
+    send = sender(far_send, far_recv)
     copies = [
         send(k, down_ref.at[place[0]], arriving.at[k], place) for k, place in enumerate(others)
     ]
-    plane_sum(part_ref, sum_ref, *scratch, work=work)
-    down_sum = down_ref[z].astype(jnp.float32)
+    cube_sum(part_ref, sum_ref, *scratch, work=work)
+    down_sum = down_ref[far].astype(jnp.float32)
     for k, copy in enumerate(copies):
         copy.wait_recv()
         down_sum = down_sum + arriving[k].astype(jnp.float32)
@@ -559,6 +750,7 @@
 def sum_gradients(part, down, rows_in, both, collective_id):
     members, pieces, piece, depth = part.shape
     low = part.dtype
+    step = 256
     vmem, anywhere = pl.BlockSpec(memory_space=pltpu.VMEM), pl.BlockSpec(memory_space=pl.ANY)
     total, gate_up, down_sum = pl.pallas_call(
         sum_gradients_kernel,
@@ -570,13 +762,14 @@
         in_specs=[vmem, vmem, anywhere, anywhere],
         out_specs=[vmem, vmem, vmem],
         scratch_shapes=[
-            pltpu.VMEM(rows_in.shape, low),
+            pltpu.VMEM((2, rows_in.shape[0], step), low),
             pltpu.VMEM(both.shape, low),
             pltpu.VMEM((down.shape[0] - 1, *down.shape[1:]), low),
+            pltpu.SemaphoreType.DMA,
             pltpu.SemaphoreType.DMA((2,)),
             pltpu.SemaphoreType.DMA((down.shape[0] - 1,)),
             pltpu.SemaphoreType.DMA((down.shape[0] - 1,)),
-            *plane_sum_scratch((pieces, piece, depth), low),
+            *cube_sum_scratch((pieces, piece, depth), low),
         ],
         cost_estimate=busy(35),
         compiler_params=pltpu.CompilerParams(
@@ -587,10 +780,8 @@
 
 
 def owner_sum_kernel(planes, part_ref, out_ref, own_sum, leaving, arriving, z_send, z_recv, *scratch):
-    sibling, along_x, along_y, _ = plane_places()
-    z, x, core, seq = (lax.axis_index(name) for name in ALL)
-    others = [(lax.rem(z + k, planes), x, core, seq) for k in range(1, planes)]
-    greet((sibling, along_x, along_y, *others))
+    plane, others, ring = other_planes(planes)
+    greet((*plane_places()[:3], *others))
     plane_sum(part_ref, own_sum, *scratch)
     send = sender(z_send, z_recv)
 
@@ -600,12 +791,12 @@
 
     lax.fori_loop(0, planes, narrow, 0)
     copies = [
-        send(k, leaving.at[place[0]], arriving.at[k], place) for k, place in enumerate(others)
+        send(k, leaving.at[ring[k]], arriving.at[k], place) for k, place in enumerate(others)
     ]
     for copy in copies:
         copy.wait_recv()
 
-    value = own_sum[z]
+    value = own_sum[plane]
     for k in range(planes - 1):
         value = value + arriving[k].astype(jnp.float32)
     out_ref[...] = value
@@ -953,7 +1144,9 @@
     bf16, f32 = jnp.bfloat16, jnp.float32
     devices = lax.axis_size(ALL)
     members = lax.axis_size(PLANE)
-    planes = lax.axis_size("z")
+    planes = lax.axis_size(PLANES)
+    cubes = lax.axis_size("far")
+    group = lax.axis_size(CUBE)
     width_rows = query_weight.shape[0]
     hidden_rows = down_weight.shape[0]
     head_width = key_weight.shape[1]
@@ -963,20 +1156,20 @@
     mix_rows = output_weight.shape[0]
     padded = up_to(width_rows + 1, 8)
     width = devices * width_rows
-    unit_count = planes * hidden_rows
+    unit_count = cubes * hidden_rows
     unit_pad = up_to(unit_count, 128)
     by_device = place_columns(devices, members, planes, width_rows, padded, False)
     by_member = place_columns(devices, members, planes, width_rows, padded, True)
 
     def column_blocks(weight):
-        pieces = weight.reshape(width_rows, planes, members, hidden_rows)
-        pieces = pieces.transpose(2, 0, 1, 3).reshape(members, width_rows, unit_count)
+        pieces = weight.reshape(width_rows, cubes, group, hidden_rows)
+        pieces = pieces.transpose(2, 0, 1, 3).reshape(group, width_rows, unit_count)
         return jnp.pad(
             pieces, ((0, 0), (0, padded - width_rows), (0, unit_pad - unit_count))
         )
 
     gate_up = jnp.concatenate([column_blocks(gate_weight), column_blocks(up_weight)], axis=2)
-    gate_up = jnp.broadcast_to(gate_up[None], (planes,) + gate_up.shape)
+    gate_up = jnp.broadcast_to(gate_up[None], (cubes,) + gate_up.shape)
     gate_up = gate_up.reshape((devices,) + gate_up.shape[2:])
 
     gains = (input_gain, query_gain, key_gain, attnout_gain, ffnin_gain, ffnout_gain)
@@ -989,12 +1182,10 @@
     output_wide = jnp.pad(output_weight, ((0, 0), (0, qkv_width - output_weight.shape[1])))
     packed = jnp.concatenate([packed, output_wide], axis=0)
     packed_all = z_gather(packed, planes, 0)
-    gate_up, down_local, packed_all = lax.optimization_barrier(
-        (gate_up, down_weight, packed_all)
-    )
-    packed_all = plane_gather(packed_all, 6)
+    packed_all, down_full = weights_gather(packed_all, down_weight, cubes, 6)
+    down_full = down_full.reshape(unit_count, down_weight.shape[1])
+    gate_up, packed_all = lax.optimization_barrier((gate_up, packed_all))
     gate_up_full = exchange(gate_up, ALL).reshape(devices * padded, 2 * unit_pad)
-    down_full = lax.all_gather(down_local, "z", axis=0, tiled=True)
     incoming = cotangent[0].astype(f32)
     local_rows = tokens.shape[1]
     offset = lax.axis_index("seq") * local_rows
@@ -1049,9 +1240,9 @@
     )
     ffnout_scale = scales.pop()
 
-    plane_in = gather_rows(ffn_in_placed, 1)
-    ffn_part, activated_low, to_gate, to_up = ffn_forward(plane_in, gate_up_full, down_full)
-    ffn_raw = plane_scatter_sum(ffn_part, 2)
+    cube_in = gather_rows(ffn_in_placed, 1)
+    ffn_part, activated_low, to_gate, to_up = ffn_forward(cube_in, gate_up_full, down_full)
+    ffn_raw = cube_scatter_sum(ffn_part, 2)
     inv_ffn = inverse_rms(ffn_raw)
     norm_ffn = ffn_raw * inv_ffn
     result = middle + norm_ffn * ffnout_scale
@@ -1061,9 +1252,9 @@
     gate_up_low, ffn_in_part, down_blocks = gather_backward(
         ffn_raw_grad, down_full, gate_up_full, to_gate, to_up, activated_low, 3
     )
-    down_blocks = down_blocks.reshape(planes, hidden_rows, down_weight.shape[1])
+    down_blocks = down_blocks.reshape(cubes, hidden_rows, down_weight.shape[1])
     ffn_in_grad, gate_up_blocks, down_wgrad = sum_gradients(
-        ffn_in_part, down_blocks, plane_in, gate_up_low, 4
+        ffn_in_part, down_blocks, cube_in, gate_up_low, 4
     )
     gate_up_terms = exchange(gate_up_blocks.reshape(devices, padded, 2 * unit_pad), ALL)
     input_grad, blocks = attention_backward(
@@ -1097,14 +1288,14 @@
     )
     share = owner_sum(blocks, 5)
     gate_up_sum = jnp.sum(
-        gate_up_terms.reshape(planes, members, padded, 2 * unit_pad).astype(f32), axis=0
+        gate_up_terms.reshape(cubes, group, padded, 2 * unit_pad).astype(f32), axis=0
     )
 
     def unit_columns(total):
         total = total[:, :width_rows, :unit_count].reshape(
-            members, width_rows, planes, hidden_rows
+            group, width_rows, cubes, hidden_rows
         )
-        return total.transpose(1, 2, 0, 3).reshape(width_rows, planes * members * hidden_rows)
+        return total.transpose(1, 2, 0, 3).reshape(width_rows, cubes * group * hidden_rows)
 
     gate_wgrad = unit_columns(gate_up_sum[:, :, :unit_pad])
     up_wgrad = unit_columns(gate_up_sum[:, :, unit_pad:])
@@ -1129,13 +1320,13 @@
 
 def solution(mesh):
     dp, seq = mesh.shape["dp"], mesh.shape["seq"]
-    split = Mesh(mesh.devices.reshape(dp // 4, 2, 2, seq), ALL)
-    rows = P(("z", "x", "core"), "seq", None)
+    split = Mesh(mesh.devices.reshape(dp // 8, 2, 2, 2, seq), ALL)
+    rows = P(("far", "z", "x", "core"), "seq", None)
     matrix, vector = P(ALL, None), P(ALL)
     return jax.shard_map(
         body,
         mesh=split,
-        in_specs=(rows, P(("z", "x", "core"), None), rows) + (matrix,) * 7 + (vector,) * 6,
+        in_specs=(rows, P(("far", "z", "x", "core"), None), rows) + (matrix,) * 7 + (vector,) * 6,
         out_specs=(rows, rows) + (matrix,) * 7 + (vector,) * 6,
         check_vma=False,
     )

time: 511 us -> 486 us (0.951)
  between operations: 14.7 us -> 1.55 us
  local copies, waits for them, and re-layouts: 38.9 us -> 32.9 us
    pallas_call x1, Pallas kernels: 42.8 us -> 62.5 us  [gather_backward(): pl.pallas_call(gather_backward_kernel, out_shape=[jax.ShapeDtypeStruct((m...]
    pallas_call x1, Pallas kernels: 82.8 us -> 67.2 us  [owner_sum(): pl.pallas_call(functools.partial(owner_sum_kernel, planes), out_shape=jax...]
    unnamed x34 -> x36, local copies, waits for them, and re-layouts: 14.3 us -> 6 us
    pallas_call x1, Pallas kernels: 40.6 us -> 33.8 us  [attention_backward(): pl.pallas_call(functools.partial(attention_backward_kernel, gain_at, widt...]
  transfers between devices with their start and end apart: 4 -> 3, of which waited for: 0 -> 0; matrix products, arithmetic and copies ran while one was open for 3% -> 6% of each run, Pallas kernels for 48% -> 47%
where the time goes in v8:
time: 486 us; the launch traced here: 481 us
  Pallas kernels  417 us (86%)
  local copies, waits for them, and re-layouts  32.9 us (7%)
  starting transfers between devices  13.6 us (3%)
  other arithmetic  12 us (2%)
    pallas_call x1, Pallas kernels, owner_sum(): pl.pallas_call(functools.partial(owner_sum_kernel, planes), out_shape=jax...  67.2 us
    pallas_call x1, Pallas kernels, gather_backward(): pl.pallas_call(gather_backward_kernel, out_shape=[jax.ShapeDtypeStruct((m...  62.5 us
    pallas_call x1, Pallas kernels, sum_gradients(): pl.pallas_call(sum_gradients_kernel, out_shape=[jax.ShapeDtypeStruct((pie...  53 us
    pallas_call x1, Pallas kernels, gather_rows(): pl.pallas_call(cube_gather_kernel, out_shape=jax.ShapeDtypeStruct((member...  52.4 us
    pallas_call x1, Pallas kernels, cube_scatter_sum(): pl.pallas_call(cube_sum_kernel, out_shape=jax.ShapeDtypeStruct(shape, jnp...  45.9 us
    pallas_call x1, Pallas kernels, weights_gather(): pl.pallas_call(functools.partial(weights_gather_kernel, cubes), out_shape...  34.2 us
    pallas_call x1, Pallas kernels, attention_backward(): pl.pallas_call(functools.partial(attention_backward_kernel, gain_at, widt...  33.8 us
    pallas_call x1, Pallas kernels, ffn_forward(): pl.pallas_call(ffn_forward_kernel, grid=(rows // ROW_BLOCK,), in_specs=[r...  30.5 us
  transfers between devices with their start and end apart: 3, of which 0 were waited for; matrix products, arithmetic and copies ran while one was open for 6% of the time, Pallas kernels for 47%

profile of v8, /device:TPU:8, one launch (start us, length us, event | category | flops | bytes accessed | tf_op | source)
XLA Modules:
  0.0 480.5 jit_solution(1964213247798823123)
XLA Ops:
  0.7 1.6 collective-permute-start
  2.2 4.1 concatenate.21
  6.4 2.9 reshape.151
  10.2 1.7 reshape.153
  13.9 22.5 %shard_map.271.own_ref = bf16[4,72,1536]{2,1,0:T(8,128)(2,1)S(1)} custom-call(bf16[72,1536]{1,0:T(8,128)(2,1)S(1)} %fusion.27.own_ref), custom_call_target="tpu_custom_call" | custom-call | bytes 60000000 | tf_op jit(solution)/shard_map/pallas_call | solution.py:332
  36.4 34.2 %shard_map.272 = (bf16[8,4,72,1536]{3,2,1,0:T(8,128)(2,1)}, bf16[2,216,1152]{2,1,0:T(8,128)(2,1)S(1)}) custom-call(bf16[4,72,1536]{2,1,0:T(8,128)(2,1)S(1)} %shard_map.271.own_ref, bf16[216,1152]{1,0:T(8,128)(2,1)S(1)} %copy-done.4), custom_call_target="tpu_custom_call" | custom-call | bytes 90000000 | tf_op jit(solution)/shard_map/pallas_call | solution.py:352
  71.6 1.9 broadcast_in_dim.12
  73.6 5.5 %all-to-all-start = ((bf16[32,40,1024]{2,1,0:T(8,128)(2,1)}), bf16[32,40,1024]{2,1,0:T(8,128)(2,1)S(1)}, u32[]{:S(2)}, u32[]{:S(2)}) async-start(bf16[32,40,1024]{2,1,0:T(8,128)(2,1)} %bitcast.69), calls=%async_computation | async-start | bytes 5242880 | tf_op jit(solution)/shard_map/all_to_all | solution.py:87
  79.1 5.3 %fusion.38 = (bf16[1152,1280]{1,0:T(8,128)(2,1)}, bf16[1152,1280]{1,0:T(8,128)(2,1)}) fusion(s32[1152]{0:T(1024)S(1)} %get-tuple-element.103, s32[1152]{0:T(1024)S(1)} %get-tuple-element.104, pred[1152]{0:T(1024)(128)(4,1)S(1)} %get-tuple-element.106, s32[1152]{0:T(1024)S(1)} %get-tuple-element.102, s32[1152]{0:T(1024)S(1)} %get-tuple-element.105, ...), kind=kLoop, calls=%fused_computation.83 | loop fusion | flops 45711360 | bytes 5918976 | tf_op jit(solution)/shard_map/convert_element_type | solution.py:69
  85.6 1.8 multiply_sine_fusion
  87.4 1.2 broadcast_select_fusion.1
  88.6 3.8 convolution_convert_fusion.row_ref
  92.3 14.8 %shard_map.273 = (bf16[256,1280]{1,0:T(8,128)(2,1)}, f32[256,1152]{1,0:T(8,128)}, f32[256,1152]{1,0:T(8,128)}, bf16[256,1024]{1,0:T(8,128)(2,1)}, f32[4,256,512]...) custom-call(bf16[512,1280]{1,0:T(8,128)(2,1)} %convolution_convert_f, ...), custom_call_target="tpu_custom_call" | custom-call | bytes 60000000 | tf_op jit(solution)/shard_map/pallas_call | solution.py:973
  107.2 1.1 copy-done.3
  108.2 52.4 %shard_map.274 = bf16[16,16,16,1280]{3,2,1,0:T(8,128)(2,1)} custom-call(bf16[16,16,1280]{2,1,0:T(8,128)(2,1)S(1)} %bitcast.66), custom_call_target="tpu_custom_call" | custom-call | bytes 105000000 | tf_op jit(solution)/shard_map/pallas_call | solution.py:376
  160.7 1.9 copy-done.2
  162.6 30.5 %shard_map.275 = (bf16[4096,1152]{1,0:T(8,128)(2,1)}, bf16[4096,512]{1,0:T(8,128)(2,1)}, f32[4096,512]{1,0:T(8,128)}, f32[4096,512]{1,0:T(8,128)}) custom-call(bf16[4096,1280]{1,0:T(8,128)(2,1)} %bitcast.67, bf16[1280,1024]{1,0:T(8,128)(2,1)S(1)} %bitcast.62, bf16[432,1152]{1,0:T(8,128)(2,1)S(1)} %bitcast.65), custom_call_target="tpu_custom_call" | custom-call | bytes 60000000 | tf_op jit(solution)/shard_map/pallas_call | solution.py:606
  193.1 45.9 %shard_map.276 = f32[16,16,1152]{2,1,0:T(8,128)S(1)} custom-call(bf16[16,16,16,1152]{3,2,1,0:T(8,128)(2,1)} %bitcast.71), custom_call_target="tpu_custom_call" | custom-call | bytes 105000000 | tf_op jit(solution)/shard_map/pallas_call | solution.py:536
  239.3 1.3 fusion.15
  240.7 1.1 fusion.21.own_ref
  241.8 62.5 %shard_map.277 = (bf16[16,16,16,1152]{3,2,1,0:T(8,128)(2,1)}, bf16[4096,1024]{1,0:T(8,128)(2,1)}, bf16[16,16,16,1280]{3,2,1,0:T(8,128)(2,1)}, bf16[432,1152]{1,0:T(8,128)(2,1)}) custom-call(bf16[16,16,1152]{2,1,0:T(8,128)(2,1)} %fusion.21.own_ref, bf16[432,1152]{1,0:T(8,128)(2,1)} %bitcast.64, bf16[1280,1024]{1,0:T(8,128)(2,1)} %bitcast.63, ...), custom_call_target="tpu_custom_call" | custom-call | bytes 105000000 | tf_op jit(solution)/shard_map/pallas_call | solution.py:677
  304.2 53.0 %shard_map.278 = (f32[16,16,1280]{2,1,0:T(8,128)}, bf16[1280,1024]{1,0:T(8,128)(2,1)}, f32[216,1152]{1,0:T(8,128)}) custom-call(bf16[16,16,16,1280]{3,2,1,0:T(8,128)(2,1)} %get-tuple-element.60.part_ref, bf16[2,216,1152]{2,1,0:T(8,128)(2,1)} %bitcast.83, bf16[4096,1280]{1,0:T(8,128)(2,1)} %bitcast.68, bf16[4096,1024]{1,0:T(8,128)(2,1)} %get-tuple-element.62.both_hbm), custom_call_target="tpu_custom_call" | custom-call | bytes 105000000 | tf_op jit(solution)/shard_map/pallas_call | solution.py:755
  357.2 6.5 %all-to-all-start.1 = ((bf16[32,40,1024]{2,1,0:T(8,128)(2,1)}), bf16[32,40,1024]{2,1,0:T(8,128)(2,1)S(1)}, u32[]{:S(2)}, u32[]{:S(2)}) async-start(bf16[32,40,1024]{2,1,0:T(8,128)(2,1)} %bitcast.76), calls=%async_computation.1 | async-start | bytes 5242880 | tf_op jit(solution)/shard_map/all_to_all | solution.py:87
  364.3 33.8 %shard_map.279 = (f32[256,1152]{1,0:T(8,128)}, bf16[8,4,72,1536]{3,2,1,0:T(8,128)(2,1)}) custom-call(f32[256,1280]{1,0:T(8,128)} %bitcast.81, bf16[256,1152]{1,0:T(8,128)(2,1)} %bitcast.72, f32[256,1152]{1,0:T(8,128)} %get-tuple-element.51.middle_ref, f32[256,1152]{1,0:T(8,128)} %get-tuple-element.64.raw_ref, bf16[256,1024]{1,0:T(8,128)(2,1)} %get-tuple-element.65.mix_ref, ...), custom_call_target="tpu_custom_call" | custom-call | bytes 90000000 | tf_op jit(solution)/shard_map/pallas_call | solution.py:1102
  398.1 67.2 %shard_map.280 = f32[72,1536]{1,0:T(8,128)S(1)} custom-call(bf16[8,4,72,1536]{3,2,1,0:T(8,128)(2,1)} %get-tuple-element.80.part_ref), custom_call_target="tpu_custom_call" | custom-call | bytes 105000000 | tf_op jit(solution)/shard_map/pallas_call | solution.py:809
  469.3 2.1 reshape.172
  471.4 1.7 copy.56
  473.0 1.8 reshape.168
  474.8 1.0 reshape.171
  476.3 1.8 reshape.166
  478.1 1.0 copy.67
  479.1 0.9 copy.68
  (68 shorter events, 10.2 us)
Async XLA Ops:
  0.6 9.5 %copy-start.10 = (bf16[36,6912]{1,0:T(8,128)(2,1)S(1)}, bf16[36,6912]{1,0:T(8,128)(2,1)}, u32[]{:S(2)}) copy-start(bf16[36,6912]{1,0:T(8,128)(2,1)} %param.24) | copy-start | bytes 1492996
  0.7 86.7 %collective-permute-start = (bf16[256,1152]{1,0:T(8,128)(2,1)}, bf16[256,1152]{1,0:T(8,128)(2,1)}, u32[]{:S(2)}, u32[]{:S(2)}) collective-permute-start(bf16[256,1152]{1,0:T(8,128)(2,1)} %bitcast.79), channel_id=1, source_target_pairs={{0,1},{1,0},{2,3},{3,2},{4,5},{5,4},{6,7},{7,6},{8,9},{9,8},{10,11... | collective-permute-start | bytes 1769480 | tf_op jit(solution)/shard_map/ppermute | solution.py:1201
  12.8 1.0 copy-start.11
  12.8 1.0 copy-start.14
  12.8 1.0 copy-start.15
  12.8 1.0 copy-start.12
  13.0 23.4 %copy-start.4 = (bf16[216,1152]{1,0:T(8,128)(2,1)S(1)}, bf16[216,1152]{1,0:T(8,128)(2,1)}, u32[]{:S(2)}) copy-start(bf16[216,1152]{1,0:T(8,128)(2,1)} %down_ref.1) | copy-start | bytes 1492996
  70.7 1.0 copy-start.1
  73.6 5.6 %copy-start.13 = (s32[1,512]{1,0:T(1,128)S(1)}, s32[1,512]{1,0:T(1,128)}, u32[]{:S(2)}) copy-start(s32[1,512]{1,0:T(1,128)} %segment_row.1) | copy-start | bytes 6148
  73.6 87.1 %all-to-all-start = ((bf16[32,40,1024]{2,1,0:T(8,128)(2,1)}), bf16[32,40,1024]{2,1,0:T(8,128)(2,1)S(1)}, u32[]{:S(2)}, u32[]{:S(2)}) async-start(bf16[32,40,1024]{2,1,0:T(8,128)(2,1)} %bitcast.69), calls=%async_computation | async-start | bytes 5242880 | tf_op jit(solution)/shard_map/all_to_all | solution.py:87
  79.1 8.3 %copy-start.7 = (bf16[1,256,1152]{2,1,0:T(8,128)(2,1)S(1)}, bf16[1,256,1152]{2,1,0:T(8,128)(2,1)}, u32[]{:S(2)}) copy-start(bf16[1,256,1152]{2,1,0:T(8,128)(2,1)} %param.16) | copy-start | bytes 1769476
  107.1 1.1 copy-start.3
  108.2 52.4 %copy-start.16 = (f32[1,1152]{1,0:T(1,128)S(1)}, f32[1,1152]{1,0:T(1,128)}, u32[]{:S(2)}) copy-start(f32[1,1152]{1,0:T(1,128)} %get-tuple-element.56) | copy-start | bytes 13828
  160.7 32.4 %copy-start = (bf16[32,40,1024]{2,1,0:T(8,128)(2,1)}, bf16[32,40,1024]{2,1,0:T(8,128)(2,1)S(1)}, u32[]{:S(2)}) copy-start(bf16[32,40,1024]{2,1,0:T(8,128)(2,1)S(1)} %all-to-all-done) | copy-start | bytes 7864324
  160.7 1.9 copy-start.2
  193.1 46.2 %copy-start.5 = (bf16[1,256,1152]{2,1,0:T(8,128)(2,1)S(1)}, bf16[1,256,1152]{2,1,0:T(8,128)(2,1)}, u32[]{:S(2)}) copy-start(bf16[1,256,1152]{2,1,0:T(8,128)(2,1)} %param.18) | copy-start | bytes 1769476
  193.1 46.2 %copy-start.6 = (f32[256,1152]{1,0:T(8,128)S(1)}, f32[256,1152]{1,0:T(8,128)}, u32[]{:S(2)}) copy-start(f32[256,1152]{1,0:T(8,128)} %get-tuple-element.51.middle_ref) | copy-start | bytes 3538948
  357.2 111.3 %all-to-all-start.1 = ((bf16[32,40,1024]{2,1,0:T(8,128)(2,1)}), bf16[32,40,1024]{2,1,0:T(8,128)(2,1)S(1)}, u32[]{:S(2)}, u32[]{:S(2)}) async-start(bf16[32,40,1024]{2,1,0:T(8,128)(2,1)} %bitcast.76), calls=%async_computation.1 | async-start | bytes 5242880 | tf_op jit(solution)/shard_map/all_to_all | solution.py:87
  476.3 1.8 copy-start.8
  476.3 2.8 copy-start.9

commit v9 on v8

--- a/solution.py
+++ b/solution.py
@@ -286,11 +286,6 @@
 )
 
 
-def cube_gather_kernel(own_ref, out_ref, *sems):
-    greet(cube_places())
-    cube_spread(own_ref, out_ref, *sems)
-
-
 def weights_gather_kernel(cubes, own_ref, down_ref, out_ref, down_out, far_send, far_recv, own_sem, *sems):
     far, others = other_cubes(cubes)
     greet((*plane_places()[:3], *others))
@@ -368,23 +363,6 @@
             collective_id=collective_id, has_side_effects=True, vmem_limit_bytes=VMEM_BYTES
         ),
     )(local, down)
-
-
-def gather_rows(local, collective_id):
-    rows, columns = local.shape
-    members = 16
-    out = pl.pallas_call(
-        cube_gather_kernel,
-        out_shape=jax.ShapeDtypeStruct((members, rows // 16, 16, columns), local.dtype),
-        in_specs=[pl.BlockSpec(memory_space=pl.ANY)],
-        out_specs=pl.BlockSpec(memory_space=pl.ANY),
-        scratch_shapes=gather_sems(21),
-        cost_estimate=busy(35),
-        compiler_params=pltpu.CompilerParams(
-            collective_id=collective_id, has_side_effects=True, vmem_limit_bytes=VMEM_BYTES
-        ),
-    )(local.reshape(rows // 16, 16, columns))
-    return out.reshape(-1, columns)
 
 
 def add_rows(target, sources, start, count):
@@ -437,8 +415,8 @@
 
 
 def cube_sum(
-    part_ref, own_sum, near, via_z, zx_in, zy_in, far_x, far_y, from_x, from_y, from_z, send_sems, recv_sems,
-    work=lambda point: None,
+    part_hbm, own_sum, mine, near, via_z, zx_in, zy_in, far_x, far_y, from_x, from_y, from_z, load_sems, send_sems,
+    recv_sems, work=lambda point: None,
 ):
     sibling, along_x, along_y, along_z = cube_places()
     pieces = own_sum.shape[0]
@@ -447,33 +425,42 @@
     send = sender(send_sems, recv_sems)
     chips = ((1, 1, 1), (1, 1, 0), (1, 0, 1), (0, 1, 0), (0, 0, 1), (0, 1, 1), (1, 0, 0), (0, 0, 0))
     z_diagonal, z_x, z_y, at_x, at_y, diagonal, at_z, here = range(8)
-    mine = [part_ref.at[cube_member(*chip, 0)] for chip in chips]
     to_sibling = [
-        send(k, part_ref.at[cube_member(*chip, 1)], near.at[k], sibling)
+        send(k, part_hbm.at[cube_member(*chip, 1)], near.at[k], sibling)
         for k, chip in enumerate(chips)
     ]
+    loads = [
+        pltpu.make_async_copy(part_hbm.at[cube_member(*chip, 0)], mine.at[k], load_sems.at[k])
+        for k, chip in enumerate(chips)
+    ]
+    for load in loads:
+        load.start()
+
+    def both_in(k):
+        to_sibling[k].wait_recv()
+        loads[k].wait()
 
     def add(k, others=(), start=0, count=pieces):
-        add_rows(near.at[k], (mine[k], near.at[k], *others), start, count)
+        add_rows(near.at[k], (mine.at[k], near.at[k], *others), start, count)
 
     work(0)
-    to_sibling[z_diagonal].wait_recv()
+    both_in(z_diagonal)
     add(z_diagonal)
     diagonal_z = send(8, near.at[z_diagonal], via_z, along_z)
-    to_sibling[z_x].wait_recv()
+    both_in(z_x)
     add(z_x)
     zx_out = send(9, near.at[z_x], zx_in, along_x)
-    to_sibling[z_y].wait_recv()
+    both_in(z_y)
     add(z_y)
     zy_out = send(10, near.at[z_y], zy_in, along_y)
-    to_sibling[at_x].wait_recv()
+    both_in(at_x)
     add(at_x, (), half, half)
     direct_x = send(13, near.at[at_x, bottom], from_x.at[bottom], along_x)
-    to_sibling[at_y].wait_recv()
+    both_in(at_y)
     add(at_y, (), 0, half)
     direct_y = send(14, near.at[at_y, top], from_y.at[top], along_y)
-    to_sibling[diagonal].wait_recv()
-    to_sibling[at_z].wait_recv()
+    both_in(diagonal)
+    both_in(at_z)
     work(1)
     diagonal_z.wait_recv()
     add(diagonal, (via_z,))
@@ -490,11 +477,11 @@
     diagonal_x.wait_recv()
     add(at_y, (far_x,), half, half)
     joint_y = send(17, near.at[at_y, bottom], from_y.at[bottom], along_y)
-    to_sibling[here].wait_recv()
+    both_in(here)
     work(3)
     for copy in (direct_x, direct_y, joint_z, joint_x, joint_y):
         copy.wait_recv()
-    add_rows(own_sum, (mine[here], near.at[here], from_x, from_y, from_z), 0, pieces)
+    add_rows(own_sum, (mine.at[here], near.at[here], from_x, from_y, from_z), 0, pieces)
     for copy in (
         *to_sibling, diagonal_z, zx_out, zy_out, direct_x, direct_y, diagonal_x, diagonal_y, joint_z, joint_x, joint_y,
     ):
@@ -509,7 +496,9 @@
 def cube_sum_scratch(shape, dtype):
     return [
         pltpu.VMEM((8, *shape), dtype),
+        pltpu.VMEM((8, *shape), dtype),
         *[pltpu.VMEM(shape, dtype)] * 8,
+        pltpu.SemaphoreType.DMA((8,)),
         pltpu.SemaphoreType.DMA((18,)),
         pltpu.SemaphoreType.DMA((18,)),
     ]
@@ -530,21 +519,19 @@
 
 
 def cube_scatter_sum(partial, collective_id):
-    members = 16
-    rows, columns = partial.shape[0] // members, partial.shape[1]
-    shape = (rows // 16, 16, columns)
+    shape = partial.shape[1:]
     out = pl.pallas_call(
         cube_sum_kernel,
         out_shape=jax.ShapeDtypeStruct(shape, jnp.float32),
-        in_specs=[pl.BlockSpec(memory_space=pltpu.VMEM)],
+        in_specs=[pl.BlockSpec(memory_space=pl.ANY)],
         out_specs=pl.BlockSpec(memory_space=pltpu.VMEM),
         scratch_shapes=cube_sum_scratch(shape, partial.dtype),
         cost_estimate=busy(35),
         compiler_params=pltpu.CompilerParams(
             collective_id=collective_id, has_side_effects=True, vmem_limit_bytes=VMEM_BYTES
         ),
-    )(partial.reshape(members, *shape))
-    return out.reshape(rows, columns)
+    )(partial)
+    return out.reshape(shape[0] * shape[1], shape[2])
 
 
 gelu_inner = 0.7978845608028654
@@ -559,85 +546,130 @@
         target[pl.ds(rows, extra)] = jnp.zeros((extra, target.shape[1]), target.dtype)
 
 
-def ffn_forward_kernel(in_ref, gate_up_ref, down_ref, part_ref, act_ref, to_gate, to_up, down, proj):
-    units = act_ref.shape[1]
-
-    @pl.when(pl.program_id(0) == 0)
-    def _():
-        pad_rows(down, down_ref)
-
-    proj[...] = matmul(in_ref[...], gate_up_ref[...])
+def block_order(rows):
+    order = [cube_member(*flips) for flips in CUBE_ORDER]
+    return order, [pl.ds(pl.multiple_of(block * rows, rows), rows) for block in order]
+
+
+def gather_forward_kernel(
+    own_ref, gate_up_ref, down_ref, rows_hbm, part_hbm, act_hbm, to_gate_hbm, to_up_hbm,
+    rows_in, down, proj, part, act, to_gate, to_up, put_sems, send_sems, recv_sems, local_sem,
+):
+    units = act.shape[2]
+    pieces, piece, columns = own_ref.shape
+    rows = pieces * piece
+    order, places = block_order(rows)
     step = 32
 
-    def one(i, carry):
-        rows = pl.ds(pl.multiple_of(i * step, step), step)
-        gate, up = proj[rows, :units], proj[rows, units:]
-        square = gate * gate
-        bend = jnp.tanh(gelu_inner * gate * (1.0 + gelu_cubic * square))
-        half = 0.5 * (1.0 + bend)
-        value = gate * half
-        slope = half + 0.5 * gate * (1.0 - bend * bend) * (
-            gelu_inner * (1.0 + 3.0 * gelu_cubic * square)
+    def puts(i):
+        slot, block, at = i % 2, order[i], places[i]
+        source = own_ref if i == 0 else rows_in.at[block]
+        pairs = (
+            (source, rows_hbm.at[block]),
+            (part.at[slot], part_hbm.at[block]),
+            (act.at[slot], act_hbm.at[at]),
+            (to_gate.at[slot], to_gate_hbm.at[at]),
+            (to_up.at[slot], to_up_hbm.at[at]),
         )
-        to_gate[rows, :] = slope * up
-        to_up[rows, :] = value
-        act_ref[rows, :] = (value * up).astype(act_ref.dtype)
-        return carry
-
-    lax.fori_loop(0, in_ref.shape[0] // step, one, 0)
-    part_ref[...] = matmul(act_ref[...], down[...]).astype(part_ref.dtype)
-
-
-ROW_BLOCK = 256
-
-
-def whole(array):
-    return pl.BlockSpec(array.shape, lambda i: (0, 0), pipeline_mode=pl.Buffered(1))
-
-
-def row_block(columns):
-    return pl.BlockSpec((ROW_BLOCK, columns), lambda i: (i, 0))
-
-
-def ffn_forward(rows_in, gate_up, down):
-    rows, depth = rows_in.shape
+        return [
+            pltpu.make_async_copy(*pair, put_sems.at[k, slot]) for k, pair in enumerate(pairs)
+        ]
+
+    def compute(i):
+        if i >= 2:
+            for put in puts(i - 2):
+                put.wait()
+        slot = i % 2
+        source = own_ref if i == 0 else rows_in.at[order[i]]
+        proj[...] = matmul(source[...].reshape(rows, columns), gate_up_ref[...])
+
+        def one(j, carry):
+            at = pl.ds(pl.multiple_of(j * step, step), step)
+            gate, up = proj[at, :units], proj[at, units:]
+            square = gate * gate
+            bend = jnp.tanh(gelu_inner * gate * (1.0 + gelu_cubic * square))
+            half = 0.5 * (1.0 + bend)
+            value = gate * half
+            slope = half + 0.5 * gate * (1.0 - bend * bend) * (
+                gelu_inner * (1.0 + 3.0 * gelu_cubic * square)
+            )
+            to_gate[slot, at, :] = slope * up
+            to_up[slot, at, :] = value
+            act[slot, at, :] = (value * up).astype(act.dtype)
+            return carry
+
+        lax.fori_loop(0, rows // step, one, 0)
+        result = matmul(act[slot], down[...]).astype(part.dtype)
+        part[slot] = result.reshape(pieces, piece, result.shape[1])
+        for put in puts(i):
+            put.start()
+
+    pad_rows(down, down_ref)
+    greet(cube_places())
+    cube_spread(own_ref, rows_in, send_sems, recv_sems, local_sem, compute)
+    for i in (len(order) - 2, len(order) - 1):
+        for put in puts(i):
+            put.wait()
+
+
+def gather_forward(own, gate_up, down, collective_id):
+    rows, depth = own.shape
+    members, piece = 16, 16
+    pieces = rows // piece
     units, columns = gate_up.shape[1] // 2, down.shape[1]
-    low = rows_in.dtype
+    low, wide = own.dtype, jnp.float32
+    shape = jax.ShapeDtypeStruct
+    vmem, anywhere = pl.BlockSpec(memory_space=pltpu.VMEM), pl.BlockSpec(memory_space=pl.ANY)
     return pl.pallas_call(
-        ffn_forward_kernel,
-        grid=(rows // ROW_BLOCK,),
-        in_specs=[row_block(depth), whole(gate_up), whole(down)],
-        out_specs=[row_block(columns), row_block(units), row_block(units), row_block(units)],
+        gather_forward_kernel,
         out_shape=[
-            jax.ShapeDtypeStruct((rows, columns), low),
-            jax.ShapeDtypeStruct((rows, units), low),
-            jax.ShapeDtypeStruct((rows, units), jnp.float32),
-            jax.ShapeDtypeStruct((rows, units), jnp.float32),
+            shape((members, pieces, piece, depth), low),
+            shape((members, pieces, piece, columns), low),
+            shape((members * rows, units), low),
+            shape((members * rows, units), wide),
+            shape((members * rows, units), wide),
         ],
+        in_specs=[vmem, vmem, vmem],
+        out_specs=[anywhere] * 5,
         scratch_shapes=[
+            pltpu.VMEM((members, pieces, piece, depth), low),
             pltpu.VMEM((units, columns), low),
-            pltpu.VMEM((ROW_BLOCK, 2 * units), jnp.float32),
+            pltpu.VMEM((rows, 2 * units), wide),
+            pltpu.VMEM((2, pieces, piece, columns), low),
+            pltpu.VMEM((2, rows, units), low),
+            pltpu.VMEM((2, rows, units), wide),
+            pltpu.VMEM((2, rows, units), wide),
+            pltpu.SemaphoreType.DMA((5, 2)),
+            *gather_sems(21),
         ],
-        cost_estimate=busy(20),
-        compiler_params=pltpu.CompilerParams(vmem_limit_bytes=VMEM_BYTES),
-    )(rows_in, gate_up, down)
+        cost_estimate=busy(40),
+        compiler_params=pltpu.CompilerParams(
+            collective_id=collective_id, has_side_effects=True, vmem_limit_bytes=60 * 2**20
+        ),
+    )(own.reshape(pieces, piece, depth), gate_up, down)
 
 
 def gather_backward_kernel(
-    own_ref, down_ref, gate_up_ref, to_gate_hbm, to_up_hbm, act_hbm, grad_ref, both_ref, part_ref,
-    down_grad_ref, down, to_gate, to_up, act, act_sem, load_sems, send_sems, recv_sems, local_sem,
+    own_ref, down_ref, gate_up_ref, to_gate_hbm, to_up_hbm, act_hbm, both_hbm, part_hbm, down_grad_ref,
+    grad, down, to_gate, to_up, act, both, part, act_sem, load_sems, put_sems, send_sems, recv_sems, local_sem,
 ):
     units = down.shape[0]
     pieces, piece, columns = own_ref.shape
     rows = pieces * piece
-    order = [cube_member(*flips) for flips in CUBE_ORDER]
+    order, places = block_order(rows)
 
     def loads(i):
-        at = pl.ds(pl.multiple_of(order[i] * rows, rows), rows)
-        slot = i % 2
+        slot, at = i % 2, places[i]
         return (
             pltpu.make_async_copy(to_gate_hbm.at[at], to_gate.at[slot], load_sems.at[0, slot]),
             pltpu.make_async_copy(to_up_hbm.at[at], to_up.at[slot], load_sems.at[1, slot]),
+        )
+
+    def puts(i):
+        slot = i % 2
+        return (
+            pltpu.make_async_copy(both.at[slot], both_hbm.at[places[i]], put_sems.at[0, slot]),
+            pltpu.make_async_copy(part.at[slot], part_hbm.at[order[i]], put_sems.at[1, slot]),
         )
 
     def compute(i):
@@ -646,14 +678,18 @@
                 load.start()
         for load in loads(i):
             load.wait()
-        block, slot = order[i], i % 2
-        at = pl.ds(pl.multiple_of(block * rows, rows), rows)
-        source = own_ref if i == 0 else grad_ref.at[block]
+        if i >= 2:
+            for put in puts(i - 2):
+                put.wait()
+        slot = i % 2
+        source = own_ref if i == 0 else grad.at[order[i]]
         act_grad = contract_cols(source[...].reshape(rows, columns), down[...])
-        both_ref[at, :units] = (act_grad * to_gate[slot]).astype(both_ref.dtype)
-        both_ref[at, units:] = (act_grad * to_up[slot]).astype(both_ref.dtype)
-        part = contract_cols(both_ref[at, :], gate_up_ref[...]).astype(part_ref.dtype)
-        part_ref[block] = part.reshape(pieces, piece, part.shape[1])
+        both[slot, :, :units] = (act_grad * to_gate[slot]).astype(both.dtype)
+        both[slot, :, units:] = (act_grad * to_up[slot]).astype(both.dtype)
+        result = contract_cols(both[slot], gate_up_ref[...]).astype(part.dtype)
+        part[slot] = result.reshape(pieces, piece, result.shape[1])
+        for put in puts(i):
+            put.start()
 
     act_load = pltpu.make_async_copy(act_hbm, act, act_sem)
     act_load.start()
@@ -661,44 +697,51 @@
         load.start()
     pad_rows(down, down_ref)
     greet(cube_places())
-    cube_spread(own_ref, grad_ref, send_sems, recv_sems, local_sem, compute)
+    cube_spread(own_ref, grad, send_sems, recv_sems, local_sem, compute)
     act_load.wait()
-    grad = grad_ref[...].reshape(len(order) * rows, columns)
-    down_grad = contract_rows(act[...], grad)
+    whole = grad[...].reshape(len(order) * rows, columns)
+    down_grad = contract_rows(act[...], whole)
     down_grad_ref[...] = down_grad[: down_ref.shape[0]].astype(down_grad_ref.dtype)
+    for i in (len(order) - 2, len(order) - 1):
+        for put in puts(i):
+            put.wait()
 
 
 def gather_backward(own, down, gate_up, to_gate, to_up, act, collective_id):
     rows, columns = own.shape
     members, piece = 16, 16
+    pieces = rows // piece
     depth, units = gate_up.shape[0], to_gate.shape[1]
-    low = own.dtype
+    low, wide = own.dtype, jnp.float32
+    shape = jax.ShapeDtypeStruct
     vmem, anywhere = pl.BlockSpec(memory_space=pltpu.VMEM), pl.BlockSpec(memory_space=pl.ANY)
-    grad, both, part, down_grad = pl.pallas_call(
+    return pl.pallas_call(
         gather_backward_kernel,
         out_shape=[
-            jax.ShapeDtypeStruct((members, rows // piece, piece, columns), low),
-            jax.ShapeDtypeStruct((members * rows, 2 * units), low),
-            jax.ShapeDtypeStruct((members, rows // piece, piece, depth), low),
-            jax.ShapeDtypeStruct(down.shape, low),
+            shape((members * rows, 2 * units), low),
+            shape((members, pieces, piece, depth), low),
+            shape(down.shape, low),
         ],
         in_specs=[vmem, vmem, vmem, anywhere, anywhere, anywhere],
-        out_specs=[vmem, vmem, vmem, vmem],
+        out_specs=[anywhere, anywhere, vmem],
         scratch_shapes=[
+            pltpu.VMEM((members, pieces, piece, columns), low),
             pltpu.VMEM((units, columns), low),
-            pltpu.VMEM((2, rows, units), jnp.float32),
-            pltpu.VMEM((2, rows, units), jnp.float32),
+            pltpu.VMEM((2, rows, units), wide),
+            pltpu.VMEM((2, rows, units), wide),
             pltpu.VMEM(act.shape, low),
+            pltpu.VMEM((2, rows, 2 * units), low),
+            pltpu.VMEM((2, pieces, piece, depth), low),
             pltpu.SemaphoreType.DMA,
+            pltpu.SemaphoreType.DMA((2, 2)),
             pltpu.SemaphoreType.DMA((2, 2)),
             *gather_sems(21),
         ],
-        cost_estimate=busy(35),
+        cost_estimate=busy(45),
         compiler_params=pltpu.CompilerParams(
             collective_id=collective_id, has_side_effects=True, vmem_limit_bytes=60 * 2**20
         ),
-    )(own.reshape(rows // piece, piece, columns), down, gate_up, to_gate, to_up, act)
-    return both, part, down_grad
+    )(own.reshape(pieces, piece, columns), down, gate_up, to_gate, to_up, act)
 
 
 def sum_gradients_kernel(
@@ -728,7 +771,7 @@
         gate_up_ref[pl.ds(i * step, step), :] = rows.astype(gate_up_ref.dtype)
 
     def work(point):
-        spread = ((0,), (1,), (2, 3), tuple(range(4, blocks)))
+        spread = ((), (0, 1), (2, 3), tuple(range(4, blocks)))
         for i in spread[point]:
             rows_of(i)
 
@@ -759,7 +802,7 @@
             jax.ShapeDtypeStruct((depth, both.shape[1]), low),
             jax.ShapeDtypeStruct(down.shape[1:], jnp.float32),
         ],
-        in_specs=[vmem, vmem, anywhere, anywhere],
+        in_specs=[anywhere, vmem, anywhere, anywhere],
         out_specs=[vmem, vmem, vmem],
         scratch_shapes=[
             pltpu.VMEM((2, rows_in.shape[0], step), low),
@@ -1182,10 +1225,10 @@
     output_wide = jnp.pad(output_weight, ((0, 0), (0, qkv_width - output_weight.shape[1])))
     packed = jnp.concatenate([packed, output_wide], axis=0)
     packed_all = z_gather(packed, planes, 0)
+    gate_up, packed_all = lax.optimization_barrier((gate_up, packed_all))
+    gate_up_full = exchange(gate_up, ALL).reshape(devices * padded, 2 * unit_pad)
     packed_all, down_full = weights_gather(packed_all, down_weight, cubes, 6)
     down_full = down_full.reshape(unit_count, down_weight.shape[1])
-    gate_up, packed_all = lax.optimization_barrier((gate_up, packed_all))
-    gate_up_full = exchange(gate_up, ALL).reshape(devices * padded, 2 * unit_pad)
     incoming = cotangent[0].astype(f32)
     local_rows = tokens.shape[1]
     offset = lax.axis_index("seq") * local_rows
@@ -1240,8 +1283,10 @@
     )
     ffnout_scale = scales.pop()
 
-    cube_in = gather_rows(ffn_in_placed, 1)
-    ffn_part, activated_low, to_gate, to_up = ffn_forward(cube_in, gate_up_full, down_full)
+    cube_in, ffn_part, activated_low, to_gate, to_up = gather_forward(
+        ffn_in_placed, gate_up_full, down_full, 1
+    )
+    cube_in = cube_in.reshape(-1, cube_in.shape[-1])
     ffn_raw = cube_scatter_sum(ffn_part, 2)
     inv_ffn = inverse_rms(ffn_raw)
     norm_ffn = ffn_raw * inv_ffn

time: 486 us -> 488 us (level)
  Pallas kernels: 417 us -> 426 us
    pallas_call x1, Pallas kernels: 34.2 us -> 71.9 us  [weights_gather(): pl.pallas_call(functools.partial(weights_gather_kernel, cubes), out_shape...]
    pallas_call x3 -> x2, Pallas kernels: 145 us -> 125 us  [the longest x1 63.8 us: gather_forward(): pl.pallas_call(gather_forward_kernel, out_shape=[shape((members, pieces,...]
  transfers between devices with their start and end apart: 3 -> 3, of which waited for: 0 -> 0; matrix products, arithmetic and copies ran while one was open for 6% -> 6% of each run, Pallas kernels for 47% -> 44%
where the time goes in v9:
time: 488 us; the launch traced here: 483 us
  Pallas kernels  426 us (87%)
  local copies, waits for them, and re-layouts  28.9 us (6%)
  other arithmetic  11.6 us (2%)
  starting transfers between devices  11.5 us (2%)
    pallas_call x1, Pallas kernels, weights_gather(): pl.pallas_call(functools.partial(weights_gather_kernel, cubes), out_shape...  71.9 us
    pallas_call x1, Pallas kernels, owner_sum(): pl.pallas_call(functools.partial(owner_sum_kernel, planes), out_shape=jax...  67.2 us
    pallas_call x1, Pallas kernels, gather_forward(): pl.pallas_call(gather_forward_kernel, out_shape=[shape((members, pieces,...  63.8 us
    pallas_call x1, Pallas kernels, gather_backward(): pl.pallas_call(gather_backward_kernel, out_shape=[shape((members * rows,...  61 us
    pallas_call x1, Pallas kernels, sum_gradients(): pl.pallas_call(sum_gradients_kernel, out_shape=[jax.ShapeDtypeStruct((pie...  49.5 us
    pallas_call x1, Pallas kernels, cube_scatter_sum(): pl.pallas_call(cube_sum_kernel, out_shape=jax.ShapeDtypeStruct(shape, jnp...  41.1 us
    pallas_call x1, Pallas kernels, attention_backward(): pl.pallas_call(functools.partial(attention_backward_kernel, gain_at, widt...  33.8 us
    pallas_call x1, Pallas kernels, z_gather(): pl.pallas_call(functools.partial(z_gather_kernel, planes), out_shape=jax....  22.5 us
  transfers between devices with their start and end apart: 3, of which 0 were waited for; matrix products, arithmetic and copies ran while one was open for 6% of the time, Pallas kernels for 44%

profile of v9, /device:TPU:8, one launch (start us, length us, event | category | flops | bytes accessed | tf_op | source)
XLA Modules:
  0.0 482.8 jit_solution(5380954689317436793)
XLA Ops:
  0.7 1.6 collective-permute-start
  2.2 4.1 concatenate.21
  6.4 2.9 reshape.148
  10.2 1.7 reshape.150
  13.0 0.7 copy.51
  13.9 22.5 %shard_map.271.own_ref = bf16[4,72,1536]{2,1,0:T(8,128)(2,1)S(1)} custom-call(bf16[72,1536]{1,0:T(8,128)(2,1)S(1)} %fusion.27.own_ref), custom_call_target="tpu_custom_call" | custom-call | bytes 60000000 | tf_op jit(solution)/shard_map/pallas_call | solution.py:327
  36.4 1.9 broadcast_in_dim.12
  38.3 5.3 %all-to-all-start = ((bf16[32,40,1024]{2,1,0:T(8,128)(2,1)}), bf16[32,40,1024]{2,1,0:T(8,128)(2,1)}, u32[]{:S(2)}, u32[]{:S(2)}) async-start(bf16[32,40,1024]{2,1,0:T(8,128)(2,1)} %bitcast.3), calls=%async_computation | async-start | bytes 5242880 | tf_op jit(solution)/shard_map/all_to_all | solution.py:87
  43.8 5.3 %fusion.38 = (bf16[1152,1280]{1,0:T(8,128)(2,1)}, bf16[1152,1280]{1,0:T(8,128)(2,1)}) fusion(s32[1152]{0:T(1024)S(1)} %get-tuple-element.105, s32[1152]{0:T(1024)S(1)} %get-tuple-element.106, pred[1152]{0:T(1024)(128)(4,1)S(1)} %get-tuple-element.108, s32[1152]{0:T(1024)S(1)} %get-tuple-element.104, s32[1152]{0:T(1024)S(1)} %get-tuple-element.107, ...), kind=kLoop, calls=%fused_computation.83 | loop fusion | flops 45711360 | bytes 5918976 | tf_op jit(solution)/shard_map/convert_element_type | solution.py:69
  49.1 0.8 copy.52.segment_column
  49.9 71.9 %shard_map.272 = (bf16[8,4,72,1536]{3,2,1,0:T(8,128)(2,1)}, bf16[2,216,1152]{2,1,0:T(8,128)(2,1)S(1)}) custom-call(bf16[4,72,1536]{2,1,0:T(8,128)(2,1)S(1)} %shard_map.271.own_ref, bf16[216,1152]{1,0:T(8,128)(2,1)S(1)} %copy-done.1), custom_call_target="tpu_custom_call" | custom-call | bytes 90000000 | tf_op jit(solution)/shard_map/pallas_call | solution.py:347
  122.1 1.8 multiply_sine_fusion
  124.0 3.8 convolution_convert_fusion.row_ref
  127.9 14.8 %shard_map.273 = (bf16[256,1280]{1,0:T(8,128)(2,1)}, f32[256,1152]{1,0:T(8,128)}, f32[256,1152]{1,0:T(8,128)}, bf16[256,1024]{1,0:T(8,128)(2,1)}, f32[4,256,512]...) custom-call(bf16[512,1280]{1,0:T(8,128)(2,1)} %convolution_convert_f, ...), custom_call_target="tpu_custom_call" | custom-call | bytes 60000000 | tf_op jit(solution)/shard_map/pallas_call | solution.py:1016
  142.7 0.7 reduce.1
  143.4 63.8 %shard_map.274 = (bf16[16,16,16,1280]{3,2,1,0:T(8,128)(2,1)}, bf16[16,16,16,1152]{3,2,1,0:T(8,128)(2,1)}, bf16[4096,512]{1,0:T(8,128)(2,1)}, f32[4096,512]{1,0:T(8,128)}, f32[4096,512]{1,0:T(8,128)}) custom-call(bf16[16,16,1280]{2,1,0:T(8,128)(2,1)} %bitcast.77, bf16[1280,1024]{1,0:T(8,128)(2,1)} %bitcast.7.gate_up_ref, bf16[432,1152]{1,0:T(8,128)(2,1)} %bitcast.61), custom_call_target="tpu_custom_call" | custom-call | bytes 120000000 | tf_op jit(solution)/shard_map/pallas_call | solution.py:623
  207.2 41.1 %shard_map.275 = f32[16,16,1152]{2,1,0:T(8,128)S(1)} custom-call(bf16[16,16,16,1152]{3,2,1,0:T(8,128)(2,1)} %get-tuple-element.56.part_ref), custom_call_target="tpu_custom_call" | custom-call | bytes 105000000 | tf_op jit(solution)/shard_map/pallas_call | solution.py:523
  248.6 1.3 fusion.15
  250.0 1.1 fusion.21.own_ref
  251.1 61.0 %shard_map.276 = (bf16[4096,1024]{1,0:T(8,128)(2,1)}, bf16[16,16,16,1280]{3,2,1,0:T(8,128)(2,1)}, bf16[432,1152]{1,0:T(8,128)(2,1)}) custom-call(bf16[16,16,1152]{2,1,0:T(8,128)(2,1)} %fusion.21.own_ref, bf16[432,1152]{1,0:T(8,128)(2,1)} %bitcast.62, bf16[1280,1024]{1,0:T(8,128)(2,1)} %bitcast.7.gate_up_ref, f32[4096,512]{1,0:T(8,128)} %get-tuple-element.58.to_gate_hbm, ...), custom_call_target="tpu_custom_call" | custom-call | bytes 135000000 | tf_op jit(solution)/shard_map/pallas_call | solution.py:718
  312.1 49.5 %shard_map.277 = (f32[16,16,1280]{2,1,0:T(8,128)}, bf16[1280,1024]{1,0:T(8,128)(2,1)}, f32[216,1152]{1,0:T(8,128)}) custom-call(bf16[16,16,16,1280]{3,2,1,0:T(8,128)(2,1)} %get-tuple-element.61.part_ref, bf16[2,216,1152]{2,1,0:T(8,128)(2,1)} %bitcast.76, bf16[4096,1280]{1,0:T(8,128)(2,1)} %bitcast.63, bf16[4096,1024]{1,0:T(8,128)(2,1)} %get-tuple-element.64.both_hbm), custom_call_target="tpu_custom_call" | custom-call | bytes 105000000 | tf_op jit(solution)/shard_map/pallas_call | solution.py:798
  361.6 4.6 all-to-all-start.1
  366.8 33.8 %shard_map.278 = (f32[256,1152]{1,0:T(8,128)}, bf16[8,4,72,1536]{3,2,1,0:T(8,128)(2,1)}) custom-call(f32[256,1280]{1,0:T(8,128)} %bitcast.74, bf16[256,1152]{1,0:T(8,128)(2,1)} %bitcast.65, f32[256,1152]{1,0:T(8,128)} %get-tuple-element.52.middle_ref, f32[256,1152]{1,0:T(8,128)} %get-tuple-element.66.raw_ref, bf16[256,1024]{1,0:T(8,128)(2,1)} %get-tuple-element.67.mix_ref, ...), custom_call_target="tpu_custom_call" | custom-call | bytes 90000000 | tf_op jit(solution)/shard_map/pallas_call | solution.py:1145
  400.6 67.2 %shard_map.279 = f32[72,1536]{1,0:T(8,128)S(1)} custom-call(bf16[8,4,72,1536]{3,2,1,0:T(8,128)(2,1)} %get-tuple-element.82.part_ref), custom_call_target="tpu_custom_call" | custom-call | bytes 105000000 | tf_op jit(solution)/shard_map/pallas_call | solution.py:852
  468.5 0.7 slice.50
  471.8 2.1 reshape.168
  473.9 1.7 copy.56
  475.5 1.8 reshape.164
  477.3 1.0 reshape.167
  478.8 1.8 reshape.162
  480.6 1.0 copy.67
  481.6 0.9 copy.68
  (59 shorter events, 7.1 us)
Async XLA Ops:
  0.6 9.5 %copy-start.7 = (bf16[36,6912]{1,0:T(8,128)(2,1)S(1)}, bf16[36,6912]{1,0:T(8,128)(2,1)}, u32[]{:S(2)}) copy-start(bf16[36,6912]{1,0:T(8,128)(2,1)} %param.24) | copy-start | bytes 1492996
  0.7 123.3 %collective-permute-start = (bf16[256,1152]{1,0:T(8,128)(2,1)}, bf16[256,1152]{1,0:T(8,128)(2,1)S(1)}, u32[]{:S(2)}, u32[]{:S(2)}) collective-permute-start(bf16[256,1152]{1,0:T(8,128)(2,1)} %bitcast.72), channel_id=1, source_target_pairs={{0,1},{1,0},{2,3},{3,2},{4,5},{5,4},{6,7},{7,6},{8,9},{9,8},{10,11... | collective-permute-start | bytes 1769480 | tf_op jit(solution)/shard_map/ppermute | solution.py:1244
  12.8 1.0 copy-start.8
  12.8 1.0 copy-start.11
  12.8 1.0 copy-start.12
  12.8 1.0 copy-start.9
  38.3 5.4 %copy-start.10 = (s32[1,512]{1,0:T(1,128)S(1)}, s32[1,512]{1,0:T(1,128)}, u32[]{:S(2)}) copy-start(s32[1,512]{1,0:T(1,128)} %segment_row.1) | copy-start | bytes 6148
  38.3 105.0 %all-to-all-start = ((bf16[32,40,1024]{2,1,0:T(8,128)(2,1)}), bf16[32,40,1024]{2,1,0:T(8,128)(2,1)}, u32[]{:S(2)}, u32[]{:S(2)}) async-start(bf16[32,40,1024]{2,1,0:T(8,128)(2,1)} %bitcast.3), calls=%async_computation | async-start | bytes 5242880 | tf_op jit(solution)/shard_map/all_to_all | solution.py:87
  43.8 6.2 %copy-start.1 = (bf16[216,1152]{1,0:T(8,128)(2,1)S(1)}, bf16[216,1152]{1,0:T(8,128)(2,1)}, u32[]{:S(2)}) copy-start(bf16[216,1152]{1,0:T(8,128)(2,1)} %down_ref.1) | copy-start | bytes 1492996
  43.8 80.1 %copy-start.4 = (bf16[1,256,1152]{2,1,0:T(8,128)(2,1)S(1)}, bf16[1,256,1152]{2,1,0:T(8,128)(2,1)}, u32[]{:S(2)}) copy-start(bf16[1,256,1152]{2,1,0:T(8,128)(2,1)} %param.16) | copy-start | bytes 1769476
  121.8 6.0 %copy-start = (bf16[2,216,1152]{2,1,0:T(8,128)(2,1)}, bf16[2,216,1152]{2,1,0:T(8,128)(2,1)S(1)}, u32[]{:S(2)}) copy-start(bf16[2,216,1152]{2,1,0:T(8,128)(2,1)S(1)} %get-tuple-element.55) | copy-start | bytes 2985988
  207.2 41.4 %copy-start.2 = (bf16[1,256,1152]{2,1,0:T(8,128)(2,1)S(1)}, bf16[1,256,1152]{2,1,0:T(8,128)(2,1)}, u32[]{:S(2)}) copy-start(bf16[1,256,1152]{2,1,0:T(8,128)(2,1)} %param.18) | copy-start | bytes 1769476
  207.2 41.4 %copy-start.3 = (f32[256,1152]{1,0:T(8,128)S(1)}, f32[256,1152]{1,0:T(8,128)}, u32[]{:S(2)}) copy-start(f32[256,1152]{1,0:T(8,128)} %get-tuple-element.52.middle_ref) | copy-start | bytes 3538948
  361.6 109.4 %all-to-all-start.1 = ((bf16[32,40,1024]{2,1,0:T(8,128)(2,1)}), bf16[32,40,1024]{2,1,0:T(8,128)(2,1)S(1)}, u32[]{:S(2)}, u32[]{:S(2)}) async-start(bf16[32,40,1024]{2,1,0:T(8,128)(2,1)} %bitcast.69), calls=%async_computation.1 | async-start | bytes 5242880 | tf_op jit(solution)/shard_map/all_to_all | solution.py:87
  478.8 1.8 copy-start.5
  478.8 2.8 copy-start.6

commit v10 on v8

--- a/solution.py
+++ b/solution.py
@@ -291,19 +291,9 @@
     cube_spread(own_ref, out_ref, *sems)
 
 
-def weights_gather_kernel(cubes, own_ref, down_ref, out_ref, down_out, far_send, far_recv, own_sem, *sems):
-    far, others = other_cubes(cubes)
-    greet((*plane_places()[:3], *others))
-    keep = pltpu.make_async_copy(down_ref, down_out.at[far], own_sem)
-    keep.start()
-    send = sender(far_send, far_recv)
-    copies = [send(k, down_ref, down_out.at[far], place) for k, place in enumerate(others)]
+def plane_gather_kernel(own_ref, out_ref, *sems):
+    greet(plane_places()[:3])
     plane_spread(own_ref, out_ref, *sems)
-    for copy in copies:
-        copy.wait_recv()
-    for copy in copies:
-        copy.wait_send()
-    keep.wait()
 
 
 def z_gather_kernel(planes, own_ref, out_ref, send_sems, recv_sems, own_sem):
@@ -346,28 +336,19 @@
     )(local)
 
 
-def weights_gather(local, down, cubes, collective_id):
+def plane_gather(local, collective_id):
     members = 8
-    anywhere = pl.BlockSpec(memory_space=pl.ANY)
     return pl.pallas_call(
-        functools.partial(weights_gather_kernel, cubes),
-        out_shape=[
-            jax.ShapeDtypeStruct((members, *local.shape), local.dtype),
-            jax.ShapeDtypeStruct((cubes, *down.shape), down.dtype),
-        ],
-        in_specs=[anywhere, anywhere],
-        out_specs=[anywhere, anywhere],
-        scratch_shapes=[
-            pltpu.SemaphoreType.DMA((cubes - 1,)),
-            pltpu.SemaphoreType.DMA((cubes - 1,)),
-            pltpu.SemaphoreType.DMA,
-            *gather_sems(13),
-        ],
+        plane_gather_kernel,
+        out_shape=jax.ShapeDtypeStruct((members, *local.shape), local.dtype),
+        in_specs=[pl.BlockSpec(memory_space=pl.ANY)],
+        out_specs=pl.BlockSpec(memory_space=pl.ANY),
+        scratch_shapes=gather_sems(13),
         cost_estimate=busy(30),
         compiler_params=pltpu.CompilerParams(
             collective_id=collective_id, has_side_effects=True, vmem_limit_bytes=VMEM_BYTES
         ),
-    )(local, down)
+    )(local)
 
 
 def gather_rows(local, collective_id):
@@ -437,8 +418,8 @@
 
 
 def cube_sum(
-    part_ref, own_sum, near, via_z, zx_in, zy_in, far_x, far_y, from_x, from_y, from_z, send_sems, recv_sems,
-    work=lambda point: None,
+    part_hbm, own_sum, mine, near, via_z, zx_in, zy_in, far_x, far_y, from_x, from_y, from_z, load_sems, send_sems,
+    recv_sems, work=lambda point: None,
 ):
     sibling, along_x, along_y, along_z = cube_places()
     pieces = own_sum.shape[0]
@@ -447,33 +428,42 @@
     send = sender(send_sems, recv_sems)
     chips = ((1, 1, 1), (1, 1, 0), (1, 0, 1), (0, 1, 0), (0, 0, 1), (0, 1, 1), (1, 0, 0), (0, 0, 0))
     z_diagonal, z_x, z_y, at_x, at_y, diagonal, at_z, here = range(8)
-    mine = [part_ref.at[cube_member(*chip, 0)] for chip in chips]
     to_sibling = [
-        send(k, part_ref.at[cube_member(*chip, 1)], near.at[k], sibling)
+        send(k, part_hbm.at[cube_member(*chip, 1)], near.at[k], sibling)
         for k, chip in enumerate(chips)
     ]
+    loads = [
+        pltpu.make_async_copy(part_hbm.at[cube_member(*chip, 0)], mine.at[k], load_sems.at[k])
+        for k, chip in enumerate(chips)
+    ]
+    for load in loads:
+        load.start()
+
+    def both_in(k):
+        to_sibling[k].wait_recv()
+        loads[k].wait()
 
     def add(k, others=(), start=0, count=pieces):
-        add_rows(near.at[k], (mine[k], near.at[k], *others), start, count)
+        add_rows(near.at[k], (mine.at[k], near.at[k], *others), start, count)
 
     work(0)
-    to_sibling[z_diagonal].wait_recv()
+    both_in(z_diagonal)
     add(z_diagonal)
     diagonal_z = send(8, near.at[z_diagonal], via_z, along_z)
-    to_sibling[z_x].wait_recv()
+    both_in(z_x)
     add(z_x)
     zx_out = send(9, near.at[z_x], zx_in, along_x)
-    to_sibling[z_y].wait_recv()
+    both_in(z_y)
     add(z_y)
     zy_out = send(10, near.at[z_y], zy_in, along_y)
-    to_sibling[at_x].wait_recv()
+    both_in(at_x)
     add(at_x, (), half, half)
     direct_x = send(13, near.at[at_x, bottom], from_x.at[bottom], along_x)
-    to_sibling[at_y].wait_recv()
+    both_in(at_y)
     add(at_y, (), 0, half)
     direct_y = send(14, near.at[at_y, top], from_y.at[top], along_y)
-    to_sibling[diagonal].wait_recv()
-    to_sibling[at_z].wait_recv()
+    both_in(diagonal)
+    both_in(at_z)
     work(1)
     diagonal_z.wait_recv()
     add(diagonal, (via_z,))
@@ -490,11 +480,11 @@
     diagonal_x.wait_recv()
     add(at_y, (far_x,), half, half)
     joint_y = send(17, near.at[at_y, bottom], from_y.at[bottom], along_y)
-    to_sibling[here].wait_recv()
+    both_in(here)
     work(3)
     for copy in (direct_x, direct_y, joint_z, joint_x, joint_y):
         copy.wait_recv()
-    add_rows(own_sum, (mine[here], near.at[here], from_x, from_y, from_z), 0, pieces)
+    add_rows(own_sum, (mine.at[here], near.at[here], from_x, from_y, from_z), 0, pieces)
     for copy in (
         *to_sibling, diagonal_z, zx_out, zy_out, direct_x, direct_y, diagonal_x, diagonal_y, joint_z, joint_x, joint_y,
     ):
@@ -509,7 +499,9 @@
 def cube_sum_scratch(shape, dtype):
     return [
         pltpu.VMEM((8, *shape), dtype),
+        pltpu.VMEM((8, *shape), dtype),
         *[pltpu.VMEM(shape, dtype)] * 8,
+        pltpu.SemaphoreType.DMA((8,)),
         pltpu.SemaphoreType.DMA((18,)),
         pltpu.SemaphoreType.DMA((18,)),
     ]
@@ -530,21 +522,19 @@
 
 
 def cube_scatter_sum(partial, collective_id):
-    members = 16
-    rows, columns = partial.shape[0] // members, partial.shape[1]
-    shape = (rows // 16, 16, columns)
+    shape = partial.shape[1:]
     out = pl.pallas_call(
         cube_sum_kernel,
         out_shape=jax.ShapeDtypeStruct(shape, jnp.float32),
-        in_specs=[pl.BlockSpec(memory_space=pltpu.VMEM)],
+        in_specs=[pl.BlockSpec(memory_space=pl.ANY)],
         out_specs=pl.BlockSpec(memory_space=pltpu.VMEM),
         scratch_shapes=cube_sum_scratch(shape, partial.dtype),
         cost_estimate=busy(35),
         compiler_params=pltpu.CompilerParams(
             collective_id=collective_id, has_side_effects=True, vmem_limit_bytes=VMEM_BYTES
         ),
-    )(partial.reshape(members, *shape))
-    return out.reshape(rows, columns)
+    )(partial)
+    return out.reshape(shape[0] * shape[1], shape[2])
 
 
 gelu_inner = 0.7978845608028654
@@ -623,21 +613,32 @@
     )(rows_in, gate_up, down)
 
 
+def block_order(rows):
+    order = [cube_member(*flips) for flips in CUBE_ORDER]
+    return order, [pl.ds(pl.multiple_of(block * rows, rows), rows) for block in order]
+
+
 def gather_backward_kernel(
-    own_ref, down_ref, gate_up_ref, to_gate_hbm, to_up_hbm, act_hbm, grad_ref, both_ref, part_ref,
-    down_grad_ref, down, to_gate, to_up, act, act_sem, load_sems, send_sems, recv_sems, local_sem,
+    own_ref, down_ref, gate_up_ref, to_gate_hbm, to_up_hbm, act_hbm, both_hbm, part_hbm, down_grad_ref,
+    grad, down, to_gate, to_up, act, both, part, act_sem, load_sems, put_sems, send_sems, recv_sems, local_sem,
 ):
     units = down.shape[0]
     pieces, piece, columns = own_ref.shape
     rows = pieces * piece
-    order = [cube_member(*flips) for flips in CUBE_ORDER]
+    order, places = block_order(rows)
 
     def loads(i):
-        at = pl.ds(pl.multiple_of(order[i] * rows, rows), rows)
-        slot = i % 2
+        slot, at = i % 2, places[i]
         return (
             pltpu.make_async_copy(to_gate_hbm.at[at], to_gate.at[slot], load_sems.at[0, slot]),
             pltpu.make_async_copy(to_up_hbm.at[at], to_up.at[slot], load_sems.at[1, slot]),
+        )
+
+    def puts(i):
+        slot = i % 2
+        return (
+            pltpu.make_async_copy(both.at[slot], both_hbm.at[places[i]], put_sems.at[0, slot]),
+            pltpu.make_async_copy(part.at[slot], part_hbm.at[order[i]], put_sems.at[1, slot]),
         )
 
     def compute(i):
@@ -646,14 +647,18 @@
                 load.start()
         for load in loads(i):
             load.wait()
-        block, slot = order[i], i % 2
-        at = pl.ds(pl.multiple_of(block * rows, rows), rows)
-        source = own_ref if i == 0 else grad_ref.at[block]
+        if i >= 2:
+            for put in puts(i - 2):
+                put.wait()
+        slot = i % 2
+        source = own_ref if i == 0 else grad.at[order[i]]
         act_grad = contract_cols(source[...].reshape(rows, columns), down[...])
-        both_ref[at, :units] = (act_grad * to_gate[slot]).astype(both_ref.dtype)
-        both_ref[at, units:] = (act_grad * to_up[slot]).astype(both_ref.dtype)
-        part = contract_cols(both_ref[at, :], gate_up_ref[...]).astype(part_ref.dtype)
-        part_ref[block] = part.reshape(pieces, piece, part.shape[1])
+        both[slot, :, :units] = (act_grad * to_gate[slot]).astype(both.dtype)
+        both[slot, :, units:] = (act_grad * to_up[slot]).astype(both.dtype)
+        result = contract_cols(both[slot], gate_up_ref[...]).astype(part.dtype)
+        part[slot] = result.reshape(pieces, piece, result.shape[1])
+        for put in puts(i):
+            put.start()
 
     act_load = pltpu.make_async_copy(act_hbm, act, act_sem)
     act_load.start()
@@ -661,44 +666,51 @@
         load.start()
     pad_rows(down, down_ref)
     greet(cube_places())
-    cube_spread(own_ref, grad_ref, send_sems, recv_sems, local_sem, compute)
+    cube_spread(own_ref, grad, send_sems, recv_sems, local_sem, compute)
     act_load.wait()
-    grad = grad_ref[...].reshape(len(order) * rows, columns)
-    down_grad = contract_rows(act[...], grad)
+    whole = grad[...].reshape(len(order) * rows, columns)
+    down_grad = contract_rows(act[...], whole)
     down_grad_ref[...] = down_grad[: down_ref.shape[0]].astype(down_grad_ref.dtype)
+    for i in (len(order) - 2, len(order) - 1):
+        for put in puts(i):
+            put.wait()
 
 
 def gather_backward(own, down, gate_up, to_gate, to_up, act, collective_id):
     rows, columns = own.shape
     members, piece = 16, 16
+    pieces = rows // piece
     depth, units = gate_up.shape[0], to_gate.shape[1]
-    low = own.dtype
+    low, wide = own.dtype, jnp.float32
+    shape = jax.ShapeDtypeStruct
     vmem, anywhere = pl.BlockSpec(memory_space=pltpu.VMEM), pl.BlockSpec(memory_space=pl.ANY)
-    grad, both, part, down_grad = pl.pallas_call(
+    return pl.pallas_call(
         gather_backward_kernel,
         out_shape=[
-            jax.ShapeDtypeStruct((members, rows // piece, piece, columns), low),
-            jax.ShapeDtypeStruct((members * rows, 2 * units), low),
-            jax.ShapeDtypeStruct((members, rows // piece, piece, depth), low),
-            jax.ShapeDtypeStruct(down.shape, low),
+            shape((members * rows, 2 * units), low),
+            shape((members, pieces, piece, depth), low),
+            shape(down.shape, low),
         ],
         in_specs=[vmem, vmem, vmem, anywhere, anywhere, anywhere],
-        out_specs=[vmem, vmem, vmem, vmem],
+        out_specs=[anywhere, anywhere, vmem],
         scratch_shapes=[
+            pltpu.VMEM((members, pieces, piece, columns), low),
             pltpu.VMEM((units, columns), low),
-            pltpu.VMEM((2, rows, units), jnp.float32),
-            pltpu.VMEM((2, rows, units), jnp.float32),
+            pltpu.VMEM((2, rows, units), wide),
+            pltpu.VMEM((2, rows, units), wide),
             pltpu.VMEM(act.shape, low),
+            pltpu.VMEM((2, rows, 2 * units), low),
+            pltpu.VMEM((2, pieces, piece, depth), low),
             pltpu.SemaphoreType.DMA,
+            pltpu.SemaphoreType.DMA((2, 2)),
             pltpu.SemaphoreType.DMA((2, 2)),
             *gather_sems(21),
         ],
-        cost_estimate=busy(35),
+        cost_estimate=busy(45),
         compiler_params=pltpu.CompilerParams(
             collective_id=collective_id, has_side_effects=True, vmem_limit_bytes=60 * 2**20
         ),
-    )(own.reshape(rows // piece, piece, columns), down, gate_up, to_gate, to_up, act)
-    return both, part, down_grad
+    )(own.reshape(pieces, piece, columns), down, gate_up, to_gate, to_up, act)
 
 
 def sum_gradients_kernel(
@@ -728,7 +740,7 @@
         gate_up_ref[pl.ds(i * step, step), :] = rows.astype(gate_up_ref.dtype)
 
     def work(point):
-        spread = ((0,), (1,), (2, 3), tuple(range(4, blocks)))
+        spread = ((), (0, 1), (2, 3), tuple(range(4, blocks)))
         for i in spread[point]:
             rows_of(i)
 
@@ -759,7 +771,7 @@
             jax.ShapeDtypeStruct((depth, both.shape[1]), low),
             jax.ShapeDtypeStruct(down.shape[1:], jnp.float32),
         ],
-        in_specs=[vmem, vmem, anywhere, anywhere],
+        in_specs=[anywhere, vmem, anywhere, anywhere],
         out_specs=[vmem, vmem, vmem],
         scratch_shapes=[
             pltpu.VMEM((2, rows_in.shape[0], step), low),
@@ -826,11 +838,13 @@
     )(blocks)
 
 
-def gain_places(blocks, planes, offset, count, per, by_member):
-    lane = lax.broadcasted_iota(jnp.int32, (256, blocks * per), 0)
-    column = lax.broadcasted_iota(jnp.int32, (256, blocks * per), 1)
-    inner = column % per
-    places = ((lane == offset + inner) & (inner < count)).astype(jnp.float32).astype(jnp.bfloat16)
+GAIN_SLOT = 128
+
+
+def gain_places(blocks, planes, count, per, by_member):
+    lane = lax.broadcasted_iota(jnp.int32, (GAIN_SLOT, blocks * per), 0)
+    inner = lax.broadcasted_iota(jnp.int32, (GAIN_SLOT, blocks * per), 1) % per
+    places = ((lane == inner) & (inner < count)).astype(jnp.float32).astype(jnp.bfloat16)
     listed = lax.broadcasted_iota(jnp.int32, (blocks, blocks * per), 0)
     block = lax.broadcasted_iota(jnp.int32, (blocks, blocks * per), 1) // per
     members = blocks // planes
@@ -865,7 +879,7 @@
 
 
 def attention_forward_kernel(
-    gain_at, width_rows, row_ref, hidden_ref, packed_ref, cos_ref, sin_ref, segment_column, segment_row, placing_ref,
+    gain_widths, width_rows, row_ref, hidden_ref, packed_ref, cos_ref, sin_ref, segment_column, segment_row, placing_ref,
     placed_ref, middle_ref, raw_ref, mix_ref, probs_ref, query_ref, key_ref, value_ref, query_raw_ref,
     key_raw_ref, qkv_ref, output_ref, input_scale, query_scale, key_scale, attnout_scale, ffnin_scale, ffnout_scale,
     gain_rows,
@@ -887,13 +901,11 @@
         qkv_ref[padded * i : padded * (i + 1), :] = block[:padded]
         natural = mix_rows * (plane * members + member)
         output_ref[natural : natural + mix_rows, :] = block[padded:, :width]
-        gain_rows[i : i + 1, :] = block[width_rows : width_rows + 1, :256].astype(f32)
-    rows = gain_rows[...].astype(bf16)
-    (at, count), *others = gain_at
-    input_scale[...] = spread_gain(rows, planes, at, count, padded, True)
-    targets = (query_scale, key_scale, attnout_scale, ffnin_scale, ffnout_scale)
-    for target, (at, count) in zip(targets, others):
-        target[...] = spread_gain(rows, planes, at, count, count, False)
+        gain_rows[i : i + 1, :] = block[width_rows : width_rows + 1, : gain_rows.shape[1]].astype(f32)
+    targets = (input_scale, query_scale, key_scale, attnout_scale, ffnin_scale, ffnout_scale)
+    for k, (target, count) in enumerate(zip(targets, gain_widths)):
+        rows = gain_rows[:, k * GAIN_SLOT : (k + 1) * GAIN_SLOT].astype(bf16)
+        target[...] = spread_gain(rows, planes, count, count if k else padded, k == 0)
 
     row = row_ref[...].astype(f32)
     normed = (row * inverse_of(row, width) * input_scale[...]).astype(bf16)
@@ -937,7 +949,7 @@
 
 
 def attention_forward(
-    row_padded, hidden, packed, cos_full, sin_full, segment_column, segment_row, placing, gain_at, width_rows, padded,
+    row_padded, hidden, packed, cos_full, sin_full, segment_column, segment_row, placing, gain_widths, width_rows, padded,
     head_width,
 ):
     bf16, f32 = jnp.bfloat16, jnp.float32
@@ -971,18 +983,18 @@
         shape((1, width), f32),
     ]
     return pl.pallas_call(
-        functools.partial(attention_forward_kernel, gain_at, width_rows),
+        functools.partial(attention_forward_kernel, gain_widths, width_rows),
         out_shape=out_shape,
         in_specs=[vmem] * 8,
         out_specs=[vmem] * len(out_shape),
-        scratch_shapes=[pltpu.VMEM((blocks, 256), f32)],
+        scratch_shapes=[pltpu.VMEM((blocks, len(gain_widths) * GAIN_SLOT), f32)],
         cost_estimate=busy(20),
         compiler_params=pltpu.CompilerParams(vmem_limit_bytes=60 * 2**20),
     )(row_padded, hidden, packed, cos_full, sin_full, segment_column, segment_row, placing)
 
 
 def attention_backward_kernel(
-    gain_at, width_rows, planes, grad_ref, incoming_ref, middle_ref, raw_ref, mix_ref, probs_ref, query_ref, key_ref,
+    gain_widths, width_rows, planes, grad_ref, incoming_ref, middle_ref, raw_ref, mix_ref, probs_ref, query_ref, key_ref,
     value_ref, query_raw_ref, key_raw_ref, row_ref, qkv_ref, output_ref, cos_ref, sin_ref, input_scale,
     query_scale, key_scale, attnout_scale, ffnin_scale, ffnout_grad, by_device, by_member,
     input_grad_ref, blocks_ref, key_value, query_grad, low_ref, leaving, arriving, send_sem, recv_sem,
@@ -1069,28 +1081,32 @@
     input_grad_ref[...] += take_back(
         back_of(normed_grad * input_scale[...], normed, inverse, width), by_member[...]
     )
-    (at, count), *others = gain_at
-    gains = collect_gain(input_gain, blocks, planes, at, count, padded, True)
-    vectors = (query_gain, key_gain, attnout_grad, ffnin_grad, ffnout_grad[...])
-    for vector, (at, count) in zip(vectors, others):
-        gains = gains + collect_gain(vector, blocks, planes, at, count, count, False)
+    vectors = (input_gain, query_gain, key_gain, attnout_grad, ffnin_grad, ffnout_grad[...])
+    gains = jnp.concatenate(
+        [
+            collect_gain(vector, blocks, planes, count, count if k else padded, k == 0)
+            for k, (vector, count) in enumerate(zip(vectors, gain_widths))
+        ],
+        axis=1,
+    )
+    lanes = gains.shape[1]
     normed = (normed * input_scale[...]).astype(bf16)
     weights = contract_rows(normed, low_ref[...])
-    row_of = lax.broadcasted_iota(jnp.int32, (padded, 256), 0)
+    row_of = lax.broadcasted_iota(jnp.int32, (padded, lanes), 0)
     columns = blocks_ref.shape[3]
     for i in range(blocks):
         member, plane = i // planes, i % planes
         piece = weights[padded * i : padded * (i + 1)]
-        first = jnp.where(row_of == width_rows, gains[i : i + 1], piece[:, :256])
-        blocks_ref[member, plane, :padded, :256] = first.astype(bf16)
-        blocks_ref[member, plane, :padded, 256:] = piece[:, 256:].astype(bf16)
+        first = jnp.where(row_of == width_rows, gains[i : i + 1], piece[:, :lanes])
+        blocks_ref[member, plane, :padded, :lanes] = first.astype(bf16)
+        blocks_ref[member, plane, :padded, lanes:] = piece[:, lanes:].astype(bf16)
         natural = mix_rows * (plane * members + member)
         blocks_ref[member, plane, padded:, :width] = output_grad[natural : natural + mix_rows]
         blocks_ref[member, plane, padded:, width:] = jnp.zeros((mix_rows, columns - width), bf16)
     copy.wait_send()
 
 
-def attention_backward(arrays, gain_at, width_rows, planes, mix_rows, collective_id):
+def attention_backward(arrays, gain_widths, width_rows, planes, mix_rows, collective_id):
     bf16, f32 = jnp.bfloat16, jnp.float32
     grad, incoming, query, key, qkv = arrays[0], arrays[1], arrays[6], arrays[7], arrays[12]
     local_rows, width = incoming.shape
@@ -1100,7 +1116,7 @@
     shape = jax.ShapeDtypeStruct
     vmem = pl.BlockSpec(memory_space=pltpu.VMEM)
     return pl.pallas_call(
-        functools.partial(attention_backward_kernel, gain_at, width_rows, planes),
+        functools.partial(attention_backward_kernel, gain_widths, width_rows, planes),
         out_shape=[
             shape((local_rows, width), f32),
             shape((members, planes, padded + mix_rows, qkv.shape[1]), bf16),
@@ -1173,19 +1189,31 @@
     gate_up = gate_up.reshape((devices,) + gate_up.shape[2:])
 
     gains = (input_gain, query_gain, key_gain, attnout_gain, ffnin_gain, ffnout_gain)
-    gain_row = jnp.concatenate(gains)
     gain_widths = [g.shape[0] for g in gains]
-    gain_row = jnp.pad(gain_row, (0, qkv_width - gain_row.shape[0]))
+    gain_row = jnp.concatenate(
+        [jnp.pad(g[None], ((0, 0), (0, GAIN_SLOT - g.shape[0]))) for g in gains], axis=1
+    )
+    gain_row = jnp.pad(gain_row, ((0, 0), (0, qkv_width - gain_row.shape[1])))
     qkv_local = jnp.concatenate([query_weight, key_weight, value_weight], axis=1)
-    packed = jnp.concatenate([qkv_local, gain_row[None]], axis=0)
+    packed = jnp.concatenate([qkv_local, gain_row], axis=0)
     packed = jnp.pad(packed, ((0, padded - width_rows - 1), (0, 0)))
     output_wide = jnp.pad(output_weight, ((0, 0), (0, qkv_width - output_weight.shape[1])))
     packed = jnp.concatenate([packed, output_wide], axis=0)
     packed_all = z_gather(packed, planes, 0)
-    packed_all, down_full = weights_gather(packed_all, down_weight, cubes, 6)
-    down_full = down_full.reshape(unit_count, down_weight.shape[1])
+    far = lax.axis_index("far")
+    down_terms = [down_weight]
+    for k in range(1, cubes):
+        shift = [(i, (i + k) % cubes) for i in range(cubes)]
+        down_terms.append(lax.ppermute(down_weight, "far", shift))
+    packed_all, *down_terms = lax.optimization_barrier((packed_all, *down_terms))
+    packed_all = plane_gather(packed_all, 6)
     gate_up, packed_all = lax.optimization_barrier((gate_up, packed_all))
     gate_up_full = exchange(gate_up, ALL).reshape(devices * padded, 2 * unit_pad)
+    down_full = jnp.zeros((cubes, *down_weight.shape), bf16)
+    for k, term in enumerate(down_terms):
+        at = lax.rem(far - k + cubes, cubes)
+        down_full = lax.dynamic_update_index_in_dim(down_full, term, at, 0)
+    down_full = down_full.reshape(unit_count, down_weight.shape[1])
     incoming = cotangent[0].astype(f32)
     local_rows = tokens.shape[1]
     offset = lax.axis_index("seq") * local_rows
@@ -1206,10 +1234,6 @@
         ]
     )
     row_padded = matmul(row_tokens, by_member).astype(bf16)
-    gain_at, at = [], 0
-    for count in gain_widths:
-        gain_at.append((at, count))
-        at += count
     (
         ffn_in_placed,
         middle,
@@ -1233,7 +1257,7 @@
         mine(segment_row)[:, None],
         segment_row[None],
         by_device,
-        gain_at,
+        gain_widths,
         width_rows,
         padded,
         head_width,
@@ -1242,6 +1266,7 @@
 
     cube_in = gather_rows(ffn_in_placed, 1)
     ffn_part, activated_low, to_gate, to_up = ffn_forward(cube_in, gate_up_full, down_full)
+    ffn_part = ffn_part.reshape(group, local_rows // 16, 16, ffn_part.shape[1])
     ffn_raw = cube_scatter_sum(ffn_part, 2)
     inv_ffn = inverse_rms(ffn_raw)
     norm_ffn = ffn_raw * inv_ffn
@@ -1280,7 +1305,7 @@
             by_device,
             by_member,
         ],
-        gain_at,
+        gain_widths,
         width_rows,
         planes,
         mix_rows,
@@ -1300,10 +1325,10 @@
     gate_wgrad = unit_columns(gate_up_sum[:, :, :unit_pad])
     up_wgrad = unit_columns(gate_up_sum[:, :, unit_pad:])
     qkv_share, output_share = share[:padded], share[padded:, : output_weight.shape[1]]
-    gain_shares, at = [], 0
-    for count in gain_widths:
-        gain_shares.append(qkv_share[width_rows, at : at + count])
-        at += count
+    gain_shares = [
+        qkv_share[width_rows, k * GAIN_SLOT : k * GAIN_SLOT + count]
+        for k, count in enumerate(gain_widths)
+    ]
     return (
         result.astype(bf16)[None],
         input_grad[None],

time: 486 us -> 483 us (level)
    pallas_call x1, Pallas kernels: 22.5 us -> 28 us  [z_gather(): pl.pallas_call(functools.partial(z_gather_kernel, planes), out_shape=jax....]
  transfers between devices with their start and end apart: 3 -> 4, of which waited for: 0 -> 0; matrix products, arithmetic and copies ran while one was open for 6% -> 6% of each run, Pallas kernels for 47% -> 49%
where the time goes in v10:
time: 483 us; the launch traced here: 477 us
  Pallas kernels  415 us (86%)
  local copies, waits for them, and re-layouts  30.2 us (6%)
  starting transfers between devices  13.7 us (3%)
  other arithmetic  12.7 us (3%)
    pallas_call x1, Pallas kernels, owner_sum(): pl.pallas_call(functools.partial(owner_sum_kernel, planes), out_shape=jax...  66.9 us
    pallas_call x1, Pallas kernels, gather_backward(): pl.pallas_call(gather_backward_kernel, out_shape=[shape((members * rows,...  59.7 us
    pallas_call x1, Pallas kernels, gather_rows(): pl.pallas_call(cube_gather_kernel, out_shape=jax.ShapeDtypeStruct((member...  53.8 us
    pallas_call x1, Pallas kernels, sum_gradients(): pl.pallas_call(sum_gradients_kernel, out_shape=[jax.ShapeDtypeStruct((pie...  50.9 us
    pallas_call x1, Pallas kernels, cube_scatter_sum(): pl.pallas_call(cube_sum_kernel, out_shape=jax.ShapeDtypeStruct(shape, jnp...  41.7 us
    pallas_call x1, Pallas kernels, plane_gather(): pl.pallas_call(plane_gather_kernel, out_shape=jax.ShapeDtypeStruct((membe...  34.8 us
    pallas_call x1, Pallas kernels, attention_backward(): pl.pallas_call(functools.partial(attention_backward_kernel, gain_widths,...  33.9 us
    pallas_call x1, Pallas kernels, ffn_forward(): pl.pallas_call(ffn_forward_kernel, grid=(rows // ROW_BLOCK,), in_specs=[r...  30.4 us
  transfers between devices with their start and end apart: 4, of which 0 were waited for; matrix products, arithmetic and copies ran while one was open for 6% of the time, Pallas kernels for 49%

profile of v10, /device:TPU:8, one launch (start us, length us, event | category | flops | bytes accessed | tf_op | source)
XLA Modules:
  0.0 476.7 jit_solution(10366371223708418919)
XLA Ops:
  0.7 2.7 collective-permute-start.1
  3.3 1.5 collective-permute-start
  5.6 1.0 convert_reduce_fusion.1
  7.2 2.9 reshape.151
  11.1 1.7 reshape.153
  15.7 28.0 %shard_map.271.own_ref = bf16[4,72,1536]{2,1,0:T(8,128)(2,1)S(1)} custom-call(bf16[72,1536]{1,0:T(8,128)(2,1)S(1)} %fusion.25.own_ref), custom_call_target="tpu_custom_call" | custom-call | bytes 60000000 | tf_op jit(solution)/shard_map/pallas_call | solution.py:322
  43.8 1.8 multiply_sine_fusion
  45.6 34.8 %shard_map.272.packed_ref = bf16[8,4,72,1536]{3,2,1,0:T(8,128)(2,1)} custom-call(bf16[4,72,1536]{2,1,0:T(8,128)(2,1)S(1)} %shard_map.271.own_ref), custom_call_target="tpu_custom_call" | custom-call | bytes 90000000 | tf_op jit(solution)/shard_map/pallas_call | solution.py:341
  80.4 1.9 broadcast_in_dim.50
  82.3 6.2 %all-to-all-start = ((bf16[32,40,1024]{2,1,0:T(8,128)(2,1)}), bf16[32,40,1024]{2,1,0:T(8,128)(2,1)S(1)}, u32[]{:S(2)}, u32[]{:S(2)}) async-start(bf16[32,40,1024]{2,1,0:T(8,128)(2,1)} %bitcast.79), calls=%async_computation | async-start | bytes 5242880 | tf_op jit(solution)/shard_map/all_to_all | solution.py:87
  88.6 5.3 %fusion.34 = (bf16[1152,1280]{1,0:T(8,128)(2,1)}, bf16[1152,1280]{1,0:T(8,128)(2,1)}) fusion(s32[1152]{0:T(1024)S(1)} %get-tuple-element.105, s32[1152]{0:T(1024)S(1)} %get-tuple-element.106, pred[1152]{0:T(1024)(128)(4,1)S(1)} %get-tuple-element.108, s32[1152]{0:T(1024)S(1)} %get-tuple-element.104, s32[1152]{0:T(1024)S(1)} %get-tuple-element.107, ...), kind=kLoop, calls=%fused_computation.88 | loop fusion | flops 45711360 | bytes 5918976 | tf_op jit(solution)/shard_map/convert_element_type | solution.py:69
  95.1 1.2 broadcast_select_fusion.1
  96.3 3.8 convolution_convert_fusion.row_ref
  100.1 14.3 %shard_map.273 = (bf16[256,1280]{1,0:T(8,128)(2,1)}, f32[256,1152]{1,0:T(8,128)}, f32[256,1152]{1,0:T(8,128)}, bf16[256,1024]{1,0:T(8,128)(2,1)}, f32[4,256,512]...) custom-call(bf16[512,1280]{1,0:T(8,128)(2,1)} %convolution_convert_f, ...), custom_call_target="tpu_custom_call" | custom-call | bytes 60000000 | tf_op jit(solution)/shard_map/pallas_call | solution.py:985
  114.5 1.1 copy-done.3
  115.5 53.8 %shard_map.274 = bf16[16,16,16,1280]{3,2,1,0:T(8,128)(2,1)} custom-call(bf16[16,16,1280]{2,1,0:T(8,128)(2,1)S(1)} %bitcast.76), custom_call_target="tpu_custom_call" | custom-call | bytes 105000000 | tf_op jit(solution)/shard_map/pallas_call | solution.py:357
  169.4 1.9 copy-done.2
  171.4 30.4 %shard_map.275 = (bf16[4096,1152]{1,0:T(8,128)(2,1)}, bf16[4096,512]{1,0:T(8,128)(2,1)}, f32[4096,512]{1,0:T(8,128)}, f32[4096,512]{1,0:T(8,128)}) custom-call(bf16[4096,1280]{1,0:T(8,128)(2,1)} %bitcast.77, bf16[1280,1024]{1,0:T(8,128)(2,1)S(1)} %bitcast.72, bf16[432,1152]{1,0:T(8,128)(2,1)S(1)} %bitcast.75), custom_call_target="tpu_custom_call" | custom-call | bytes 60000000 | tf_op jit(solution)/shard_map/pallas_call | solution.py:596
  201.9 41.7 %shard_map.276 = f32[16,16,1152]{2,1,0:T(8,128)S(1)} custom-call(bf16[16,16,16,1152]{3,2,1,0:T(8,128)(2,1)} %bitcast.81), custom_call_target="tpu_custom_call" | custom-call | bytes 105000000 | tf_op jit(solution)/shard_map/pallas_call | solution.py:526
  243.8 1.3 fusion.15
  245.2 1.1 fusion.21.own_ref
  246.3 59.7 %shard_map.277 = (bf16[4096,1024]{1,0:T(8,128)(2,1)}, bf16[16,16,16,1280]{3,2,1,0:T(8,128)(2,1)}, bf16[432,1152]{1,0:T(8,128)(2,1)}) custom-call(bf16[16,16,1152]{2,1,0:T(8,128)(2,1)} %fusion.21.own_ref, bf16[432,1152]{1,0:T(8,128)(2,1)} %bitcast.74, bf16[1280,1024]{1,0:T(8,128)(2,1)} %bitcast.73, f32[4096,512]{1,0:T(8,128)} %get-tuple-element.59.to_gate_hbm, ...), custom_call_target="tpu_custom_call" | custom-call | bytes 135000000 | tf_op jit(solution)/shard_map/pallas_call | solution.py:687
  306.1 50.9 %shard_map.278 = (f32[16,16,1280]{2,1,0:T(8,128)}, bf16[1280,1024]{1,0:T(8,128)(2,1)}, f32[216,1152]{1,0:T(8,128)}) custom-call(bf16[16,16,16,1280]{3,2,1,0:T(8,128)(2,1)} %get-tuple-element.62.part_ref, bf16[2,216,1152]{2,1,0:T(8,128)(2,1)} %bitcast.93, bf16[4096,1280]{1,0:T(8,128)(2,1)} %bitcast.78, bf16[4096,1024]{1,0:T(8,128)(2,1)} %get-tuple-element.64.both_hbm), custom_call_target="tpu_custom_call" | custom-call | bytes 105000000 | tf_op jit(solution)/shard_map/pallas_call | solution.py:767
  357.0 3.3 all-to-all-start.1
  360.9 33.9 %shard_map.279 = (f32[256,1152]{1,0:T(8,128)}, bf16[8,4,72,1536]{3,2,1,0:T(8,128)(2,1)}) custom-call(f32[256,1280]{1,0:T(8,128)} %bitcast.91, bf16[256,1152]{1,0:T(8,128)(2,1)} %bitcast.82, f32[256,1152]{1,0:T(8,128)} %get-tuple-element.52.middle_ref, f32[256,1152]{1,0:T(8,128)} %get-tuple-element.66.raw_ref, bf16[256,1024]{1,0:T(8,128)(2,1)} %get-tuple-element.67.mix_ref, ...), custom_call_target="tpu_custom_call" | custom-call | bytes 90000000 | tf_op jit(solution)/shard_map/pallas_call | solution.py:1118
  394.8 66.9 %shard_map.280 = f32[72,1536]{1,0:T(8,128)S(1)} custom-call(bf16[8,4,72,1536]{3,2,1,0:T(8,128)(2,1)} %get-tuple-element.82.part_ref), custom_call_target="tpu_custom_call" | custom-call | bytes 105000000 | tf_op jit(solution)/shard_map/pallas_call | solution.py:821
  465.6 2.1 reshape.172
  467.6 1.7 copy.56
  469.3 1.8 reshape.168
  471.1 1.0 reshape.171
  472.5 1.8 reshape.166
  474.3 1.0 copy.74
  (88 shorter events, 12.4 us)
Async XLA Ops:
  0.6 10.5 %copy-start.9 = (bf16[36,6912]{1,0:T(8,128)(2,1)S(1)}, bf16[36,6912]{1,0:T(8,128)(2,1)}, u32[]{:S(2)}) copy-start(bf16[36,6912]{1,0:T(8,128)(2,1)} %param.24) | copy-start | bytes 1492996
  0.7 45.0 %collective-permute-start.1 = (bf16[216,1152]{1,0:T(8,128)(2,1)}, bf16[216,1152]{1,0:T(8,128)(2,1)S(1)}, u32[]{:S(2)}, u32[]{:S(2)}) collective-permute-start(bf16[216,1152]{1,0:T(8,128)(2,1)} %param.25), channel_id=1, source_target_pairs={{0,16},{16,0},{1,17},{17,1},{2,18},{18,2},{3,19},{19,3},{4,20},{20... | collective-permute-start | bytes 1493000 | tf_op jit(solution)/shard_map/ppermute | solution.py:1207
  3.3 91.8 %collective-permute-start = (bf16[256,1152]{1,0:T(8,128)(2,1)}, bf16[256,1152]{1,0:T(8,128)(2,1)}, u32[]{:S(2)}, u32[]{:S(2)}) collective-permute-start(bf16[256,1152]{1,0:T(8,128)(2,1)} %bitcast.89), channel_id=1, source_target_pairs={{0,1},{1,0},{2,3},{3,2},{4,5},{5,4},{6,7},{7,6},{8,9},{9,8},{10,11... | collective-permute-start | bytes 1769480 | tf_op jit(solution)/shard_map/ppermute | solution.py:1229
  10.7 3.1 copy-start.18
  10.7 3.1 copy-start.19
  10.7 3.1 copy-start.20
  10.7 3.2 copy-start.21
  10.7 3.2 copy-start.22
  10.7 3.2 copy-start.13
  10.7 3.2 copy-start.15
  10.8 3.2 copy-start.16
  10.8 3.2 copy-start.14
  45.6 34.8 %copy-start.11 = (bf16[216,1152]{1,0:T(8,128)(2,1)}, bf16[216,1152]{1,0:T(8,128)(2,1)S(1)}, u32[]{:S(2)}) copy-start(bf16[216,1152]{1,0:T(8,128)(2,1)S(1)} %collective-permute-done.1) | copy-start | bytes 1492996
  82.3 87.1 %all-to-all-start = ((bf16[32,40,1024]{2,1,0:T(8,128)(2,1)}), bf16[32,40,1024]{2,1,0:T(8,128)(2,1)S(1)}, u32[]{:S(2)}, u32[]{:S(2)}) async-start(bf16[32,40,1024]{2,1,0:T(8,128)(2,1)} %bitcast.79), calls=%async_computation | async-start | bytes 5242880 | tf_op jit(solution)/shard_map/all_to_all | solution.py:87
  88.6 5.4 %copy-start.10 = (bf16[216,1152]{1,0:T(8,128)(2,1)S(1)}, bf16[216,1152]{1,0:T(8,128)(2,1)}, u32[]{:S(2)}) copy-start(bf16[216,1152]{1,0:T(8,128)(2,1)} %param.25) | copy-start | bytes 1492996
  88.6 5.5 %copy-start.12 = (bf16[216,1152]{1,0:T(8,128)(2,1)S(1)}, bf16[216,1152]{1,0:T(8,128)(2,1)}, u32[]{:S(2)}) copy-start(bf16[216,1152]{1,0:T(8,128)(2,1)} %copy-done.11) | copy-start | bytes 1492996
  93.9 1.2 copy-start.6
  94.1 1.0 copy-start.1
  114.5 1.1 copy-start.3
  115.5 53.8 %copy-start.17 = (f32[1,1152]{1,0:T(1,128)S(1)}, f32[1,1152]{1,0:T(1,128)}, u32[]{:S(2)}) copy-start(f32[1,1152]{1,0:T(1,128)} %get-tuple-element.58) | copy-start | bytes 13828
  169.4 32.4 %copy-start = (bf16[32,40,1024]{2,1,0:T(8,128)(2,1)}, bf16[32,40,1024]{2,1,0:T(8,128)(2,1)S(1)}, u32[]{:S(2)}) copy-start(bf16[32,40,1024]{2,1,0:T(8,128)(2,1)S(1)} %all-to-all-done) | copy-start | bytes 7864324
  169.4 1.9 copy-start.2
  201.8 42.0 %copy-start.4 = (bf16[1,256,1152]{2,1,0:T(8,128)(2,1)S(1)}, bf16[1,256,1152]{2,1,0:T(8,128)(2,1)}, u32[]{:S(2)}) copy-start(bf16[1,256,1152]{2,1,0:T(8,128)(2,1)} %param.18) | copy-start | bytes 1769476
  201.8 42.0 %copy-start.5 = (f32[256,1152]{1,0:T(8,128)S(1)}, f32[256,1152]{1,0:T(8,128)}, u32[]{:S(2)}) copy-start(f32[256,1152]{1,0:T(8,128)} %get-tuple-element.52.middle_ref) | copy-start | bytes 3538948
  357.0 107.7 %all-to-all-start.1 = ((bf16[32,40,1024]{2,1,0:T(8,128)(2,1)}), bf16[32,40,1024]{2,1,0:T(8,128)(2,1)S(1)}, u32[]{:S(2)}, u32[]{:S(2)}) async-start(bf16[32,40,1024]{2,1,0:T(8,128)(2,1)} %bitcast.86), calls=%async_computation.1 | async-start | bytes 5242880 | tf_op jit(solution)/shard_map/all_to_all | solution.py:87
  472.5 1.8 copy-start.7
  472.5 2.8 copy-start.8

commit v11 on v10

--- a/solution.py
+++ b/solution.py
@@ -2,6 +2,7 @@
 
 import jax
 import jax.numpy as jnp
+import numpy as np
 from jax import lax
 from jax.experimental import pallas as pl
 from jax.experimental.pallas import tpu as pltpu
@@ -61,12 +62,13 @@
 
 
 def place_columns(blocks, members, planes, rows, padded, by_member):
-    source = lax.broadcasted_iota(jnp.int32, (blocks * rows, blocks * padded), 0)
-    target = lax.broadcasted_iota(jnp.int32, (blocks * rows, blocks * padded), 1)
-    block = source // rows
+    source = np.arange(blocks * rows)
+    block, inner = source // rows, source % rows
     if by_member:
         block = block % members * planes + block // members
-    return (target == block * padded + source % rows).astype(jnp.bfloat16)
+    placing = np.zeros((blocks * rows, blocks * padded), np.float32)
+    placing[source, block * padded + inner] = 1.0
+    return jnp.asarray(placing.astype(jnp.bfloat16))
 
 
 def take_back(padded_values, placing):
@@ -291,9 +293,19 @@
     cube_spread(own_ref, out_ref, *sems)
 
 
-def plane_gather_kernel(own_ref, out_ref, *sems):
-    greet(plane_places()[:3])
+def weights_gather_kernel(cubes, own_ref, down_ref, out_ref, down_out, far_send, far_recv, own_sem, *sems):
+    far, others = other_cubes(cubes)
+    greet((*plane_places()[:3], *others))
+    keep = pltpu.make_async_copy(down_ref, down_out.at[far], own_sem)
+    keep.start()
+    send = sender(far_send, far_recv)
+    copies = [send(k, down_ref, down_out.at[far], place) for k, place in enumerate(others)]
     plane_spread(own_ref, out_ref, *sems)
+    for copy in copies:
+        copy.wait_recv()
+    for copy in copies:
+        copy.wait_send()
+    keep.wait()
 
 
 def z_gather_kernel(planes, own_ref, out_ref, send_sems, recv_sems, own_sem):
@@ -336,19 +348,28 @@
     )(local)
 
 
-def plane_gather(local, collective_id):
+def weights_gather(local, down, cubes, collective_id):
     members = 8
+    anywhere = pl.BlockSpec(memory_space=pl.ANY)
     return pl.pallas_call(
-        plane_gather_kernel,
-        out_shape=jax.ShapeDtypeStruct((members, *local.shape), local.dtype),
-        in_specs=[pl.BlockSpec(memory_space=pl.ANY)],
-        out_specs=pl.BlockSpec(memory_space=pl.ANY),
-        scratch_shapes=gather_sems(13),
+        functools.partial(weights_gather_kernel, cubes),
+        out_shape=[
+            jax.ShapeDtypeStruct((members, *local.shape), local.dtype),
+            jax.ShapeDtypeStruct((cubes, *down.shape), down.dtype),
+        ],
+        in_specs=[anywhere, anywhere],
+        out_specs=[anywhere, anywhere],
+        scratch_shapes=[
+            pltpu.SemaphoreType.DMA((cubes - 1,)),
+            pltpu.SemaphoreType.DMA((cubes - 1,)),
+            pltpu.SemaphoreType.DMA,
+            *gather_sems(13),
+        ],
         cost_estimate=busy(30),
         compiler_params=pltpu.CompilerParams(
             collective_id=collective_id, has_side_effects=True, vmem_limit_bytes=VMEM_BYTES
         ),
-    )(local)
+    )(local, down)
 
 
 def gather_rows(local, collective_id):
@@ -556,29 +577,34 @@
     def _():
         pad_rows(down, down_ref)
 
-    proj[...] = matmul(in_ref[...], gate_up_ref[...])
-    step = 32
-
-    def one(i, carry):
-        rows = pl.ds(pl.multiple_of(i * step, step), step)
-        gate, up = proj[rows, :units], proj[rows, units:]
-        square = gate * gate
-        bend = jnp.tanh(gelu_inner * gate * (1.0 + gelu_cubic * square))
-        half = 0.5 * (1.0 + bend)
-        value = gate * half
-        slope = half + 0.5 * gate * (1.0 - bend * bend) * (
-            gelu_inner * (1.0 + 3.0 * gelu_cubic * square)
-        )
-        to_gate[rows, :] = slope * up
-        to_up[rows, :] = value
-        act_ref[rows, :] = (value * up).astype(act_ref.dtype)
-        return carry
-
-    lax.fori_loop(0, in_ref.shape[0] // step, one, 0)
-    part_ref[...] = matmul(act_ref[...], down[...]).astype(part_ref.dtype)
-
-
-ROW_BLOCK = 256
+    step = 64
+    half_rows = in_ref.shape[0] // 2
+
+    def mid(base):
+        for i in range(half_rows // step):
+            rows = pl.ds(base + i * step, step)
+            gate, up = proj[rows, :units], proj[rows, units:]
+            square = gate * gate
+            bend = jnp.tanh(gelu_inner * gate * (1.0 + gelu_cubic * square))
+            half = 0.5 * (1.0 + bend)
+            value = gate * half
+            slope = half + 0.5 * gate * (1.0 - bend * bend) * (
+                gelu_inner * (1.0 + 3.0 * gelu_cubic * square)
+            )
+            to_gate[rows, :] = slope * up
+            to_up[rows, :] = value
+            act_ref[rows, :] = (value * up).astype(act_ref.dtype)
+
+    first, second = pl.ds(0, half_rows), pl.ds(half_rows, half_rows)
+    proj[first, :] = matmul(in_ref[first, :], gate_up_ref[...])
+    proj[second, :] = matmul(in_ref[second, :], gate_up_ref[...])
+    mid(0)
+    part_ref[first, :] = matmul(act_ref[first, :], down[...]).astype(part_ref.dtype)
+    mid(half_rows)
+    part_ref[second, :] = matmul(act_ref[second, :], down[...]).astype(part_ref.dtype)
+
+
+ROW_BLOCK = 512
 
 
 def whole(array):
@@ -791,6 +817,34 @@
     return total.reshape(pieces * piece, depth), gate_up, down_sum
 
 
+def unit_sum_kernel(terms_ref, gate_ref, up_ref):
+    cubes, group, _, lanes = terms_ref.shape
+    rows, hidden = gate_ref.shape
+    units, half = hidden // (cubes * group), lanes // 2
+    for member in range(group):
+        total = terms_ref[0, member].astype(jnp.float32)
+        for cube in range(1, cubes):
+            total = total + terms_ref[cube, member].astype(jnp.float32)
+        for cube in range(cubes):
+            at = (cube * group + member) * units
+            gate_ref[:, at : at + units] = total[:rows, cube * units : (cube + 1) * units]
+            up_ref[:, at : at + units] = total[
+                :rows, half + cube * units : half + (cube + 1) * units
+            ]
+
+
+def unit_sum(terms, rows, hidden):
+    vmem = pl.BlockSpec(memory_space=pltpu.VMEM)
+    return pl.pallas_call(
+        unit_sum_kernel,
+        out_shape=[jax.ShapeDtypeStruct((rows, hidden), jnp.float32)] * 2,
+        in_specs=[vmem],
+        out_specs=[vmem, vmem],
+        cost_estimate=busy(5),
+        compiler_params=pltpu.CompilerParams(vmem_limit_bytes=VMEM_BYTES),
+    )(terms)
+
+
 def owner_sum_kernel(planes, part_ref, out_ref, own_sum, leaving, arriving, z_send, z_recv, *scratch):
     plane, others, ring = other_planes(planes)
     greet((*plane_places()[:3], *others))
@@ -839,6 +893,48 @@
 
 
 GAIN_SLOT = 128
+TILE_ROWS, TILE_LANES = 8, 128
+
+
+def packed_strips(rows, width, columns):
+    across, into = width // TILE_LANES, columns // TILE_LANES
+    strips, tile, tiles = [], 0, rows // TILE_ROWS * across
+    while tile < tiles:
+        run = min(across - tile % across, into - tile % into)
+        strips.append(
+            (
+                tile // across * TILE_ROWS,
+                tile % across * TILE_LANES,
+                tile // into * TILE_ROWS,
+                tile % into * TILE_LANES,
+                run * TILE_LANES,
+            )
+        )
+        tile += run
+    return strips, up_to(tiles, into) // into * TILE_ROWS
+
+
+def pack_tiles(array, columns):
+    strips, rows = packed_strips(*array.shape, columns)
+    lines = []
+    for row in range(0, rows, TILE_ROWS):
+        parts = [
+            array[r : r + TILE_ROWS, c : c + n] for r, c, to, _, n in strips if to == row
+        ]
+        line = jnp.concatenate(parts, axis=1)
+        lines.append(jnp.pad(line, ((0, 0), (0, columns - line.shape[1]))))
+    return jnp.concatenate(lines, axis=0)
+
+
+def unpack_tiles(array, rows, width):
+    strips, _ = packed_strips(rows, width, array.shape[1])
+    lines = []
+    for row in range(0, rows, TILE_ROWS):
+        parts = [
+            array[to : to + TILE_ROWS, at : at + n] for r, _, to, at, n in strips if r == row
+        ]
+        lines.append(jnp.concatenate(parts, axis=1))
+    return jnp.concatenate(lines, axis=0)
 
 
 def gain_places(blocks, planes, count, per, by_member):
@@ -888,8 +984,9 @@
     members, planes, piece, _ = packed_ref.shape
     blocks = members * planes
     padded = qkv_ref.shape[0] // blocks
-    mix_rows = piece - padded
     width = hidden_ref.shape[1]
+    mix_rows = output_ref.shape[0] // blocks
+    strips, _ = packed_strips(mix_rows, width, packed_ref.shape[3])
     local_rows, full_rows = hidden_ref.shape[0], row_ref.shape[0]
     head = key_ref.shape[1]
     heads = query_ref.shape[1] // head
@@ -900,7 +997,9 @@
         block = packed_ref[member, plane]
         qkv_ref[padded * i : padded * (i + 1), :] = block[:padded]
         natural = mix_rows * (plane * members + member)
-        output_ref[natural : natural + mix_rows, :] = block[padded:, :width]
+        for r, c, to, at, n in strips:
+            tiles = block[padded + to : padded + to + TILE_ROWS, at : at + n]
+            output_ref[natural + r : natural + r + TILE_ROWS, c : c + n] = tiles
         gain_rows[i : i + 1, :] = block[width_rows : width_rows + 1, : gain_rows.shape[1]].astype(f32)
     targets = (input_scale, query_scale, key_scale, attnout_scale, ffnin_scale, ffnout_scale)
     for k, (target, count) in enumerate(zip(targets, gain_widths)):
@@ -1003,8 +1102,9 @@
     members = blocks_ref.shape[0]
     blocks = members * planes
     padded = qkv_ref.shape[0] // blocks
-    mix_rows = blocks_ref.shape[2] - padded
+    mix_rows = output_ref.shape[0] // blocks
     local_rows, width = incoming_ref.shape
+    strips, _ = packed_strips(mix_rows, width, blocks_ref.shape[3])
     head = key_ref.shape[1]
     heads = query_ref.shape[1] // head
     half = head // 2
@@ -1101,8 +1201,13 @@
         blocks_ref[member, plane, :padded, :lanes] = first.astype(bf16)
         blocks_ref[member, plane, :padded, lanes:] = piece[:, lanes:].astype(bf16)
         natural = mix_rows * (plane * members + member)
-        blocks_ref[member, plane, padded:, :width] = output_grad[natural : natural + mix_rows]
-        blocks_ref[member, plane, padded:, width:] = jnp.zeros((mix_rows, columns - width), bf16)
+        for r, c, to, at, n in strips:
+            tiles = output_grad[natural + r : natural + r + TILE_ROWS, c : c + n]
+            blocks_ref[member, plane, padded + to : padded + to + TILE_ROWS, at : at + n] = tiles
+        _, _, to, at, n = strips[-1]
+        if at + n < columns:
+            rest = jnp.zeros((TILE_ROWS, columns - at - n), bf16)
+            blocks_ref[member, plane, padded + to : padded + to + TILE_ROWS, at + n :] = rest
     copy.wait_send()
 
 
@@ -1112,6 +1217,7 @@
     local_rows, width = incoming.shape
     members = 8
     padded = qkv.shape[0] // (members * planes)
+    _, packed_rows = packed_strips(mix_rows, width, qkv.shape[1])
     pair = pltpu.VMEM((local_rows, 2 * key.shape[1]), bf16)
     shape = jax.ShapeDtypeStruct
     vmem = pl.BlockSpec(memory_space=pltpu.VMEM)
@@ -1119,7 +1225,7 @@
         functools.partial(attention_backward_kernel, gain_widths, width_rows, planes),
         out_shape=[
             shape((local_rows, width), f32),
-            shape((members, planes, padded + mix_rows, qkv.shape[1]), bf16),
+            shape((members, planes, padded + packed_rows, qkv.shape[1]), bf16),
         ],
         in_specs=[vmem] * len(arrays),
         out_specs=[vmem] * 2,
@@ -1197,23 +1303,14 @@
     qkv_local = jnp.concatenate([query_weight, key_weight, value_weight], axis=1)
     packed = jnp.concatenate([qkv_local, gain_row], axis=0)
     packed = jnp.pad(packed, ((0, padded - width_rows - 1), (0, 0)))
-    output_wide = jnp.pad(output_weight, ((0, 0), (0, qkv_width - output_weight.shape[1])))
-    packed = jnp.concatenate([packed, output_wide], axis=0)
+    packed = jnp.concatenate([packed, pack_tiles(output_weight, qkv_width)], axis=0)
     packed_all = z_gather(packed, planes, 0)
-    far = lax.axis_index("far")
-    down_terms = [down_weight]
-    for k in range(1, cubes):
-        shift = [(i, (i + k) % cubes) for i in range(cubes)]
-        down_terms.append(lax.ppermute(down_weight, "far", shift))
-    packed_all, *down_terms = lax.optimization_barrier((packed_all, *down_terms))
-    packed_all = plane_gather(packed_all, 6)
+    other_tokens = lax.ppermute(tokens[0], "seq", [(0, 1), (1, 0)])
+    packed_all, other_tokens = lax.optimization_barrier((packed_all, other_tokens))
+    packed_all, down_full = weights_gather(packed_all, down_weight, cubes, 6)
+    down_full = down_full.reshape(unit_count, down_weight.shape[1])
     gate_up, packed_all = lax.optimization_barrier((gate_up, packed_all))
     gate_up_full = exchange(gate_up, ALL).reshape(devices * padded, 2 * unit_pad)
-    down_full = jnp.zeros((cubes, *down_weight.shape), bf16)
-    for k, term in enumerate(down_terms):
-        at = lax.rem(far - k + cubes, cubes)
-        down_full = lax.dynamic_update_index_in_dim(down_full, term, at, 0)
-    down_full = down_full.reshape(unit_count, down_weight.shape[1])
     incoming = cotangent[0].astype(f32)
     local_rows = tokens.shape[1]
     offset = lax.axis_index("seq") * local_rows
@@ -1224,9 +1321,7 @@
 
     cos_full, sin_full = rope_tables(doc_positions(segment_row), head_width)
 
-    other_half = [(0, 1), (1, 0)]
     first = lax.axis_index("seq") == 0
-    other_tokens = lax.ppermute(tokens[0], "seq", other_half)
     row_tokens = jnp.concatenate(
         [
             jnp.where(first, tokens[0], other_tokens),
@@ -1312,19 +1407,10 @@
         7,
     )
     share = owner_sum(blocks, 5)
-    gate_up_sum = jnp.sum(
-        gate_up_terms.reshape(cubes, group, padded, 2 * unit_pad).astype(f32), axis=0
-    )
-
-    def unit_columns(total):
-        total = total[:, :width_rows, :unit_count].reshape(
-            group, width_rows, cubes, hidden_rows
-        )
-        return total.transpose(1, 2, 0, 3).reshape(width_rows, cubes * group * hidden_rows)
-
-    gate_wgrad = unit_columns(gate_up_sum[:, :, :unit_pad])
-    up_wgrad = unit_columns(gate_up_sum[:, :, unit_pad:])
-    qkv_share, output_share = share[:padded], share[padded:, : output_weight.shape[1]]
+    gate_wgrad, up_wgrad = unit_sum(
+        gate_up_terms.reshape(cubes, group, padded, 2 * unit_pad), width_rows, gate_weight.shape[1]
+    )
+    qkv_share, output_share = share[:padded], unpack_tiles(share[padded:], *output_weight.shape)
     gain_shares = [
         qkv_share[width_rows, k * GAIN_SLOT : k * GAIN_SLOT + count]
         for k, count in enumerate(gain_widths)

time: 483 us -> 452 us (0.936)
  Pallas kernels: 415 us -> 394 us
  other arithmetic: 12.7 us -> 7.67 us
    pallas_call x1, Pallas kernels: 28 us -> 20.4 us  [z_gather(): pl.pallas_call(functools.partial(z_gather_kernel, planes), out_shape=jax....]
    pallas_call x1, Pallas kernels: 30.4 us -> 23.4 us  [ffn_forward(): pl.pallas_call(ffn_forward_kernel, grid=(rows // ROW_BLOCK,), in_specs=[r...]
    reshape x4 -> x0, local copies, waits for them, and re-layouts: 6.71 us -> none  [the longest x2 3.62 us: unit_columns(): total.transpose(1, 2, 0, 3).reshape(width_rows, cubes * group * hidden_rows)]
    pallas_call x1, Pallas kernels: 66.9 us -> 60.9 us  [owner_sum(): pl.pallas_call(functools.partial(owner_sum_kernel, planes), out_shape=jax...]
    convert_element_type x1 -> x0, other arithmetic: 5.31 us -> none  [place_columns(): return (target == block * padded + source % rows).astype(jnp.bfloat16)]
    unnamed x53 -> x35, local copies, waits for them, and re-layouts: 6.75 us -> 10.1 us
    pallas_call x1 -> x2, Pallas kernels: 34.8 us -> 33.1 us  [the longest x1 30.9 us: weights_gather(): pl.pallas_call(functools.partial(weights_gather_kernel, cubes), out_shape...]
  transfers between devices with their start and end apart: 4 -> 3, of which waited for: 0 -> 0; matrix products, arithmetic and copies ran while one was open for 6% -> 6% of each run, Pallas kernels for 49% -> 41%
where the time goes in v11:
time: 452 us; the launch traced here: 446 us
  Pallas kernels  394 us (87%)
  local copies, waits for them, and re-layouts  25.9 us (6%)
  starting transfers between devices  12.5 us (3%)
  other arithmetic  7.67 us (2%)
  matrix products  4.8 us (1%)
    pallas_call x1, Pallas kernels, owner_sum(): pl.pallas_call(functools.partial(owner_sum_kernel, planes), out_shape=jax...  60.9 us
    pallas_call x1, Pallas kernels, gather_backward(): pl.pallas_call(gather_backward_kernel, out_shape=[shape((members * rows,...  59.7 us
    pallas_call x1, Pallas kernels, gather_rows(): pl.pallas_call(cube_gather_kernel, out_shape=jax.ShapeDtypeStruct((member...  54.7 us
    pallas_call x1, Pallas kernels, sum_gradients(): pl.pallas_call(sum_gradients_kernel, out_shape=[jax.ShapeDtypeStruct((pie...  52.4 us
    pallas_call x1, Pallas kernels, cube_scatter_sum(): pl.pallas_call(cube_sum_kernel, out_shape=jax.ShapeDtypeStruct(shape, jnp...  42 us
    pallas_call x1, Pallas kernels, attention_backward(): pl.pallas_call(functools.partial(attention_backward_kernel, gain_widths,...  33.6 us
    pallas_call x1, Pallas kernels, weights_gather(): pl.pallas_call(functools.partial(weights_gather_kernel, cubes), out_shape...  30.9 us
    pallas_call x1, Pallas kernels, ffn_forward(): pl.pallas_call(ffn_forward_kernel, grid=(rows // ROW_BLOCK,), in_specs=[r...  23.4 us
  transfers between devices with their start and end apart: 3, of which 0 were waited for; matrix products, arithmetic and copies ran while one was open for 6% of the time, Pallas kernels for 41%

profile of v11, /device:TPU:8, one launch (start us, length us, event | category | flops | bytes accessed | tf_op | source)
XLA Modules:
  0.0 446.4 jit_solution(6622842702184431483)
XLA Ops:
  0.7 1.6 collective-permute-start
  2.2 0.7 fusion.25
  3.0 0.7 fusion.23
  7.7 0.9 fusion.17
  9.4 20.4 %shard_map.289.own_ref = bf16[4,64,1536]{2,1,0:T(8,128)(2,1)S(1)} custom-call(bf16[64,1536]{1,0:T(8,128)(2,1)S(1)} %fusion.16.own_ref), custom_call_target="tpu_custom_call" | custom-call | bytes 60000000 | tf_op jit(solution)/shard_map/pallas_call | solution.py:334
  29.8 1.7 reshape.139
  32.4 2.9 reshape.141
  36.4 0.7 copy.39
  37.5 30.9 %shard_map.290 = (bf16[8,4,64,1536]{3,2,1,0:T(8,128)(2,1)}, bf16[2,216,1152]{2,1,0:T(8,128)(2,1)S(1)}) custom-call(bf16[4,64,1536]{2,1,0:T(8,128)(2,1)S(1)} %shard_map.289.own_ref, bf16[216,1152]{1,0:T(8,128)(2,1)S(1)} %copy-done.4), custom_call_target="tpu_custom_call" | custom-call | bytes 90000000 | tf_op jit(solution)/shard_map/pallas_call | solution.py:354
  68.3 1.9 broadcast_in_dim.46
  70.3 5.5 %all-to-all-start = ((bf16[32,40,1024]{2,1,0:T(8,128)(2,1)}), bf16[32,40,1024]{2,1,0:T(8,128)(2,1)S(1)}, u32[]{:S(2)}, u32[]{:S(2)}) async-start(bf16[32,40,1024]{2,1,0:T(8,128)(2,1)} %bitcast.68), calls=%async_computation | async-start | bytes 5242880 | tf_op jit(solution)/shard_map/all_to_all | solution.py:89
  75.8 0.8 copy.40.segment_column
  76.9 1.8 multiply_sine_fusion
  78.7 1.2 broadcast_select_fusion.1
  79.9 4.8 %convolution_convert_fusion.row_ref = bf16[512,1280]{1,0:T(8,128)(2,1)} fusion(bf16[1152,1280]{1,0:T(8,128)(2,1)} %constant.30.clone.by_member, bf16[256,1152]{1,0:T(8,128)(2,1)S(1)} %get-tuple-element.95, bf16[256,1152]{1,0:T(8,128)(2,1)S(1)} %get-tuple-element.94), kind=kOutput, calls=%fused_computation | convolution fusion | flops 1512964096 | bytes 5439488 | tf_op jit(solution)/shard_map/dot_general | solution.py:40
  84.7 14.1 %shard_map.291 = (bf16[256,1280]{1,0:T(8,128)(2,1)}, f32[256,1152]{1,0:T(8,128)}, f32[256,1152]{1,0:T(8,128)}, bf16[256,1024]{1,0:T(8,128)(2,1)}, f32[4,256,512]...) custom-call(bf16[512,1280]{1,0:T(8,128)(2,1)} %convolution_convert_f, ...), custom_call_target="tpu_custom_call" | custom-call | bytes 60000000 | tf_op jit(solution)/shard_map/pallas_call | solution.py:1084
  98.9 1.1 copy-done.3
  99.9 54.7 %shard_map.292 = bf16[16,16,16,1280]{3,2,1,0:T(8,128)(2,1)} custom-call(bf16[16,16,1280]{2,1,0:T(8,128)(2,1)S(1)} %bitcast.65), custom_call_target="tpu_custom_call" | custom-call | bytes 105000000 | tf_op jit(solution)/shard_map/pallas_call | solution.py:378
  154.7 1.9 copy-done.2
  156.7 23.4 %shard_map.293 = (bf16[4096,1152]{1,0:T(8,128)(2,1)}, bf16[4096,512]{1,0:T(8,128)(2,1)}, f32[4096,512]{1,0:T(8,128)}, f32[4096,512]{1,0:T(8,128)}) custom-call(bf16[4096,1280]{1,0:T(8,128)(2,1)} %bitcast.66, bf16[1280,1024]{1,0:T(8,128)(2,1)S(1)} %bitcast.60, bf16[432,1152]{1,0:T(8,128)(2,1)S(1)} %bitcast.64), custom_call_target="tpu_custom_call" | custom-call | bytes 60000000 | tf_op jit(solution)/shard_map/pallas_call | solution.py:622
  180.1 42.0 %shard_map.294 = f32[16,16,1152]{2,1,0:T(8,128)S(1)} custom-call(bf16[16,16,16,1152]{3,2,1,0:T(8,128)(2,1)} %bitcast.69), custom_call_target="tpu_custom_call" | custom-call | bytes 105000000 | tf_op jit(solution)/shard_map/pallas_call | solution.py:547
  222.3 0.8 copy-done.5
  223.1 1.3 fusion.5
  224.5 1.1 fusion.11.own_ref
  225.6 59.7 %shard_map.295 = (bf16[4096,1024]{1,0:T(8,128)(2,1)}, bf16[16,16,16,1280]{3,2,1,0:T(8,128)(2,1)}, bf16[432,1152]{1,0:T(8,128)(2,1)}) custom-call(bf16[16,16,1152]{2,1,0:T(8,128)(2,1)} %fusion.11.own_ref, bf16[432,1152]{1,0:T(8,128)(2,1)} %bitcast.63, bf16[1280,1024]{1,0:T(8,128)(2,1)} %bitcast.61, f32[4096,512]{1,0:T(8,128)} %get-tuple-element.63.to_gate_hbm, ...), custom_call_target="tpu_custom_call" | custom-call | bytes 135000000 | tf_op jit(solution)/shard_map/pallas_call | solution.py:713
  285.3 52.4 %shard_map.296 = (f32[16,16,1280]{2,1,0:T(8,128)}, bf16[1280,1024]{1,0:T(8,128)(2,1)}, f32[216,1152]{1,0:T(8,128)}) custom-call(bf16[16,16,16,1280]{3,2,1,0:T(8,128)(2,1)} %get-tuple-element.66.part_ref, bf16[2,216,1152]{2,1,0:T(8,128)(2,1)} %bitcast.79, bf16[4096,1280]{1,0:T(8,128)(2,1)} %bitcast.67, bf16[4096,1024]{1,0:T(8,128)(2,1)} %get-tuple-element.68.both_hbm), custom_call_target="tpu_custom_call" | custom-call | bytes 105000000 | tf_op jit(solution)/shard_map/pallas_call | solution.py:793
  337.7 5.5 %all-to-all-start.1 = ((bf16[32,40,1024]{2,1,0:T(8,128)(2,1)}), bf16[32,40,1024]{2,1,0:T(8,128)(2,1)S(1)}, u32[]{:S(2)}, u32[]{:S(2)}) async-start(bf16[32,40,1024]{2,1,0:T(8,128)(2,1)} %bitcast.72), calls=%async_computation.1 | async-start | bytes 5242880 | tf_op jit(solution)/shard_map/all_to_all | solution.py:89
  343.8 33.6 %shard_map.297 = (f32[256,1152]{1,0:T(8,128)}, bf16[8,4,64,1536]{3,2,1,0:T(8,128)(2,1)}) custom-call(f32[256,1280]{1,0:T(8,128)} %bitcast.77, bf16[256,1152]{1,0:T(8,128)(2,1)} %bitcast.70, f32[256,1152]{1,0:T(8,128)} %get-tuple-element.57.middle_ref, f32[256,1152]{1,0:T(8,128)} %get-tuple-element.70.raw_ref, bf16[256,1024]{1,0:T(8,128)(2,1)} %get-tuple-element.71.mix_ref, ...), custom_call_target="tpu_custom_call" | custom-call | bytes 90000000 | tf_op jit(solution)/shard_map/pallas_call | solution.py:1224
  377.4 60.9 %shard_map.298 = f32[64,1536]{1,0:T(8,128)S(1)} custom-call(bf16[8,4,64,1536]{3,2,1,0:T(8,128)(2,1)} %get-tuple-element.86.part_ref), custom_call_target="tpu_custom_call" | custom-call | bytes 105000000 | tf_op jit(solution)/shard_map/pallas_call | solution.py:875
  441.3 2.2 shard_map.299
  443.5 1.0 copy.52
  445.2 0.9 copy.53
  (60 shorter events, 11.9 us)
Async XLA Ops:
  0.6 29.1 %copy-start.11 = (bf16[36,6912]{1,0:T(8,128)(2,1)S(1)}, bf16[36,6912]{1,0:T(8,128)(2,1)}, u32[]{:S(2)}) copy-start(bf16[36,6912]{1,0:T(8,128)(2,1)} %param.25) | copy-start | bytes 1492996
  0.7 36.5 %collective-permute-start = (bf16[256,1152]{1,0:T(8,128)(2,1)}, bf16[256,1152]{1,0:T(8,128)(2,1)S(1)}, u32[]{:S(2)}, u32[]{:S(2)}) collective-permute-start(bf16[256,1152]{1,0:T(8,128)(2,1)} %bitcast.73), channel_id=1, source_target_pairs={{0,1},{1,0},{2,3},{3,2},{4,5},{5,4},{6,7},{7,6},{8,9},{9,8},{10,11... | collective-permute-start | bytes 1769480 | tf_op jit(solution)/shard_map/ppermute | solution.py:1308
  36.4 1.0 copy-start.4
  37.5 32.8 %copy-start.10 = (bf16[256,1152]{1,0:T(8,128)(2,1)}, bf16[256,1152]{1,0:T(8,128)(2,1)S(1)}, u32[]{:S(2)}) copy-start(bf16[256,1152]{1,0:T(8,128)(2,1)S(1)} %collective-permute-done) | copy-start | bytes 1769476
  68.3 2.0 copy-start.1
  70.3 5.5 %copy-start.12 = (s32[1,512]{1,0:T(1,128)S(1)}, s32[1,512]{1,0:T(1,128)}, u32[]{:S(2)}) copy-start(s32[1,512]{1,0:T(1,128)} %segment_row.1) | copy-start | bytes 6148
  70.3 8.4 %copy-start.7 = (bf16[1,256,1152]{2,1,0:T(8,128)(2,1)S(1)}, bf16[1,256,1152]{2,1,0:T(8,128)(2,1)}, u32[]{:S(2)}) copy-start(bf16[1,256,1152]{2,1,0:T(8,128)(2,1)} %param.18) | copy-start | bytes 1769476
  70.3 84.4 %all-to-all-start = ((bf16[32,40,1024]{2,1,0:T(8,128)(2,1)}), bf16[32,40,1024]{2,1,0:T(8,128)(2,1)S(1)}, u32[]{:S(2)}, u32[]{:S(2)}) async-start(bf16[32,40,1024]{2,1,0:T(8,128)(2,1)} %bitcast.68), calls=%async_computation | async-start | bytes 5242880 | tf_op jit(solution)/shard_map/all_to_all | solution.py:89
  98.9 1.1 copy-start.3
  99.9 54.7 %copy-start.13 = (f32[1,1152]{1,0:T(1,128)S(1)}, f32[1,1152]{1,0:T(1,128)}, u32[]{:S(2)}) copy-start(f32[1,1152]{1,0:T(1,128)} %get-tuple-element.62) | copy-start | bytes 13828
  154.7 25.4 %copy-start = (bf16[32,40,1024]{2,1,0:T(8,128)(2,1)}, bf16[32,40,1024]{2,1,0:T(8,128)(2,1)S(1)}, u32[]{:S(2)}) copy-start(bf16[32,40,1024]{2,1,0:T(8,128)(2,1)S(1)} %all-to-all-done) | copy-start | bytes 7864324
  154.7 1.9 copy-start.2
  180.1 42.3 %copy-start.6 = (f32[256,1152]{1,0:T(8,128)S(1)}, f32[256,1152]{1,0:T(8,128)}, u32[]{:S(2)}) copy-start(f32[256,1152]{1,0:T(8,128)} %get-tuple-element.57.middle_ref) | copy-start | bytes 3538948
  222.1 1.1 copy-start.5
  337.7 103.7 %all-to-all-start.1 = ((bf16[32,40,1024]{2,1,0:T(8,128)(2,1)}), bf16[32,40,1024]{2,1,0:T(8,128)(2,1)S(1)}, u32[]{:S(2)}, u32[]{:S(2)}) async-start(bf16[32,40,1024]{2,1,0:T(8,128)(2,1)} %bitcast.72), calls=%async_computation.1 | async-start | bytes 5242880 | tf_op jit(solution)/shard_map/all_to_all | solution.py:89
  441.3 2.2 copy-start.8
  443.5 1.6 copy-start.9
